TPU v7x, 32 devices: a whole 2x2x4 slice. The times are simulated.
32 devices in a mesh: dp: 8 (over z, x), seq: 4 (over y, core).
Axes of the slice: x: 2, y: 2, z: 4, core: 2. Of those that a mesh axis runs over, the one named last changes fastest.
Arguments:
- layer_input: bfloat16 [16, 2048, 1024], P('dp', 'seq'), may hold values from -6 to 6
- segment_ids: int32 [16, 2048], P('dp'), may hold values from 0 to 7, never falling along the last dimension, each value on 1 to 1024 neighbouring positions
- gain_attn: bfloat16 [1024], P(('dp', 'seq')), may hold values from 0.5 to 1.5
- w_query: bfloat16 [1024, 256], P(('dp', 'seq')), may hold values from -0.1875 to 0.1875
- w_key: bfloat16 [1024, 256], P(('dp', 'seq')), may hold values from -0.1875 to 0.1875
- w_value: bfloat16 [1024, 1024], P(('dp', 'seq')), may hold values from -0.1875 to 0.1875
- w_out: bfloat16 [1024, 1024], P(('dp', 'seq')), may hold values from -2 to 2
- gain_mlp: bfloat16 [1024], P(('dp', 'seq')), may hold values from 0.5 to 1.5
- w_gate: bfloat16 [1024, 2752], P(('dp', 'seq')), may hold values from -0.1875 to 0.1875
- w_up: bfloat16 [1024, 2752], P(('dp', 'seq')), may hold values from -0.1875 to 0.1875
- w_down: bfloat16 [2752, 1024], P(None, ('dp', 'seq')), may hold values from -0.109375 to 0.109375
- grad_output: bfloat16 [16, 2048, 1024], P('dp', 'seq'), may hold values from -6 to 6
Outputs:
- layer_output: bfloat16 [16, 2048, 1024], P('dp', 'seq')
- grad_input: float32 [16, 2048, 1024], P('dp', 'seq')
- grad_gain_attn: float32 [1024], P(('dp', 'seq'))
- grad_query: float32 [1024, 256], P(('dp', 'seq'))
- grad_key: float32 [1024, 256], P(('dp', 'seq'))
- grad_value: float32 [1024, 1024], P(('dp', 'seq'))
- grad_out: float32 [1024, 1024], P(('dp', 'seq'))
- grad_gain_mlp: float32 [1024], P(('dp', 'seq'))
- grad_gate: float32 [1024, 2752], P(('dp', 'seq'))
- grad_up: float32 [1024, 2752], P(('dp', 'seq'))
- grad_down: float32 [2752, 1024], P(None, ('dp', 'seq'))
Inputs may be any that keep to these rules, and one draw needn't show every extreme that they name: `segment_ids`: within each row the ids never fall; each document has 1 to 1024 positions, and one has exactly 1024.
All inputs are finite; a program needn't handle non-finite values.
Results may differ from a plain program's by a relative error of at most 0.0099.
Values may be sent and summed in bfloat16 or wider, within the bound.
No kernel may reach another device: no remote copies, remote signals or barrier semaphores. Data moves between devices by JAX's collectives and lax.ppermute only.
A program may use at most 256 MiB of HBM per device.

v0:
```python
import jax
import jax.numpy as jnp
from jax import lax
from jax.sharding import PartitionSpec as P

HEADS = 16
FEAT = 16
LEN = 2048
BLOCK = 512


epsilon = 1e-05
maximum_precision = lax.Precision.HIGHEST


def for_sending(array):

    def short(part):
        return part.astype(jnp.bfloat16) if part.dtype == jnp.float32 else part

    return jax.tree.map(short, array)


def across_rows(left, right):
    return lax.dot_general(
        left, right, (((0,), (0,)), ((), ())), preferred_element_type=jnp.float32
    )


def against(left, matrix):
    return lax.dot_general(
        left, matrix, (((1,), (1,)), ((), ())), preferred_element_type=jnp.float32
    )


def split_packed(packed):
    query_rows = packed[..., :FEAT]
    key_rows = packed[..., FEAT : 2 * FEAT]
    values = packed[..., 2 * FEAT :].astype(jnp.float32)
    return (query_rows, key_rows, values)


def block_terms(query_rows, key_rows, segments, begin_position):
    stop_position = begin_position + BLOCK
    scores = jnp.einsum(
        "pyg,jyg->ypj",
        query_rows[begin_position:stop_position],
        key_rows[:stop_position],
        preferred_element_type=jnp.float32,
    ) * FEAT ** (-0.5)
    q_places = begin_position + jnp.arange(BLOCK)
    k_places = jnp.arange(stop_position)
    kept_mask = (q_places[:, None] >= k_places[None, :]) & (
        segments[begin_position:stop_position][:, None] == segments[:stop_position][None, :]
    )
    weights = jnp.where(kept_mask[None], 1.0 + scores + 0.5 * scores * scores, 0.0)
    return (scores, kept_mask[None], weights)


def attend_row(pair):
    packed, segments = pair
    query_rows, key_rows, values = split_packed(packed)
    mixed_parts = []
    denom_parts = []
    for begin_position in range(0, LEN, BLOCK):
        scores, kept_mask, weights = block_terms(query_rows, key_rows, segments, begin_position)
        numerator = jnp.einsum(
            "hqk,khc->qhc", weights, values[: begin_position + BLOCK], precision=maximum_precision
        )
        denominator = jnp.sum(weights, axis=2).T
        mixed_parts.append(numerator / denominator[:, :, None])
        denom_parts.append(denominator)
    return (jnp.concatenate(mixed_parts, 0), jnp.concatenate(denom_parts, 0))


def attend_back(bundle):
    packed, segments, mixed, denominator, d_mixed = bundle
    query_rows, key_rows, values = split_packed(packed)
    complete_query_rows = query_rows.astype(jnp.float32)
    complete_key_rows = key_rows.astype(jnp.float32)
    d_mixed = d_mixed.astype(jnp.float32)
    d_numer = d_mixed / denominator[:, :, None]
    d_denom = -jnp.sum(d_mixed * mixed, axis=2) / denominator
    d_query_parts = []
    d_keys = jnp.zeros_like(complete_key_rows)
    d_values = jnp.zeros_like(values)
    for begin_position in range(0, LEN, BLOCK):
        stop_position = begin_position + BLOCK
        scores, kept_mask, weights = block_terms(query_rows, key_rows, segments, begin_position)
        d_weights = jnp.einsum(
            "qhc,khc->hqk",
            d_numer[begin_position:stop_position],
            values[:stop_position],
            precision=maximum_precision,
        )
        d_weights = jnp.where(
            kept_mask, d_weights + d_denom[begin_position:stop_position].T[:, :, None], 0.0
        )
        d_values = d_values.at[:stop_position].add(
            jnp.einsum(
                "hqk,qhc->khc",
                weights,
                d_numer[begin_position:stop_position],
                precision=maximum_precision,
            )
        )
        score_gradient = d_weights * (1.0 + scores) * FEAT ** (-0.5)
        d_query_parts.append(
            jnp.einsum(
                "ouw,wor->uor",
                score_gradient,
                complete_key_rows[:stop_position],
                precision=maximum_precision,
            )
        )
        d_keys = d_keys.at[:stop_position].add(
            jnp.einsum(
                "urs,ruw->suw",
                score_gradient,
                complete_query_rows[begin_position:stop_position],
                precision=maximum_precision,
            )
        )
    d_query = jnp.concatenate(d_query_parts, 0)
    return jnp.concatenate([d_query, d_keys, d_values], axis=2).astype(jnp.bfloat16)


def norm_forward(values):
    scale = lax.rsqrt(jnp.mean(values * values, axis=1, keepdims=True) + epsilon)
    return (scale, values * scale)


def norm_backward(d_scaled, gain, scale, normed):
    d_normed = d_scaled * gain
    return scale * (d_normed - normed * jnp.mean(d_normed * normed, axis=1, keepdims=True))


def per_device(
    layer_input,
    segment_ids,
    gain_attn,
    w_query,
    w_key,
    w_value,
    w_out,
    gain_mlp,
    w_gate,
    w_up,
    w_down,
    grad_output,
):
    rows, shard_len, width = layer_input.shape
    count = rows * shard_len
    value_dim = width // HEADS
    attn_set = (
        lax.all_gather(gain_attn, ("dp", "seq"), axis=0, tiled=True),
        lax.all_gather(w_query, ("dp", "seq"), axis=0, tiled=True),
        lax.all_gather(w_key, ("dp", "seq"), axis=0, tiled=True),
        lax.all_gather(w_value, ("dp", "seq"), axis=0, tiled=True),
        lax.all_gather(w_out, ("dp", "seq"), axis=0, tiled=True),
    )
    gain_one, query_w, key_w, value_w, out_w = attn_set
    tokens = layer_input.reshape(count, width).astype(jnp.float32)
    scale_one, normed_one = norm_forward(tokens)
    a_one = (normed_one * gain_one.astype(jnp.float32)).astype(jnp.bfloat16)
    query_rows = jnp.dot(a_one, query_w, preferred_element_type=jnp.float32).astype(jnp.bfloat16)
    key_rows = jnp.dot(a_one, key_w, preferred_element_type=jnp.float32).astype(jnp.bfloat16)
    values = jnp.dot(a_one, value_w, preferred_element_type=jnp.float32).astype(jnp.bfloat16)
    packed = jnp.concatenate(
        [
            query_rows.reshape(rows, shard_len, HEADS, FEAT),
            key_rows.reshape(rows, shard_len, HEADS, FEAT),
            values.reshape(rows, shard_len, HEADS, value_dim),
        ],
        axis=3,
    )
    by_heads = lax.all_to_all(packed, "seq", split_axis=2, concat_axis=1, tiled=True)
    mixed, denominator = lax.map(attend_row, (by_heads, segment_ids))
    mixed_seq = lax.all_to_all(
        mixed.astype(jnp.bfloat16), "seq", split_axis=1, concat_axis=2, tiled=True
    )
    mixed_cat = mixed_seq.reshape(count, width)
    x_two = tokens + jnp.dot(mixed_cat, out_w, preferred_element_type=jnp.float32)
    mlp_set = (
        lax.all_gather(gain_mlp, ("dp", "seq"), axis=0, tiled=True),
        lax.all_gather(w_gate, ("dp", "seq"), axis=0, tiled=True),
        lax.all_gather(w_up, ("dp", "seq"), axis=0, tiled=True),
        lax.all_gather(w_down, ("dp", "seq"), axis=1, tiled=True),
    )
    gain_two, gate_w, up_w, down_w = mlp_set
    scale_two, normed_two = norm_forward(x_two)
    a_two = (normed_two * gain_two.astype(jnp.float32)).astype(jnp.bfloat16)
    gate = jnp.dot(a_two, gate_w, preferred_element_type=jnp.float32)
    up_values = jnp.dot(a_two, up_w, preferred_element_type=jnp.float32)
    sigma = jax.nn.sigmoid(gate)
    silu_gate = gate * sigma
    hidden = (silu_gate * up_values).astype(jnp.bfloat16)
    result = (x_two + jnp.dot(hidden, down_w, preferred_element_type=jnp.float32)).astype(
        jnp.bfloat16
    )
    gain_two, gate_w, up_w, down_w = (
        lax.all_gather(gain_mlp, ("dp", "seq"), axis=0, tiled=True),
        lax.all_gather(w_gate, ("dp", "seq"), axis=0, tiled=True),
        lax.all_gather(w_up, ("dp", "seq"), axis=0, tiled=True),
        lax.all_gather(w_down, ("dp", "seq"), axis=1, tiled=True),
    )
    cotangent = grad_output.reshape(count, width)
    grad_down = across_rows(hidden, cotangent)
    d_hidden = against(cotangent, down_w)
    d_gate = (d_hidden * up_values * sigma * (1.0 + gate * (1.0 - sigma))).astype(jnp.bfloat16)
    d_up = (d_hidden * silu_gate).astype(jnp.bfloat16)
    grad_gate = across_rows(a_two, d_gate)
    grad_up = across_rows(a_two, d_up)
    d_a_two = against(d_gate, gate_w) + against(d_up, up_w)
    grad_gain_two = jnp.sum(d_a_two * normed_two, axis=0)
    d_x_two = cotangent.astype(jnp.float32) + norm_backward(
        d_a_two, gain_two.astype(jnp.float32), scale_two, normed_two
    )
    mlp_sums = (
        lax.psum_scatter(grad_gain_two, ("dp", "seq"), scatter_dimension=0, tiled=True),
        lax.psum_scatter(grad_gate, ("dp", "seq"), scatter_dimension=0, tiled=True),
        lax.psum_scatter(grad_up, ("dp", "seq"), scatter_dimension=0, tiled=True),
        lax.psum_scatter(grad_down, ("dp", "seq"), scatter_dimension=1, tiled=True),
    )
    gain_one, query_w, key_w, value_w, out_w = (
        lax.all_gather(gain_attn, ("dp", "seq"), axis=0, tiled=True),
        lax.all_gather(w_query, ("dp", "seq"), axis=0, tiled=True),
        lax.all_gather(w_key, ("dp", "seq"), axis=0, tiled=True),
        lax.all_gather(w_value, ("dp", "seq"), axis=0, tiled=True),
        lax.all_gather(w_out, ("dp", "seq"), axis=0, tiled=True),
    )
    d_branch = d_x_two.astype(jnp.bfloat16)
    grad_out = across_rows(mixed_cat, d_branch)
    d_mixed = (
        against(d_branch, out_w).astype(jnp.bfloat16).reshape(rows, shard_len, HEADS, value_dim)
    )
    d_mixed_heads = lax.all_to_all(d_mixed, "seq", split_axis=2, concat_axis=1, tiled=True)
    d_packed = lax.map(attend_back, (by_heads, segment_ids, mixed, denominator, d_mixed_heads))
    d_packed_seq = jax.tree.map(
        lambda part, own: part.astype(own.dtype),
        lax.all_to_all(for_sending(d_packed), "seq", split_axis=1, concat_axis=2, tiled=True),
        d_packed,
    )
    d_query = d_packed_seq[..., :FEAT].reshape(count, HEADS * FEAT)
    d_keys = d_packed_seq[..., FEAT : 2 * FEAT].reshape(count, HEADS * FEAT)
    d_values = d_packed_seq[..., 2 * FEAT :].reshape(count, width)
    grad_query = across_rows(a_one, d_query)
    grad_key = across_rows(a_one, d_keys)
    grad_value = across_rows(a_one, d_values)
    d_a_one = against(d_query, query_w) + against(d_keys, key_w) + against(d_values, value_w)
    grad_gain_one = jnp.sum(d_a_one * normed_one, axis=0)
    d_tokens = d_x_two + norm_backward(d_a_one, gain_one.astype(jnp.float32), scale_one, normed_one)
    attn_sums = (
        lax.psum_scatter(grad_gain_one, ("dp", "seq"), scatter_dimension=0, tiled=True),
        lax.psum_scatter(grad_query, ("dp", "seq"), scatter_dimension=0, tiled=True),
        lax.psum_scatter(grad_key, ("dp", "seq"), scatter_dimension=0, tiled=True),
        lax.psum_scatter(grad_value, ("dp", "seq"), scatter_dimension=0, tiled=True),
        lax.psum_scatter(grad_out, ("dp", "seq"), scatter_dimension=0, tiled=True),
    )
    return (
        result.reshape(rows, shard_len, width),
        d_tokens.reshape(rows, shard_len, width),
        attn_sums[0],
        attn_sums[1],
        attn_sums[2],
        attn_sums[3],
        attn_sums[4],
        mlp_sums[0],
        mlp_sums[1],
        mlp_sums[2],
        mlp_sums[3],
    )


def solution(mesh):
    placed = (
        P("dp", "seq", None),
        P("dp", None),
        P(("dp", "seq")),
        P(("dp", "seq"), None),
        P(("dp", "seq"), None),
        P(("dp", "seq"), None),
        P(("dp", "seq"), None),
        P(("dp", "seq")),
        P(("dp", "seq"), None),
        P(("dp", "seq"), None),
        P(None, ("dp", "seq")),
        P("dp", "seq", None),
    )
    return jax.shard_map(
        per_device,
        mesh=mesh,
        in_specs=placed,
        out_specs=(
            P("dp", "seq", None),
            P("dp", "seq", None),
            P(("dp", "seq")),
            P(("dp", "seq"), None),
            P(("dp", "seq"), None),
            P(("dp", "seq"), None),
            P(("dp", "seq"), None),
            P(("dp", "seq")),
            P(("dp", "seq"), None),
            P(("dp", "seq"), None),
            P(None, ("dp", "seq")),
        ),
        check_vma=False,
    )
```

profile of v0, /device:TPU:0, one launch (start us, length us, event | category | flops | bytes accessed | tf_op | source)
XLA Modules:
  0.0 1945.8 jit_solution(10871861632818804791)
XLA Ops:
  11.7 42.1 %all-reduce.7 = (bf16[1024]{0:T(1024)(128)(2,1)S(1)}, bf16[1024]{0:T(1024)(128)(2,1)}) all-reduce(bf16[1024]{0:T(1024)(128)(2,1)S(1)} %dynamic-update-slice.40, bf16[1024]{0:T(1024)(128)(2,1)S(1)} %dynamic-update-slice.41), channel_id=1, replica_groups=mesh['dp'=8,'seq'=4] {'dp','seq'}, use_global_device_ids=true, to_apply=%add.2 | all-reduce | flops 2048 | bytes 8192
  56.7 42.3 %all_gather.38 = bf16[1024,256]{1,0:T(8,128)(2,1)S(1)} all-gather(bf16[32,256]{1,0:T(8,128)(2,1)} %param.40), channel_id=1, replica_groups=mesh['dp'=8,'seq'=4] {'dp','seq'}, dimensions={0}, use_global_device_ids=true | all-gather | bytes 540672 | tf_op jit(solution)/shard_map/all_gather | solution.py:158
  102.4 38.6 %all_gather.37 = bf16[1024,256]{1,0:T(8,128)(2,1)S(1)} all-gather(bf16[32,256]{1,0:T(8,128)(2,1)S(1)} %copy-done.39), channel_id=1, replica_groups=mesh['dp'=8,'seq'=4] {'dp','seq'}, dimensions={0}, use_global_device_ids=true | all-gather | bytes 540672 | tf_op jit(solution)/shard_map/all_gather | solution.py:157
  159.4 13.2 pad_maximum_fusion
  176.9 45.5 %all-to-all-done = bf16[2,512,16,96]{1,0,3,2:T(2,128)(2,1)S(1)} async-done(((bf16[2,512,16,96]{1,0,3,2:T(2,128)(2,1)}), bf16[2,512,16,96]{1,0,3,2:T(2,128)(2,1)S(1)}, u32[]{:S(2)}, u32[]{:S(2)}) %all-to-all-start) | async-done | bytes 3145760 | tf_op jit(solution)/shard_map/all_to_all | solution.py:177
  232.7 140.7 %while.38 = (s32[]{:T(128)}, f32[2,2048,4,64]{1,3,2,0:T(8,128)}, f32[2,2048,4]{1,2,0:T(4,128)S(1)}, bf16[2,2048,4,96]{1,3,2,0:T(8,128)(2,1)}, s32[2,2048]{1,0:T(...) while((s32[]{:T(128)}, f32[2,2048,4,64]{1,3,2,0:T(8,128)}, f32[2,2048,4]{1,2,0:T(4,128)S(1)}, ...), condition=%wide.region_6.7_spmd, body=%wide.region_1.6_spmd.sunk | while | flops 8516027904 | bytes 137717984 | solution.py:178
  291.5 16.0 fusion.376
  346.6 16.0 fusion.376
  390.4 25.6 %all-to-all-done.1 = bf16[4,2,131072]{2,1,0:T(2,128)(2,1)S(1)} async-done(((bf16[4,2,131072]{2,1,0:T(2,128)(2,1)}), bf16[4,2,131072]{2,1,0:T(2,128)(2,1)S(1)}, u32[]{:S(2)}, u32[]{:S(2)}) %all-to-all-start.1) | async-done | bytes 2097184 | tf_op jit(solution)/shard_map/all_to_all | solution.py:179
  442.2 12.1 fusion.230
  465.7 21.1 %multiply_convert_fusion = (bf16[1024,2752]{0,1:T(8,128)(2,1)}, bf16[1024,2752]{0,1:T(8,128)(2,1)S(1)}, bf16[1024,2752]{0,1:T(8,128)(2,1)}) fusion(f32[1024,2752]{0,1:T(8,128)} %fusion.229, f32[1024,2752]{0,1:T(8,128)} %fusion.230, bf16[1024,1024]{1,0:T(8,128)(2,1)} %bitcast.372, bf16[2752,1024]{0,1:T(8,128)(2,1)} %all-gather.14.cloned.1.call-done), kind=kOutput, calls=%fused_computation.237 | convolution fusion | flops 5813633024 | bytes 47185920 | tf_op jit(solution)/shard_map/dot_general | solution.py:31
  494.6 12.5 multiply_reduce_fusion
  523.5 25.7 %all-to-all-done.2 = bf16[2,512,16,64]{1,0,3,2:T(2,128)(2,1)S(1)} async-done(((bf16[2,512,16,64]{1,0,3,2:T(2,128)(2,1)}), bf16[2,512,16,64]{1,0,3,2:T(2,128)(2,1)S(1)}, u32[]{:S(2)}, u32[]{:S(2)}) %all-to-all-start.2) | async-done | bytes 2097184 | tf_op jit(solution)/shard_map/all_to_all | solution.py:237
  556.6 300.5 %while.39 = (s32[]{:T(128)}, bf16[2,2048,4,96]{1,3,2,0:T(8,128)(2,1)}, bf16[2,2048,4,96]{1,3,2,0:T(8,128)(2,1)}, s32[2,2048]{1,0:T(2,128)S(1)}, bf16[2,2048,4,64...) while((s32[]{:T(128)}, ...), condition=%wide.region_11.12_spmd, body=%wide.region_9.11_spmd.sunk | while | flops 20612556800 | bytes 472771200 | solution.py:238
  606.4 13.0 fusion.438
  649.1 16.5 fusion.441
  665.6 17.4 multiply_multiply_fusion.11
  752.6 12.9 fusion.438
  795.0 16.7 fusion.441
  811.8 17.4 multiply_multiply_fusion.11
  871.3 46.3 %all-to-all-done.3 = bf16[2,2048,4,96]{3,2,0,1:T(4,128)(2,1)} async-done(((bf16[2,2048,4,96]{3,2,0,1:T(4,128)(2,1)}), bf16[2,2048,4,96]{3,2,0,1:T(4,128)(2,1)}, u32[]{:S(2)}, u32[]{:S(2)}) %all-to-all-start.3) | async-done | bytes 3145760 | tf_op jit(solution)/shard_map/all_to_all | solution.py:241
  950.3 12.0 fusion.238
  962.4 11.9 fusion.237
  974.4 12.0 fusion.239
  986.5 11.6 add_convert_fusion
  1006.2 37.1 %all-reduce.6 = (f32[1024]{0:T(1024)S(1)}, f32[1024]{0:T(1024)S(1)}) all-reduce(f32[1024]{0:T(1024)S(1)} %get-tuple-element.342, f32[1024]{0:T(1024)S(1)} %copy-done.41), channel_id=2, replica_groups=mesh['dp'=8,'seq'=4] {'dp','seq'}, use_global_device_ids=true, to_apply=%region_14.15.clone | all-reduce | flops 2048 | bytes 16384
  1061.0 133.6 %reduce-scatter.10.cloned.1.call-done = f32[32,256]{1,0:T(8,128)} async-done(((f32[1024,256]{1,0:T(8,128)}), f32[32,256]{1,0:T(8,128)}) %reduce-scatter.10.cloned.1.call-update) | async-done | bytes 32784 | tf_op jit(solution)/shard_map/reduce_scatter | solution.py:256
  1194.6 139.6 %reduce-scatter.14.cloned.1.call-done = f32[32,1024]{1,0:T(8,128)} async-done(((f32[1024,1024]{1,0:T(8,128)}), f32[32,1024]{1,0:T(8,128)}) %reduce-scatter.14.cloned.1.call-update) | async-done | bytes 131088 | tf_op jit(solution)/shard_map/reduce_scatter | solution.py:258
  1334.2 139.5 %reduce-scatter.12.cloned.1.call-done = f32[32,1024]{1,0:T(8,128)} async-done(((f32[1024,1024]{1,0:T(8,128)}), f32[32,1024]{1,0:T(8,128)}) %reduce-scatter.12.cloned.1.call-update) | async-done | bytes 131088 | tf_op jit(solution)/shard_map/reduce_scatter | solution.py:257
  1473.7 153.7 %reduce-scatter.18.cloned.1.call-done = f32[32,2752]{1,0:T(8,128)} async-done(((f32[1024,2752]{1,0:T(8,128)}), f32[32,2752]{1,0:T(8,128)}) %reduce-scatter.18.cloned.1.call-update) | async-done | bytes 352272 | tf_op jit(solution)/shard_map/reduce_scatter | solution.py:222
  1627.4 155.7 %reduce-scatter.16.cloned.1.call-done = f32[32,2752]{1,0:T(8,128)} async-done(((f32[1024,2752]{1,0:T(8,128)}), f32[32,2752]{1,0:T(8,128)}) %reduce-scatter.16.cloned.1.call-update) | async-done | bytes 352272 | tf_op jit(solution)/shard_map/reduce_scatter | solution.py:221
  1783.1 155.6 %reduce-scatter.20.cloned.1.call-done = f32[2752,32]{0,1:T(8,128)} async-done(((f32[2752,1024]{0,1:T(8,128)}), f32[2752,32]{0,1:T(8,128)}) %reduce-scatter.20.cloned.1.call-update) | async-done | bytes 352272 | tf_op jit(solution)/shard_map/reduce_scatter | solution.py:223
  (340 shorter events, 477.2 us)
Async XLA Ops:
  7.2 91.8 %copy-start.8 = (bf16[2,512,1024]{2,1,0:T(8,128)(2,1)S(1)}, bf16[2,512,1024]{2,1,0:T(8,128)(2,1)}, u32[]{:S(2)}) copy-start(bf16[2,512,1024]{2,1,0:T(8,128)(2,1)} %param.36) | copy-start | bytes 6291460
  7.2 139.6 %all-gather.6.cloned.1.call-start = ((), (), s32[]{:S(2)}) async-start(), calls=%async_computation.11 | async-start | bytes 2162688 | tf_op jit(solution)/shard_map/all_gather | solution.py:159
  7.9 426.9 %all-gather.8.cloned.1.call-start = ((), (), s32[]{:S(2)}) async-start(), calls=%async_computation.12 | async-start | bytes 2162688 | tf_op jit(solution)/shard_map/all_gather | solution.py:160
  8.7 433.5 %all-gather.12.cloned.1.call-start = ((), (), s32[]{:S(2)}) async-start(), calls=%async_computation.14 | async-start | bytes 5947392 | tf_op jit(solution)/shard_map/all_gather | solution.py:187
  9.4 444.9 %all-gather.10.cloned.1.call-start = ((), (), s32[]{:S(2)}) async-start(), calls=%async_computation.13 | async-start | bytes 5947392 | tf_op jit(solution)/shard_map/all_gather | solution.py:186
  53.7 45.8 %copy-start.35 = (f32[1024]{0:T(1024)}, f32[1024]{0:T(1024)S(1)}, u32[]{:S(2)}) copy-start(f32[1024]{0:T(1024)S(1)} %convert_element_type.95) | copy-start | bytes 12292
  56.7 42.9 %copy-start.37 = (f32[1,4,2,128]{3,1,2,0:T(4,128)}, f32[1,4,2,128]{3,1,2,0:T(4,128)S(1)}, u32[]{:S(2)}) copy-start(f32[1,4,2,128]{3,1,2,0:T(4,128)S(1)} %copy.82) | copy-start | bytes 12292
  172.6 49.9 %all-to-all-start = ((bf16[2,512,16,96]{1,0,3,2:T(2,128)(2,1)}), bf16[2,512,16,96]{1,0,3,2:T(2,128)(2,1)S(1)}, u32[]{:S(2)}, u32[]{:S(2)}) async-start(bf16[2,512,16,96]{1,0,3,2:T(2,128)(2,1)} %pad_maximum_fusion), calls=%async_computation | async-start | bytes 6291456 | tf_op jit(solution)/shard_map/all_to_all | solution.py:177
  176.3 289.4 %all-gather.14.cloned.1.call-start = ((), (), s32[]{:S(2)}) async-start(), calls=%async_computation.15 | async-start | bytes 5947392 | tf_op jit(solution)/shard_map/all_gather | solution.py:188
  291.5 16.0 copy-start.11
  346.6 16.0 copy-start.11
  386.7 29.3 %all-to-all-start.1 = ((bf16[4,2,131072]{2,1,0:T(2,128)(2,1)}), bf16[4,2,131072]{2,1,0:T(2,128)(2,1)S(1)}, u32[]{:S(2)}, u32[]{:S(2)}) async-start(bf16[4,2,131072]{2,1,0:T(2,128)(2,1)} %reshape.962), calls=%async_computation.1 | async-start | bytes 4194304 | tf_op jit(solution)/shard_map/all_to_all | solution.py:179
  420.0 14.9 copy-start.9
  442.1 12.2 copy-start.27
  465.7 21.1 %copy-start.43 = (bf16[1024,2752]{1,0:T(8,128)(2,1)S(1)}, bf16[1024,2752]{1,0:T(8,128)(2,1)}, u32[]{:S(2)}) copy-start(bf16[1024,2752]{1,0:T(8,128)(2,1)} %all-gather.10.cloned.1.call-done) | copy-start | bytes 16908292
  494.6 12.5 copy-start.32
  519.9 29.3 %all-to-all-start.2 = ((bf16[2,512,16,64]{1,0,3,2:T(2,128)(2,1)}), bf16[2,512,16,64]{1,0,3,2:T(2,128)(2,1)S(1)}, u32[]{:S(2)}, u32[]{:S(2)}) async-start(bf16[2,512,16,64]{1,0,3,2:T(2,128)(2,1)} %reshape.949), calls=%async_computation.2 | async-start | bytes 4194304 | tf_op jit(solution)/shard_map/all_to_all | solution.py:237
  565.1 39.4 %copy-start.2 = (bf16[2048,4,96]{0,2,1:T(8,128)(2,1)}, bf16[2048,4,96]{0,2,1:T(8,128)(2,1)S(1)}, u32[]{:S(2)}) copy-start(bf16[2048,4,96]{0,2,1:T(8,128)(2,1)S(1)} %dynamic-slice_bitcast_fusion.7) | copy-start | bytes 4718596 | tf_op jit(solution)/shard_map/while
  567.3 39.2 %copy-start.4 = (f32[2048,4,64]{0,2,1:T(8,128)}, f32[2048,4,64]{0,2,1:T(8,128)S(1)}, u32[]{:S(2)}) copy-start(f32[2048,4,64]{0,2,1:T(8,128)S(1)} %convert_divide_fusion.2) | copy-start | bytes 6291460 | tf_op jit(solution)/shard_map/while
  682.9 10.5 copy-start
  711.3 39.4 %copy-start.2 = (bf16[2048,4,96]{0,2,1:T(8,128)(2,1)}, bf16[2048,4,96]{0,2,1:T(8,128)(2,1)S(1)}, u32[]{:S(2)}) copy-start(bf16[2048,4,96]{0,2,1:T(8,128)(2,1)S(1)} %dynamic-slice_bitcast_fusion.7) | copy-start | bytes 4718596 | tf_op jit(solution)/shard_map/while
  713.4 39.2 %copy-start.4 = (f32[2048,4,64]{0,2,1:T(8,128)}, f32[2048,4,64]{0,2,1:T(8,128)S(1)}, u32[]{:S(2)}) copy-start(f32[2048,4,64]{0,2,1:T(8,128)S(1)} %convert_divide_fusion.2) | copy-start | bytes 6291460 | tf_op jit(solution)/shard_map/while
  829.1 10.5 copy-start
  864.3 53.2 %all-to-all-start.3 = ((bf16[2,2048,4,96]{3,2,0,1:T(4,128)(2,1)}), bf16[2,2048,4,96]{3,2,0,1:T(4,128)(2,1)}, u32[]{:S(2)}, u32[]{:S(2)}) async-start(bf16[2,2048,4,96]{3,2,0,1:T(4,128)(2,1)} %copy.73), calls=%async_computation.3 | async-start | bytes 8388608 | tf_op jit(solution)/shard_map/all_to_all | solution.py:241
  869.3 191.7 %reduce-scatter.8.cloned.1.call-start = ((), (), s32[]{:S(2)}) async-start(), calls=%async_computation.16 | async-start | bytes 1081344 | tf_op jit(solution)/shard_map/reduce_scatter | solution.py:255
  928.5 266.0 %reduce-scatter.10.cloned.1.call-start = ((), (), s32[]{:S(2)}) async-start(), calls=%async_computation.17 | async-start | bytes 1081344 | tf_op jit(solution)/shard_map/reduce_scatter | solution.py:256
  932.7 401.5 %reduce-scatter.14.cloned.1.call-start = ((), (), s32[]{:S(2)}) async-start(), calls=%async_computation.19 | async-start | bytes 4325376 | tf_op jit(solution)/shard_map/reduce_scatter | solution.py:258
  939.9 533.8 %reduce-scatter.12.cloned.1.call-start = ((), (), s32[]{:S(2)}) async-start(), calls=%async_computation.18 | async-start | bytes 4325376 | tf_op jit(solution)/shard_map/reduce_scatter | solution.py:257
  950.3 677.2 %reduce-scatter.18.cloned.1.call-start = ((), (), s32[]{:S(2)}) async-start(), calls=%async_computation.21 | async-start | bytes 11894784 | tf_op jit(solution)/shard_map/reduce_scatter | solution.py:222
  962.4 820.7 %reduce-scatter.16.cloned.1.call-start = ((), (), s32[]{:S(2)}) async-start(), calls=%async_computation.20 | async-start | bytes 11894784 | tf_op jit(solution)/shard_map/reduce_scatter | solution.py:221
  974.4 964.3 %reduce-scatter.20.cloned.1.call-start = ((), (), s32[]{:S(2)}) async-start(), calls=%async_computation.22 | async-start | bytes 11894784 | tf_op jit(solution)/shard_map/reduce_scatter | solution.py:223
  986.5 11.6 copy-start.26
  (47 other events, 242.6 us)
Sparse Core Ops, SparseCore 0:
  10.9 59.4 all-gather.5
  73.2 55.8 all-gather.7
  132.0 76.8 all-gather.11
  211.6 65.9 all-gather.9
  280.3 66.2 all-gather.13
  928.7 132.2 reduce-scatter.7
  1063.9 130.6 reduce-scatter.9
  1197.4 136.7 reduce-scatter.13
  1337.0 136.6 reduce-scatter.11
  1476.4 150.9 reduce-scatter.17
  1630.3 152.7 reduce-scatter.15
  1785.9 152.7 reduce-scatter.19
where the time goes:
time: 1960 us; the launch traced here: 1950 us
  waiting for transfers between devices  1030 us (53%)
  matrix products  500 us (26%)
  blocking collectives  160 us (8%)
  local copies, waits for them, and re-layouts  125 us (6%)
  other arithmetic  53.9 us (3%)
  loops' own time  40.4 us (2%)
    reduce_scatter x1, waiting for transfers between devices, per_device(): lax.psum_scatter(grad_gate, ('dp', 'seq'), scatter_dimension=0, tiled=True)  156 us
    reduce_scatter x1, waiting for transfers between devices, per_device(): lax.psum_scatter(grad_down, ('dp', 'seq'), scatter_dimension=1, tiled=True)  156 us
    reduce_scatter x1, waiting for transfers between devices, per_device(): lax.psum_scatter(grad_up, ('dp', 'seq'), scatter_dimension=0, tiled=True)  154 us
    reduce_scatter x1, waiting for transfers between devices, per_device(): lax.psum_scatter(grad_out, ('dp', 'seq'), scatter_dimension=0, tiled=True)  140 us
    reduce_scatter x1, waiting for transfers between devices, per_device(): lax.psum_scatter(grad_value, ('dp', 'seq'), scatter_dimension=0, tiled=True)  140 us
    reduce_scatter x1, waiting for transfers between devices, per_device(): lax.psum_scatter(grad_key, ('dp', 'seq'), scatter_dimension=0, tiled=True)  134 us
    dot_general x8, matrix products, attend_back(): jnp.einsum('hqk,qhc->khc', weights, d_numer[begin_position:stop_position]...  85.2 us
    unnamed x2, blocking collectives  79.2 us
  transfers between devices with their start and end apart: 16, of which 11 were waited for; matrix products, arithmetic and copies ran while one was open for 15% of the time, Pallas kernels for 0%

commit v1 on v0

--- a/solution.py
+++ b/solution.py
@@ -1,6 +1,11 @@
+import functools
+
 import jax
 import jax.numpy as jnp
+import numpy as np
 from jax import lax
+from jax.experimental import pallas as pl
+from jax.experimental.pallas import tpu as pltpu
 from jax.sharding import PartitionSpec as P
 
 HEADS = 16
@@ -11,14 +16,6 @@
 
 epsilon = 1e-05
 maximum_precision = lax.Precision.HIGHEST
-
-
-def for_sending(array):
-
-    def short(part):
-        return part.astype(jnp.bfloat16) if part.dtype == jnp.float32 else part
-
-    return jax.tree.map(short, array)
 
 
 def across_rows(left, right):
@@ -135,7 +132,174 @@
     return scale * (d_normed - normed * jnp.mean(d_normed * normed, axis=1, keepdims=True))
 
 
+def fold(count):
+    return [0] + list(range(1, count, 2)) + list(range(2, count, 2))[::-1]
+
+
+class Line:
+    def __init__(self, axis, axis_size, stride, count):
+        self.axis, self.stride, self.count = axis, stride, count
+        self.order = fold(count)
+        self.pairs = []
+        for index in range(axis_size):
+            place = (index // stride) % count
+            ring = self.order.index(place)
+            goal = self.order[(ring + 1) % count]
+            self.pairs.append((index, index + (goal - place) * stride))
+
+    def send(self, array):
+        return lax.ppermute(array, self.axis, self.pairs)
+
+    def place_back(self, steps):
+        own = (lax.axis_index(self.axis) // self.stride) % self.count
+        rank = jnp.asarray([self.order.index(p) for p in range(self.count)], jnp.int32)[own]
+        return jnp.asarray(self.order, jnp.int32)[(rank - steps) % self.count]
+
+
+class Slice:
+    def __init__(self, dp, seq):
+        self.dp, self.seq, self.devices = dp, seq, dp * seq
+        self.lines = {
+            "z": Line("dp", dp, 2, dp // 2),
+            "x": Line("dp", dp, 1, 2),
+            "y": Line("seq", seq, 2, seq // 2),
+            "c": Line("seq", seq, 1, 2),
+        }
+
+    def device_of(self, back):
+        at = {d: self.lines[d].place_back(back[d]) for d in "zxyc"}
+        return ((at["z"] * 2 + at["x"]) * (self.seq // 2) + at["y"]) * 2 + at["c"]
+
+
+def assemble(pieces, places, block, devices):
+    columns = pieces[0].shape[1]
+    counts = [piece.shape[0] // block for piece in pieces]
+
+    def kernel(places_ref, *refs):
+        piece_refs, out_ref, held, in_sems, out_sems = (
+            refs[: len(pieces)],
+            *refs[len(pieces) :],
+        )
+        loads, begin = [], 0
+        for number, piece_ref in enumerate(piece_refs):
+            rows = counts[number] * block
+            load = pltpu.make_async_copy(
+                piece_ref, held.at[pl.ds(begin * block, rows)], in_sems.at[number]
+            )
+            load.start()
+            loads.append(load)
+            begin += counts[number]
+        stores, begin = [], 0
+        for number, load in enumerate(loads):
+            load.wait()
+            for i in range(begin, begin + counts[number]):
+                to = pl.multiple_of(places_ref[i] * block, block)
+                store = pltpu.make_async_copy(
+                    held.at[pl.ds(i * block, block)], out_ref.at[pl.ds(to, block)], out_sems.at[i]
+                )
+                store.start()
+                stores.append(store)
+            begin += counts[number]
+        for store in stores:
+            store.wait()
+
+    size = devices * block * columns * pieces[0].dtype.itemsize
+    return pl.pallas_call(
+        kernel,
+        out_shape=jax.ShapeDtypeStruct((devices * block, columns), pieces[0].dtype),
+        in_specs=[pl.BlockSpec(memory_space=pltpu.SMEM)]
+        + [pl.BlockSpec(memory_space=pl.ANY)] * len(pieces),
+        out_specs=pl.BlockSpec(memory_space=pl.ANY),
+        scratch_shapes=[
+            pltpu.VMEM((devices * block, columns), pieces[0].dtype),
+            pltpu.SemaphoreType.DMA((len(pieces),)),
+            pltpu.SemaphoreType.DMA((devices,)),
+        ],
+        cost_estimate=pl.CostEstimate(flops=0, bytes_accessed=2 * size, transcendentals=0),
+        name="assemble",
+    )(places, *pieces)
+
+
+def gather_rows(part, shape, route):
+    block, columns = part.shape
+    if block % 16:
+        return lax.all_gather(part, ("dp", "seq"), axis=0, tiled=True)
+    held = [(part, [dict(z=0, x=0, y=0, c=0)])]
+    for dim in route:
+        if len(held) > 1 and sum(len(names) for _, names in held) <= 4:
+            held = [
+                (jnp.concatenate([a for a, _ in held], 0), [n for _, names in held for n in names])
+            ]
+        came = []
+        for array, names in held:
+            for step in range(1, shape.lines[dim].count):
+                array = shape.lines[dim].send(array)
+                came.append((array, [dict(n, **{dim: step}) for n in names]))
+        held = held + came
+    places = jnp.stack([shape.device_of(n) for _, names in held for n in names])
+    return assemble([a for a, _ in held], places, block, shape.devices)
+
+
+def column_order(shape, width, route):
+    block = width // shape.devices
+    names = [dict()]
+    for dim in route:
+        names = [dict(n, **{dim: s}) for n in names for s in range(shape.lines[dim].count)]
+    places = jnp.stack([shape.device_of(n) for n in names])
+    return (places[:, None] * block + jnp.arange(block)[None, :]).reshape(width)
+
+
+def reorder(left, order):
+    width = left.shape[1]
+    pick = (jnp.arange(width)[:, None] == order[None, :]).astype(jnp.bfloat16)
+    return jnp.dot(left, pick, preferred_element_type=jnp.float32).astype(jnp.bfloat16)
+
+
+def scatter_rows(left, right, shape, route):
+    width = left.shape[1]
+    if (width // shape.devices) % 16:
+        return lax.psum_scatter(
+            across_rows(left, right), ("dp", "seq"), scatter_dimension=0, tiled=True
+        )
+    left = reorder(left, column_order(shape, width, route))
+    first, second = (shape.lines[d] for d in route[:2])
+    half = width // first.count
+    came = None
+    for step in range(1, first.count):
+        term = across_rows(left[:, step * half : (step + 1) * half], right)
+        term = term if came is None else term + came.astype(jnp.float32)
+        came = first.send(term.astype(jnp.bfloat16))
+    rows = half // second.count
+    arrived, came = came, None
+
+    def term_of(step):
+        low, high = step * rows, (step + 1) * rows
+        return across_rows(left[:, low:high], right) + arrived[low:high].astype(jnp.float32)
+
+    for step in range(1, second.count):
+        term = term_of(step)
+        term = term if came is None else term + came.astype(jnp.float32)
+        came = second.send(term.astype(jnp.bfloat16))
+    total = term_of(0) + came.astype(jnp.float32)
+    for dim in route[2:]:
+        line = shape.lines[dim]
+        rows = total.shape[0] // line.count
+        came = None
+        for step in range(1, line.count):
+            term = total[step * rows : (step + 1) * rows]
+            term = term if came is None else term + came.astype(jnp.float32)
+            came = line.send(term.astype(jnp.bfloat16))
+        total = total[:rows] + came.astype(jnp.float32)
+    return total
+
+
+def gain_gradient(weights, gradients, gain):
+    products = jnp.sum(weights.astype(jnp.float32) * gradients, axis=1)
+    return products / gain.astype(jnp.float32)
+
+
 def per_device(
+    shape,
     layer_input,
     segment_ids,
     gain_attn,
@@ -152,25 +316,29 @@
     rows, shard_len, width = layer_input.shape
     count = rows * shard_len
     value_dim = width // HEADS
-    attn_set = (
-        lax.all_gather(gain_attn, ("dp", "seq"), axis=0, tiled=True),
-        lax.all_gather(w_query, ("dp", "seq"), axis=0, tiled=True),
-        lax.all_gather(w_key, ("dp", "seq"), axis=0, tiled=True),
-        lax.all_gather(w_value, ("dp", "seq"), axis=0, tiled=True),
-        lax.all_gather(w_out, ("dp", "seq"), axis=0, tiled=True),
-    )
-    gain_one, query_w, key_w, value_w, out_w = attn_set
+    features = HEADS * FEAT
+    qkv_part = jnp.concatenate([w_query, w_key, w_value], axis=1)
+    down_part = w_down.T
+    gains = jnp.stack([gain_attn, gain_mlp], axis=1)
+    gains = jnp.pad(gains, ((0, 0), (0, 126)))
+    head = gather_rows(jnp.concatenate([qkv_part, gains], axis=1), shape, "zxyc")
+    qkv_w = head[:, : 2 * features + width]
+    gain_one = head[:, 2 * features + width].astype(jnp.float32)
+    gain_two = head[:, 2 * features + width + 1].astype(jnp.float32)
+    out_w = gather_rows(w_out, shape, "xyzc")
+    gate_w = gather_rows(w_gate, shape, "zxyc")
+    up_w = gather_rows(w_up, shape, "zyxc")
+    down_w = gather_rows(down_part, shape, "xyzc")
+
     tokens = layer_input.reshape(count, width).astype(jnp.float32)
     scale_one, normed_one = norm_forward(tokens)
-    a_one = (normed_one * gain_one.astype(jnp.float32)).astype(jnp.bfloat16)
-    query_rows = jnp.dot(a_one, query_w, preferred_element_type=jnp.float32).astype(jnp.bfloat16)
-    key_rows = jnp.dot(a_one, key_w, preferred_element_type=jnp.float32).astype(jnp.bfloat16)
-    values = jnp.dot(a_one, value_w, preferred_element_type=jnp.float32).astype(jnp.bfloat16)
+    a_one = (normed_one * gain_one).astype(jnp.bfloat16)
+    qkv = jnp.dot(a_one, qkv_w, preferred_element_type=jnp.float32).astype(jnp.bfloat16)
     packed = jnp.concatenate(
         [
-            query_rows.reshape(rows, shard_len, HEADS, FEAT),
-            key_rows.reshape(rows, shard_len, HEADS, FEAT),
-            values.reshape(rows, shard_len, HEADS, value_dim),
+            qkv[:, :features].reshape(rows, shard_len, HEADS, FEAT),
+            qkv[:, features : 2 * features].reshape(rows, shard_len, HEADS, FEAT),
+            qkv[:, 2 * features :].reshape(rows, shard_len, HEADS, value_dim),
         ],
         axis=3,
     )
@@ -181,94 +349,61 @@
     )
     mixed_cat = mixed_seq.reshape(count, width)
     x_two = tokens + jnp.dot(mixed_cat, out_w, preferred_element_type=jnp.float32)
-    mlp_set = (
-        lax.all_gather(gain_mlp, ("dp", "seq"), axis=0, tiled=True),
-        lax.all_gather(w_gate, ("dp", "seq"), axis=0, tiled=True),
-        lax.all_gather(w_up, ("dp", "seq"), axis=0, tiled=True),
-        lax.all_gather(w_down, ("dp", "seq"), axis=1, tiled=True),
-    )
-    gain_two, gate_w, up_w, down_w = mlp_set
     scale_two, normed_two = norm_forward(x_two)
-    a_two = (normed_two * gain_two.astype(jnp.float32)).astype(jnp.bfloat16)
+    a_two = (normed_two * gain_two).astype(jnp.bfloat16)
     gate = jnp.dot(a_two, gate_w, preferred_element_type=jnp.float32)
     up_values = jnp.dot(a_two, up_w, preferred_element_type=jnp.float32)
     sigma = jax.nn.sigmoid(gate)
     silu_gate = gate * sigma
     hidden = (silu_gate * up_values).astype(jnp.bfloat16)
-    result = (x_two + jnp.dot(hidden, down_w, preferred_element_type=jnp.float32)).astype(
-        jnp.bfloat16
-    )
-    gain_two, gate_w, up_w, down_w = (
-        lax.all_gather(gain_mlp, ("dp", "seq"), axis=0, tiled=True),
-        lax.all_gather(w_gate, ("dp", "seq"), axis=0, tiled=True),
-        lax.all_gather(w_up, ("dp", "seq"), axis=0, tiled=True),
-        lax.all_gather(w_down, ("dp", "seq"), axis=1, tiled=True),
-    )
+    result = (x_two + against(hidden, down_w)).astype(jnp.bfloat16)
+
     cotangent = grad_output.reshape(count, width)
-    grad_down = across_rows(hidden, cotangent)
-    d_hidden = against(cotangent, down_w)
+    grad_down = scatter_rows(cotangent, hidden, shape, "czxy")
+    d_hidden = jnp.dot(cotangent, down_w, preferred_element_type=jnp.float32)
     d_gate = (d_hidden * up_values * sigma * (1.0 + gate * (1.0 - sigma))).astype(jnp.bfloat16)
     d_up = (d_hidden * silu_gate).astype(jnp.bfloat16)
-    grad_gate = across_rows(a_two, d_gate)
-    grad_up = across_rows(a_two, d_up)
+    grad_gate = scatter_rows(a_two, d_gate, shape, "cyxz")
+    grad_up = scatter_rows(a_two, d_up, shape, "cxyz")
     d_a_two = against(d_gate, gate_w) + against(d_up, up_w)
-    grad_gain_two = jnp.sum(d_a_two * normed_two, axis=0)
     d_x_two = cotangent.astype(jnp.float32) + norm_backward(
-        d_a_two, gain_two.astype(jnp.float32), scale_two, normed_two
-    )
-    mlp_sums = (
-        lax.psum_scatter(grad_gain_two, ("dp", "seq"), scatter_dimension=0, tiled=True),
-        lax.psum_scatter(grad_gate, ("dp", "seq"), scatter_dimension=0, tiled=True),
-        lax.psum_scatter(grad_up, ("dp", "seq"), scatter_dimension=0, tiled=True),
-        lax.psum_scatter(grad_down, ("dp", "seq"), scatter_dimension=1, tiled=True),
-    )
-    gain_one, query_w, key_w, value_w, out_w = (
-        lax.all_gather(gain_attn, ("dp", "seq"), axis=0, tiled=True),
-        lax.all_gather(w_query, ("dp", "seq"), axis=0, tiled=True),
-        lax.all_gather(w_key, ("dp", "seq"), axis=0, tiled=True),
-        lax.all_gather(w_value, ("dp", "seq"), axis=0, tiled=True),
-        lax.all_gather(w_out, ("dp", "seq"), axis=0, tiled=True),
+        d_a_two, gain_two, scale_two, normed_two
     )
     d_branch = d_x_two.astype(jnp.bfloat16)
-    grad_out = across_rows(mixed_cat, d_branch)
+    grad_out = scatter_rows(mixed_cat, d_branch, shape, "cxyz")
     d_mixed = (
         against(d_branch, out_w).astype(jnp.bfloat16).reshape(rows, shard_len, HEADS, value_dim)
     )
     d_mixed_heads = lax.all_to_all(d_mixed, "seq", split_axis=2, concat_axis=1, tiled=True)
     d_packed = lax.map(attend_back, (by_heads, segment_ids, mixed, denominator, d_mixed_heads))
-    d_packed_seq = jax.tree.map(
-        lambda part, own: part.astype(own.dtype),
-        lax.all_to_all(for_sending(d_packed), "seq", split_axis=1, concat_axis=2, tiled=True),
-        d_packed,
-    )
-    d_query = d_packed_seq[..., :FEAT].reshape(count, HEADS * FEAT)
-    d_keys = d_packed_seq[..., FEAT : 2 * FEAT].reshape(count, HEADS * FEAT)
-    d_values = d_packed_seq[..., 2 * FEAT :].reshape(count, width)
-    grad_query = across_rows(a_one, d_query)
-    grad_key = across_rows(a_one, d_keys)
-    grad_value = across_rows(a_one, d_values)
-    d_a_one = against(d_query, query_w) + against(d_keys, key_w) + against(d_values, value_w)
-    grad_gain_one = jnp.sum(d_a_one * normed_one, axis=0)
-    d_tokens = d_x_two + norm_backward(d_a_one, gain_one.astype(jnp.float32), scale_one, normed_one)
-    attn_sums = (
-        lax.psum_scatter(grad_gain_one, ("dp", "seq"), scatter_dimension=0, tiled=True),
-        lax.psum_scatter(grad_query, ("dp", "seq"), scatter_dimension=0, tiled=True),
-        lax.psum_scatter(grad_key, ("dp", "seq"), scatter_dimension=0, tiled=True),
-        lax.psum_scatter(grad_value, ("dp", "seq"), scatter_dimension=0, tiled=True),
-        lax.psum_scatter(grad_out, ("dp", "seq"), scatter_dimension=0, tiled=True),
-    )
+    d_packed_seq = lax.all_to_all(d_packed, "seq", split_axis=1, concat_axis=2, tiled=True)
+    d_qkv = jnp.concatenate(
+        [
+            d_packed_seq[..., :FEAT].reshape(count, features),
+            d_packed_seq[..., FEAT : 2 * FEAT].reshape(count, features),
+            d_packed_seq[..., 2 * FEAT :].reshape(count, width),
+        ],
+        axis=1,
+    )
+    grad_qkv = scatter_rows(a_one, d_qkv, shape, "cyxz")
+    d_a_one = against(d_qkv, qkv_w)
+    d_tokens = d_x_two + norm_backward(d_a_one, gain_one, scale_one, normed_one)
     return (
         result.reshape(rows, shard_len, width),
         d_tokens.reshape(rows, shard_len, width),
-        attn_sums[0],
-        attn_sums[1],
-        attn_sums[2],
-        attn_sums[3],
-        attn_sums[4],
-        mlp_sums[0],
-        mlp_sums[1],
-        mlp_sums[2],
-        mlp_sums[3],
+        gain_gradient(qkv_part, grad_qkv, gain_attn),
+        grad_qkv[:, :features],
+        grad_qkv[:, features : 2 * features],
+        grad_qkv[:, 2 * features :],
+        grad_out,
+        gain_gradient(
+            jnp.concatenate([w_gate, w_up], axis=1),
+            jnp.concatenate([grad_gate, grad_up], axis=1),
+            gain_mlp,
+        ),
+        grad_gate,
+        grad_up,
+        grad_down.T,
     )
 
 
@@ -288,7 +423,7 @@
         P("dp", "seq", None),
     )
     return jax.shard_map(
-        per_device,
+        functools.partial(per_device, Slice(mesh.shape["dp"], mesh.shape["seq"])),
         mesh=mesh,
         in_specs=placed,
         out_specs=(

time: 1960 us -> 1150 us (0.59)
  waiting for transfers between devices: 1030 us -> 170 us
  blocking collectives: 160 us -> 0 us
  local copies, waits for them, and re-layouts: 125 us -> 214 us
  starting transfers between devices: 16.8 us -> 79.7 us
  other arithmetic: 53.9 us -> 83.2 us
  Pallas kernels: 0 us -> 25.1 us
    reduce_scatter x7 -> x0, waiting for transfers between devices: 889 us -> none  [the longest x1 156 us: per_device(): lax.psum_scatter(grad_gate, ('dp', 'seq'), scatter_dimension=0, tiled=True)]
    ppermute x0 -> x78, waiting for transfers between devices: none -> 153 us  [send(): return lax.ppermute(array, self.axis, self.pairs)]
    all_gather x2 -> x0, blocking collectives: 80.9 us -> none  [the longest x1 42.3 us: per_device(): lax.all_gather(w_key, ('dp', 'seq'), axis=0, tiled=True)]
    unnamed x2 -> x0, blocking collectives: 79.2 us -> none
    ppermute x0 -> x78, starting transfers between devices: none -> 63 us  [send(): return lax.ppermute(array, self.axis, self.pairs)]
    ppermute x0 -> x26, local copies, waits for them, and re-layouts: none -> 57 us  [send(): return lax.ppermute(array, self.axis, self.pairs)]
    all_to_all x1, waiting for transfers between devices: 45.5 us -> 0.01 us  [per_device(): lax.all_to_all(packed, 'seq', split_axis=2, concat_axis=1, tiled=True)]
    all_to_all x1, waiting for transfers between devices: 46.3 us -> 16.2 us  [per_device(): lax.all_to_all(d_packed, 'seq', split_axis=1, concat_axis=2, tiled=True)]
  transfers between devices with their start and end apart: 16 -> 82, of which waited for: 11 -> 22; matrix products, arithmetic and copies ran while one was open for 15% -> 58% of each run, Pallas kernels for 0% -> 2%
where the time goes in v1:
time: 1150 us; the launch traced here: 1130 us
  matrix products  515 us (45%)
  local copies, waits for them, and re-layouts  214 us (19%)
  waiting for transfers between devices  170 us (15%)
  other arithmetic  83.2 us (7%)
  starting transfers between devices  79.7 us (7%)
  loops' own time  38.9 us (3%)
  Pallas kernels  25.1 us (2%)
    ppermute x78, waiting for transfers between devices, send(): return lax.ppermute(array, self.axis, self.pairs)  153 us
    dot_general x8, matrix products, attend_back(): jnp.einsum('hqk,qhc->khc', weights, d_numer[begin_position:stop_position]...  85.3 us
    dot_general x8, matrix products, attend_back(): jnp.einsum('qhc,khc->hqk', d_numer[begin_position:stop_position], values[...  70.8 us
    dot_general x8, matrix products, attend_row(): jnp.einsum('hqk,khc->qhc', weights, values[:begin_position + BLOCK], prec...  63.2 us
    ppermute x78, starting transfers between devices, send(): return lax.ppermute(array, self.axis, self.pairs)  63 us
    dot_general x17, matrix products, across_rows(): lax.dot_general(left, right, (((0,), (0,)), ((), ())), preferred_element_...  60 us
    ppermute x26, local copies, waits for them, and re-layouts, send(): return lax.ppermute(array, self.axis, self.pairs)  57 us
    dot_general x16, matrix products, block_terms(): jnp.einsum('pyg,jyg->ypj', query_rows[begin_position:stop_position], key_...  46.3 us
  transfers between devices with their start and end apart: 82, of which 22 were waited for; matrix products, arithmetic and copies ran while one was open for 58% of the time, Pallas kernels for 2%

profile of v1, /device:TPU:0, one launch (start us, length us, event | category | flops | bytes accessed | tf_op | source)
XLA Modules:
  0.0 1133.7 jit_solution(9381528754653368924)
XLA Ops:
  45.0 8.4 collective-permute-done.4.refs_2_
  89.1 13.2 %pad_maximum_fusion = bf16[2,512,16,96]{1,0,3,2:T(2,128)(2,1)} fusion(bf16[2,512,16,64]{1,0,3,2:T(2,128)(2,1)S(1)} %reshape.5647, bf16[2,512,16,16]{1,0,3,2:T(2,128)(2,1)S(1)} %reshape.5646, bf16[2,512,16,16]{1,0,3,2:T(2,128)(2,1)S(1)} %reshape.5645), kind=kLoop, calls=%fused_computation.276 | loop fusion | flops 3145728 | bytes 6291456 | tf_op jit(solution)/shard_map/concatenate | solution.py:337
  121.8 18.7 %collective-permute-done.13.refs_2_ = bf16[128,1024]{1,0:T(8,128)(2,1)S(1)} collective-permute-done((bf16[128,1024]{1,0:T(8,128)(2,1)}, bf16[128,1024]{1,0:T(8,128)(2,1)S(1)}, u32[]{:S(2)}, u32[]{:S(2)}) %collective-permute-start.13) | collective-permute-done | bytes 262176 | tf_op jit(solution)/shard_map/ppermute | solution.py:151
  169.5 13.7 %collective-permute-done.33 = bf16[128,2752]{0,1:T(8,128)(2,1)} collective-permute-done((bf16[128,2752]{0,1:T(8,128)(2,1)}, bf16[128,2752]{0,1:T(8,128)(2,1)}, u32[]{:S(2)}, u32[]{:S(2)}) %collective-permute-start.33) | collective-permute-done | bytes 704544 | tf_op jit(solution)/shard_map/ppermute | solution.py:151
  183.2 138.9 %while.38 = (s32[]{:T(128)}, f32[2,2048,4,64]{1,3,2,0:T(8,128)}, f32[2,2048,4]{1,2,0:T(4,128)S(1)}, bf16[2,2048,4,96]{1,3,2,0:T(8,128)(2,1)S(1)}, s32[2,2048]{1,...) while((s32[]{:T(128)}, f32[2,2048,4,64]{1,3,2,0:T(8,128)}, f32[2,2048,4]{1,2,0:T(4,128)S(1)}, ...), condition=%wide.region_6.7_spmd, body=%wide.region_1.6_spmd.sunk | while | flops 8516027904 | bytes 137717984 | solution.py:346
  232.1 8.6 fusion.437
  240.7 16.0 %fusion.438 = f32[512,4,64]{0,2,1:T(8,128)S(1)} fusion(f32[4,512,2048]{2,1,0:T(8,128)} %get-tuple-element.543, pred[512,2048]{1,0:T(8,128)(4,1)S(1)} %fusion.436, bf16[2048,4,96]{0,2,1:T(8,128)(2,1)S(1)} %dynamic-slice_bitcast_fusion.6, f32[512,4]{0,1:T(4,128)S(1)} %bitcast.467), kind=kOutput, calls=%fused_computation.44.clone.1 | convolution fusion | flops 3246522368 | bytes 19406848 | tf_op jit(solution)/shard_map/while/body/eval_jaxpr/hqk,khc->qhc/dot_general | solution.py:64
  285.7 8.6 fusion.437
  294.4 16.0 %fusion.438 = f32[512,4,64]{0,2,1:T(8,128)S(1)} fusion(f32[4,512,2048]{2,1,0:T(8,128)} %get-tuple-element.543, pred[512,2048]{1,0:T(8,128)(4,1)S(1)} %fusion.436, bf16[2048,4,96]{0,2,1:T(8,128)(2,1)S(1)} %dynamic-slice_bitcast_fusion.6, f32[512,4]{0,1:T(4,128)S(1)} %bitcast.467), kind=kOutput, calls=%fused_computation.44.clone.1 | convolution fusion | flops 3246522368 | bytes 19406848 | tf_op jit(solution)/shard_map/while/body/eval_jaxpr/hqk,khc->qhc/dot_general | solution.py:64
  353.7 31.3 %collective-permute-done.24 = bf16[128,2752]{0,1:T(8,128)(2,1)} collective-permute-done((bf16[128,2752]{0,1:T(8,128)(2,1)}, bf16[128,2752]{0,1:T(8,128)(2,1)}, u32[]{:S(2)}, u32[]{:S(2)}) %collective-permute-start.24) | collective-permute-done | bytes 704544 | tf_op jit(solution)/shard_map/ppermute | solution.py:151
  462.2 10.2 copy.2759
  487.4 9.4 fusion.300
  496.7 9.0 fusion.299
  505.7 20.1 %fusion.210 = (bf16[1024,2752]{0,1:T(8,128)(2,1)}, bf16[1024,2752]{0,1:T(8,128)(2,1)}, bf16[1024,2752]{0,1:T(8,128)(2,1)}) fusion(f32[1024,2752]{0,1:T(8,128)} %fusion.300, f32[1024,2752]{0,1:T(8,128)} %fusion.299, bf16[1024,2752]{1,0:T(8,128)(2,1)} %assemble.9, bf16[1024,1024]{1,0:T(8,128)(2,1)S(1)} %bitcast.432), kind=kOutput, calls=%fused_computation.241 | convolution fusion | flops 5813633024 | bytes 47185920 | tf_op jit(solution)/shard_map/dot_general | solution.py:363
  525.8 11.8 %add_convert_fusion = bf16[1024,1024]{1,0:T(8,128)(2,1)} fusion(f32[1024,1024]{1,0:T(8,128)} %copy-done.13, bf16[1024,2752]{0,1:T(8,128)(2,1)} %get-tuple-element.436, bf16[1024,2752]{1,0:T(8,128)(2,1)} %assemble.9), kind=kOutput, calls=%fused_computation.271 | convolution fusion | flops 5773459456 | bytes 17563648 | tf_op jit(solution)/shard_map/dot_general | solution.py:28
  537.7 9.9 fusion.301
  547.6 10.1 multiply_reduce_fusion
  644.2 298.9 %while.39 = (s32[]{:T(128)}, bf16[2,2048,4,96]{1,3,2,0:T(8,128)(2,1)}, bf16[2,2048,4,96]{1,3,2,0:T(8,128)(2,1)}, s32[2,2048]{1,0:T(2,128)S(1)}, bf16[2,2048,4,64...) while((s32[]{:T(128)}, ...), condition=%wide.region_11.12_spmd, body=%wide.region_9.11_spmd.sunk | while | flops 20612556800 | bytes 489024128 | solution.py:378
  668.9 9.4 fusion.497
  693.4 13.0 %fusion.500 = f32[2048,4,64]{0,2,1:T(8,128)} fusion(f32[2048,4,64]{0,2,1:T(8,128)} %fusion.497, f32[4,512,1536]{2,1,0:T(8,128)S(1)} %fusion.498, pred[512,1536]{1,0:T(8,128)(4,1)S(1)} %copy-done.8, f32[2048,4,64]{0,2,1:T(8,128)S(1)} %convert_divide_fusion.4), kind=kOutput, calls=%fused_computation.134.clone.1 | convolution fusion | flops 2435186688 | bytes 17039360 | tf_op jit(solution)/shard_map/while/body/eval_jaxpr/hqk,qhc->khc/dot_general | solution.py:97
  706.5 9.3 multiply_multiply_fusion.10
  736.2 16.5 %fusion.503 = bf16[1,2048,4,64]{1,3,2,0:T(8,128)(2,1)} fusion(f32[2048,4,64]{0,2,1:T(8,128)} %fusion.500, f32[4,512,2048]{2,1,0:T(8,128)S(1)} %fusion.501, pred[512,2048]{1,0:T(8,128)(4,1)S(1)} %copy-done.7, f32[2048,4,64]{0,2,1:T(8,128)S(1)} %copy-done.5), kind=kOutput, calls=%fused_computation.139.clone.1 | convolution fusion | flops 3247439872 | bytes 21495808 | tf_op jit(solution)/shard_map/while/body/eval_jaxpr/hqk,qhc->khc/dot_general | solution.py:97
  752.7 17.5 %multiply_multiply_fusion.11 = f32[4,512,2048]{2,1,0:T(8,128)} fusion(f32[4,512,2048]{2,1,0:T(8,128)} %copy-done.1, f32[4,512]{1,0:T(4,128)S(1)} %get-tuple-element.570, pred[512,2048]{1,0:T(8,128)(4,1)S(1)} %copy-done.7, bf16[2048,4,96]{0,2,1:T(8,128)(2,1)S(1)} %copy-done.3, f32[2048,4,64]{0,2,1:T(8,128)S(1)} %copy-done.5), kind=kOutput, calls=%fused_computation.85.clone.1 | convolution fusion | flops 3246391296 | bytes 36184064 | tf_op jit(solution)/shard_map/while/body/eval_jaxpr/qhc,khc->hqk/dot_general | solution.py:87
  770.2 9.4 fusion.506
  815.3 9.4 fusion.497
  840.0 13.0 %fusion.500 = f32[2048,4,64]{0,2,1:T(8,128)} fusion(f32[2048,4,64]{0,2,1:T(8,128)} %fusion.497, f32[4,512,1536]{2,1,0:T(8,128)S(1)} %fusion.498, pred[512,1536]{1,0:T(8,128)(4,1)S(1)} %copy-done.8, f32[2048,4,64]{0,2,1:T(8,128)S(1)} %convert_divide_fusion.4), kind=kOutput, calls=%fused_computation.134.clone.1 | convolution fusion | flops 2435186688 | bytes 17039360 | tf_op jit(solution)/shard_map/while/body/eval_jaxpr/hqk,qhc->khc/dot_general | solution.py:97
  853.0 9.3 multiply_multiply_fusion.10
  882.6 16.7 %fusion.503 = bf16[1,2048,4,64]{1,3,2,0:T(8,128)(2,1)} fusion(f32[2048,4,64]{0,2,1:T(8,128)} %fusion.500, f32[4,512,2048]{2,1,0:T(8,128)S(1)} %fusion.501, pred[512,2048]{1,0:T(8,128)(4,1)S(1)} %copy-done.7, f32[2048,4,64]{0,2,1:T(8,128)S(1)} %copy-done.5), kind=kOutput, calls=%fused_computation.139.clone.1 | convolution fusion | flops 3247439872 | bytes 21495808 | tf_op jit(solution)/shard_map/while/body/eval_jaxpr/hqk,qhc->khc/dot_general | solution.py:97
  899.3 17.4 %multiply_multiply_fusion.11 = f32[4,512,2048]{2,1,0:T(8,128)} fusion(f32[4,512,2048]{2,1,0:T(8,128)} %copy-done.1, f32[4,512]{1,0:T(4,128)S(1)} %get-tuple-element.570, pred[512,2048]{1,0:T(8,128)(4,1)S(1)} %copy-done.7, bf16[2048,4,96]{0,2,1:T(8,128)(2,1)S(1)} %copy-done.3, f32[2048,4,64]{0,2,1:T(8,128)S(1)} %copy-done.5), kind=kOutput, calls=%fused_computation.85.clone.1 | convolution fusion | flops 3246391296 | bytes 36184064 | tf_op jit(solution)/shard_map/while/body/eval_jaxpr/qhc,khc->hqk/dot_general | solution.py:87
  916.8 9.4 fusion.506
  987.6 16.2 %all-to-all-done.3 = bf16[2,2048,4,96]{3,2,0,1:T(4,128)(2,1)} async-done(((bf16[2,2048,4,96]{3,2,0,1:T(4,128)(2,1)}), bf16[2,2048,4,96]{3,2,0,1:T(4,128)(2,1)}, u32[]{:S(2)}, u32[]{:S(2)}) %all-to-all-start.3) | async-done | bytes 3145760 | tf_op jit(solution)/shard_map/all_to_all | solution.py:379
  1092.7 12.5 %collective-permute-done.49 = bf16[256,1536]{1,0:T(8,128)(2,1)S(1)} collective-permute-done((bf16[256,1536]{1,0:T(8,128)(2,1)S(1)}, bf16[256,1536]{1,0:T(8,128)(2,1)S(1)}, u32[]{:S(2)}, u32[]{:S(2)}) %collective-permute-start.49) | collective-permute-done | bytes 786464 | tf_op jit(solution)/shard_map/ppermute | solution.py:151
  (700 shorter events, 691.5 us)
Async XLA Ops:
  62.2 45.4 %collective-permute-start.40 = (bf16[64,2752]{1,0:T(8,128)(2,1)}, bf16[64,2752]{1,0:T(8,128)(2,1)}, u32[]{:S(2)}, u32[]{:S(2)}) collective-permute-start(bf16[64,2752]{1,0:T(8,128)(2,1)} %pad_maximum_fusion.3), channel_id=1, source_target_pairs={{0,2},{1,3},{2,0},{3,1},{4,6},{5,7},{6,4},{7,5},{8,10},{9,11},{10,... | collective-permute-start | bytes 1056776 | tf_op jit(solution)/shard_map/ppermute | solution.py:151
  62.7 49.5 %collective-permute-start.30 = (bf16[32,2752]{1,0:T(8,128)(2,1)}, bf16[32,2752]{1,0:T(8,128)(2,1)}, u32[]{:S(2)}, u32[]{:S(2)}) collective-permute-start(bf16[32,2752]{1,0:T(8,128)(2,1)} %copy-done.69), channel_id=1, source_target_pairs={{0,8},{4,12},{8,24},{12,28},{16,0},{20,4},{24,16},{28,20},{1,9},{5... | collective-permute-start | bytes 528392 | tf_op jit(solution)/shard_map/ppermute | solution.py:151
  64.9 56.9 %collective-permute-start.15 = (bf16[128,1024]{1,0:T(8,128)(2,1)}, bf16[128,1024]{1,0:T(8,128)(2,1)}, u32[]{:S(2)}, u32[]{:S(2)}) collective-permute-start(bf16[128,1024]{1,0:T(8,128)(2,1)} %constant_dynamic-update-slice_fusion.refs_0_), channel_id=1, source_target_pairs={{0,1},{1,0},{2,3},{3,2},{4,5},{5,4},{6,7},{7,6},{8,9},{9,8},{10,11... | collective-permute-start | bytes 786440 | tf_op jit(solution)/shard_map/ppermute | solution.py:151
  65.0 49.6 %collective-permute-start.12 = (bf16[128,1024]{1,0:T(8,128)(2,1)}, bf16[128,1024]{1,0:T(8,128)(2,1)}, u32[]{:S(2)}, u32[]{:S(2)}) collective-permute-start(bf16[128,1024]{1,0:T(8,128)(2,1)} %constant_dynamic-update-slice_fusion.refs_0_), channel_id=1, source_target_pairs={{0,8},{4,12},{8,24},{12,28},{16,0},{20,4},{24,16},{28,20},{1,9},{5... | collective-permute-start | bytes 786440 | tf_op jit(solution)/shard_map/ppermute | solution.py:151
  67.1 49.6 %collective-permute-start.21 = (bf16[32,2752]{1,0:T(8,128)(2,1)}, bf16[32,2752]{1,0:T(8,128)(2,1)}, u32[]{:S(2)}, u32[]{:S(2)}) collective-permute-start(bf16[32,2752]{1,0:T(8,128)(2,1)} %collective-permute-done.20), channel_id=1, source_target_pairs={{0,8},{4,12},{8,24},{12,28},{16,0},{20,4},{24,16},{28,20},{1,9},{5... | collective-permute-start | bytes 528392 | tf_op jit(solution)/shard_map/ppermute | solution.py:151
  102.3 51.6 %all-to-all-start = ((bf16[2,512,16,96]{1,0,3,2:T(2,128)(2,1)}), bf16[2,512,16,96]{1,0,3,2:T(2,128)(2,1)S(1)}, u32[]{:S(2)}, u32[]{:S(2)}) async-start(bf16[2,512,16,96]{1,0,3,2:T(2,128)(2,1)} %pad_maximum_fusion), calls=%async_computation | async-start | bytes 6291456 | tf_op jit(solution)/shard_map/all_to_all | solution.py:345
  111.8 39.5 %collective-permute-start.44 = (bf16[128,2752]{0,1:T(8,128)(2,1)}, bf16[128,2752]{0,1:T(8,128)(2,1)}, u32[]{:S(2)}, u32[]{:S(2)}) collective-permute-start(bf16[128,2752]{0,1:T(8,128)(2,1)} %copy.2780), channel_id=1, source_target_pairs={{0,1},{1,0},{2,3},{3,2},{4,5},{5,4},{6,7},{7,6},{8,9},{9,8},{10,11... | collective-permute-start | bytes 2113544 | tf_op jit(solution)/shard_map/ppermute | solution.py:151
  112.2 39.1 %collective-permute-start.41 = (bf16[128,2752]{0,1:T(8,128)(2,1)}, bf16[128,2752]{0,1:T(8,128)(2,1)}, u32[]{:S(2)}, u32[]{:S(2)}) collective-permute-start(bf16[128,2752]{0,1:T(8,128)(2,1)} %copy.2780), channel_id=1, source_target_pairs={{0,8},{4,12},{8,24},{12,28},{16,0},{20,4},{24,16},{28,20},{1,9},{5... | collective-permute-start | bytes 2113544 | tf_op jit(solution)/shard_map/ppermute | solution.py:151
  162.8 182.0 %collective-permute-start.32 = (bf16[128,2752]{0,1:T(8,128)(2,1)}, bf16[128,2752]{0,1:T(8,128)(2,1)}, u32[]{:S(2)}, u32[]{:S(2)}) collective-permute-start(bf16[128,2752]{0,1:T(8,128)(2,1)} %copy.2770), channel_id=1, source_target_pairs={{0,2},{1,3},{2,0},{3,1},{4,6},{5,7},{6,4},{7,5},{8,10},{9,11},{10,... | collective-permute-start | bytes 2113544 | tf_op jit(solution)/shard_map/ppermute | solution.py:151
  164.9 180.4 %collective-permute-start.18 = (bf16[128,1024]{1,0:T(8,128)(2,1)}, bf16[128,1024]{1,0:T(8,128)(2,1)}, u32[]{:S(2)}, u32[]{:S(2)}) collective-permute-start(bf16[128,1024]{1,0:T(8,128)(2,1)} %collective-permute-done.14.refs_3_), channel_id=1, source_target_pairs={{0,1},{1,0},{2,3},{3,2},{4,5},{5,4},{6,7},{7,6},{8,9},{9,8},{10,11... | collective-permute-start | bytes 786440 | tf_op jit(solution)/shard_map/ppermute | solution.py:151
  169.5 177.8 %collective-permute-start.45 = (bf16[128,2752]{0,1:T(8,128)(2,1)}, bf16[128,2752]{0,1:T(8,128)(2,1)}, u32[]{:S(2)}, u32[]{:S(2)}) collective-permute-start(bf16[128,2752]{0,1:T(8,128)(2,1)} %collective-permute-done.41), channel_id=1, source_target_pairs={{0,1},{1,0},{2,3},{3,2},{4,5},{5,4},{6,7},{7,6},{8,9},{9,8},{10,11... | collective-permute-start | bytes 2113544 | tf_op jit(solution)/shard_map/ppermute | solution.py:151
  169.5 177.8 %collective-permute-start.42 = (bf16[128,2752]{0,1:T(8,128)(2,1)}, bf16[128,2752]{0,1:T(8,128)(2,1)}, u32[]{:S(2)}, u32[]{:S(2)}) collective-permute-start(bf16[128,2752]{0,1:T(8,128)(2,1)} %collective-permute-done.41), channel_id=1, source_target_pairs={{0,8},{4,12},{8,24},{12,28},{16,0},{20,4},{24,16},{28,20},{1,9},{5... | collective-permute-start | bytes 2113544 | tf_op jit(solution)/shard_map/ppermute | solution.py:151
  183.2 164.9 %collective-permute-start.27 = (bf16[128,2752]{0,1:T(8,128)(2,1)}, bf16[128,2752]{0,1:T(8,128)(2,1)}, u32[]{:S(2)}, u32[]{:S(2)}) collective-permute-start(bf16[128,2752]{0,1:T(8,128)(2,1)} %collective-permute-done.23), channel_id=1, source_target_pairs={{0,1},{1,0},{2,3},{3,2},{4,5},{5,4},{6,7},{7,6},{8,9},{9,8},{10,11... | collective-permute-start | bytes 2113544 | tf_op jit(solution)/shard_map/ppermute | solution.py:151
  340.1 117.9 %all-to-all-start.1 = ((bf16[4,2,131072]{2,1,0:T(2,128)(2,1)}), bf16[4,2,131072]{2,1,0:T(2,128)(2,1)S(1)}, u32[]{:S(2)}, u32[]{:S(2)}) async-start(bf16[4,2,131072]{2,1,0:T(2,128)(2,1)} %reshape.5719), calls=%async_computation.1 | async-start | bytes 4194304 | tf_op jit(solution)/shard_map/all_to_all | solution.py:347
  345.3 39.7 %collective-permute-start.24 = (bf16[128,2752]{0,1:T(8,128)(2,1)}, bf16[128,2752]{0,1:T(8,128)(2,1)}, u32[]{:S(2)}, u32[]{:S(2)}) collective-permute-start(bf16[128,2752]{0,1:T(8,128)(2,1)} %collective-permute-done.22), channel_id=1, source_target_pairs={{0,2},{1,3},{2,0},{3,1},{4,6},{5,7},{6,4},{7,5},{8,10},{9,11},{10,... | collective-permute-start | bytes 2113544 | tf_op jit(solution)/shard_map/ppermute | solution.py:151
  347.3 37.7 %collective-permute-start.37 = (bf16[128,2752]{0,1:T(8,128)(2,1)}, bf16[128,2752]{0,1:T(8,128)(2,1)S(1)}, u32[]{:S(2)}, u32[]{:S(2)}) collective-permute-start(bf16[128,2752]{0,1:T(8,128)(2,1)} %collective-permute-done.33), channel_id=1, source_target_pairs={{0,1},{1,0},{2,3},{3,2},{4,5},{5,4},{6,7},{7,6},{8,9},{9,8},{10,11... | collective-permute-start | bytes 2113544 | tf_op jit(solution)/shard_map/ppermute | solution.py:151
  347.3 38.2 %collective-permute-start.34 = (bf16[128,2752]{0,1:T(8,128)(2,1)}, bf16[128,2752]{0,1:T(8,128)(2,1)S(1)}, u32[]{:S(2)}, u32[]{:S(2)}) collective-permute-start(bf16[128,2752]{0,1:T(8,128)(2,1)} %collective-permute-done.32), channel_id=1, source_target_pairs={{0,4},{4,0},{8,12},{12,8},{16,20},{20,16},{24,28},{28,24},{1,5},{5... | collective-permute-start | bytes 2113544 | tf_op jit(solution)/shard_map/ppermute | solution.py:151
  353.5 74.0 %collective-permute-start.36 = (bf16[128,2752]{0,1:T(8,128)(2,1)}, bf16[128,2752]{0,1:T(8,128)(2,1)}, u32[]{:S(2)}, u32[]{:S(2)}) collective-permute-start(bf16[128,2752]{0,1:T(8,128)(2,1)} %collective-permute-done.32), channel_id=1, source_target_pairs={{0,1},{1,0},{2,3},{3,2},{4,5},{5,4},{6,7},{7,6},{8,9},{9,8},{10,11... | collective-permute-start | bytes 2113544 | tf_op jit(solution)/shard_map/ppermute | solution.py:151
  385.0 62.5 %collective-permute-start.46 = (bf16[128,2752]{0,1:T(8,128)(2,1)}, bf16[128,2752]{0,1:T(8,128)(2,1)}, u32[]{:S(2)}, u32[]{:S(2)}) collective-permute-start(bf16[128,2752]{0,1:T(8,128)(2,1)} %collective-permute-done.42), channel_id=1, source_target_pairs={{0,1},{1,0},{2,3},{3,2},{4,5},{5,4},{6,7},{7,6},{8,9},{9,8},{10,11... | collective-permute-start | bytes 2113544 | tf_op jit(solution)/shard_map/ppermute | solution.py:151
  385.0 44.7 %collective-permute-start.28 = (bf16[128,2752]{0,1:T(8,128)(2,1)}, bf16[128,2752]{0,1:T(8,128)(2,1)}, u32[]{:S(2)}, u32[]{:S(2)}) collective-permute-start(bf16[128,2752]{0,1:T(8,128)(2,1)} %collective-permute-done.24), channel_id=1, source_target_pairs={{0,1},{1,0},{2,3},{3,2},{4,5},{5,4},{6,7},{7,6},{8,9},{9,8},{10,11... | collective-permute-start | bytes 2113544 | tf_op jit(solution)/shard_map/ppermute | solution.py:151
  385.5 52.5 %collective-permute-start.38 = (bf16[128,2752]{0,1:T(8,128)(2,1)S(1)}, bf16[128,2752]{0,1:T(8,128)(2,1)}, u32[]{:S(2)}, u32[]{:S(2)}) collective-permute-start(bf16[128,2752]{0,1:T(8,128)(2,1)S(1)} %collective-permute-done.34), channel_id=1, source_target_pairs={{0,1},{1,0},{2,3},{3,2},{4,5},{5,4},{6,7},{7,6},{8,9},{9,8},{10,11... | collective-permute-start | bytes 2113544 | tf_op jit(solution)/shard_map/ppermute | solution.py:151
  385.6 64.1 %collective-permute-start.47 = (bf16[128,2752]{0,1:T(8,128)(2,1)S(1)}, bf16[128,2752]{0,1:T(8,128)(2,1)}, u32[]{:S(2)}, u32[]{:S(2)}) collective-permute-start(bf16[128,2752]{0,1:T(8,128)(2,1)S(1)} %collective-permute-done.43), channel_id=1, source_target_pairs={{0,1},{1,0},{2,3},{3,2},{4,5},{5,4},{6,7},{7,6},{8,9},{9,8},{10,11... | collective-permute-start | bytes 2113544 | tf_op jit(solution)/shard_map/ppermute | solution.py:151
  573.0 60.4 %all-to-all-start.2 = ((bf16[2,512,16,64]{1,0,3,2:T(2,128)(2,1)}), bf16[2,512,16,64]{1,0,3,2:T(2,128)(2,1)}, u32[]{:S(2)}, u32[]{:S(2)}) async-start(bf16[2,512,16,64]{1,0,3,2:T(2,128)(2,1)} %reshape.5651), calls=%async_computation.2 | async-start | bytes 4194304 | tf_op jit(solution)/shard_map/all_to_all | solution.py:377
  632.8 324.1 %collective-permute-start.72 = (bf16[512,2752]{0,1:T(8,128)(2,1)}, bf16[512,2752]{0,1:T(8,128)(2,1)}, u32[]{:S(2)}, u32[]{:S(2)}) collective-permute-start(bf16[512,2752]{0,1:T(8,128)(2,1)} %convolution_convert_fusion.6), channel_id=1, source_target_pairs={{0,1},{1,0},{2,3},{3,2},{4,5},{5,4},{6,7},{7,6},{8,9},{9,8},{10,11... | collective-permute-start | bytes 8454152 | tf_op jit(solution)/shard_map/ppermute | solution.py:151
  632.8 328.8 %collective-permute-start.66 = (bf16[512,2752]{0,1:T(8,128)(2,1)}, bf16[512,2752]{0,1:T(8,128)(2,1)}, u32[]{:S(2)}, u32[]{:S(2)}) collective-permute-start(bf16[512,2752]{0,1:T(8,128)(2,1)} %convolution_convert_fusion.4), channel_id=1, source_target_pairs={{0,1},{1,0},{2,3},{3,2},{4,5},{5,4},{6,7},{7,6},{8,9},{9,8},{10,11... | collective-permute-start | bytes 8454152 | tf_op jit(solution)/shard_map/ppermute | solution.py:151
  633.4 339.2 %collective-permute-start.60 = (bf16[512,2752]{0,1:T(8,128)(2,1)}, bf16[512,2752]{0,1:T(8,128)(2,1)}, u32[]{:S(2)}, u32[]{:S(2)}) collective-permute-start(bf16[512,2752]{0,1:T(8,128)(2,1)} %convolution_convert_fusion.5), channel_id=1, source_target_pairs={{0,1},{1,0},{2,3},{3,2},{4,5},{5,4},{6,7},{7,6},{8,9},{9,8},{10,11... | collective-permute-start | bytes 8454152 | tf_op jit(solution)/shard_map/ppermute | solution.py:151
  641.9 313.3 %collective-permute-start.59 = (bf16[32,1024]{1,0:T(8,128)(2,1)}, bf16[32,1024]{1,0:T(8,128)(2,1)}, u32[]{:S(2)}, u32[]{:S(2)}) collective-permute-start(bf16[32,1024]{1,0:T(8,128)(2,1)} %fusion.291), channel_id=1, source_target_pairs={{0,8},{4,12},{8,24},{12,28},{16,0},{20,4},{24,16},{28,20},{1,9},{5... | collective-permute-start | bytes 196616 | tf_op jit(solution)/shard_map/ppermute | solution.py:151
  950.3 53.5 %all-to-all-start.3 = ((bf16[2,2048,4,96]{3,2,0,1:T(4,128)(2,1)}), bf16[2,2048,4,96]{3,2,0,1:T(4,128)(2,1)}, u32[]{:S(2)}, u32[]{:S(2)}) async-start(bf16[2,2048,4,96]{3,2,0,1:T(4,128)(2,1)} %copy.2791), calls=%async_computation.3 | async-start | bytes 8388608 | tf_op jit(solution)/shard_map/all_to_all | solution.py:379
  971.4 61.9 %collective-permute-start.67 = (bf16[256,2752]{0,1:T(8,128)(2,1)}, bf16[256,2752]{0,1:T(8,128)(2,1)}, u32[]{:S(2)}, u32[]{:S(2)}) collective-permute-start(bf16[256,2752]{0,1:T(8,128)(2,1)} %add_convert_fusion.1), channel_id=1, source_target_pairs={{0,4},{4,0},{8,12},{12,8},{16,20},{20,16},{24,28},{28,24},{1,5},{5... | collective-permute-start | bytes 4227080 | tf_op jit(solution)/shard_map/ppermute | solution.py:151
  981.7 60.6 %collective-permute-start.61 = (bf16[256,2752]{0,1:T(8,128)(2,1)}, bf16[256,2752]{0,1:T(8,128)(2,1)}, u32[]{:S(2)}, u32[]{:S(2)}) collective-permute-start(bf16[256,2752]{0,1:T(8,128)(2,1)} %add_convert_fusion.2), channel_id=1, source_target_pairs={{0,2},{1,3},{2,0},{3,1},{4,6},{5,7},{6,4},{7,5},{8,10},{9,11},{10,... | collective-permute-start | bytes 4227080 | tf_op jit(solution)/shard_map/ppermute | solution.py:151
  985.9 44.9 %collective-permute-start.74 = (bf16[128,2752]{0,1:T(8,128)(2,1)}, bf16[128,2752]{0,1:T(8,128)(2,1)}, u32[]{:S(2)}, u32[]{:S(2)}) collective-permute-start(bf16[128,2752]{0,1:T(8,128)(2,1)} %add_convert_fusion.5), channel_id=1, source_target_pairs={{0,8},{4,12},{8,24},{12,28},{16,0},{20,4},{24,16},{28,20},{1,9},{5... | collective-permute-start | bytes 2113544 | tf_op jit(solution)/shard_map/ppermute | solution.py:151
  1026.3 60.5 %collective-permute-start.48 = (bf16[512,1536]{1,0:T(8,128)(2,1)}, bf16[512,1536]{1,0:T(8,128)(2,1)}, u32[]{:S(2)}, u32[]{:S(2)}) collective-permute-start(bf16[512,1536]{1,0:T(8,128)(2,1)} %convolution_convert_fusion.8), channel_id=1, source_target_pairs={{0,1},{1,0},{2,3},{3,2},{4,5},{5,4},{6,7},{7,6},{8,9},{9,8},{10,11... | collective-permute-start | bytes 4718600 | tf_op jit(solution)/shard_map/ppermute | solution.py:151
  (170 other events, 2249.4 us)

commit v2 on v1

--- a/solution.py
+++ b/solution.py
@@ -8,118 +8,400 @@
 from jax.experimental.pallas import tpu as pltpu
 from jax.sharding import PartitionSpec as P
 
+LONGEST = 1024
 HEADS = 16
 FEAT = 16
-LEN = 2048
-BLOCK = 512
+LANES = 128
+GROUP = LANES // FEAT
+PIECES = FEAT // 2 + 2
+WIDE = PIECES * LANES
+
+
+def dot(left, right, dims=((1,), (0,))):
+    return lax.dot_general(left, right, (dims, ((), ())), preferred_element_type=jnp.float32)
+
+
+def rolls(scaled):
+    table = np.zeros((LANES, WIDE), np.float32)
+    for d in range(FEAT // 2 + 1):
+        factor = (1 / 32 if d == 0 else 1 / 16) if scaled else 1.0
+        for lane in range(LANES):
+            head, a = divmod(lane, FEAT)
+            if d < FEAT // 2 or a < FEAT // 2:
+                table[head * FEAT + (a + d) % FEAT, (d + 1) * LANES + lane] = factor
+    return table
+
+
+def piece_of(number, rows, factors, lin, axis):
+    if number == 0:
+        return rows.astype(jnp.float32) * lin
+    products = rows.astype(jnp.float32) * factors
+    if number < PIECES - 1:
+        return products
+    place = lax.broadcasted_iota(jnp.int32, products.shape, axis)
+    return jnp.where(place % FEAT == FEAT // 2, 1.0, products)
+
+
+def head_mask(lanes_per_head, first_head, shape):
+    row_head = lax.broadcasted_iota(jnp.int32, shape, 0) // FEAT
+    lane_head = lax.broadcasted_iota(jnp.int32, shape, 1) // lanes_per_head + first_head
+    return row_head == lane_head
+
+
+def fold_heads(full, value_dim):
+    per = LANES // value_dim
+    total = None
+    for part in range(full.shape[1] // LANES):
+        piece = full[:, part * LANES : (part + 1) * LANES]
+        piece = jnp.where(head_mask(value_dim, part * per, piece.shape), piece, 0.0)
+        total = piece if total is None else total + piece
+    return total + pltpu.roll(total, value_dim, 1)
+
+
+def halves(state):
+    state = state.astype(jnp.float32)
+    turned = pltpu.roll(state, LANES // 2, 1)
+    low = lax.broadcasted_iota(jnp.int32, state.shape, 1) < LANES // 2
+    return jnp.where(low, state, turned), jnp.where(low, turned, state)
+
+
+def spread_heads(values, value_dim, width):
+    per = LANES // value_dim
+    return jnp.concatenate(
+        [
+            jnp.where(head_mask(value_dim, part * per, values.shape), values, 0.0)
+            for part in range(width // LANES)
+        ],
+        axis=1,
+    )
+
+
+def turned(block):
+    return block.astype(jnp.float32).T.astype(jnp.bfloat16)
+
+
+def tail_kernel(value_dim, k_ref, v_ref, seg_ref, pick_ref, out_ref):
+    seg = seg_ref[...]
+    last = seg[-1:, :]
+    keep = (seg == last).astype(jnp.float32)
+    values = (v_ref[...].astype(jnp.float32) * keep).astype(jnp.bfloat16)
+    ones = jnp.broadcast_to(keep, (seg.shape[0], LANES)).astype(jnp.bfloat16)
+    keys = turned(k_ref[...])
+    low = lax.broadcasted_iota(jnp.int32, (LANES, LANES), 1) < value_dim
+    for number in range(PIECES):
+        span = slice(number * LANES, (number + 1) * LANES)
+        factors = dot(pick_ref[span, :], keys) if number else None
+        piece = piece_of(number, keys, factors, 1.0, 0).astype(jnp.bfloat16)
+        folded = fold_heads(dot(piece, values), value_dim)
+        out_ref[0, 0, span, :] = jnp.where(low, folded, dot(piece, ones)).astype(out_ref.dtype)
+
+
+def masks_of(seg_ref, seg_row_ref, begin, block):
+    stop = begin + block
+    rows = begin + lax.broadcasted_iota(jnp.int32, (block, stop), 0)
+    columns = lax.broadcasted_iota(jnp.int32, (block, stop), 1)
+    same = seg_ref[begin:stop, :] == seg_row_ref[0, :, :stop]
+    return ((rows >= columns) & same).astype(jnp.float32)
+
+
+def own_lanes(array, lanes_per_head, head):
+    place = lax.broadcasted_iota(jnp.int32, array.shape, 1) // lanes_per_head
+    return jnp.where(place == head, array, jnp.zeros_like(array))
+
+
+def near_kernel(value_dim, block, q_ref, k_ref, v_ref, seg_ref, seg_row_ref, top_ref, den_ref):
+    length = q_ref.shape[0]
+    per = LANES // value_dim
+    low = lax.broadcasted_iota(jnp.int32, (block, LANES), 1) < value_dim
+    for begin in range(0, length, block):
+        stop = begin + block
+        mask = masks_of(seg_ref, seg_row_ref, begin, block)
+        queries = q_ref[begin:stop, :] * jnp.bfloat16(FEAT ** (-0.5))
+        keys = k_ref[:stop, :]
+        ones = jnp.ones((stop, LANES), jnp.bfloat16)
+        for pair in range(GROUP // per):
+            span = slice(pair * LANES, (pair + 1) * LANES)
+            values = jnp.concatenate([v_ref[:stop, span], ones], axis=1)
+            sides = []
+            for side in range(per):
+                scores = dot(
+                    own_lanes(queries, FEAT, pair * per + side), keys, ((1,), (1,))
+                )
+                weights = (((0.5 * scores + 1.0) * scores + 1.0) * mask).astype(jnp.bfloat16)
+                sides.append(dot(weights, values))
+            top_ref[begin:stop, span] = jnp.where(low, sides[0][:, :LANES], sides[1][:, :LANES])
+            den_ref[begin:stop, span] = jnp.where(low, sides[0][:, LANES:], sides[1][:, LANES:])
+
+
+def features(rows, pick_ref, lin):
+    pieces = []
+    for number in range(PIECES):
+        span = slice(number * LANES, (number + 1) * LANES)
+        factors = dot(rows, pick_ref[:, span]) if number else None
+        pieces.append(piece_of(number, rows, factors, lin, 1).astype(jnp.bfloat16))
+    return jnp.concatenate(pieces, axis=1)
+
+
+def far_kernel(
+    value_dim, q_ref, seg_ref, state_ref, top_ref, den_ref, pick_ref, y_ref, inverse_ref,
+    values_ref, sums_ref,
+):
+    width = top_ref.shape[1]
+    for number in range(PIECES):
+        span = slice(number * LANES, (number + 1) * LANES)
+        values, sums = halves(state_ref[0, 0, span, :])
+        values_ref[span, :] = spread_heads(values, value_dim, width).astype(jnp.bfloat16)
+        sums_ref[span, :] = spread_heads(sums, value_dim, width).astype(jnp.bfloat16)
+    seg = seg_ref[...]
+    keep = (seg == seg[:1, :]).astype(jnp.float32)
+    phi = features(q_ref[...], pick_ref, FEAT ** (-0.5))
+    top = top_ref[...] + keep * dot(phi, values_ref[...])
+    inverse = 1.0 / (den_ref[...] + keep * dot(phi, sums_ref[...]))
+    y_ref[...] = (top * inverse).astype(y_ref.dtype)
+    inverse_ref[...] = inverse
+
+
+def lane_sums(product, value_dim, side):
+    place = lax.broadcasted_iota(jnp.int32, product.shape, 1) // value_dim
+    return jnp.sum(jnp.where(place == side, product, 0.0), axis=1, keepdims=True)
+
+
+def d_den_of(pair, value_dim, dy_ref, y_ref, inverse_ref):
+    span = slice(pair * LANES, (pair + 1) * LANES)
+    product = dy_ref[:, span].astype(jnp.float32) * y_ref[:, span].astype(jnp.float32)
+    product = product * inverse_ref[:, span]
+    return [-lane_sums(product, value_dim, side) for side in range(LANES // value_dim)]
+
+
+def d_den_lanes(value_dim, dy_ref, y_ref, inverse_ref):
+    per = LANES // value_dim
+    shape = (dy_ref.shape[0], LANES)
+    place = lax.broadcasted_iota(jnp.int32, shape, 1) // FEAT
+    total = jnp.zeros(shape, jnp.float32)
+    for pair in range(GROUP // per):
+        for side, column in enumerate(d_den_of(pair, value_dim, dy_ref, y_ref, inverse_ref)):
+            total = jnp.where(place == pair * per + side, column, total)
+    return total
+
+
+def head_kernel(
+    value_dim, q_ref, dy_ref, y_ref, inverse_ref, seg_ref, pick_ref, out_ref
+):
+    seg = seg_ref[...]
+    keep = (seg == seg[:1, :]).astype(jnp.float32)
+    d_top = (dy_ref[...].astype(jnp.float32) * inverse_ref[...] * keep).astype(jnp.bfloat16)
+    d_den = (d_den_lanes(value_dim, dy_ref, y_ref, inverse_ref) * keep).astype(jnp.bfloat16)
+    queries = turned(q_ref[...])
+    low = lax.broadcasted_iota(jnp.int32, (LANES, LANES), 1) < value_dim
+    for number in range(PIECES):
+        span = slice(number * LANES, (number + 1) * LANES)
+        factors = dot(pick_ref[span, :], queries) if number else None
+        piece = piece_of(number, queries, factors, FEAT ** (-0.5), 0).astype(jnp.bfloat16)
+        folded = fold_heads(dot(piece, d_top), value_dim)
+        sums = jnp.where(head_mask(FEAT, 0, (LANES, LANES)), dot(piece, d_den), 0.0)
+        sums = jnp.sum(sums, axis=1, keepdims=True) * (1 / FEAT)
+        out_ref[0, 0, span, :] = jnp.where(low, folded, sums).astype(out_ref.dtype)
+
+
+def from_features(d_phi, rows, pick_ref, lin):
+    total = d_phi[:, :LANES] * lin
+    x = rows.astype(jnp.float32)
+    scaled = []
+    for number in range(1, PIECES):
+        span = slice(number * LANES, (number + 1) * LANES)
+        total = total + d_phi[:, span] * dot(rows, pick_ref[:, span])
+        scaled.append((d_phi[:, span] * x).astype(jnp.bfloat16))
+    return total + dot(jnp.concatenate(scaled, axis=1), pick_ref[:, LANES:], ((1,), (1,)))
+
+
+def near_back_kernel(
+    value_dim, block, q_ref, k_ref, v_ref, dy_ref, y_ref, inverse_ref, seg_ref, seg_row_ref,
+    state_ref, pick_ref, dq_ref, dk_ref, dv_ref, values_ref, sums_ref, dq_sum,
+):
+    length, width = dy_ref.shape
+    per = LANES // value_dim
+    seg = seg_ref[...]
+    keep = (seg == seg[:1, :]).astype(jnp.float32)
+    for number in range(PIECES):
+        span = slice(number * LANES, (number + 1) * LANES)
+        values, sums = halves(state_ref[0, 0, span, :])
+        values_ref[span, :] = spread_heads(values, value_dim, width).astype(jnp.bfloat16)
+        sums = jnp.where(head_mask(FEAT, 0, sums.shape), sums, 0.0) * (1 / FEAT)
+        sums_ref[span, :] = sums.astype(jnp.bfloat16)
+    d_top = (dy_ref[...].astype(jnp.float32) * inverse_ref[...] * keep).astype(jnp.bfloat16)
+    d_den = (d_den_lanes(value_dim, dy_ref, y_ref, inverse_ref) * keep).astype(jnp.bfloat16)
+    d_phi = dot(d_top, values_ref[...], ((1,), (1,))) + dot(d_den, sums_ref[...], ((1,), (1,)))
+    dq_sum[...] = from_features(d_phi, q_ref[...], pick_ref, FEAT ** (-0.5))
+    dk_ref[...] = jnp.zeros_like(dk_ref)
+    dv_ref[...] = jnp.zeros_like(dv_ref)
+    for begin in range(0, length, block):
+        stop = begin + block
+        mask = masks_of(seg_ref, seg_row_ref, begin, block)
+        queries = q_ref[begin:stop, :] * jnp.bfloat16(FEAT ** (-0.5))
+        keys = k_ref[:stop, :] * jnp.bfloat16(FEAT ** (-0.5))
+        for pair in range(GROUP // per):
+            span = slice(pair * LANES, (pair + 1) * LANES)
+            d_mixed = dy_ref[begin:stop, span].astype(jnp.float32)
+            inverse = inverse_ref[begin:stop, span]
+            d_numer = (d_mixed * inverse).astype(jnp.bfloat16)
+            product = d_mixed * inverse * y_ref[begin:stop, span].astype(jnp.float32)
+            values = v_ref[:stop, span]
+            for side in range(per):
+                head = pair * per + side
+                own_q = own_lanes(queries, FEAT, head)
+                own_dn = own_lanes(d_numer, value_dim, side)
+                scores = dot(own_q, k_ref[:stop, :], ((1,), (1,)))
+                weights = (((0.5 * scores + 1.0) * scores + 1.0) * mask).astype(jnp.bfloat16)
+                d_weights = dot(own_dn, values, ((1,), (1,))) - lane_sums(product, value_dim, side)
+                d_scores = (d_weights * ((scores + 1.0) * mask)).astype(jnp.bfloat16)
+                dv_ref[:stop, span] += dot(weights, own_dn, ((0,), (0,)))
+                dq_sum[begin:stop, :] += dot(d_scores, own_lanes(keys, FEAT, head))
+                dk_ref[:stop, :] += dot(d_scores, own_q, ((0,), (0,)))
+    dq_ref[...] = dq_sum[...].astype(dq_ref.dtype)
+
+
+def far_back_kernel(
+    value_dim, k_ref, v_ref, seg_ref, state_ref, dk_in_ref, dv_in_ref, pick_ref, dk_ref, dv_ref,
+    values_ref, sums_ref,
+):
+    length, width = dv_ref.shape
+    for number in range(PIECES):
+        span = slice(number * LANES, (number + 1) * LANES)
+        values, sums = halves(state_ref[0, 0, span, :])
+        values_ref[span, :] = spread_heads(values, value_dim, width).astype(jnp.bfloat16)
+        sums_ref[span, :] = (sums * (1 / LANES)).astype(jnp.bfloat16)
+    seg = seg_ref[...]
+    keep = (seg == seg[-1:, :]).astype(jnp.float32)
+    keys = k_ref[...]
+    ones = jnp.ones((length, LANES), jnp.bfloat16)
+    d_phi = dot(v_ref[...], values_ref[...], ((1,), (1,))) + dot(ones, sums_ref[...], ((1,), (1,)))
+    dk = dk_in_ref[...] + keep * from_features(d_phi, keys, pick_ref, 1.0)
+    dk_ref[...] = dk.astype(dk_ref.dtype)
+    phi = features(keys, pick_ref, 1.0)
+    dv_ref[...] = (dv_in_ref[...] + keep * dot(phi, values_ref[...])).astype(dv_ref.dtype)
+
+
+class Attention:
+    def __init__(self, rows, length, width):
+        self.rows, self.length = rows, length
+        self.value_dim = width // HEADS
+        self.groups = HEADS // GROUP
+        self.wide = GROUP * self.value_dim
+        self.block = min(256, length)
+        self.count = rows * length
+        length_, groups, wide = length, self.groups, self.wide
+        self.q = pl.BlockSpec((length, LANES), lambda r, g: (r, g))
+        self.k = pl.BlockSpec((length, LANES), lambda r, g: (r, groups + g))
+        self.v = pl.BlockSpec((length, wide), lambda r, g: (r, 2 * groups * LANES // wide + g))
+        self.y = pl.BlockSpec((length, wide), lambda r, g: (r, g))
+        self.seg = pl.BlockSpec((length, 1), lambda r, g: (r, 0))
+        self.seg_row = pl.BlockSpec((1, 1, length), lambda r, g: (r, 0, 0))
+        self.state = pl.BlockSpec((1, 1, WIDE, LANES), lambda r, g: (r, g, 0, 0))
+        self.whole = pl.BlockSpec((LANES, WIDE), lambda r, g: (0, 0))
+        self.whole_t = pl.BlockSpec((WIDE, LANES), lambda r, g: (0, 0))
+        self.scaled = jnp.asarray(rolls(True), jnp.bfloat16)
+        self.plain = jnp.asarray(rolls(False), jnp.bfloat16)
+        self.state_shape = jax.ShapeDtypeStruct((rows, groups, WIDE, LANES), jnp.bfloat16)
+        self.narrow = HEADS * FEAT
+
+    def shape(self, columns, dtype):
+        return jax.ShapeDtypeStruct((self.count, columns), dtype)
+
+    def call(self, kernel, specs, outs, out_specs, scratch, passes, name):
+        flops = self.rows * self.groups * GROUP * passes * 2 * 256**3
+        return pl.pallas_call(
+            kernel,
+            grid=(self.rows, self.groups),
+            in_specs=specs,
+            out_specs=out_specs,
+            out_shape=outs,
+            scratch_shapes=scratch,
+            compiler_params=pltpu.CompilerParams(
+                dimension_semantics=("arbitrary", "arbitrary"), vmem_limit_bytes=48 * 2**20
+            ),
+            cost_estimate=pl.CostEstimate(
+                flops=flops, bytes_accessed=2**22, transcendentals=0
+            ),
+            name=name,
+        )
+
+    def tail(self, qkv, seg):
+        return self.call(
+            functools.partial(tail_kernel, self.value_dim),
+            [self.k, self.v, self.seg, self.whole_t],
+            self.state_shape, self.state, [], 5, "attn_tail",
+        )(qkv, qkv, seg, self.plain.T)
+
+    def near(self, qkv, seg, seg_row):
+        out = self.shape(self.groups * self.wide, jnp.float32)
+        return self.call(
+            functools.partial(near_kernel, self.value_dim, self.block),
+            [self.q, self.k, self.v, self.seg, self.seg_row],
+            [out, out], [self.y, self.y], [], 8, "attn_near",
+        )(qkv, qkv, qkv, seg, seg_row)
+
+    def states(self):
+        return pltpu.VMEM((WIDE, self.wide), jnp.bfloat16)
+
+    def far(self, qkv, seg, state, top, den):
+        out = self.groups * self.wide
+        return self.call(
+            functools.partial(far_kernel, self.value_dim),
+            [self.q, self.seg, self.state, self.y, self.y, self.whole],
+            [self.shape(out, jnp.bfloat16), self.shape(out, jnp.float32)],
+            [self.y, self.y], [self.states(), self.states()], 8, "attn_far",
+        )(qkv, seg, state, top, den, self.scaled)
+
+    def head(self, qkv, dy, y, inverse, seg):
+        return self.call(
+            functools.partial(head_kernel, self.value_dim),
+            [self.q, self.y, self.y, self.y, self.seg, self.whole_t],
+            self.state_shape, self.state, [], 5, "attn_head",
+        )(qkv, dy, y, inverse, seg, self.scaled.T)
+
+    def near_back(self, qkv, dy, y, inverse, seg, seg_row, state):
+        wide = self.groups * self.wide
+        return self.call(
+            functools.partial(near_back_kernel, self.value_dim, self.block),
+            [self.q, self.k, self.v, self.y, self.y, self.y, self.seg, self.seg_row, self.state,
+             self.whole],
+            [self.shape(self.narrow, jnp.bfloat16), self.shape(self.narrow, jnp.float32),
+             self.shape(wide, jnp.float32)],
+            [self.q, self.q, self.y],
+            [self.states(), pltpu.VMEM((WIDE, LANES), jnp.bfloat16),
+             pltpu.VMEM((self.length, LANES), jnp.float32)], 24, "attn_near_back",
+        )(qkv, qkv, qkv, dy, y, inverse, seg, seg_row, state, self.scaled)
+
+    def far_back(self, qkv, seg, state, dk, dv):
+        wide = self.groups * self.wide
+        return self.call(
+            functools.partial(far_back_kernel, self.value_dim),
+            [self.k, self.v, self.seg, self.state, self.q, self.y, self.whole],
+            [self.shape(self.narrow, jnp.bfloat16), self.shape(wide, jnp.bfloat16)],
+            [self.q, self.y],
+            [self.states(), pltpu.VMEM((WIDE, LANES), jnp.bfloat16)], 9, "attn_far_back",
+        )(qkv, qkv, seg, state, dk, dv, self.plain)
+
+
+def pass_states(own, whole, linked, steps, axis, shift, size):
+    pairs = [(i, i + shift) for i in range(size) if 0 <= i + shift < size]
+    pick = lambda flag, array: jnp.where(flag[:, None, None, None], array, jnp.zeros_like(array))
+    came = None
+    for _ in range(steps):
+        total = own if came is None else own + pick(whole, came)
+        came = pick(linked, lax.ppermute(total, axis, pairs))
+    return came
 
 
 epsilon = 1e-05
-maximum_precision = lax.Precision.HIGHEST
 
 
 def across_rows(left, right):
-    return lax.dot_general(
-        left, right, (((0,), (0,)), ((), ())), preferred_element_type=jnp.float32
-    )
+    return dot(left, right, ((0,), (0,)))
 
 
 def against(left, matrix):
-    return lax.dot_general(
-        left, matrix, (((1,), (1,)), ((), ())), preferred_element_type=jnp.float32
-    )
-
-
-def split_packed(packed):
-    query_rows = packed[..., :FEAT]
-    key_rows = packed[..., FEAT : 2 * FEAT]
-    values = packed[..., 2 * FEAT :].astype(jnp.float32)
-    return (query_rows, key_rows, values)
-
-
-def block_terms(query_rows, key_rows, segments, begin_position):
-    stop_position = begin_position + BLOCK
-    scores = jnp.einsum(
-        "pyg,jyg->ypj",
-        query_rows[begin_position:stop_position],
-        key_rows[:stop_position],
-        preferred_element_type=jnp.float32,
-    ) * FEAT ** (-0.5)
-    q_places = begin_position + jnp.arange(BLOCK)
-    k_places = jnp.arange(stop_position)
-    kept_mask = (q_places[:, None] >= k_places[None, :]) & (
-        segments[begin_position:stop_position][:, None] == segments[:stop_position][None, :]
-    )
-    weights = jnp.where(kept_mask[None], 1.0 + scores + 0.5 * scores * scores, 0.0)
-    return (scores, kept_mask[None], weights)
-
-
-def attend_row(pair):
-    packed, segments = pair
-    query_rows, key_rows, values = split_packed(packed)
-    mixed_parts = []
-    denom_parts = []
-    for begin_position in range(0, LEN, BLOCK):
-        scores, kept_mask, weights = block_terms(query_rows, key_rows, segments, begin_position)
-        numerator = jnp.einsum(
-            "hqk,khc->qhc", weights, values[: begin_position + BLOCK], precision=maximum_precision
-        )
-        denominator = jnp.sum(weights, axis=2).T
-        mixed_parts.append(numerator / denominator[:, :, None])
-        denom_parts.append(denominator)
-    return (jnp.concatenate(mixed_parts, 0), jnp.concatenate(denom_parts, 0))
-
-
-def attend_back(bundle):
-    packed, segments, mixed, denominator, d_mixed = bundle
-    query_rows, key_rows, values = split_packed(packed)
-    complete_query_rows = query_rows.astype(jnp.float32)
-    complete_key_rows = key_rows.astype(jnp.float32)
-    d_mixed = d_mixed.astype(jnp.float32)
-    d_numer = d_mixed / denominator[:, :, None]
-    d_denom = -jnp.sum(d_mixed * mixed, axis=2) / denominator
-    d_query_parts = []
-    d_keys = jnp.zeros_like(complete_key_rows)
-    d_values = jnp.zeros_like(values)
-    for begin_position in range(0, LEN, BLOCK):
-        stop_position = begin_position + BLOCK
-        scores, kept_mask, weights = block_terms(query_rows, key_rows, segments, begin_position)
-        d_weights = jnp.einsum(
-            "qhc,khc->hqk",
-            d_numer[begin_position:stop_position],
-            values[:stop_position],
-            precision=maximum_precision,
-        )
-        d_weights = jnp.where(
-            kept_mask, d_weights + d_denom[begin_position:stop_position].T[:, :, None], 0.0
-        )
-        d_values = d_values.at[:stop_position].add(
-            jnp.einsum(
-                "hqk,qhc->khc",
-                weights,
-                d_numer[begin_position:stop_position],
-                precision=maximum_precision,
-            )
-        )
-        score_gradient = d_weights * (1.0 + scores) * FEAT ** (-0.5)
-        d_query_parts.append(
-            jnp.einsum(
-                "ouw,wor->uor",
-                score_gradient,
-                complete_key_rows[:stop_position],
-                precision=maximum_precision,
-            )
-        )
-        d_keys = d_keys.at[:stop_position].add(
-            jnp.einsum(
-                "urs,ruw->suw",
-                score_gradient,
-                complete_query_rows[begin_position:stop_position],
-                precision=maximum_precision,
-            )
-        )
-    d_query = jnp.concatenate(d_query_parts, 0)
-    return jnp.concatenate([d_query, d_keys, d_values], axis=2).astype(jnp.bfloat16)
+    return dot(left, matrix, ((1,), (1,)))
 
 
 def norm_forward(values):
@@ -315,16 +597,15 @@
 ):
     rows, shard_len, width = layer_input.shape
     count = rows * shard_len
-    value_dim = width // HEADS
-    features = HEADS * FEAT
+    narrow = HEADS * FEAT
     qkv_part = jnp.concatenate([w_query, w_key, w_value], axis=1)
     down_part = w_down.T
     gains = jnp.stack([gain_attn, gain_mlp], axis=1)
     gains = jnp.pad(gains, ((0, 0), (0, 126)))
     head = gather_rows(jnp.concatenate([qkv_part, gains], axis=1), shape, "zxyc")
-    qkv_w = head[:, : 2 * features + width]
-    gain_one = head[:, 2 * features + width].astype(jnp.float32)
-    gain_two = head[:, 2 * features + width + 1].astype(jnp.float32)
+    qkv_w = head[:, : 2 * narrow + width]
+    gain_one = head[:, 2 * narrow + width].astype(jnp.float32)
+    gain_two = head[:, 2 * narrow + width + 1].astype(jnp.float32)
     out_w = gather_rows(w_out, shape, "xyzc")
     gate_w = gather_rows(w_gate, shape, "zxyc")
     up_w = gather_rows(w_up, shape, "zyxc")
@@ -334,20 +615,20 @@
     scale_one, normed_one = norm_forward(tokens)
     a_one = (normed_one * gain_one).astype(jnp.bfloat16)
     qkv = jnp.dot(a_one, qkv_w, preferred_element_type=jnp.float32).astype(jnp.bfloat16)
-    packed = jnp.concatenate(
-        [
-            qkv[:, :features].reshape(rows, shard_len, HEADS, FEAT),
-            qkv[:, features : 2 * features].reshape(rows, shard_len, HEADS, FEAT),
-            qkv[:, 2 * features :].reshape(rows, shard_len, HEADS, value_dim),
-        ],
-        axis=3,
-    )
-    by_heads = lax.all_to_all(packed, "seq", split_axis=2, concat_axis=1, tiled=True)
-    mixed, denominator = lax.map(attend_row, (by_heads, segment_ids))
-    mixed_seq = lax.all_to_all(
-        mixed.astype(jnp.bfloat16), "seq", split_axis=1, concat_axis=2, tiled=True
-    )
-    mixed_cat = mixed_seq.reshape(count, width)
+    attention = Attention(rows, shard_len, width)
+    place = lax.axis_index("seq")
+    own_seg = lax.dynamic_slice_in_dim(segment_ids, place * shard_len, shard_len, 1)
+    before = jnp.maximum(place * shard_len - 1, 0)
+    after = jnp.minimum((place + 1) * shard_len, segment_ids.shape[1] - 1)
+    first, last = own_seg[:, 0], own_seg[:, -1]
+    from_before = lax.dynamic_index_in_dim(segment_ids, before, 1, keepdims=False) == first
+    from_after = lax.dynamic_index_in_dim(segment_ids, after, 1, keepdims=False) == last
+    seg, seg_row = own_seg.reshape(count, 1), own_seg.reshape(rows, 1, shard_len)
+    reach = min(shape.seq - 1, -(-(LONGEST - 1) // shard_len))
+    tail = attention.tail(qkv, seg)
+    earlier = pass_states(tail, first == last, from_before, reach, "seq", 1, shape.seq)
+    top, den = attention.near(qkv, seg, seg_row)
+    mixed_cat, inverse = attention.far(qkv, seg, earlier, top, den)
     x_two = tokens + jnp.dot(mixed_cat, out_w, preferred_element_type=jnp.float32)
     scale_two, normed_two = norm_forward(x_two)
     a_two = (normed_two * gain_two).astype(jnp.bfloat16)
@@ -371,20 +652,14 @@
     )
     d_branch = d_x_two.astype(jnp.bfloat16)
     grad_out = scatter_rows(mixed_cat, d_branch, shape, "cxyz")
-    d_mixed = (
-        against(d_branch, out_w).astype(jnp.bfloat16).reshape(rows, shard_len, HEADS, value_dim)
+    d_mixed = against(d_branch, out_w).astype(jnp.bfloat16)
+    ahead = attention.head(qkv, d_mixed, mixed_cat, inverse, seg)
+    later = pass_states(ahead, first == last, from_after, reach, "seq", -1, shape.seq)
+    d_query, d_keys, d_values = attention.near_back(
+        qkv, d_mixed, mixed_cat, inverse, seg, seg_row, earlier
     )
-    d_mixed_heads = lax.all_to_all(d_mixed, "seq", split_axis=2, concat_axis=1, tiled=True)
-    d_packed = lax.map(attend_back, (by_heads, segment_ids, mixed, denominator, d_mixed_heads))
-    d_packed_seq = lax.all_to_all(d_packed, "seq", split_axis=1, concat_axis=2, tiled=True)
-    d_qkv = jnp.concatenate(
-        [
-            d_packed_seq[..., :FEAT].reshape(count, features),
-            d_packed_seq[..., FEAT : 2 * FEAT].reshape(count, features),
-            d_packed_seq[..., 2 * FEAT :].reshape(count, width),
-        ],
-        axis=1,
-    )
+    d_keys, d_values = attention.far_back(qkv, seg, later, d_keys, d_values)
+    d_qkv = jnp.concatenate([d_query, d_keys, d_values], axis=1)
     grad_qkv = scatter_rows(a_one, d_qkv, shape, "cyxz")
     d_a_one = against(d_qkv, qkv_w)
     d_tokens = d_x_two + norm_backward(d_a_one, gain_one, scale_one, normed_one)
@@ -392,9 +667,9 @@
         result.reshape(rows, shard_len, width),
         d_tokens.reshape(rows, shard_len, width),
         gain_gradient(qkv_part, grad_qkv, gain_attn),
-        grad_qkv[:, :features],
-        grad_qkv[:, features : 2 * features],
-        grad_qkv[:, 2 * features :],
+        grad_qkv[:, :narrow],
+        grad_qkv[:, narrow : 2 * narrow],
+        grad_qkv[:, 2 * narrow :],
         grad_out,
         gain_gradient(
             jnp.concatenate([w_gate, w_up], axis=1),

time: 1150 us -> 652 us (0.57)
  matrix products: 515 us -> 174 us
  local copies, waits for them, and re-layouts: 214 us -> 93.6 us
  Pallas kernels: 25.1 us -> 125 us
  waiting for transfers between devices: 170 us -> 104 us
  other arithmetic: 83.2 us -> 40.4 us
  loops' own time: 38.9 us -> 0 us
  starting transfers between devices: 79.7 us -> 96 us
    dot_general x78 -> x22, matrix products: 448 us -> 109 us  [dot(): lax.dot_general(left, right, (dims, ((), ())), preferred_element_type=jnp...]
    pallas_call x0 -> x6, Pallas kernels: none -> 99.5 us  [the longest x1 38.8 us: near_back(): self.call(functools.partial(near_back_kernel, self.value_dim, self.block)...]
    ppermute x78, waiting for transfers between devices: 153 us -> 104 us  [send(): return lax.ppermute(array, self.axis, self.pairs)]
    another operation x2 -> x0, loops' own time: 38.9 us -> none  [the longest x1 31.8 us: per_device(): mixed, denominator = lax.map(attend_row, (by_heads, segment_ids))]
    all_to_all x6 -> x0, local copies, waits for them, and re-layouts: 32.7 us -> none  [the longest x1 10.2 us: per_device(): lax.all_to_all(mixed.astype(jnp.bfloat16), 'seq', split_axis=1, concat_ax...]
    while x65 -> x0, local copies, waits for them, and re-layouts: 26.9 us -> none
    ppermute x78, starting transfers between devices: 63 us -> 88.9 us  [send(): return lax.ppermute(array, self.axis, self.pairs)]
    unnamed x196 -> x179, local copies, waits for them, and re-layouts: 33.3 us -> 13.5 us
  transfers between devices with their start and end apart: 82 -> 82, of which waited for: 22 -> 28; matrix products, arithmetic and copies ran while one was open for 58% -> 30% of each run, Pallas kernels for 2% -> 18%
where the time goes in v2:
time: 652 us; the launch traced here: 642 us
  matrix products  174 us (27%)
  Pallas kernels  125 us (19%)
  waiting for transfers between devices  104 us (16%)
  starting transfers between devices  96 us (15%)
  local copies, waits for them, and re-layouts  93.6 us (14%)
  other arithmetic  40.4 us (6%)
  between operations  9.01 us (1%)
    dot_general x22, matrix products, dot(): lax.dot_general(left, right, (dims, ((), ())), preferred_element_type=jnp...  109 us
    ppermute x78, waiting for transfers between devices, send(): return lax.ppermute(array, self.axis, self.pairs)  104 us
    ppermute x78, starting transfers between devices, send(): return lax.ppermute(array, self.axis, self.pairs)  88.9 us
    ppermute x26, local copies, waits for them, and re-layouts, send(): return lax.ppermute(array, self.axis, self.pairs)  56.4 us
    pallas_call x1, Pallas kernels, near_back(): self.call(functools.partial(near_back_kernel, self.value_dim, self.block)...  38.8 us
    pallas_call x5, Pallas kernels, assemble(): pl.pallas_call(kernel, out_shape=jax.ShapeDtypeStruct((devices * block, c...  25.2 us
    dot_general x5, matrix products, reorder(): jnp.dot(left, pick, preferred_element_type=jnp.float32).astype(jnp.bfloat16)  20.3 us
    dot_general x1, matrix products, per_device(): d_hidden = jnp.dot(cotangent, down_w, preferred_element_type=jnp.float32)  20.3 us
  transfers between devices with their start and end apart: 82, of which 28 were waited for; matrix products, arithmetic and copies ran while one was open for 30% of the time, Pallas kernels for 18%

profile of v2, /device:TPU:0, one launch (start us, length us, event | category | flops | bytes accessed | tf_op | source)
XLA Modules:
  0.0 641.7 jit_solution(4779277139553665721)
XLA Ops:
  33.8 7.1 %collective-permute-done.2 = bf16[32,1664]{1,0:T(8,128)(2,1)S(1)} collective-permute-done((bf16[32,1664]{1,0:T(8,128)(2,1)S(1)}, bf16[32,1664]{1,0:T(8,128)(2,1)S(1)}, u32[]{:S(2)}, u32[]{:S(2)}) %collective-permute-start.2) | collective-permute-done | bytes 106528 | tf_op jit(solution)/shard_map/ppermute | solution.py:433
  54.6 6.2 collective-permute-done.33
  98.0 10.8 %attn_tail.1 = bf16[2,2,1280,128]{3,2,1,0:T(8,128)(2,1)S(1)} custom-call(bf16[1024,1536]{1,0:T(8,128)(2,1)S(1)} %convolution_convert_fusion.3.k_ref.v_ref.q_ref, bf16[1024,1536]{1,0:T(8,128)(2,1)S(1)} %convolution_convert_fusion.3.k_ref.v_ref.q_ref, s32[1024,1]{1,0:T(8,128)S(1)} %bitcast.149, bf16[1280,128]{1,0:T(8,128)(2,1)S(1)} %copy-done.5), custom_call_target="tpu_custom_call" | custom-call | flops 5368709120 | bytes 4194304 | tf_op jit(solution)/shard_map/attn_tail/pallas_call | solution.py:329
  117.3 5.3 convert_bitcast_fusion
  122.6 8.5 %collective-permute-done.26 = bf16[128,2752]{0,1:T(8,128)(2,1)} collective-permute-done((bf16[128,2752]{0,1:T(8,128)(2,1)}, bf16[128,2752]{0,1:T(8,128)(2,1)}, u32[]{:S(2)}, u32[]{:S(2)}) %collective-permute-start.26) | collective-permute-done | bytes 704544 | tf_op jit(solution)/shard_map/ppermute | solution.py:433
  154.9 11.2 %collective-permute-start.38 = (bf16[128,2752]{0,1:T(8,128)(2,1)}, bf16[128,2752]{0,1:T(8,128)(2,1)}, u32[]{:S(2)}, u32[]{:S(2)}) collective-permute-start(bf16[128,2752]{0,1:T(8,128)(2,1)} %collective-permute-done.34), channel_id=1, source_target_pairs={{0,1},{1,0},{2,3},{3,2},{4,5},{5,4},{6,7},{7,6},{8,9},{9,8},{10,11... | collective-permute-start | bytes 2113544 | tf_op jit(solution)/shard_map/ppermute | solution.py:433
  177.9 7.6 %collective-permute-done.45 = bf16[128,2752]{0,1:T(8,128)(2,1)} collective-permute-done((bf16[128,2752]{0,1:T(8,128)(2,1)}, bf16[128,2752]{0,1:T(8,128)(2,1)}, u32[]{:S(2)}, u32[]{:S(2)}) %collective-permute-start.45) | collective-permute-done | bytes 704544 | tf_op jit(solution)/shard_map/ppermute | solution.py:433
  185.5 10.0 %attn_near.1 = (f32[1024,1024]{1,0:T(8,128)}, f32[1024,1024]{1,0:T(8,128)}) custom-call(bf16[1024,1536]{1,0:T(8,128)(2,1)S(1)} %copy-done.7, bf16[1024,1536]{1,0:T(8,128)(2,1)S(1)} %copy-done.7, bf16[1024,1536]{1,0:T(8,128)(2,1)S(1)} %copy-done.7, s32[1024,1]{1,0:T(8,128)S(1)} %bitcast.150, s32[2,1,512]{2,1,0:T(1,128)S(1)} %reshape.4838.seg_row_ref), custom_call_target="tpu_custom_call" | custom-call | flops 8589934592 | bytes 4194304 | tf_op jit(solution)/shard_map/attn_near/pallas_call | solution.py:337
  215.8 6.0 assemble.7
  224.1 6.0 assemble.8
  235.8 6.1 assemble.9
  242.2 11.3 %attn_far.1 = (bf16[1024,1024]{1,0:T(8,128)(2,1)S(1)}, f32[1024,1024]{1,0:T(8,128)}) custom-call(bf16[1024,1536]{1,0:T(8,128)(2,1)} %copy-done.6, s32[1024,1]{1,0:T(8,128)S(1)} %bitcast.151, bf16[2,2,1280,128]{3,2,1,0:T(8,128)(2,1)S(1)} %broadcast_select_fusion.1.state_ref, f32[1024,1024]{1,0:T(8,128)} %get-tuple-element.20.top_ref, ...), custom_call_target="tpu_custom_call" | custom-call | flops 8589934592 | bytes 4194304 | tf_op jit(solution)/shard_map/attn_far/pallas_call | solution.py:348
  261.9 9.0 %fusion.85 = f32[1024,2752]{0,1:T(8,128)} fusion(bf16[1024,1024]{1,0:T(8,128)(2,1)S(1)} %multiply_convert_fusion.1, bf16[1024,2752]{1,0:T(8,128)(2,1)S(1)} %bitcast.160), kind=kOutput, calls=%fused_computation.186 | convolution fusion | flops 5771362304 | bytes 19005440 | tf_op jit(solution)/shard_map/dot_general | solution.py:635
  270.8 9.0 %fusion.86 = f32[1024,2752]{0,1:T(8,128)} fusion(bf16[1024,1024]{1,0:T(8,128)(2,1)S(1)} %multiply_convert_fusion.1, bf16[1024,2752]{1,0:T(8,128)(2,1)S(1)} %bitcast.162), kind=kOutput, calls=%fused_computation.187 | convolution fusion | flops 5771362304 | bytes 19005440 | tf_op jit(solution)/shard_map/dot_general | solution.py:636
  279.8 20.3 %fusion.2 = (bf16[1024,2752]{0,1:T(8,128)(2,1)}, bf16[1024,2752]{0,1:T(8,128)(2,1)}, bf16[1024,2752]{0,1:T(8,128)(2,1)}) fusion(f32[1024,2752]{0,1:T(8,128)} %fusion.86, f32[1024,2752]{0,1:T(8,128)} %fusion.85, bf16[1024,2752]{1,0:T(8,128)(2,1)} %assemble.9, bf16[1024,1024]{1,0:T(8,128)(2,1)S(1)} %bitcast.158), kind=kOutput, calls=%fused_computation.4 | convolution fusion | flops 5813633024 | bytes 47185920 | tf_op jit(solution)/shard_map/dot_general | solution.py:644
  300.1 7.8 %convolution_convert_fusion.1 = bf16[512,2752]{0,1:T(8,128)(2,1)} fusion(bf16[1024,2752]{0,1:T(8,128)(2,1)} %get-tuple-element.69, bf16[1024,1024]{1,0:T(8,128)(2,1)} %fusion.34), kind=kOutput, calls=%fused_computation.10 | convolution fusion | flops 2887090176 | bytes 9502720 | tf_op jit(solution)/shard_map/dot_general | solution.py:21
  320.0 9.8 %add_convert_fusion = bf16[1024,1024]{1,0:T(8,128)(2,1)} fusion(f32[1024,1024]{1,0:T(8,128)S(1)} %copy-done.11, bf16[1024,2752]{0,1:T(8,128)(2,1)S(1)} %bitcast.156, bf16[1024,2752]{1,0:T(8,128)(2,1)} %assemble.9), kind=kOutput, calls=%fused_computation.34 | convolution fusion | flops 5773459456 | bytes 17563648 | tf_op jit(solution)/shard_map/dot_general | solution.py:21
  334.3 11.2 %fusion.87 = f32[1024,1024]{1,0:T(8,128)} fusion(bf16[1024,2752]{0,1:T(8,128)(2,1)} %get-tuple-element.70, bf16[1024,2752]{1,0:T(8,128)(2,1)} %assemble.8), kind=kOutput, calls=%fused_computation.188 | convolution fusion | flops 5771362304 | bytes 15466496 | tf_op jit(solution)/shard_map/dot_general | solution.py:21
  345.5 12.5 %multiply_reduce_fusion = (f32[1024]{0:T(1024)S(1)}, f32[1024,1024]{1,0:T(8,128)}) fusion(f32[1024,1024]{1,0:T(8,128)S(1)} %copy-done.11, f32[1024]{0:T(1024)S(1)} %add_rsqrt_fusion, f32[1024]{0:T(1024)S(1)} %get-tuple-element.62, f32[1024,1024]{1,0:T(8,128)} %fusion.87, bf16[1024,2752]{0,1:T(8,128)(2,1)} %get-tuple-element.69, bf16[1024,2752]{1,0:T(8,128)(2,1)} %assemble.7), kind=kOutput, calls=%fused_computation.32 | convolution fusion | flops 5776604160 | bytes 23867392 | tf_op jit(solution)/shard_map/dot_general | solution.py:21
  366.5 38.8 %attn_near_back.1 = (bf16[1024,256]{1,0:T(8,128)(2,1)S(1)}, f32[1024,256]{1,0:T(8,128)S(1)}, f32[1024,1024]{1,0:T(8,128)}) custom-call(bf16[1024,1536]{1,0:T(8,128)(2,1)} %copy-done.6, bf16[1024,1536]{1,0:T(8,128)(2,1)} %copy-done.6, bf16[1024,1536]{1,0:T(8,128)(2,1)} %copy-done.6, bf16[1024,1024]{1,0:T(8,128)(2,1)S(1)} %convolution_convert_fusion.5.dy_ref, ...), custom_call_target="tpu_custom_call" | custom-call | flops 25769803776 | bytes 4194304 | tf_op jit(solution)/shard_map/attn_near_back/pallas_call | solution.py:364
  405.3 15.0 %attn_head.1 = bf16[2,2,1280,128]{3,2,1,0:T(8,128)(2,1)S(1)} custom-call(bf16[1024,1536]{1,0:T(8,128)(2,1)} %copy-done.6, bf16[1024,1024]{1,0:T(8,128)(2,1)S(1)} %convolution_convert_fusion.5.dy_ref, bf16[1024,1024]{1,0:T(8,128)(2,1)} %copy-done.8, f32[1024,1024]{1,0:T(8,128)} %get-tuple-element.23.inverse_ref, s32[1024,1]{1,0:T(8,128)S(1)} %bitcast.153, ...), custom_call_target="tpu_custom_call" | custom-call | flops 5368709120 | bytes 4194304 | tf_op jit(solution)/shard_map/attn_head/pallas_call | solution.py:356
  426.3 7.2 %convolution_convert_fusion = bf16[512,2752]{0,1:T(8,128)(2,1)} fusion(bf16[1024,2752]{0,1:T(8,128)(2,1)} %get-tuple-element.70, bf16[1024,1024]{1,0:T(8,128)(2,1)S(1)} %copy-done.70), kind=kOutput, calls=%fused_computation.9 | convolution fusion | flops 2887090176 | bytes 9502720 | tf_op jit(solution)/shard_map/dot_general | solution.py:21
  440.0 10.0 %collective-permute-done.59 = bf16[256,1024]{1,0:T(8,128)(2,1)S(1)} collective-permute-done((bf16[256,1024]{1,0:T(8,128)(2,1)S(1)}, bf16[256,1024]{1,0:T(8,128)(2,1)S(1)}, u32[]{:S(2)}, u32[]{:S(2)}) %collective-permute-start.59) | collective-permute-done | bytes 524320 | tf_op jit(solution)/shard_map/ppermute | solution.py:433
  455.5 4.7 collective-permute-done.60
  477.0 13.6 %attn_far_back.1 = (bf16[1024,256]{1,0:T(8,128)(2,1)S(1)}, bf16[1024,1024]{1,0:T(8,128)(2,1)S(1)}) custom-call(bf16[1024,1536]{1,0:T(8,128)(2,1)} %copy-done.6, bf16[1024,1536]{1,0:T(8,128)(2,1)} %copy-done.6, s32[1024,1]{1,0:T(8,128)S(1)} %bitcast.154, bf16[2,2,1280,128]{3,2,1,0:T(8,128)(2,1)S(1)} %broadcast_select_fusion.state_ref, ...), custom_call_target="tpu_custom_call" | custom-call | flops 9663676416 | bytes 4194304 | tf_op jit(solution)/shard_map/attn_far_back/pallas_call | solution.py:377
  493.1 5.1 convolution_convert_fusion.4
  498.2 5.5 fusion.9
  511.9 5.9 add_convert_fusion.2
  519.5 6.4 %collective-permute-done.77 = bf16[128,2752]{0,1:T(8,128)(2,1)S(1)} collective-permute-done((bf16[128,2752]{0,1:T(8,128)(2,1)S(1)}, bf16[128,2752]{0,1:T(8,128)(2,1)S(1)}, u32[]{:S(2)}, u32[]{:S(2)}) %collective-permute-start.77) | collective-permute-done | bytes 704544 | tf_op jit(solution)/shard_map/ppermute | solution.py:433
  562.3 10.3 %collective-permute-done.71 = bf16[256,2752]{0,1:T(8,128)(2,1)} collective-permute-done((bf16[256,2752]{0,1:T(8,128)(2,1)}, bf16[256,2752]{0,1:T(8,128)(2,1)}, u32[]{:S(2)}, u32[]{:S(2)}) %collective-permute-start.71) | collective-permute-done | bytes 1409056 | tf_op jit(solution)/shard_map/ppermute | solution.py:433
  627.8 6.0 collective-permute-done.56
  634.5 5.0 collective-permute-done.57
  (476 shorter events, 323.4 us)
Async XLA Ops:
  0.7 26.8 %collective-permute-start.21 = (bf16[32,2752]{1,0:T(8,128)(2,1)}, bf16[32,2752]{1,0:T(8,128)(2,1)S(1)}, u32[]{:S(2)}, u32[]{:S(2)}) collective-permute-start(bf16[32,2752]{1,0:T(8,128)(2,1)} %param.2582), channel_id=1, source_target_pairs={{0,8},{4,12},{8,24},{12,28},{16,0},{20,4},{24,16},{28,20},{1,9},{5... | collective-permute-start | bytes 528392 | tf_op jit(solution)/shard_map/ppermute | solution.py:433
  5.4 21.3 %collective-permute-start = (bf16[32,1664]{1,0:T(8,128)(2,1)S(1)}, bf16[32,1664]{1,0:T(8,128)(2,1)}, u32[]{:S(2)}, u32[]{:S(2)}) collective-permute-start(bf16[32,1664]{1,0:T(8,128)(2,1)S(1)} %pad_maximum_fusion.4), channel_id=1, source_target_pairs={{0,8},{4,12},{8,24},{12,28},{16,0},{20,4},{24,16},{28,20},{1,9},{5... | collective-permute-start | bytes 319496 | tf_op jit(solution)/shard_map/ppermute | solution.py:433
  9.5 19.8 %collective-permute-start.31 = (bf16[32,2752]{1,0:T(8,128)(2,1)}, bf16[32,2752]{1,0:T(8,128)(2,1)S(1)}, u32[]{:S(2)}, u32[]{:S(2)}) collective-permute-start(bf16[32,2752]{1,0:T(8,128)(2,1)} %param.2583), channel_id=1, source_target_pairs={{0,8},{4,12},{8,24},{12,28},{16,0},{20,4},{24,16},{28,20},{1,9},{5... | collective-permute-start | bytes 528392 | tf_op jit(solution)/shard_map/ppermute | solution.py:433
  27.1 37.6 %collective-permute-start.42 = (bf16[64,2752]{1,0:T(8,128)(2,1)S(1)}, bf16[64,2752]{1,0:T(8,128)(2,1)S(1)}, u32[]{:S(2)}, u32[]{:S(2)}) collective-permute-start(bf16[64,2752]{1,0:T(8,128)(2,1)S(1)} %pad_maximum_fusion.2), channel_id=1, source_target_pairs={{0,2},{1,3},{2,0},{3,1},{4,6},{5,7},{6,4},{7,5},{8,10},{9,11},{10,... | collective-permute-start | bytes 1056776 | tf_op jit(solution)/shard_map/ppermute | solution.py:433
  54.5 20.8 %collective-permute-start.6 = (bf16[128,1664]{1,0:T(8,128)(2,1)}, bf16[128,1664]{1,0:T(8,128)(2,1)}, u32[]{:S(2)}, u32[]{:S(2)}) collective-permute-start(bf16[128,1664]{1,0:T(8,128)(2,1)} %pad_maximum_fusion.1.refs_0_), channel_id=1, source_target_pairs={{0,1},{1,0},{2,3},{3,2},{4,5},{5,4},{6,7},{7,6},{8,9},{9,8},{10,11... | collective-permute-start | bytes 1277960 | tf_op jit(solution)/shard_map/ppermute | solution.py:433
  85.2 24.1 %collective-permute-start.34 = (bf16[128,2752]{0,1:T(8,128)(2,1)}, bf16[128,2752]{0,1:T(8,128)(2,1)}, u32[]{:S(2)}, u32[]{:S(2)}) collective-permute-start(bf16[128,2752]{0,1:T(8,128)(2,1)} %copy.2723), channel_id=1, source_target_pairs={{0,2},{1,3},{2,0},{3,1},{4,6},{5,7},{6,4},{7,5},{8,10},{9,11},{10,... | collective-permute-start | bytes 2113544 | tf_op jit(solution)/shard_map/ppermute | solution.py:433
  90.9 20.5 %collective-permute-start.35 = (bf16[128,2752]{0,1:T(8,128)(2,1)}, bf16[128,2752]{0,1:T(8,128)(2,1)}, u32[]{:S(2)}, u32[]{:S(2)}) collective-permute-start(bf16[128,2752]{0,1:T(8,128)(2,1)} %copy.2723), channel_id=1, source_target_pairs={{0,4},{4,0},{8,12},{12,8},{16,20},{20,16},{24,28},{28,24},{1,5},{5... | collective-permute-start | bytes 2113544 | tf_op jit(solution)/shard_map/ppermute | solution.py:433
  109.3 57.2 %collective-permute-start.10 = (bf16[2,2,1280,128]{3,2,1,0:T(8,128)(2,1)S(1)}, bf16[2,2,1280,128]{3,2,1,0:T(8,128)(2,1)S(1)}, u32[]{:S(2)}, u32[]{:S(2)}) collective-permute-start(bf16[2,2,1280,128]{3,2,1,0:T(8,128)(2,1)S(1)} %attn_tail.1), channel_id=1, source_target_pairs={{0,1},{1,2},{2,3},{4,5},{5,6},{6,7},{8,9},{9,10},{10,11},{12,13},{... | collective-permute-start | bytes 3932168 | tf_op jit(solution)/shard_map/ppermute | solution.py:392
  113.4 41.5 %collective-permute-start.28 = (bf16[128,2752]{0,1:T(8,128)(2,1)}, bf16[128,2752]{0,1:T(8,128)(2,1)}, u32[]{:S(2)}, u32[]{:S(2)}) collective-permute-start(bf16[128,2752]{0,1:T(8,128)(2,1)} %collective-permute-done.24), channel_id=1, source_target_pairs={{0,1},{1,0},{2,3},{3,2},{4,5},{5,4},{6,7},{7,6},{8,9},{9,8},{10,11... | collective-permute-start | bytes 2113544 | tf_op jit(solution)/shard_map/ppermute | solution.py:433
  113.4 52.6 %collective-permute-start.29 = (bf16[128,2752]{0,1:T(8,128)(2,1)}, bf16[128,2752]{0,1:T(8,128)(2,1)}, u32[]{:S(2)}, u32[]{:S(2)}) collective-permute-start(bf16[128,2752]{0,1:T(8,128)(2,1)} %collective-permute-done.25), channel_id=1, source_target_pairs={{0,1},{1,0},{2,3},{3,2},{4,5},{5,4},{6,7},{7,6},{8,9},{9,8},{10,11... | collective-permute-start | bytes 2113544 | tf_op jit(solution)/shard_map/ppermute | solution.py:433
  114.4 51.7 %collective-permute-start.44 = (bf16[128,2752]{0,1:T(8,128)(2,1)}, bf16[128,2752]{0,1:T(8,128)(2,1)}, u32[]{:S(2)}, u32[]{:S(2)}) collective-permute-start(bf16[128,2752]{0,1:T(8,128)(2,1)} %collective-permute-done.43), channel_id=1, source_target_pairs={{0,8},{4,12},{8,24},{12,28},{16,0},{20,4},{24,16},{28,20},{1,9},{5... | collective-permute-start | bytes 2113544 | tf_op jit(solution)/shard_map/ppermute | solution.py:433
  131.1 38.1 %collective-permute-start.36 = (bf16[128,2752]{0,1:T(8,128)(2,1)}, bf16[128,2752]{0,1:T(8,128)(2,1)}, u32[]{:S(2)}, u32[]{:S(2)}) collective-permute-start(bf16[128,2752]{0,1:T(8,128)(2,1)} %collective-permute-done.34), channel_id=1, source_target_pairs={{0,4},{4,0},{8,12},{12,8},{16,20},{20,16},{24,28},{28,24},{1,5},{5... | collective-permute-start | bytes 2113544 | tf_op jit(solution)/shard_map/ppermute | solution.py:433
  154.9 20.1 %collective-permute-start.38 = (bf16[128,2752]{0,1:T(8,128)(2,1)}, bf16[128,2752]{0,1:T(8,128)(2,1)}, u32[]{:S(2)}, u32[]{:S(2)}) collective-permute-start(bf16[128,2752]{0,1:T(8,128)(2,1)} %collective-permute-done.34), channel_id=1, source_target_pairs={{0,1},{1,0},{2,3},{3,2},{4,5},{5,4},{6,7},{7,6},{8,9},{9,8},{10,11... | collective-permute-start | bytes 2113544 | tf_op jit(solution)/shard_map/ppermute | solution.py:433
  169.2 72.8 %collective-permute-start.11 = (bf16[2,2,1280,128]{3,2,1,0:T(8,128)(2,1)}, bf16[2,2,1280,128]{3,2,1,0:T(8,128)(2,1)S(1)}, u32[]{:S(2)}, u32[]{:S(2)}) collective-permute-start(bf16[2,2,1280,128]{3,2,1,0:T(8,128)(2,1)} %select_add_fusion.1), channel_id=1, source_target_pairs={{0,1},{1,2},{2,3},{4,5},{5,6},{6,7},{8,9},{9,10},{10,11},{12,13},{... | collective-permute-start | bytes 3932168 | tf_op jit(solution)/shard_map/ppermute | solution.py:392
  175.0 57.3 %collective-permute-start.48 = (bf16[128,2752]{0,1:T(8,128)(2,1)}, bf16[128,2752]{0,1:T(8,128)(2,1)S(1)}, u32[]{:S(2)}, u32[]{:S(2)}) collective-permute-start(bf16[128,2752]{0,1:T(8,128)(2,1)} %collective-permute-done.44), channel_id=1, source_target_pairs={{0,1},{1,0},{2,3},{3,2},{4,5},{5,4},{6,7},{7,6},{8,9},{9,8},{10,11... | collective-permute-start | bytes 2113544 | tf_op jit(solution)/shard_map/ppermute | solution.py:433
  177.4 36.1 %collective-permute-start.30 = (bf16[128,2752]{0,1:T(8,128)(2,1)}, bf16[128,2752]{0,1:T(8,128)(2,1)}, u32[]{:S(2)}, u32[]{:S(2)}) collective-permute-start(bf16[128,2752]{0,1:T(8,128)(2,1)} %collective-permute-done.26), channel_id=1, source_target_pairs={{0,1},{1,0},{2,3},{3,2},{4,5},{5,4},{6,7},{7,6},{8,9},{9,8},{10,11... | collective-permute-start | bytes 2113544 | tf_op jit(solution)/shard_map/ppermute | solution.py:433
  177.5 44.3 %collective-permute-start.40 = (bf16[128,2752]{0,1:T(8,128)(2,1)}, bf16[128,2752]{0,1:T(8,128)(2,1)}, u32[]{:S(2)}, u32[]{:S(2)}) collective-permute-start(bf16[128,2752]{0,1:T(8,128)(2,1)} %collective-permute-done.36), channel_id=1, source_target_pairs={{0,1},{1,0},{2,3},{3,2},{4,5},{5,4},{6,7},{7,6},{8,9},{9,8},{10,11... | collective-permute-start | bytes 2113544 | tf_op jit(solution)/shard_map/ppermute | solution.py:433
  185.5 48.0 %collective-permute-start.49 = (bf16[128,2752]{0,1:T(8,128)(2,1)}, bf16[128,2752]{0,1:T(8,128)(2,1)}, u32[]{:S(2)}, u32[]{:S(2)}) collective-permute-start(bf16[128,2752]{0,1:T(8,128)(2,1)} %collective-permute-done.45), channel_id=1, source_target_pairs={{0,1},{1,0},{2,3},{3,2},{4,5},{5,4},{6,7},{7,6},{8,9},{9,8},{10,11... | collective-permute-start | bytes 2113544 | tf_op jit(solution)/shard_map/ppermute | solution.py:433
  366.0 67.5 %collective-permute-start.58 = (bf16[512,1024]{1,0:T(8,128)(2,1)}, bf16[512,1024]{1,0:T(8,128)(2,1)}, u32[]{:S(2)}, u32[]{:S(2)}) collective-permute-start(bf16[512,1024]{1,0:T(8,128)(2,1)} %convolution_convert_fusion.6), channel_id=1, source_target_pairs={{0,1},{1,0},{2,3},{3,2},{4,5},{5,4},{6,7},{7,6},{8,9},{9,8},{10,11... | collective-permute-start | bytes 3145736 | tf_op jit(solution)/shard_map/ppermute | solution.py:433
  420.3 33.6 %collective-permute-start.50 = (bf16[2,2,1280,128]{3,2,1,0:T(8,128)(2,1)S(1)}, bf16[2,2,1280,128]{3,2,1,0:T(8,128)(2,1)S(1)}, u32[]{:S(2)}, u32[]{:S(2)}) collective-permute-start(bf16[2,2,1280,128]{3,2,1,0:T(8,128)(2,1)S(1)} %attn_head.1), channel_id=1, source_target_pairs={{1,0},{2,1},{3,2},{5,4},{6,5},{7,6},{9,8},{10,9},{11,10},{13,12},{... | collective-permute-start | bytes 3932168 | tf_op jit(solution)/shard_map/ppermute | solution.py:392
  454.2 22.6 %collective-permute-start.51 = (bf16[2,2,1280,128]{3,2,1,0:T(8,128)(2,1)S(1)}, bf16[2,2,1280,128]{3,2,1,0:T(8,128)(2,1)S(1)}, u32[]{:S(2)}, u32[]{:S(2)}) collective-permute-start(bf16[2,2,1280,128]{3,2,1,0:T(8,128)(2,1)S(1)} %select_add_fusion), channel_id=1, source_target_pairs={{1,0},{2,1},{3,2},{5,4},{6,5},{7,6},{9,8},{10,9},{11,10},{13,12},{... | collective-permute-start | bytes 3932168 | tf_op jit(solution)/shard_map/ppermute | solution.py:392
  469.5 34.3 %collective-permute-start.76 = (bf16[512,2752]{0,1:T(8,128)(2,1)}, bf16[512,2752]{0,1:T(8,128)(2,1)}, u32[]{:S(2)}, u32[]{:S(2)}) collective-permute-start(bf16[512,2752]{0,1:T(8,128)(2,1)} %convolution_convert_fusion.2), channel_id=1, source_target_pairs={{0,1},{1,0},{2,3},{3,2},{4,5},{5,4},{6,7},{7,6},{8,9},{9,8},{10,11... | collective-permute-start | bytes 8454152 | tf_op jit(solution)/shard_map/ppermute | solution.py:433
  469.5 42.4 %collective-permute-start.64 = (bf16[512,2752]{0,1:T(8,128)(2,1)}, bf16[512,2752]{0,1:T(8,128)(2,1)}, u32[]{:S(2)}, u32[]{:S(2)}) collective-permute-start(bf16[512,2752]{0,1:T(8,128)(2,1)} %convolution_convert_fusion.1), channel_id=1, source_target_pairs={{0,1},{1,0},{2,3},{3,2},{4,5},{5,4},{6,7},{7,6},{8,9},{9,8},{10,11... | collective-permute-start | bytes 8454152 | tf_op jit(solution)/shard_map/ppermute | solution.py:433
  470.0 58.6 %collective-permute-start.70 = (bf16[512,2752]{0,1:T(8,128)(2,1)}, bf16[512,2752]{0,1:T(8,128)(2,1)}, u32[]{:S(2)}, u32[]{:S(2)}) collective-permute-start(bf16[512,2752]{0,1:T(8,128)(2,1)} %convolution_convert_fusion), channel_id=1, source_target_pairs={{0,1},{1,0},{2,3},{3,2},{4,5},{5,4},{6,7},{7,6},{8,9},{9,8},{10,11... | collective-permute-start | bytes 8454152 | tf_op jit(solution)/shard_map/ppermute | solution.py:433
  498.2 43.9 %collective-permute-start.52 = (bf16[512,1536]{1,0:T(8,128)(2,1)}, bf16[512,1536]{1,0:T(8,128)(2,1)}, u32[]{:S(2)}, u32[]{:S(2)}) collective-permute-start(bf16[512,1536]{1,0:T(8,128)(2,1)} %convolution_convert_fusion.4), channel_id=1, source_target_pairs={{0,1},{1,0},{2,3},{3,2},{4,5},{5,4},{6,7},{7,6},{8,9},{9,8},{10,11... | collective-permute-start | bytes 4718600 | tf_op jit(solution)/shard_map/ppermute | solution.py:433
  517.8 35.0 %collective-permute-start.65 = (bf16[256,2752]{0,1:T(8,128)(2,1)}, bf16[256,2752]{0,1:T(8,128)(2,1)S(1)}, u32[]{:S(2)}, u32[]{:S(2)}) collective-permute-start(bf16[256,2752]{0,1:T(8,128)(2,1)} %add_convert_fusion.2), channel_id=1, source_target_pairs={{0,2},{1,3},{2,0},{3,1},{4,6},{5,7},{6,4},{7,5},{8,10},{9,11},{10,... | collective-permute-start | bytes 4227080 | tf_op jit(solution)/shard_map/ppermute | solution.py:433
  528.1 19.9 %collective-permute-start.78 = (bf16[128,2752]{0,1:T(8,128)(2,1)}, bf16[128,2752]{0,1:T(8,128)(2,1)S(1)}, u32[]{:S(2)}, u32[]{:S(2)}) collective-permute-start(bf16[128,2752]{0,1:T(8,128)(2,1)} %add_convert_fusion.4), channel_id=1, source_target_pairs={{0,8},{4,12},{8,24},{12,28},{16,0},{20,4},{24,16},{28,20},{1,9},{5... | collective-permute-start | bytes 2113544 | tf_op jit(solution)/shard_map/ppermute | solution.py:433
  538.4 34.1 %collective-permute-start.71 = (bf16[256,2752]{0,1:T(8,128)(2,1)}, bf16[256,2752]{0,1:T(8,128)(2,1)}, u32[]{:S(2)}, u32[]{:S(2)}) collective-permute-start(bf16[256,2752]{0,1:T(8,128)(2,1)} %add_convert_fusion.1), channel_id=1, source_target_pairs={{0,4},{4,0},{8,12},{12,8},{16,20},{20,16},{24,28},{28,24},{1,5},{5... | collective-permute-start | bytes 4227080 | tf_op jit(solution)/shard_map/ppermute | solution.py:433
  546.3 58.4 %collective-permute-start.53 = (bf16[256,1536]{1,0:T(8,128)(2,1)}, bf16[256,1536]{1,0:T(8,128)(2,1)}, u32[]{:S(2)}, u32[]{:S(2)}) collective-permute-start(bf16[256,1536]{1,0:T(8,128)(2,1)} %fusion.23), channel_id=1, source_target_pairs={{0,2},{1,3},{2,0},{3,1},{4,6},{5,7},{6,4},{7,5},{8,10},{9,11},{10,... | collective-permute-start | bytes 2359304 | tf_op jit(solution)/shard_map/ppermute | solution.py:433
  550.3 35.7 %collective-permute-start.79 = (bf16[128,2752]{0,1:T(8,128)(2,1)}, bf16[128,2752]{0,1:T(8,128)(2,1)}, u32[]{:S(2)}, u32[]{:S(2)}) collective-permute-start(bf16[128,2752]{0,1:T(8,128)(2,1)} %add_convert_fusion.3), channel_id=1, source_target_pairs={{0,8},{4,12},{8,24},{12,28},{16,0},{20,4},{24,16},{28,20},{1,9},{5... | collective-permute-start | bytes 2113544 | tf_op jit(solution)/shard_map/ppermute | solution.py:433
  560.8 31.9 %collective-permute-start.66 = (bf16[128,2752]{0,1:T(8,128)(2,1)}, bf16[128,2752]{0,1:T(8,128)(2,1)}, u32[]{:S(2)}, u32[]{:S(2)}) collective-permute-start(bf16[128,2752]{0,1:T(8,128)(2,1)} %copy.2748), channel_id=1, source_target_pairs={{0,4},{4,0},{8,12},{12,8},{16,20},{20,16},{24,28},{28,24},{1,5},{5... | collective-permute-start | bytes 2113544 | tf_op jit(solution)/shard_map/ppermute | solution.py:433
  592.2 20.1 %collective-permute-start.80 = (bf16[64,2752]{1,0:T(8,128)(2,1)}, bf16[64,2752]{1,0:T(8,128)(2,1)S(1)}, u32[]{:S(2)}, u32[]{:S(2)}) collective-permute-start(bf16[64,2752]{1,0:T(8,128)(2,1)} %slice.439), channel_id=1, source_target_pairs={{0,4},{4,0},{8,12},{12,8},{16,20},{20,16},{24,28},{28,24},{1,5},{5... | collective-permute-start | bytes 1056776 | tf_op jit(solution)/shard_map/ppermute | solution.py:433
  (131 other events, 1532.7 us)

commit v3 on v2

--- a/solution.py
+++ b/solution.py
@@ -396,10 +396,6 @@
 epsilon = 1e-05
 
 
-def across_rows(left, right):
-    return dot(left, right, ((0,), (0,)))
-
-
 def against(left, matrix):
     return dot(left, matrix, ((1,), (1,)))
 
@@ -453,31 +449,32 @@
         return ((at["z"] * 2 + at["x"]) * (self.seq // 2) + at["y"]) * 2 + at["c"]
 
 
-def assemble(pieces, places, block, devices):
-    columns = pieces[0].shape[1]
-    counts = [piece.shape[0] // block for piece in pieces]
+def assemble(pieces, columns, block, devices, shape):
+    arrays = [array for array, _, _ in pieces]
+    counts = [len(names) for _, names, _ in pieces]
+    places = jnp.stack([shape.device_of(n) for _, names, _ in pieces for n in names])
+    held = sum(array.size for array in arrays) // columns
 
     def kernel(places_ref, *refs):
-        piece_refs, out_ref, held, in_sems, out_sems = (
-            refs[: len(pieces)],
-            *refs[len(pieces) :],
-        )
-        loads, begin = [], 0
+        piece_refs = refs[: len(pieces)]
+        out_ref = refs[len(pieces)]
+        buffers = refs[len(pieces) + 1 : 2 * len(pieces) + 1]
+        in_sems, out_sems = refs[2 * len(pieces) + 1 :]
+        loads = []
         for number, piece_ref in enumerate(piece_refs):
-            rows = counts[number] * block
-            load = pltpu.make_async_copy(
-                piece_ref, held.at[pl.ds(begin * block, rows)], in_sems.at[number]
-            )
+            load = pltpu.make_async_copy(piece_ref, buffers[number], in_sems.at[number])
             load.start()
             loads.append(load)
-            begin += counts[number]
         stores, begin = [], 0
         for number, load in enumerate(loads):
             load.wait()
-            for i in range(begin, begin + counts[number]):
-                to = pl.multiple_of(places_ref[i] * block, block)
+            span = pl.ds(pieces[number][2], arrays[number].shape[1])
+            for i in range(counts[number]):
+                to = pl.multiple_of(places_ref[begin + i] * block, block)
                 store = pltpu.make_async_copy(
-                    held.at[pl.ds(i * block, block)], out_ref.at[pl.ds(to, block)], out_sems.at[i]
+                    buffers[number].at[pl.ds(i * block, block)],
+                    out_ref.at[pl.ds(to, block), span],
+                    out_sems.at[begin + i],
                 )
                 store.start()
                 stores.append(store)
@@ -485,94 +482,225 @@
         for store in stores:
             store.wait()
 
-    size = devices * block * columns * pieces[0].dtype.itemsize
+    size = held * columns * arrays[0].dtype.itemsize
     return pl.pallas_call(
         kernel,
-        out_shape=jax.ShapeDtypeStruct((devices * block, columns), pieces[0].dtype),
+        out_shape=jax.ShapeDtypeStruct((devices * block, columns), arrays[0].dtype),
         in_specs=[pl.BlockSpec(memory_space=pltpu.SMEM)]
         + [pl.BlockSpec(memory_space=pl.ANY)] * len(pieces),
         out_specs=pl.BlockSpec(memory_space=pl.ANY),
-        scratch_shapes=[
-            pltpu.VMEM((devices * block, columns), pieces[0].dtype),
+        scratch_shapes=[pltpu.VMEM(array.shape, array.dtype) for array in arrays]
+        + [
             pltpu.SemaphoreType.DMA((len(pieces),)),
-            pltpu.SemaphoreType.DMA((devices,)),
+            pltpu.SemaphoreType.DMA((sum(counts),)),
         ],
         cost_estimate=pl.CostEstimate(flops=0, bytes_accessed=2 * size, transcendentals=0),
         name="assemble",
-    )(places, *pieces)
+    )(places, *arrays)
+
+
+class Gathering:
+    def __init__(self, shape, array, names=None):
+        self.shape, self.array = shape, array
+        self.names = names or [dict(z=0, x=0, y=0, c=0)]
+
+    def came(self, dim):
+        line, array, out = self.shape.lines[dim], self.array, []
+        for step in range(1, line.count):
+            array = line.send(array)
+            out.append((array, [dict(n, **{dim: step}) for n in self.names]))
+        return out
+
+    def along(self, dim):
+        came = self.came(dim)
+        array = jnp.concatenate([self.array] + [a for a, _ in came], 0)
+        return Gathering(self.shape, array, self.names + [n for _, names in came for n in names])
+
+    def columns(self, low, high):
+        return Gathering(self.shape, self.array[:, low:high], self.names)
+
+    def pieces(self, dim, first_column=0):
+        found = [(self.array, self.names)] + self.came(dim)
+        return [(array, names, first_column) for array, names in found]
+
+
+def small_blocks(part):
+    return part.shape[0] % 16 != 0
 
 
 def gather_rows(part, shape, route):
-    block, columns = part.shape
+    if small_blocks(part):
+        return lax.all_gather(part, ("dp", "seq"), axis=0, tiled=True)
+    held = Gathering(shape, part)
+    for dim in route[:-1]:
+        held = held.along(dim)
+    return assemble(held.pieces(route[-1]), part.shape[1], part.shape[0], shape.devices, shape)
+
+
+def gather_first(part, shape, waiting):
+    if small_blocks(part):
+        return lax.all_gather(part, ("dp", "seq"), axis=0, tiled=True), waiting
+    columns = part.shape[1]
+    cut = columns // 2 // LANES * LANES + LANES
+    held = Gathering(shape, part).along("z")
+    one, two = held.columns(0, cut).along("x"), held.columns(cut, columns).along("y")
+    one.array, two.array, waiting = lax.optimization_barrier((one.array, two.array, waiting))
+    one, two = one.along("y"), two.along("x")
+    pieces = one.pieces("c") + two.pieces("c", cut)
+    return assemble(pieces, columns, part.shape[0], shape.devices, shape), waiting
+
+
+LAYOUT = "cyxz"
+
+
+def picker(shape, width):
+    block = width // shape.devices
     if block % 16:
-        return lax.all_gather(part, ("dp", "seq"), axis=0, tiled=True)
-    held = [(part, [dict(z=0, x=0, y=0, c=0)])]
+        order = jnp.arange(width)
+    else:
+        names = [dict()]
+        for dim in LAYOUT:
+            names = [dict(n, **{dim: s}) for n in names for s in range(shape.lines[dim].count)]
+        places = jnp.stack([shape.device_of(n) for n in names])
+        order = (places[:, None] * block + jnp.arange(block)[None, :]).reshape(width)
+    return (jnp.arange(width)[:, None] == order[None, :]).astype(jnp.bfloat16)
+
+
+def turned_rows(pick, left):
+    return dot(pick, left, ((0,), (1,))).astype(jnp.bfloat16)
+
+
+def scatter_rows(kept, sent, shape, route):
+    half, columns = kept.shape
+    block = 2 * half // shape.devices
+    if block % 16:
+        whole = jnp.concatenate([kept, sent], 0)
+        return lax.psum_scatter(
+            whole.astype(jnp.float32), ("dp", "seq"), scatter_dimension=0, tiled=True
+        )
+    dims = list(LAYOUT[1:])
+    form = [shape.lines[d].count for d in dims] + [block, columns]
+    arrived = shape.lines["c"].send(sent).reshape(form)
+    total = kept.reshape(form)
     for dim in route:
-        if len(held) > 1 and sum(len(names) for _, names in held) <= 4:
-            held = [
-                (jnp.concatenate([a for a, _ in held], 0), [n for _, names in held for n in names])
-            ]
-        came = []
-        for array, names in held:
-            for step in range(1, shape.lines[dim].count):
-                array = shape.lines[dim].send(array)
-                came.append((array, [dict(n, **{dim: step}) for n in names]))
-        held = held + came
-    places = jnp.stack([shape.device_of(n) for _, names in held for n in names])
-    return assemble([a for a, _ in held], places, block, shape.devices)
-
-
-def column_order(shape, width, route):
-    block = width // shape.devices
-    names = [dict()]
-    for dim in route:
-        names = [dict(n, **{dim: s}) for n in names for s in range(shape.lines[dim].count)]
-    places = jnp.stack([shape.device_of(n) for n in names])
-    return (places[:, None] * block + jnp.arange(block)[None, :]).reshape(width)
-
-
-def reorder(left, order):
-    width = left.shape[1]
-    pick = (jnp.arange(width)[:, None] == order[None, :]).astype(jnp.bfloat16)
-    return jnp.dot(left, pick, preferred_element_type=jnp.float32).astype(jnp.bfloat16)
-
-
-def scatter_rows(left, right, shape, route):
-    width = left.shape[1]
-    if (width // shape.devices) % 16:
-        return lax.psum_scatter(
-            across_rows(left, right), ("dp", "seq"), scatter_dimension=0, tiled=True
-        )
-    left = reorder(left, column_order(shape, width, route))
-    first, second = (shape.lines[d] for d in route[:2])
-    half = width // first.count
-    came = None
-    for step in range(1, first.count):
-        term = across_rows(left[:, step * half : (step + 1) * half], right)
-        term = term if came is None else term + came.astype(jnp.float32)
-        came = first.send(term.astype(jnp.bfloat16))
-    rows = half // second.count
-    arrived, came = came, None
-
-    def term_of(step):
-        low, high = step * rows, (step + 1) * rows
-        return across_rows(left[:, low:high], right) + arrived[low:high].astype(jnp.float32)
-
-    for step in range(1, second.count):
-        term = term_of(step)
-        term = term if came is None else term + came.astype(jnp.float32)
-        came = second.send(term.astype(jnp.bfloat16))
-    total = term_of(0) + came.astype(jnp.float32)
-    for dim in route[2:]:
-        line = shape.lines[dim]
-        rows = total.shape[0] // line.count
+        line, axis = shape.lines[dim], dims.index(dim)
+
+        def term_of(step):
+            term = lax.index_in_dim(total, step, axis, False).astype(jnp.float32)
+            if arrived is not None:
+                term = term + lax.index_in_dim(arrived, step, axis, False).astype(jnp.float32)
+            return term
+
         came = None
         for step in range(1, line.count):
-            term = total[step * rows : (step + 1) * rows]
+            term = term_of(step)
             term = term if came is None else term + came.astype(jnp.float32)
             came = line.send(term.astype(jnp.bfloat16))
-        total = total[:rows] + came.astype(jnp.float32)
-    return total
+        total, arrived = term_of(0) + came.astype(jnp.float32), None
+        dims.pop(axis)
+    return total.reshape(block, columns)
+
+
+def scatter_product(turned, right, shape, route):
+    half = turned.shape[0] // 2
+    sent = dot(turned[half:], right).astype(jnp.bfloat16)
+    kept = dot(turned[:half], right).astype(jnp.bfloat16)
+    return scatter_rows(kept, sent, shape, route)
+
+
+FF_TILE = 256
+
+
+def mlp_kernel(
+    block, a_ref, g_ref, at_ref, gt_ref, x_ref, gain_ref, gate_ref, up_ref, down_ref, y_ref,
+    dx_ref, dxo_ref, *rest,
+):
+    grads, (out_sum, hidden_ref, d_gate_ref, d_up_ref) = rest[:6], rest[6:]
+    count = a_ref.shape[0]
+    step = pl.program_id(0)
+
+    @pl.when(step == 0)
+    def _():
+        out_sum[...] = jnp.zeros_like(out_sum)
+        dx_ref[...] = jnp.zeros_like(dx_ref)
+
+    for begin in range(0, count, block):
+        span = slice(begin, begin + block)
+        a, g = a_ref[span, :], g_ref[span, :]
+        gate, up = dot(a, gate_ref[...]), dot(a, up_ref[...])
+        d_hidden = dot(g, down_ref[...])
+        sigma = jax.nn.sigmoid(gate)
+        silu = gate * sigma
+        hidden = (silu * up).astype(jnp.bfloat16)
+        d_gate = (d_hidden * up * (sigma + silu * (1.0 - sigma))).astype(jnp.bfloat16)
+        d_up = (d_hidden * silu).astype(jnp.bfloat16)
+        hidden_ref[span, :], d_gate_ref[span, :], d_up_ref[span, :] = hidden, d_gate, d_up
+        out_sum[span, :] += dot(hidden, down_ref[...], ((1,), (1,)))
+        dx_ref[span, :] += dot(d_gate, gate_ref[...], ((1,), (1,))) + dot(
+            d_up, up_ref[...], ((1,), (1,))
+        )
+    half = at_ref.shape[0] // 2
+    for number, (left, right) in enumerate(
+        ((at_ref, d_gate_ref), (at_ref, d_up_ref), (gt_ref, hidden_ref))
+    ):
+        for part in range(2):
+            rows = slice(part * half, (part + 1) * half)
+            grads[2 * number + part][...] = dot(left[rows, :], right[...]).astype(jnp.bfloat16)
+
+    @pl.when(step == pl.num_programs(0) - 1)
+    def _():
+        for begin in range(0, count, block):
+            span = slice(begin, begin + block)
+            x = x_ref[span, :]
+            y_ref[span, :] = (x + out_sum[span, :]).astype(y_ref.dtype)
+            scale = lax.rsqrt(jnp.mean(x * x, axis=1, keepdims=True) + epsilon)
+            normed = x * scale
+            d_normed = dx_ref[span, :] * gain_ref[...]
+            mean = jnp.mean(d_normed * normed, axis=1, keepdims=True)
+            dx = g_ref[span, :].astype(jnp.float32) + scale * (d_normed - normed * mean)
+            dx_ref[span, :] = dx
+            dxo_ref[span, :] = dx.astype(dxo_ref.dtype)
+
+
+def feed_forward(a, g, a_turned, g_turned, x, gain, gate_w, up_w, down_w):
+    count, width = a.shape
+    hidden = gate_w.shape[1]
+    tiles = hidden // FF_TILE
+    half = width // 2
+
+    def held(rows, columns):
+        return pl.BlockSpec((rows, columns), lambda j: (0, 0), pipeline_mode=pl.Buffered(1))
+
+    def tile(rows):
+        return pl.BlockSpec((rows, FF_TILE), lambda j: (0, j))
+
+    out = pl.pallas_call(
+        functools.partial(mlp_kernel, min(256, count)),
+        grid=(tiles,),
+        in_specs=[held(count, width)] * 2
+        + [held(width, count)] * 2
+        + [held(count, width), held(1, width)]
+        + [tile(width)] * 3,
+        out_specs=[held(count, width)] * 3 + [tile(half)] * 6,
+        out_shape=[
+            jax.ShapeDtypeStruct((count, width), jnp.bfloat16),
+            jax.ShapeDtypeStruct((count, width), jnp.float32),
+            jax.ShapeDtypeStruct((count, width), jnp.bfloat16),
+        ]
+        + [jax.ShapeDtypeStruct((half, hidden), jnp.bfloat16)] * 6,
+        scratch_shapes=[pltpu.VMEM((count, width), jnp.float32)]
+        + [pltpu.VMEM((count, FF_TILE), jnp.bfloat16)] * 3,
+        compiler_params=pltpu.CompilerParams(
+            dimension_semantics=("arbitrary",), vmem_limit_bytes=60 * 2**20
+        ),
+        cost_estimate=pl.CostEstimate(
+            flops=18 * count * width * hidden,
+            bytes_accessed=12 * width * hidden + 20 * count * width,
+            transcendentals=count * hidden,
+        ),
+        name="mlp",
+    )(a, g, a_turned, g_turned, x, gain, gate_w, up_w, down_w)
+    return out[0], out[1], out[2], out[3:5], out[5:7], out[7:9]
 
 
 def gain_gradient(weights, gradients, gain):
@@ -597,20 +725,29 @@
 ):
     rows, shard_len, width = layer_input.shape
     count = rows * shard_len
-    narrow = HEADS * FEAT
+    narrow, hidden = HEADS * FEAT, w_gate.shape[1]
+    qkv_columns = 2 * narrow + width
     qkv_part = jnp.concatenate([w_query, w_key, w_value], axis=1)
-    down_part = w_down.T
-    gains = jnp.stack([gain_attn, gain_mlp], axis=1)
-    gains = jnp.pad(gains, ((0, 0), (0, 126)))
-    head = gather_rows(jnp.concatenate([qkv_part, gains], axis=1), shape, "zxyc")
-    qkv_w = head[:, : 2 * narrow + width]
-    gain_one = head[:, 2 * narrow + width].astype(jnp.float32)
-    gain_two = head[:, 2 * narrow + width + 1].astype(jnp.float32)
-    out_w = gather_rows(w_out, shape, "xyzc")
-    gate_w = gather_rows(w_gate, shape, "zxyc")
-    up_w = gather_rows(w_up, shape, "zyxc")
-    down_w = gather_rows(down_part, shape, "xyzc")
-
+    gains = jnp.pad(jnp.stack([gain_attn, gain_mlp], axis=1), ((0, 0), (0, LANES - 2)))
+    spare = ((0, 0), (0, -hidden % FF_TILE))
+    parts = (
+        w_out,
+        jnp.pad(w_gate, spare),
+        jnp.pad(w_up, spare),
+        jnp.pad(w_down.T, spare),
+    )
+    first_part = jnp.concatenate([qkv_part, gains], axis=1)
+    gathered, parts = gather_first(first_part, shape, parts)
+    qkv_w = gathered[:, :qkv_columns]
+    gain_one = gathered[:, qkv_columns].astype(jnp.float32)[None, :]
+    gain_two = gathered[:, qkv_columns + 1].astype(jnp.float32)[None, :]
+    out_w = gather_rows(parts[0], shape, "zyxc")
+    gate_w = gather_rows(parts[1], shape, "zxyc")
+    up_w = gather_rows(parts[2], shape, "zyxc")
+    down_w = gather_rows(parts[3], shape, "xyzc")
+
+    pick = picker(shape, width)
+    cotangent = grad_output.reshape(count, width)
     tokens = layer_input.reshape(count, width).astype(jnp.float32)
     scale_one, normed_one = norm_forward(tokens)
     a_one = (normed_one * gain_one).astype(jnp.bfloat16)
@@ -632,26 +769,21 @@
     x_two = tokens + jnp.dot(mixed_cat, out_w, preferred_element_type=jnp.float32)
     scale_two, normed_two = norm_forward(x_two)
     a_two = (normed_two * gain_two).astype(jnp.bfloat16)
-    gate = jnp.dot(a_two, gate_w, preferred_element_type=jnp.float32)
-    up_values = jnp.dot(a_two, up_w, preferred_element_type=jnp.float32)
-    sigma = jax.nn.sigmoid(gate)
-    silu_gate = gate * sigma
-    hidden = (silu_gate * up_values).astype(jnp.bfloat16)
-    result = (x_two + against(hidden, down_w)).astype(jnp.bfloat16)
-
-    cotangent = grad_output.reshape(count, width)
-    grad_down = scatter_rows(cotangent, hidden, shape, "czxy")
-    d_hidden = jnp.dot(cotangent, down_w, preferred_element_type=jnp.float32)
-    d_gate = (d_hidden * up_values * sigma * (1.0 + gate * (1.0 - sigma))).astype(jnp.bfloat16)
-    d_up = (d_hidden * silu_gate).astype(jnp.bfloat16)
-    grad_gate = scatter_rows(a_two, d_gate, shape, "cyxz")
-    grad_up = scatter_rows(a_two, d_up, shape, "cxyz")
-    d_a_two = against(d_gate, gate_w) + against(d_up, up_w)
-    d_x_two = cotangent.astype(jnp.float32) + norm_backward(
-        d_a_two, gain_two, scale_two, normed_two
+    result, d_x_two, d_branch, gate_sums, up_sums, down_sums = feed_forward(
+        a_two,
+        cotangent,
+        turned_rows(pick, a_two),
+        turned_rows(pick, cotangent),
+        x_two,
+        gain_two,
+        gate_w,
+        up_w,
+        down_w,
     )
-    d_branch = d_x_two.astype(jnp.bfloat16)
-    grad_out = scatter_rows(mixed_cat, d_branch, shape, "cxyz")
+    grad_gate = scatter_rows(*gate_sums, shape, "yxz")[:, :hidden]
+    grad_up = scatter_rows(*up_sums, shape, "xyz")[:, :hidden]
+    grad_down = scatter_rows(*down_sums, shape, "zxy")[:, :hidden]
+    grad_out = scatter_product(turned_rows(pick, mixed_cat), d_branch, shape, "xyz")
     d_mixed = against(d_branch, out_w).astype(jnp.bfloat16)
     ahead = attention.head(qkv, d_mixed, mixed_cat, inverse, seg)
     later = pass_states(ahead, first == last, from_after, reach, "seq", -1, shape.seq)
@@ -660,7 +792,7 @@
     )
     d_keys, d_values = attention.far_back(qkv, seg, later, d_keys, d_values)
     d_qkv = jnp.concatenate([d_query, d_keys, d_values], axis=1)
-    grad_qkv = scatter_rows(a_one, d_qkv, shape, "cyxz")
+    grad_qkv = scatter_product(turned_rows(pick, a_one), d_qkv, shape, "yxz")
     d_a_one = against(d_qkv, qkv_w)
     d_tokens = d_x_two + norm_backward(d_a_one, gain_one, scale_one, normed_one)
     return (

time: 652 us -> 536 us (0.82)
  matrix products: 174 us -> 38.8 us
  Pallas kernels: 125 us -> 195 us
  local copies, waits for them, and re-layouts: 93.6 us -> 45.4 us
  waiting for transfers between devices: 104 us -> 120 us
  other arithmetic: 40.4 us -> 26.6 us
    dot_general x22 -> x10, matrix products: 109 us -> 32.8 us  [dot(): lax.dot_general(left, right, (dims, ((), ())), preferred_element_type=jnp...]
    pallas_call x0 -> x1, Pallas kernels: none -> 72.1 us  [feed_forward(): pl.pallas_call(functools.partial(mlp_kernel, min(256, count)), grid=(tile...]
    dot_general x8 -> x0, matrix products: 58.5 us -> none  [the longest x5 20.3 us: reorder(): jnp.dot(left, pick, preferred_element_type=jnp.float32).astype(jnp.bfloat16)]
    ppermute x26 -> x0, local copies, waits for them, and re-layouts: 56.4 us -> none  [send(): return lax.ppermute(array, self.axis, self.pairs)]
    ppermute x78 -> x63, waiting for transfers between devices: 104 us -> 119 us  [send(): return lax.ppermute(array, self.axis, self.pairs)]
    add x15 -> x14, other arithmetic: 14.9 us -> 2.84 us  [the longest x13 2.77 us: scatter_rows(): total, arrived = (term_of(0) + came.astype(jnp.float32), None)]
    unnamed x179 -> x132, local copies, waits for them, and re-layouts: 13.5 us -> 25 us
    slice x15 -> x3, local copies, waits for them, and re-layouts: 12.9 us -> 1.61 us  [the longest x1 1.38 us: term_of(): term = lax.index_in_dim(total, step, axis, False).astype(jnp.float32)]
  transfers between devices with their start and end apart: 82 -> 67, of which waited for: 28 -> 26; matrix products, arithmetic and copies ran while one was open for 30% -> 18% of each run, Pallas kernels for 18% -> 22%
where the time goes in v3:
time: 536 us; the launch traced here: 530 us
  Pallas kernels  195 us (36%)
  waiting for transfers between devices  120 us (22%)
  starting transfers between devices  95.2 us (18%)
  local copies, waits for them, and re-layouts  45.4 us (8%)
  matrix products  38.8 us (7%)
  other arithmetic  26.6 us (5%)
  between operations  8.98 us (2%)
    ppermute x63, waiting for transfers between devices, send(): return lax.ppermute(array, self.axis, self.pairs)  119 us
    ppermute x63, starting transfers between devices, send(): return lax.ppermute(array, self.axis, self.pairs)  82 us
    pallas_call x1, Pallas kernels, feed_forward(): pl.pallas_call(functools.partial(mlp_kernel, min(256, count)), grid=(tile...  72.1 us
    pallas_call x1, Pallas kernels, near_back(): self.call(functools.partial(near_back_kernel, self.value_dim, self.block)...  39.2 us
    dot_general x10, matrix products, dot(): lax.dot_general(left, right, (dims, ((), ())), preferred_element_type=jnp...  32.8 us
    unnamed x132, local copies, waits for them, and re-layouts  25 us
    pallas_call x5, Pallas kernels, assemble(): pl.pallas_call(kernel, out_shape=jax.ShapeDtypeStruct((devices * block, c...  23.5 us
    pallas_call x1, Pallas kernels, head(): self.call(functools.partial(head_kernel, self.value_dim), [self.q, self.y...  15 us
  transfers between devices with their start and end apart: 67, of which 26 were waited for; matrix products, arithmetic and copies ran while one was open for 18% of the time, Pallas kernels for 22%

profile of v3, /device:TPU:0, one launch (start us, length us, event | category | flops | bytes accessed | tf_op | source)
XLA Modules:
  0.0 529.6 jit_solution(15196541205429692376)
XLA Ops:
  16.1 5.4 %fusion.28.gt_ref = bf16[1024,1024]{1,0:T(8,128)(2,1)} fusion(bf16[1024,1024]{1,0:T(8,128)(2,1)} %bitcast.298, s32[1024]{0:T(1024)S(1)} %add.12867), kind=kOutput, calls=%fused_computation.36 | convolution fusion | flops 2150629376 | bytes 4198400 | tf_op jit(solution)/shard_map/dot_general | solution.py:21
  51.1 4.5 collective-permute-done.11
  88.6 7.0 %collective-permute-done.15 = bf16[256,1024]{1,0:T(8,128)(2,1)S(1)} collective-permute-done((bf16[256,1024]{1,0:T(8,128)(2,1)S(1)}, bf16[256,1024]{1,0:T(8,128)(2,1)S(1)}, u32[]{:S(2)}, u32[]{:S(2)}) %collective-permute-start.15) | collective-permute-done | bytes 524320 | tf_op jit(solution)/shard_map/ppermute | solution.py:429
  97.2 5.6 %collective-permute-done.26 = bf16[128,2816]{1,0:T(8,128)(2,1)S(1)} collective-permute-done((bf16[128,2816]{1,0:T(8,128)(2,1)S(1)}, bf16[128,2816]{1,0:T(8,128)(2,1)S(1)}, u32[]{:S(2)}, u32[]{:S(2)}) %collective-permute-start.26) | collective-permute-done | bytes 720928 | tf_op jit(solution)/shard_map/ppermute | solution.py:429
  106.4 4.3 assemble.5
  114.0 3.6 convolution_convert_fusion.k_ref.v_ref.q_ref
  117.7 10.8 %attn_tail.1 = bf16[2,2,1280,128]{3,2,1,0:T(8,128)(2,1)S(1)} custom-call(bf16[1024,1536]{1,0:T(8,128)(2,1)S(1)} %convolution_convert_fusion.k_ref.v_ref.q_ref, bf16[1024,1536]{1,0:T(8,128)(2,1)S(1)} %convolution_convert_fusion.k_ref.v_ref.q_ref, s32[1024,1]{1,0:T(8,128)S(1)} %bitcast.271, bf16[1280,128]{1,0:T(8,128)(2,1)S(1)} %copy-done.3), custom_call_target="tpu_custom_call" | custom-call | flops 5368709120 | bytes 4194304 | tf_op jit(solution)/shard_map/attn_tail/pallas_call | solution.py:329
  136.6 10.0 %attn_near.1 = (f32[1024,1024]{1,0:T(8,128)}, f32[1024,1024]{1,0:T(8,128)}) custom-call(bf16[1024,1536]{1,0:T(8,128)(2,1)S(1)} %convolution_convert_fusion.k_ref.v_ref.q_ref, bf16[1024,1536]{1,0:T(8,128)(2,1)S(1)} %convolution_convert_fusion.k_ref.v_ref.q_ref, bf16[1024,1536]{1,0:T(8,128)(2,1)S(1)} %convolution_convert_fusion.k_ref.v_ref.q_ref, ...), custom_call_target="tpu_custom_call" | custom-call | flops 8589934592 | bytes 4194304 | tf_op jit(solution)/shard_map/attn_near/pallas_call | solution.py:337
  146.6 5.2 collective-permute-done.32
  154.0 8.3 %collective-permute-start.10 = (bf16[2,2,1280,128]{3,2,1,0:T(8,128)(2,1)}, bf16[2,2,1280,128]{3,2,1,0:T(8,128)(2,1)}, u32[]{:S(2)}, u32[]{:S(2)}) collective-permute-start(bf16[2,2,1280,128]{3,2,1,0:T(8,128)(2,1)} %select_add_fusion.1), channel_id=1, source_target_pairs={{0,1},{1,2},{2,3},{4,5},{5,6},{6,7},{8,9},{9,10},{10,11},{12,13},{... | collective-permute-start | bytes 3932168 | tf_op jit(solution)/shard_map/ppermute | solution.py:392
  179.7 10.6 %attn_far.1 = (bf16[1024,1024]{1,0:T(8,128)(2,1)S(1)}, f32[1024,1024]{1,0:T(8,128)}) custom-call(bf16[1024,1536]{1,0:T(8,128)(2,1)} %copy-done.4, s32[1024,1]{1,0:T(8,128)S(1)} %bitcast.273, bf16[2,2,1280,128]{3,2,1,0:T(8,128)(2,1)S(1)} %broadcast_select_fusion.1.state_ref, f32[1024,1024]{1,0:T(8,128)} %get-tuple-element.37.top_ref, ...), custom_call_target="tpu_custom_call" | custom-call | flops 8589934592 | bytes 4194304 | tf_op jit(solution)/shard_map/attn_far/pallas_call | solution.py:348
  194.8 3.7 fusion.34
  198.5 3.7 fusion.25.at_ref
  202.2 5.3 assemble.8.up_ref
  207.5 5.2 assemble.7.gate_ref
  212.8 5.2 assemble.9.down_ref
  218.0 72.1 %mlp.1 = (bf16[1024,1024]{1,0:T(8,128)(2,1)}, f32[1024,1024]{1,0:T(8,128)}, bf16[1024,1024]{1,0:T(8,128)(2,1)}, bf16[512,2816]{1,0:T(8,128)(2,1)}, bf16[512,2816...) custom-call(bf16[1024,1024]{1,0:T(8,128)(2,1)} %copy-done.23, ...), custom_call_target="tpu_custom_call" | custom-call | flops 53150220288 | bytes 55574528 | tf_op jit(solution)/shard_map/mlp/pallas_call | solution.py:677
  293.4 12.9 %collective-permute-start.43 = (bf16[512,1024]{1,0:T(8,128)(2,1)S(1)}, bf16[512,1024]{1,0:T(8,128)(2,1)S(1)}, u32[]{:S(2)}, u32[]{:S(2)}) collective-permute-start(bf16[512,1024]{1,0:T(8,128)(2,1)S(1)} %convolution_convert_fusion.4), channel_id=1, source_target_pairs={{0,1},{1,0},{2,3},{3,2},{4,5},{5,4},{6,7},{7,6},{8,9},{9,8},{10,11... | collective-permute-start | bytes 3145736 | tf_op jit(solution)/shard_map/ppermute | solution.py:429
  306.3 3.7 fusion.31
  314.9 15.0 %attn_head.1 = bf16[2,2,1280,128]{3,2,1,0:T(8,128)(2,1)S(1)} custom-call(bf16[1024,1536]{1,0:T(8,128)(2,1)} %copy-done.4, bf16[1024,1024]{1,0:T(8,128)(2,1)S(1)} %convolution_convert_fusion.3.dy_ref, bf16[1024,1024]{1,0:T(8,128)(2,1)} %copy-done.5, f32[1024,1024]{1,0:T(8,128)} %get-tuple-element.47.inverse_ref, s32[1024,1]{1,0:T(8,128)S(1)} %bitcast.274, ...), custom_call_target="tpu_custom_call" | custom-call | flops 5368709120 | bytes 4194304 | tf_op jit(solution)/shard_map/attn_head/pallas_call | solution.py:356
  334.6 39.2 %attn_near_back.1 = (bf16[1024,256]{1,0:T(8,128)(2,1)S(1)}, f32[1024,256]{1,0:T(8,128)S(1)}, f32[1024,1024]{1,0:T(8,128)}) custom-call(bf16[1024,1536]{1,0:T(8,128)(2,1)} %copy-done.4, bf16[1024,1536]{1,0:T(8,128)(2,1)} %copy-done.4, bf16[1024,1536]{1,0:T(8,128)(2,1)} %copy-done.4, bf16[1024,1024]{1,0:T(8,128)(2,1)S(1)} %convolution_convert_fusion.3.dy_ref, ...), custom_call_target="tpu_custom_call" | custom-call | flops 25769803776 | bytes 4194304 | tf_op jit(solution)/shard_map/attn_near_back/pallas_call | solution.py:364
  386.1 3.7 collective-permute-done.48
  390.6 14.0 %attn_far_back.1 = (bf16[1024,256]{1,0:T(8,128)(2,1)S(1)}, bf16[1024,1024]{1,0:T(8,128)(2,1)S(1)}) custom-call(bf16[1024,1536]{1,0:T(8,128)(2,1)} %copy-done.4, bf16[1024,1536]{1,0:T(8,128)(2,1)} %copy-done.4, s32[1024,1]{1,0:T(8,128)S(1)} %bitcast.276, bf16[2,2,1280,128]{3,2,1,0:T(8,128)(2,1)S(1)} %broadcast_select_fusion.state_ref, ...), custom_call_target="tpu_custom_call" | custom-call | flops 9663676416 | bytes 4194304 | tf_op jit(solution)/shard_map/attn_far_back/pallas_call | solution.py:377
  407.9 5.7 %fusion.4 = (f32[1024]{0:T(1024)S(1)}, f32[1024,1024]{1,0:T(8,128)S(1)}) fusion(bf16[2,512,1024]{2,1,0:T(8,128)(2,1)S(1)} %copy-done.8, f32[1024]{0:T(1024)S(1)} %copy-done.41, f32[1024]{0:T(1024)S(1)} %bitcast.294, bf16[1024,1536]{1,0:T(8,128)(2,1)} %constant_dynamic-update-slice_fusion.43, bf16[1024,1664]{1,0:T(8,128)(2,1)S(1)} %copy-done.10), kind=kOutput, calls=%fused_computation.7 | convolution fusion | flops 3226467328 | bytes 12595200 | tf_op jit(solution)/shard_map/dot_general | solution.py:21
  415.4 5.4 %collective-permute-start.37 = (bf16[512,1536]{1,0:T(8,128)(2,1)S(1)}, bf16[512,1536]{1,0:T(8,128)(2,1)S(1)}, u32[]{:S(2)}, u32[]{:S(2)}) collective-permute-start(bf16[512,1536]{1,0:T(8,128)(2,1)S(1)} %convolution_convert_fusion.1), channel_id=1, source_target_pairs={{0,1},{1,0},{2,3},{3,2},{4,5},{5,4},{6,7},{7,6},{8,9},{9,8},{10,11... | collective-permute-start | bytes 4718600 | tf_op jit(solution)/shard_map/ppermute | solution.py:429
  431.1 14.8 %collective-permute-done.62 = bf16[2,2,32,2816]{3,2,0,1:T(8,128)(2,1)S(1)} collective-permute-done((bf16[2,2,32,2816]{3,2,0,1:T(8,128)(2,1)S(1)}, bf16[2,2,32,2816]{3,2,0,1:T(8,128)(2,1)S(1)}, u32[]{:S(2)}, u32[]{:S(2)}) %collective-permute-start.62) | collective-permute-done | bytes 720928 | tf_op jit(solution)/shard_map/ppermute | solution.py:429
  446.6 17.8 %collective-permute-done.50 = bf16[2,4,32,2816]{3,2,1,0:T(8,128)(2,1)S(1)} collective-permute-done((bf16[2,4,32,2816]{3,2,1,0:T(8,128)(2,1)S(1)}, bf16[2,4,32,2816]{3,2,1,0:T(8,128)(2,1)S(1)}, u32[]{:S(2)}, u32[]{:S(2)}) %collective-permute-start.50) | collective-permute-done | bytes 1441824 | tf_op jit(solution)/shard_map/ppermute | solution.py:429
  469.0 12.3 %collective-permute-done.38 = bf16[2,4,32,1536]{3,2,1,0:T(8,128)(2,1)S(1)} collective-permute-done((bf16[2,4,32,1536]{3,2,1,0:T(8,128)(2,1)S(1)}, bf16[2,4,32,1536]{3,2,1,0:T(8,128)(2,1)S(1)}, u32[]{:S(2)}, u32[]{:S(2)}) %collective-permute-start.38) | collective-permute-done | bytes 786464 | tf_op jit(solution)/shard_map/ppermute | solution.py:429
  484.6 11.5 %collective-permute-done.57 = bf16[4,32,2816]{2,1,0:T(8,128)(2,1)S(1)} collective-permute-done((bf16[4,32,2816]{2,1,0:T(8,128)(2,1)S(1)}, bf16[4,32,2816]{2,1,0:T(8,128)(2,1)S(1)}, u32[]{:S(2)}, u32[]{:S(2)}) %collective-permute-start.57) | collective-permute-done | bytes 720928 | tf_op jit(solution)/shard_map/ppermute | solution.py:429
  500.3 4.5 collective-permute-done.58
  509.5 5.8 %collective-permute-done.40 = bf16[32,1536]{1,0:T(8,128)(2,1)S(1)} collective-permute-done((bf16[32,1536]{1,0:T(8,128)(2,1)S(1)}, bf16[32,1536]{1,0:T(8,128)(2,1)S(1)}, u32[]{:S(2)}, u32[]{:S(2)}) %collective-permute-start.40) | collective-permute-done | bytes 98336 | tf_op jit(solution)/shard_map/ppermute | solution.py:429
  517.9 3.7 collective-permute-done.41
  (359 shorter events, 180.3 us)
Async XLA Ops:
  2.3 19.8 %collective-permute-start = (bf16[32,1664]{1,0:T(8,128)(2,1)S(1)}, bf16[32,1664]{1,0:T(8,128)(2,1)S(1)}, u32[]{:S(2)}, u32[]{:S(2)}) collective-permute-start(bf16[32,1664]{1,0:T(8,128)(2,1)S(1)} %pad_maximum_fusion.9), channel_id=1, source_target_pairs={{0,8},{4,12},{8,24},{12,28},{16,0},{20,4},{24,16},{28,20},{1,9},{5... | collective-permute-start | bytes 319496 | tf_op jit(solution)/shard_map/ppermute | solution.py:429
  43.5 19.2 %collective-permute-start.29 = (bf16[32,2816]{1,0:T(8,128)(2,1)S(1)}, bf16[32,2816]{1,0:T(8,128)(2,1)S(1)}, u32[]{:S(2)}, u32[]{:S(2)}) collective-permute-start(bf16[32,2816]{1,0:T(8,128)(2,1)S(1)} %pad.17), channel_id=1, source_target_pairs={{0,4},{4,0},{8,12},{12,8},{16,20},{20,16},{24,28},{28,24},{1,5},{5... | collective-permute-start | bytes 540680 | tf_op jit(solution)/shard_map/ppermute | solution.py:429
  49.8 28.6 %collective-permute-start.7 = (bf16[256,768]{1,0:T(8,128)(2,1)S(1)}, bf16[256,768]{1,0:T(8,128)(2,1)S(1)}, u32[]{:S(2)}, u32[]{:S(2)}) collective-permute-start(bf16[256,768]{1,0:T(8,128)(2,1)S(1)} %pad_maximum_fusion.5), channel_id=1, source_target_pairs={{0,4},{4,0},{8,12},{12,8},{16,20},{20,16},{24,28},{28,24},{1,5},{5... | collective-permute-start | bytes 1179656 | tf_op jit(solution)/shard_map/ppermute | solution.py:429
  60.7 20.5 %collective-permute-start.5 = (bf16[256,896]{1,0:T(8,128)(2,1)S(1)}, bf16[256,896]{1,0:T(8,128)(2,1)S(1)}, u32[]{:S(2)}, u32[]{:S(2)}) collective-permute-start(bf16[256,896]{1,0:T(8,128)(2,1)S(1)} %pad_maximum_fusion.3), channel_id=1, source_target_pairs={{0,2},{1,3},{2,0},{3,1},{4,6},{5,7},{6,4},{7,5},{8,10},{9,11},{10,... | collective-permute-start | bytes 1376264 | tf_op jit(solution)/shard_map/ppermute | solution.py:429
  62.7 19.3 %collective-permute-start.30 = (bf16[64,2816]{1,0:T(8,128)(2,1)S(1)}, bf16[64,2816]{1,0:T(8,128)(2,1)S(1)}, u32[]{:S(2)}, u32[]{:S(2)}) collective-permute-start(bf16[64,2816]{1,0:T(8,128)(2,1)S(1)} %pad_maximum_fusion.6), channel_id=1, source_target_pairs={{0,2},{1,3},{2,0},{3,1},{4,6},{5,7},{6,4},{7,5},{8,10},{9,11},{10,... | collective-permute-start | bytes 1081352 | tf_op jit(solution)/shard_map/ppermute | solution.py:429
  80.5 23.5 %collective-permute-start.8 = (bf16[512,768]{1,0:T(8,128)(2,1)S(1)}, bf16[512,768]{1,0:T(8,128)(2,1)S(1)}, u32[]{:S(2)}, u32[]{:S(2)}) collective-permute-start(bf16[512,768]{1,0:T(8,128)(2,1)S(1)} %constant_dynamic-update-slice_fusion.2.refs_2_), channel_id=1, source_target_pairs={{0,1},{1,0},{2,3},{3,2},{4,5},{5,4},{6,7},{7,6},{8,9},{9,8},{10,11... | collective-permute-start | bytes 2359304 | tf_op jit(solution)/shard_map/ppermute | solution.py:429
  82.1 24.3 %collective-permute-start.6 = (bf16[512,896]{1,0:T(8,128)(2,1)S(1)}, bf16[512,896]{1,0:T(8,128)(2,1)}, u32[]{:S(2)}, u32[]{:S(2)}) collective-permute-start(bf16[512,896]{1,0:T(8,128)(2,1)S(1)} %constant_dynamic-update-slice_fusion.refs_0_), channel_id=1, source_target_pairs={{0,1},{1,0},{2,3},{3,2},{4,5},{5,4},{6,7},{7,6},{8,9},{9,8},{10,11... | collective-permute-start | bytes 2752520 | tf_op jit(solution)/shard_map/ppermute | solution.py:429
  83.3 49.5 %collective-permute-start.31 = (bf16[128,2816]{1,0:T(8,128)(2,1)}, bf16[128,2816]{1,0:T(8,128)(2,1)}, u32[]{:S(2)}, u32[]{:S(2)}) collective-permute-start(bf16[128,2816]{1,0:T(8,128)(2,1)} %pad_maximum_fusion.2), channel_id=1, source_target_pairs={{0,8},{4,12},{8,24},{12,28},{16,0},{20,4},{24,16},{28,20},{1,9},{5... | collective-permute-start | bytes 2162696 | tf_op jit(solution)/shard_map/ppermute | solution.py:429
  95.6 35.2 %collective-permute-start.20 = (bf16[128,2816]{1,0:T(8,128)(2,1)}, bf16[128,2816]{1,0:T(8,128)(2,1)S(1)}, u32[]{:S(2)}, u32[]{:S(2)}) collective-permute-start(bf16[128,2816]{1,0:T(8,128)(2,1)} %pad_maximum_fusion), channel_id=1, source_target_pairs={{0,4},{4,0},{8,12},{12,8},{16,20},{20,16},{24,28},{28,24},{1,5},{5... | collective-permute-start | bytes 2162696 | tf_op jit(solution)/shard_map/ppermute | solution.py:429
  102.7 60.5 %collective-permute-start.16 = (bf16[512,1024]{1,0:T(8,128)(2,1)}, bf16[512,1024]{1,0:T(8,128)(2,1)}, u32[]{:S(2)}, u32[]{:S(2)}) collective-permute-start(bf16[512,1024]{1,0:T(8,128)(2,1)} %constant_dynamic-update-slice_fusion.9.refs_0_), channel_id=1, source_target_pairs={{0,1},{1,0},{2,3},{3,2},{4,5},{5,4},{6,7},{7,6},{8,9},{9,8},{10,11... | collective-permute-start | bytes 3145736 | tf_op jit(solution)/shard_map/ppermute | solution.py:429
  104.9 67.1 %collective-permute-start.27 = (bf16[256,2816]{1,0:T(8,128)(2,1)}, bf16[256,2816]{1,0:T(8,128)(2,1)}, u32[]{:S(2)}, u32[]{:S(2)}) collective-permute-start(bf16[256,2816]{1,0:T(8,128)(2,1)} %get-tuple-element.78), channel_id=1, source_target_pairs={{0,4},{4,0},{8,12},{12,8},{16,20},{20,16},{24,28},{28,24},{1,5},{5... | collective-permute-start | bytes 4325384 | tf_op jit(solution)/shard_map/ppermute | solution.py:429
  128.5 24.2 %collective-permute-start.9 = (bf16[2,2,1280,128]{3,2,1,0:T(8,128)(2,1)S(1)}, bf16[2,2,1280,128]{3,2,1,0:T(8,128)(2,1)S(1)}, u32[]{:S(2)}, u32[]{:S(2)}) collective-permute-start(bf16[2,2,1280,128]{3,2,1,0:T(8,128)(2,1)S(1)} %attn_tail.1), channel_id=1, source_target_pairs={{0,1},{1,2},{2,3},{4,5},{5,6},{6,7},{8,9},{9,10},{10,11},{12,13},{... | collective-permute-start | bytes 3932168 | tf_op jit(solution)/shard_map/ppermute | solution.py:392
  131.9 43.1 %collective-permute-start.21 = (bf16[256,2816]{1,0:T(8,128)(2,1)}, bf16[256,2816]{1,0:T(8,128)(2,1)S(1)}, u32[]{:S(2)}, u32[]{:S(2)}) collective-permute-start(bf16[256,2816]{1,0:T(8,128)(2,1)} %get-tuple-element.80), channel_id=1, source_target_pairs={{0,2},{1,3},{2,0},{3,1},{4,6},{5,7},{6,4},{7,5},{8,10},{9,11},{10,... | collective-permute-start | bytes 4325384 | tf_op jit(solution)/shard_map/ppermute | solution.py:429
  154.0 24.2 %collective-permute-start.10 = (bf16[2,2,1280,128]{3,2,1,0:T(8,128)(2,1)}, bf16[2,2,1280,128]{3,2,1,0:T(8,128)(2,1)}, u32[]{:S(2)}, u32[]{:S(2)}) collective-permute-start(bf16[2,2,1280,128]{3,2,1,0:T(8,128)(2,1)} %select_add_fusion.1), channel_id=1, source_target_pairs={{0,1},{1,2},{2,3},{4,5},{5,6},{6,7},{8,9},{9,10},{10,11},{12,13},{... | collective-permute-start | bytes 3932168 | tf_op jit(solution)/shard_map/ppermute | solution.py:392
  172.0 40.8 %collective-permute-start.34 = (bf16[512,2816]{1,0:T(8,128)(2,1)}, bf16[512,2816]{1,0:T(8,128)(2,1)}, u32[]{:S(2)}, u32[]{:S(2)}) collective-permute-start(bf16[512,2816]{1,0:T(8,128)(2,1)} %constant_dynamic-update-slice_fusion.37.refs_0_), channel_id=1, source_target_pairs={{0,1},{1,0},{2,3},{3,2},{4,5},{5,4},{6,7},{7,6},{8,9},{9,8},{10,11... | collective-permute-start | bytes 8650760 | tf_op jit(solution)/shard_map/ppermute | solution.py:429
  174.5 27.7 %collective-permute-start.28 = (bf16[512,2816]{1,0:T(8,128)(2,1)}, bf16[512,2816]{1,0:T(8,128)(2,1)}, u32[]{:S(2)}, u32[]{:S(2)}) collective-permute-start(bf16[512,2816]{1,0:T(8,128)(2,1)} %constant_dynamic-update-slice_fusion.31.refs_0_), channel_id=1, source_target_pairs={{0,1},{1,0},{2,3},{3,2},{4,5},{5,4},{6,7},{7,6},{8,9},{9,8},{10,11... | collective-permute-start | bytes 8650760 | tf_op jit(solution)/shard_map/ppermute | solution.py:429
  176.3 31.2 %collective-permute-start.22 = (bf16[512,2816]{1,0:T(8,128)(2,1)}, bf16[512,2816]{1,0:T(8,128)(2,1)}, u32[]{:S(2)}, u32[]{:S(2)}) collective-permute-start(bf16[512,2816]{1,0:T(8,128)(2,1)} %constant_dynamic-update-slice_fusion.20.refs_0_), channel_id=1, source_target_pairs={{0,1},{1,0},{2,3},{3,2},{4,5},{5,4},{6,7},{7,6},{8,9},{9,8},{10,11... | collective-permute-start | bytes 8650760 | tf_op jit(solution)/shard_map/ppermute | solution.py:429
  311.5 19.7 %collective-permute-start.44 = (bf16[2,4,32,1024]{3,2,1,0:T(8,128)(2,1)S(1)}, bf16[2,4,32,1024]{3,2,1,0:T(8,128)(2,1)S(1)}, u32[]{:S(2)}, u32[]{:S(2)}) collective-permute-start(bf16[2,4,32,1024]{3,2,1,0:T(8,128)(2,1)S(1)} %fusion.52), channel_id=1, source_target_pairs={{0,4},{4,0},{8,12},{12,8},{16,20},{20,16},{24,28},{28,24},{1,5},{5... | collective-permute-start | bytes 1572872 | tf_op jit(solution)/shard_map/ppermute | solution.py:429
  329.9 46.6 %collective-permute-start.35 = (bf16[2,2,1280,128]{3,2,1,0:T(8,128)(2,1)S(1)}, bf16[2,2,1280,128]{3,2,1,0:T(8,128)(2,1)S(1)}, u32[]{:S(2)}, u32[]{:S(2)}) collective-permute-start(bf16[2,2,1280,128]{3,2,1,0:T(8,128)(2,1)S(1)} %attn_head.1), channel_id=1, source_target_pairs={{1,0},{2,1},{3,2},{5,4},{6,5},{7,6},{9,8},{10,9},{11,10},{13,12},{... | collective-permute-start | bytes 3932168 | tf_op jit(solution)/shard_map/ppermute | solution.py:392
  331.5 42.5 %collective-permute-start.45 = (bf16[4,32,1024]{2,1,0:T(8,128)(2,1)S(1)}, bf16[4,32,1024]{2,1,0:T(8,128)(2,1)S(1)}, u32[]{:S(2)}, u32[]{:S(2)}) collective-permute-start(bf16[4,32,1024]{2,1,0:T(8,128)(2,1)S(1)} %fusion.65), channel_id=1, source_target_pairs={{0,2},{1,3},{2,0},{3,1},{4,6},{5,7},{6,4},{7,5},{8,10},{9,11},{10,... | collective-permute-start | bytes 786440 | tf_op jit(solution)/shard_map/ppermute | solution.py:429
  373.7 51.5 %collective-permute-start.61 = (bf16[512,2816]{1,0:T(8,128)(2,1)}, bf16[512,2816]{1,0:T(8,128)(2,1)S(1)}, u32[]{:S(2)}, u32[]{:S(2)}) collective-permute-start(bf16[512,2816]{1,0:T(8,128)(2,1)} %get-tuple-element.58), channel_id=1, source_target_pairs={{0,1},{1,0},{2,3},{3,2},{4,5},{5,4},{6,7},{7,6},{8,9},{9,8},{10,11... | collective-permute-start | bytes 8650760 | tf_op jit(solution)/shard_map/ppermute | solution.py:429
  382.3 44.7 %collective-permute-start.49 = (bf16[512,2816]{1,0:T(8,128)(2,1)}, bf16[512,2816]{1,0:T(8,128)(2,1)}, u32[]{:S(2)}, u32[]{:S(2)}) collective-permute-start(bf16[512,2816]{1,0:T(8,128)(2,1)} %get-tuple-element.54), channel_id=1, source_target_pairs={{0,1},{1,0},{2,3},{3,2},{4,5},{5,4},{6,7},{7,6},{8,9},{9,8},{10,11... | collective-permute-start | bytes 8650760 | tf_op jit(solution)/shard_map/ppermute | solution.py:429
  382.3 47.8 %collective-permute-start.55 = (bf16[512,2816]{1,0:T(8,128)(2,1)}, bf16[512,2816]{1,0:T(8,128)(2,1)S(1)}, u32[]{:S(2)}, u32[]{:S(2)}) collective-permute-start(bf16[512,2816]{1,0:T(8,128)(2,1)} %get-tuple-element.56), channel_id=1, source_target_pairs={{0,1},{1,0},{2,3},{3,2},{4,5},{5,4},{6,7},{7,6},{8,9},{9,8},{10,11... | collective-permute-start | bytes 8650760 | tf_op jit(solution)/shard_map/ppermute | solution.py:429
  415.4 30.8 %collective-permute-start.37 = (bf16[512,1536]{1,0:T(8,128)(2,1)S(1)}, bf16[512,1536]{1,0:T(8,128)(2,1)S(1)}, u32[]{:S(2)}, u32[]{:S(2)}) collective-permute-start(bf16[512,1536]{1,0:T(8,128)(2,1)S(1)} %convolution_convert_fusion.1), channel_id=1, source_target_pairs={{0,1},{1,0},{2,3},{3,2},{4,5},{5,4},{6,7},{7,6},{8,9},{9,8},{10,11... | collective-permute-start | bytes 4718600 | tf_op jit(solution)/shard_map/ppermute | solution.py:429
  426.6 19.3 %collective-permute-start.62 = (bf16[2,2,32,2816]{3,2,0,1:T(8,128)(2,1)S(1)}, bf16[2,2,32,2816]{3,2,0,1:T(8,128)(2,1)S(1)}, u32[]{:S(2)}, u32[]{:S(2)}) collective-permute-start(bf16[2,2,32,2816]{3,2,0,1:T(8,128)(2,1)S(1)} %fusion.47), channel_id=1, source_target_pairs={{0,8},{4,12},{8,24},{12,28},{16,0},{20,4},{24,16},{28,20},{1,9},{5... | collective-permute-start | bytes 2162696 | tf_op jit(solution)/shard_map/ppermute | solution.py:429
  430.0 34.5 %collective-permute-start.50 = (bf16[2,4,32,2816]{3,2,1,0:T(8,128)(2,1)S(1)}, bf16[2,4,32,2816]{3,2,1,0:T(8,128)(2,1)S(1)}, u32[]{:S(2)}, u32[]{:S(2)}) collective-permute-start(bf16[2,4,32,2816]{3,2,1,0:T(8,128)(2,1)S(1)} %bitcast.286), channel_id=1, source_target_pairs={{0,2},{1,3},{2,0},{3,1},{4,6},{5,7},{6,4},{7,5},{8,10},{9,11},{10,... | collective-permute-start | bytes 4325384 | tf_op jit(solution)/shard_map/ppermute | solution.py:429
  430.5 35.0 %collective-permute-start.56 = (bf16[2,4,32,2816]{3,2,1,0:T(8,128)(2,1)S(1)}, bf16[2,4,32,2816]{3,2,1,0:T(8,128)(2,1)S(1)}, u32[]{:S(2)}, u32[]{:S(2)}) collective-permute-start(bf16[2,4,32,2816]{3,2,1,0:T(8,128)(2,1)S(1)} %fusion.37), channel_id=1, source_target_pairs={{0,4},{4,0},{8,12},{12,8},{16,20},{20,16},{24,28},{28,24},{1,5},{5... | collective-permute-start | bytes 4325384 | tf_op jit(solution)/shard_map/ppermute | solution.py:429
  446.1 20.5 %collective-permute-start.63 = (bf16[2,2,32,2816]{3,2,0,1:T(8,128)(2,1)S(1)}, bf16[2,2,32,2816]{3,2,0,1:T(8,128)(2,1)S(1)}, u32[]{:S(2)}, u32[]{:S(2)}) collective-permute-start(bf16[2,2,32,2816]{3,2,0,1:T(8,128)(2,1)S(1)} %fusion.40), channel_id=1, source_target_pairs={{0,8},{4,12},{8,24},{12,28},{16,0},{20,4},{24,16},{28,20},{1,9},{5... | collective-permute-start | bytes 2162696 | tf_op jit(solution)/shard_map/ppermute | solution.py:429
  446.6 34.7 %collective-permute-start.38 = (bf16[2,4,32,1536]{3,2,1,0:T(8,128)(2,1)S(1)}, bf16[2,4,32,1536]{3,2,1,0:T(8,128)(2,1)S(1)}, u32[]{:S(2)}, u32[]{:S(2)}) collective-permute-start(bf16[2,4,32,1536]{3,2,1,0:T(8,128)(2,1)S(1)} %bitcast.291), channel_id=1, source_target_pairs={{0,2},{1,3},{2,0},{3,1},{4,6},{5,7},{6,4},{7,5},{8,10},{9,11},{10,... | collective-permute-start | bytes 2359304 | tf_op jit(solution)/shard_map/ppermute | solution.py:429
  466.1 30.1 %collective-permute-start.57 = (bf16[4,32,2816]{2,1,0:T(8,128)(2,1)S(1)}, bf16[4,32,2816]{2,1,0:T(8,128)(2,1)S(1)}, u32[]{:S(2)}, u32[]{:S(2)}) collective-permute-start(bf16[4,32,2816]{2,1,0:T(8,128)(2,1)S(1)} %fusion.49), channel_id=1, source_target_pairs={{0,2},{1,3},{2,0},{3,1},{4,6},{5,7},{6,4},{7,5},{8,10},{9,11},{10,... | collective-permute-start | bytes 2162696 | tf_op jit(solution)/shard_map/ppermute | solution.py:429
  466.9 30.8 %collective-permute-start.64 = (bf16[2,2,32,2816]{3,2,0,1:T(8,128)(2,1)S(1)}, bf16[2,2,32,2816]{3,2,0,1:T(8,128)(2,1)S(1)}, u32[]{:S(2)}, u32[]{:S(2)}) collective-permute-start(bf16[2,2,32,2816]{3,2,0,1:T(8,128)(2,1)S(1)} %fusion.41), channel_id=1, source_target_pairs={{0,8},{4,12},{8,24},{12,28},{16,0},{20,4},{24,16},{28,20},{1,9},{5... | collective-permute-start | bytes 2162696 | tf_op jit(solution)/shard_map/ppermute | solution.py:429
  481.6 23.4 %collective-permute-start.39 = (bf16[4,32,1536]{2,1,0:T(8,128)(2,1)S(1)}, bf16[4,32,1536]{2,1,0:T(8,128)(2,1)S(1)}, u32[]{:S(2)}, u32[]{:S(2)}) collective-permute-start(bf16[4,32,1536]{2,1,0:T(8,128)(2,1)S(1)} %fusion.54), channel_id=1, source_target_pairs={{0,4},{4,0},{8,12},{12,8},{16,20},{20,16},{24,28},{28,24},{1,5},{5... | collective-permute-start | bytes 1179656 | tf_op jit(solution)/shard_map/ppermute | solution.py:429
  (89 other events, 846.2 us)

commit v4 on v3

v4 whole, which is shorter than its diff:
```python
import functools

import jax
import jax.numpy as jnp
import numpy as np
from jax import lax
from jax.experimental import pallas as pl
from jax.experimental.pallas import tpu as pltpu
from jax.sharding import PartitionSpec as P

LONGEST = 1024
HEADS = 16
FEAT = 16
LANES = 128
GROUP = LANES // FEAT
PIECES = FEAT // 2 + 2
WIDE = PIECES * LANES
PACKED = WIDE // 2 + 16


def dot(left, right, dims=((1,), (0,))):
    return lax.dot_general(left, right, (dims, ((), ())), preferred_element_type=jnp.float32)


def rolls(scaled):
    zero = lax.optimization_barrier(jnp.int32(0))
    row = lax.broadcasted_iota(jnp.int32, (LANES, WIDE), 0) + zero
    column = lax.broadcasted_iota(jnp.int32, (LANES, WIDE), 1)
    d, lane = column // LANES - 1, column % LANES
    a = lane % FEAT
    goal = lane - a + (a + d) % FEAT
    found = (row == goal) & (d >= 0) & ((d < FEAT // 2) | (a < FEAT // 2))
    factor = jnp.where(d == 0, 1 / 32, 1 / 16) if scaled else 1.0
    return jnp.where(found, factor, 0.0).astype(jnp.bfloat16)


def features(rows, factors, lin, axis):
    x = rows.astype(jnp.float32)
    pieces = [x * lin]
    for number in range(PIECES - 1):
        span = slice(number * LANES, (number + 1) * LANES)
        piece = x * (factors[:, span] if axis else factors[span, :])
        if number == PIECES - 2:
            place = lax.broadcasted_iota(jnp.int32, piece.shape, axis)
            piece = jnp.where(place % FEAT == FEAT // 2, 1.0, piece)
        pieces.append(piece)
    return jnp.concatenate([piece.astype(jnp.bfloat16) for piece in pieces], axis=axis)


def turned_features(rows, turned_pick_ref, lin):
    turned = rows.astype(jnp.float32).T.astype(jnp.bfloat16)
    return features(turned, dot(turned_pick_ref[LANES:, :], turned), lin, 0)


def upright_features(rows, pick_ref, lin):
    return features(rows, dot(rows, pick_ref[:, LANES:]), lin, 1)


def head_mask(lanes_per_head, first_head):
    row_head = lax.broadcasted_iota(jnp.int32, (LANES, LANES), 0) // FEAT
    lane_head = lax.broadcasted_iota(jnp.int32, (LANES, LANES), 1) // lanes_per_head + first_head
    return row_head == lane_head


def head_masks(value_dim):
    per = LANES // value_dim
    return [head_mask(value_dim, part * per) for part in range(GROUP // per)]


def low_half():
    return lax.broadcasted_iota(jnp.int32, (LANES, LANES), 1) < LANES // 2


def piece_spans():
    return [slice(number * LANES, (number + 1) * LANES) for number in range(PIECES)]


def fold_heads(rows, masks):
    total = None
    for part, mask in enumerate(masks):
        piece = jnp.where(mask, rows[:, part * LANES : (part + 1) * LANES], 0.0)
        total = piece if total is None else total + piece
    return total + pltpu.roll(total, LANES // 2, 1)


def diagonal():
    row = lax.broadcasted_iota(jnp.int32, (LANES, LANES), 0)
    return row == lax.broadcasted_iota(jnp.int32, (LANES, LANES), 1)


def pack_state(out_ref, pieces):
    low, straight = low_half(), diagonal()
    for number in range(0, PIECES, 2):
        rows = slice(number // 2 * LANES, (number // 2 + 1) * LANES)
        values = jnp.where(low, pieces[number][0], pieces[number + 1][0])
        out_ref[0, 0, rows, :] = values.astype(out_ref.dtype)
    sums = [jnp.sum(jnp.where(straight, s, 0.0), axis=0, keepdims=True) for _, s in pieces]
    sums.append(jnp.zeros((PACKED - WIDE // 2 - PIECES, LANES), jnp.float32))
    out_ref[0, 0, WIDE // 2 :, :] = jnp.concatenate(sums, axis=0).astype(out_ref.dtype)


def spread_state(state_ref, wide_ref, value_dim, sums_of):
    masks, low, straight = head_masks(value_dim), low_half(), diagonal()
    all_sums = state_ref[0, 0, WIDE // 2 :, :].astype(jnp.float32)
    for number, span in enumerate(piece_spans()):
        rows = slice(number // 2 * LANES, (number // 2 + 1) * LANES)
        state = state_ref[0, 0, rows, :].astype(jnp.float32)
        turned = pltpu.roll(state, LANES // 2, 1)
        values = jnp.where(low, turned, state) if number % 2 else jnp.where(low, state, turned)
        sums = jnp.where(straight, all_sums[number : number + 1, :], 0.0)
        sums = jnp.broadcast_to(jnp.sum(sums, axis=1, keepdims=True), (LANES, LANES))
        parts = [jnp.where(mask, values, 0.0) for mask in masks] + sums_of(sums, masks)
        for place, part in enumerate(parts):
            wide_ref[span, slice(place * LANES, (place + 1) * LANES)] = part.astype(jnp.bfloat16)


def own_lanes(array, lanes_per_head, head):
    place = lax.broadcasted_iota(jnp.int32, array.shape, 1) // lanes_per_head
    return jnp.where(place == head, array, jnp.zeros_like(array))


Q, K, V = slice(0, LANES), slice(LANES, 2 * LANES), slice(2 * LANES, None)


def tail_kernel(value_dim, x_ref, seg_ref, pick_ref, out_ref):
    seg = seg_ref[...]
    keep = (seg == seg[-1:, :]).astype(jnp.float32)
    values = (x_ref[:, V].astype(jnp.float32) * keep).astype(jnp.bfloat16)
    ones = jnp.broadcast_to(keep, (seg.shape[0], LANES)).astype(jnp.bfloat16)
    phi = turned_features(x_ref[:, K], pick_ref, 1.0)
    full = dot(phi, jnp.concatenate([values, ones], axis=1))
    width, masks = values.shape[1], head_masks(value_dim)
    pack_state(
        out_ref,
        [(fold_heads(full[span, :width], masks), full[span, width:]) for span in piece_spans()],
    )


def masks_of(seg_ref, seg_row_ref, begin, block):
    stop = begin + block
    rows = begin + lax.broadcasted_iota(jnp.int32, (block, stop), 0)
    columns = lax.broadcasted_iota(jnp.int32, (block, stop), 1)
    same = seg_ref[begin:stop, :] == seg_row_ref[0, :, :stop]
    return ((rows >= columns) & same).astype(jnp.float32)


def near_kernel(value_dim, block, x_ref, seg_ref, seg_row_ref, top_ref, den_ref):
    length = x_ref.shape[0]
    low = lax.broadcasted_iota(jnp.int32, (block, LANES), 1) < value_dim
    for begin in range(0, length, block):
        stop = begin + block
        mask = masks_of(seg_ref, seg_row_ref, begin, block)
        queries = x_ref[begin:stop, Q] * jnp.bfloat16(FEAT ** (-0.5))
        keys = x_ref[:stop, K]
        ones = jnp.ones((stop, LANES), jnp.bfloat16)
        for pair in range(GROUP // 2):
            span = slice(pair * LANES, (pair + 1) * LANES)
            first = 2 * LANES + pair * LANES
            values = jnp.concatenate([x_ref[:stop, first : first + LANES], ones], axis=1)
            sides = []
            for head in (2 * pair, 2 * pair + 1):
                scores = dot(own_lanes(queries, FEAT, head), keys, ((1,), (1,)))
                weights = (((0.5 * scores + 1.0) * scores + 1.0) * mask).astype(jnp.bfloat16)
                sides.append(dot(weights, values))
            top_ref[begin:stop, span] = jnp.where(low, sides[0][:, :LANES], sides[1][:, :LANES])
            den_ref[begin:stop, span] = jnp.where(low, sides[0][:, LANES:], sides[1][:, LANES:])


def far_kernel(value_dim, x_ref, seg_ref, state_ref, top_ref, den_ref, pick_ref, *rest):
    y_ref, inverse_ref, state_wide = rest[-3:]
    width = top_ref.shape[1]
    spread_state(
        state_ref, state_wide, value_dim,
        lambda sums, masks: [jnp.where(mask, sums, 0.0) for mask in masks],
    )
    seg = seg_ref[...]
    keep = (seg == seg[:1, :]).astype(jnp.float32)
    far = dot(upright_features(x_ref[:, Q], pick_ref, FEAT ** (-0.5)), state_wide[...])
    top = top_ref[...] + keep * far[:, :width]
    inverse = 1.0 / (den_ref[...] + keep * far[:, width:])
    y_ref[...] = (top * inverse).astype(y_ref.dtype)
    inverse_ref[...] = inverse


def head_kernel(
    value_dim, x_ref, dy_ref, y_ref, inverse_ref, seg_ref, pick_ref, out_ref, dn_ref, dd_ref
):
    width = dy_ref.shape[1]
    d_top = dy_ref[...].astype(jnp.float32) * inverse_ref[...]
    product = d_top * y_ref[...].astype(jnp.float32)
    large = product.astype(jnp.bfloat16)
    small = (product - large.astype(jnp.float32)).astype(jnp.bfloat16)
    row = lax.broadcasted_iota(jnp.int32, (width, LANES), 0) // value_dim
    lane = lax.broadcasted_iota(jnp.int32, (width, LANES), 1) // FEAT
    adder = jnp.where(row == lane, -1.0, 0.0).astype(jnp.bfloat16)
    d_den = dot(large, adder) + dot(small, adder)
    rounded = d_den.astype(jnp.bfloat16).astype(jnp.float32)
    place = lax.broadcasted_iota(jnp.int32, d_den.shape, 1) % FEAT
    d_den = jnp.where(place < FEAT // 2, rounded, d_den - rounded)
    seg = seg_ref[...]
    keep = (seg == seg[:1, :]).astype(jnp.float32)
    dn_ref[...] = d_top.astype(jnp.bfloat16)
    dd_ref[...] = d_den.astype(jnp.bfloat16)
    d_both = [(d_top * keep).astype(jnp.bfloat16), (d_den * keep).astype(jnp.bfloat16)]
    full = dot(
        turned_features(x_ref[:, Q], pick_ref, FEAT ** (-0.5)), jnp.concatenate(d_both, axis=1)
    )
    masks, own, pieces = head_masks(value_dim), head_mask(FEAT, 0), []
    for span in piece_spans():
        sums = jnp.where(own, full[span, width:], 0.0)
        sums = jnp.sum(sums, axis=1, keepdims=True) * (2 / FEAT)
        pieces.append((fold_heads(full[span, :width], masks), sums))
    pack_state(out_ref, pieces)


def from_features(d_phi, rows, pick_ref, lin):
    x = rows.astype(jnp.float32)
    factors = dot(rows, pick_ref[:, LANES:])
    total, scaled = d_phi[:, :LANES] * lin, []
    for number in range(PIECES - 1):
        span = slice(number * LANES, (number + 1) * LANES)
        piece = d_phi[:, (number + 1) * LANES : (number + 2) * LANES]
        total = total + piece * factors[:, span]
        scaled.append((piece * x).astype(jnp.bfloat16))
    return total + dot(jnp.concatenate(scaled, axis=1), pick_ref[:, LANES:], ((1,), (1,)))


def near_back_kernel(
    value_dim, block, x_ref, dn_ref, dd_ref, seg_ref, seg_row_ref, state_ref, pick_ref,
    dq_ref, dk_ref, dv_ref, state_wide, dq_sum,
):
    length, width = dn_ref.shape
    own = head_mask(FEAT, 0)
    spread_state(
        state_ref, state_wide, value_dim,
        lambda sums, masks: [jnp.where(own, sums, 0.0) * (2 / FEAT)],
    )
    keep = seg_ref[...] == seg_ref[:1, :]
    d_both = jnp.concatenate([dn_ref[...], dd_ref[...]], axis=1)
    d_phi = dot(jnp.where(keep, d_both, jnp.zeros_like(d_both)), state_wide[...], ((1,), (1,)))
    dq_sum[...] = from_features(d_phi, x_ref[:, Q], pick_ref, FEAT ** (-0.5))
    scale = jnp.bfloat16(FEAT ** (-0.5))
    low = lax.broadcasted_iota(jnp.int32, (block, LANES), 1) < value_dim
    for begin in range(0, length, block):
        stop, count = begin + block, length - begin
        key_place = lax.broadcasted_iota(jnp.int32, (block, count), 0)
        query_place = lax.broadcasted_iota(jnp.int32, (block, count), 1)
        same = seg_ref[begin:stop, :] == seg_row_ref[0, :, begin:]
        mask = ((query_place >= key_place) & same).astype(jnp.float32)
        queries = x_ref[begin:, Q] * scale
        keys = x_ref[begin:stop, K]
        dd = dd_ref[begin:, :]
        dk = jnp.zeros((block, LANES), jnp.float32)
        for pair in range(GROUP // 2):
            span = slice(pair * LANES, (pair + 1) * LANES)
            first = 2 * LANES + pair * LANES
            values = x_ref[begin:stop, first : first + LANES]
            dn = dn_ref[begin:, span]
            d_both = jnp.concatenate([dn, dd], axis=1)
            sides = []
            for side in range(2):
                head = 2 * pair + side
                own_keys = own_lanes(keys, FEAT, head)
                ones = own_lanes(jnp.full((block, LANES), 2 / FEAT, jnp.bfloat16), FEAT, head)
                own_values = own_lanes(values, value_dim, side)
                scores = dot(own_keys, queries, ((1,), (1,)))
                weights = (((0.5 * scores + 1.0) * scores + 1.0) * mask).astype(jnp.bfloat16)
                d_weights = dot(
                    jnp.concatenate([own_values, ones], axis=1), d_both, ((1,), (1,))
                )
                d_scores = (d_weights * ((scores + 1.0) * mask)).astype(jnp.bfloat16)
                sides.append(dot(weights, dn))
                dk = dk + own_lanes(dot(d_scores, queries), FEAT, head)
                dq_sum[begin:, :] += dot(d_scores, own_keys * scale, ((0,), (0,)))
            dv_ref[begin:stop, span] = jnp.where(low, sides[0], sides[1])
        dk_ref[begin:stop, :] = dk
    dq_ref[...] = dq_sum[...].astype(dq_ref.dtype)


def far_back_kernel(
    value_dim, x_ref, seg_ref, state_ref, dq_ref, dk_ref, dv_ref, pick_ref, out_ref, state_wide
):
    length, width = dv_ref.shape
    spread_state(state_ref, state_wide, value_dim, lambda sums, masks: [sums * (1 / LANES)])
    seg = seg_ref[...]
    keep = (seg == seg[-1:, :]).astype(jnp.float32)
    keys = x_ref[:, K]
    ones = jnp.ones((length, LANES), jnp.bfloat16)
    d_phi = dot(jnp.concatenate([x_ref[:, V], ones], axis=1), state_wide[...], ((1,), (1,)))
    dk = dk_ref[...] + keep * from_features(d_phi, keys, pick_ref, 1.0)
    dv = dv_ref[...] + keep * dot(upright_features(keys, pick_ref, 1.0), state_wide[:, :width])
    out_ref[:, Q] = dq_ref[...]
    out_ref[:, K] = dk.astype(out_ref.dtype)
    out_ref[:, V] = dv.astype(out_ref.dtype)


class Attention:
    def __init__(self, rows, length, width):
        self.rows, self.length = rows, length
        self.value_dim = width // HEADS
        self.groups = HEADS // GROUP
        self.wide = GROUP * self.value_dim
        self.across = 2 * LANES + self.wide
        self.block = min(256, length)
        self.count = rows * length
        self.scaled, self.plain = rolls(True), rolls(False)
        self.all = range(self.groups)

    def specs(self, groups, own=False):
        first = 0 if own else groups[0]

        def rows_of(columns):
            return pl.BlockSpec((self.length, columns), lambda r, g: (r, first + g))

        return dict(
            x=rows_of(self.across),
            values=rows_of(self.wide),
            narrow=rows_of(LANES),
            seg=pl.BlockSpec((self.length, 1), lambda r, g: (r, 0)),
            seg_row=pl.BlockSpec((1, 1, self.length), lambda r, g: (r, 0, 0)),
            state=pl.BlockSpec((1, 1, PACKED, LANES), lambda r, g: (r, first + g, 0, 0)),
            pick=pl.BlockSpec((LANES, WIDE), lambda r, g: (0, 0)),
            turned_pick=pl.BlockSpec((WIDE, LANES), lambda r, g: (0, 0)),
        )

    def shape(self, columns, dtype, groups):
        return jax.ShapeDtypeStruct((self.count, columns * len(groups)), dtype)

    def state_shape(self, groups):
        return jax.ShapeDtypeStruct((self.rows, len(groups), PACKED, LANES), jnp.bfloat16)

    def wide_state(self, columns):
        return pltpu.VMEM((WIDE, columns), jnp.bfloat16)

    def call(self, kernel, groups, specs, outs, out_specs, scratch, passes, name):
        return pl.pallas_call(
            functools.partial(kernel, self.value_dim),
            grid=(self.rows, len(groups)),
            in_specs=specs,
            out_specs=out_specs,
            out_shape=outs,
            scratch_shapes=scratch,
            compiler_params=pltpu.CompilerParams(
                dimension_semantics=("arbitrary", "arbitrary"), vmem_limit_bytes=56 * 2**20
            ),
            cost_estimate=pl.CostEstimate(
                flops=self.rows * len(groups) * GROUP * passes * 2**26 * self.length // 512,
                bytes_accessed=2**21,
                transcendentals=0,
            ),
            name=name,
        )

    def tail(self, x, seg):
        at = self.specs(self.all)
        return self.call(
            tail_kernel, self.all, [at["x"], at["seg"], at["turned_pick"]],
            self.state_shape(self.all), at["state"], [], 5, "attn_tail",
        )(x, seg, self.plain.T)

    def near(self, x, seg, seg_row):
        def kernel(value_dim, *refs):
            near_kernel(value_dim, self.block, *refs)

        at = self.specs(self.all)
        out = self.shape(self.wide, jnp.float32, self.all)
        return self.call(
            kernel, self.all, [at["x"], at["seg"], at["seg_row"]],
            [out, out], [at["values"]] * 2, [], 8, "attn_near",
        )(x, seg, seg_row)

    def far(self, x, seg, state, top, den):
        at = self.specs(self.all)
        return self.call(
            far_kernel, self.all,
            [at["x"], at["seg"], at["state"], at["values"], at["values"], at["pick"]],
            [self.shape(self.wide, dtype, self.all) for dtype in (jnp.bfloat16, jnp.float32)],
            [at["values"]] * 2, [self.wide_state(2 * self.wide)], 8, "attn_far",
        )(x, seg, state, top, den, self.scaled)

    def head(self, x, dy, y, inverse, seg):
        at = self.specs(self.all)
        return self.call(
            head_kernel, self.all,
            [at["x"], at["values"], at["values"], at["values"], at["seg"], at["turned_pick"]],
            [self.state_shape(self.all), self.shape(self.wide, jnp.bfloat16, self.all),
             self.shape(LANES, jnp.bfloat16, self.all)],
            [at["state"], at["values"], at["narrow"]], [], 5, "attn_head",
        )(x, dy, y, inverse, seg, self.scaled.T)

    def near_back(self, x, dn, dd, seg, seg_row, state, groups):
        def kernel(value_dim, *refs):
            near_back_kernel(value_dim, self.block, *refs)

        at, out = self.specs(groups), self.specs(groups, own=True)
        return self.call(
            kernel, groups,
            [at["x"], at["values"], at["narrow"], at["seg"], at["seg_row"], at["state"],
             at["pick"]],
            [self.shape(LANES, jnp.bfloat16, groups), self.shape(LANES, jnp.float32, groups),
             self.shape(self.wide, jnp.float32, groups)],
            [out["narrow"], out["narrow"], out["values"]],
            [self.wide_state(self.wide + LANES), pltpu.VMEM((self.length, LANES), jnp.float32)],
            24, "attn_near_back",
        )(x, dn, dd, seg, seg_row, state, self.scaled)

    def far_back(self, x, seg, state, dq, dk, dv, groups):
        at, out = self.specs(groups), self.specs(groups, own=True)
        return self.call(
            far_back_kernel, groups,
            [at["x"], at["seg"], at["state"], out["narrow"], out["narrow"], out["values"],
             at["pick"]],
            self.shape(self.across, jnp.bfloat16, groups), out["x"],
            [self.wide_state(self.wide + LANES)], 9, "attn_far_back",
        )(x, seg, state, dq, dk, dv, self.plain)


class Passing:
    def __init__(self, whole, steps, size):
        self.whole, self.steps, self.size = whole, steps, size

    def start(self, own, linked, shift):
        self.own, self.linked, self.left = own, linked, self.steps
        self.pairs = [(i, i + shift) for i in range(self.size) if 0 <= i + shift < self.size]
        self.go(own)

    def go(self, array):
        self.sent, self.left = array, self.left - 1
        self.came = self.pick(self.linked, lax.ppermute(array, "seq", self.pairs))

    @staticmethod
    def pick(flag, array):
        return jnp.where(flag[:, None, None, None], array, jnp.zeros_like(array))

    def rest(self, *hold):
        while self.left:
            came = after(self.came, *hold) if hold else self.came
            self.go(self.own + self.pick(self.whole, came))


epsilon = 1e-05


def against(left, matrix):
    return dot(left, matrix, ((1,), (1,)))


def norm_forward(values):
    scale = lax.rsqrt(jnp.mean(values * values, axis=1, keepdims=True) + epsilon)
    return (scale, values * scale)


def norm_backward(d_scaled, gain, scale, normed):
    d_normed = d_scaled * gain
    return scale * (d_normed - normed * jnp.mean(d_normed * normed, axis=1, keepdims=True))


def fold(count):
    return [0] + list(range(1, count, 2)) + list(range(2, count, 2))[::-1]


class Line:
    def __init__(self, axis, axis_size, stride, count):
        self.axis, self.size, self.stride, self.count = axis, axis_size, stride, count
        self.order = fold(count)

    def send(self, array, steps=1):
        pairs = []
        for index in range(self.size):
            place = (index // self.stride) % self.count
            goal = self.order[(self.order.index(place) + steps) % self.count]
            pairs.append((index, index + (goal - place) * self.stride))
        return lax.ppermute(array, self.axis, pairs)

    def place_back(self, steps):
        own = (lax.axis_index(self.axis) // self.stride) % self.count
        rank = jnp.asarray([self.order.index(p) for p in range(self.count)], jnp.int32)[own]
        return jnp.asarray(self.order, jnp.int32)[(rank - steps) % self.count]


class Slice:
    def __init__(self, dp, seq):
        self.dp, self.seq, self.devices = dp, seq, dp * seq
        self.lines = {
            "z": Line("dp", dp, 2, dp // 2),
            "x": Line("dp", dp, 1, 2),
            "y": Line("seq", seq, 2, seq // 2),
            "c": Line("seq", seq, 1, 2),
        }
        if dp % 4 == 0:
            self.lines["w"] = Line("dp", dp, 4, dp // 4)
            self.lines["u"] = Line("dp", dp, 2, 2)

    def device_of(self, back):
        at = {d: self.lines[d].place_back(back[d]) for d in back}
        z = at["z"] if "z" in at else at["w"] * 2 + at["u"]
        return ((z * 2 + at["x"]) * (self.seq // 2) + at["y"]) * 2 + at["c"]


def after(array, *others):
    return lax.optimization_barrier((array, *others))[0]


def assemble(pieces, widths, block, shape):
    arrays = [array for array, _, _ in pieces]
    dtype = arrays[0].dtype
    places = jnp.stack([shape.device_of(n) for _, names, _ in pieces for n in names])
    copies = sum(len(names) * len(spans) for _, names, spans in pieces)
    windows = [
        (min(span[0] for span in spans), max(span[0] + span[1] for span in spans))
        for _, _, spans in pieces
    ]
    held = [(array.shape[0], high - low) for array, (low, high) in zip(arrays, windows)]

    def kernel(places_ref, *refs):
        piece_refs, refs = refs[: len(pieces)], refs[len(pieces) :]
        out_refs, refs = refs[: len(widths)], refs[len(widths) :]
        buffers, (in_sems, out_sems) = refs[: len(pieces)], refs[len(pieces) :]
        loads = []
        for number, piece_ref in enumerate(piece_refs):
            low, high = windows[number]
            load = pltpu.make_async_copy(
                piece_ref.at[:, pl.ds(low, high - low)], buffers[number], in_sems.at[number]
            )
            load.start()
            loads.append(load)
        stores, begin = [], 0
        for number, (load, (_, names, spans)) in enumerate(zip(loads, pieces)):
            load.wait()
            for i in range(len(names)):
                to = pl.multiple_of(places_ref[begin + i] * block, block)
                for low, width, output, column in spans:
                    store = pltpu.make_async_copy(
                        buffers[number].at[pl.ds(i * block, block), pl.ds(low - windows[number][0], width)],
                        out_refs[output].at[pl.ds(to, block), pl.ds(column, width)],
                        out_sems.at[len(stores)],
                    )
                    store.start()
                    stores.append(store)
            begin += len(names)
        for store in stores:
            store.wait()

    size = sum(tall * wide for tall, wide in held) * dtype.itemsize
    return pl.pallas_call(
        kernel,
        out_shape=[jax.ShapeDtypeStruct((shape.devices * block, w), dtype) for w in widths],
        in_specs=[pl.BlockSpec(memory_space=pltpu.SMEM)]
        + [pl.BlockSpec(memory_space=pl.ANY)] * len(pieces),
        out_specs=[pl.BlockSpec(memory_space=pl.ANY)] * len(widths),
        scratch_shapes=[pltpu.VMEM(size, dtype) for size in held]
        + [
            pltpu.SemaphoreType.DMA((len(pieces),)),
            pltpu.SemaphoreType.DMA((copies,)),
        ],
        cost_estimate=pl.CostEstimate(flops=0, bytes_accessed=2 * size, transcendentals=0),
        name="assemble",
    )(places, *arrays)


class Gathering:
    def __init__(self, shape, array, names=None):
        self.shape, self.array = shape, array
        self.names = names or [dict(z=0, x=0, y=0, c=0)]

    def came(self, dim, direct=False, hold=()):
        line, array, out = self.shape.lines[dim], self.array, []
        for step in range(1, line.count):
            array = line.send(self.array, step) if direct else line.send(array)
            if step <= len(hold):
                array = after(array, *hold[step - 1])
            out.append((array, [dict(n, **{dim: step}) for n in self.names]))
        return out

    def along(self, dim, direct=False, hold=()):
        came = self.came(dim, direct, hold)
        array = jnp.concatenate([self.array] + [a for a, _ in came], 0)
        return Gathering(self.shape, array, self.names + [n for _, names in came for n in names])

    def columns(self, low, high):
        return Gathering(self.shape, self.array[:, low:high], self.names)

    def pieces(self, dim, spans):
        found = [(self.array, self.names)] + self.came(dim)
        return [(array, names, spans) for array, names in found]


def spans_of(low, high, homes):
    spans = []
    for begin, width, output, column in homes:
        first, last = max(low, begin), min(high, begin + width)
        if first < last:
            spans.append((first - low, last - first, output, column + first - begin))
    return spans


def side_by_side(widths):
    return [(sum(widths[:i]), width, i, 0) for i, width in enumerate(widths)]


class TwoWays:
    def __init__(self, parts, shape, homes=None, widths=None):
        own = [part.shape[1] for part in parts]
        self.homes, self.widths = homes or side_by_side(own), widths or own
        self.block, self.shape = parts[0].shape[0], shape
        self.columns = sum(own)
        self.cut = -(-self.columns // 2 // LANES) * LANES
        self.held = Gathering(shape, jnp.concatenate(parts, axis=1))

    def first(self, *hold):
        self.held = self.held.along("z", True, [hold] * 8 if hold else ())

    def second(self, *hold):
        hold = [hold] if hold else ()
        self.one = self.held.columns(0, self.cut).along("x", False, hold)
        self.two = self.held.columns(self.cut, self.columns).along("y", False, hold)

    def third(self, *hold):
        hold = [hold] if hold else ()
        self.one, self.two = self.one.along("y", False, hold), self.two.along("x", False, hold)

    def last(self):
        self.ends = [self.one.came("c"), self.two.came("c")]

    def output(self, *outputs):
        homes = [(b, w, outputs.index(o), c) for b, w, o, c in self.homes if o in outputs]
        pieces = []
        for half, low, high, came in (
            (self.one, 0, self.cut, self.ends[0]),
            (self.two, self.cut, self.columns, self.ends[1]),
        ):
            spans = spans_of(low, high, homes)
            found = [(half.array, half.names)] + came
            pieces += [(array, names, spans) for array, names in found if spans]
        return assemble(pieces, [self.widths[o] for o in outputs], self.block, self.shape)


LAYOUT = "cyxwu"


def picker(shape, width):
    block = width // shape.devices
    if block % 16:
        order = jnp.arange(width)
    else:
        names = [dict()]
        for dim in LAYOUT:
            names = [dict(n, **{dim: s}) for n in names for s in range(shape.lines[dim].count)]
        places = jnp.stack([shape.device_of(n) for n in names])
        order = (places[:, None] * block + jnp.arange(block)[None, :]).reshape(width)
    return (jnp.arange(width)[:, None] == order[None, :]).astype(jnp.bfloat16)


def turned_rows(pick, left):
    return dot(pick, left, ((0,), (1,))).astype(jnp.bfloat16)


class Scattering:
    def __init__(self, shape, kept, arrived):
        half, columns = kept.shape
        self.shape, self.dims = shape, LAYOUT[1:]
        form = [shape.lines[d].count for d in self.dims] + [2 * half // shape.devices, columns]
        self.parts = [[kept.reshape(form), arrived.reshape(form)]]

    def beside(self, other):
        self.parts = self.parts + other.parts
        return self

    def term_of(self, step):
        found = []
        for terms in self.parts:
            own = [lax.index_in_dim(t, step, self.axis, False) for t in terms]
            found.append(functools.reduce(jnp.add, [t.astype(jnp.float32) for t in own]))
        return jnp.concatenate(found, axis=-1)

    def start(self, dim, *hold):
        self.line, self.axis, self.step = self.shape.lines[dim], self.dims.index(dim), 1
        self.dims = self.dims.replace(dim, "")
        if hold:
            self.parts = [[after(t, *hold) for t in terms] for terms in self.parts]
        self.sent = self.term_of(1).astype(jnp.bfloat16)
        self.came = self.line.send(self.sent)
        return self

    def advance(self, *hold):
        came = after(self.came, *hold) if hold else self.came
        self.step += 1
        total = self.term_of(self.step % self.line.count) + came.astype(jnp.float32)
        if self.step < self.line.count:
            self.sent = total.astype(jnp.bfloat16)
            self.came = self.line.send(self.sent)
        else:
            self.parts, self.came = [[total]], None
        return self

    def along(self, dim):
        self.start(dim)
        while self.came is not None:
            self.advance()
        return self


def scatter_whole(kept, sent):
    whole = jnp.concatenate([kept, sent], 0).astype(jnp.float32)
    return lax.psum_scatter(whole, ("dp", "seq"), scatter_dimension=0, tiled=True)


FF_TILE = 256


def mlp_kernel(
    block, begins, ends, a_ref, g_ref, at_ref, gt_ref, gate_ref, up_ref, down_ref, *refs
):
    if not begins:
        y_in_ref, da_in_ref, *refs = refs
    if ends:
        x_ref, gain_ref, y_ref, dxo_ref, da_sum, kept_ref, sent_ref, *refs, y_sum = refs
    else:
        y_sum, da_sum, kept_ref, sent_ref, *refs = refs
    hidden_ref, d_gate_ref, d_up_ref = refs
    count = a_ref.shape[0]
    step = pl.program_id(0)

    @pl.when(step == 0)
    def _():
        y_sum[...] = jnp.zeros_like(y_sum) if begins else y_in_ref[...]
        da_sum[...] = jnp.zeros_like(da_sum) if begins else da_in_ref[...]

    for begin in range(0, count, block):
        span = slice(begin, begin + block)
        a, g = a_ref[span, :], g_ref[span, :]
        gate, up = dot(a, gate_ref[...]), dot(a, up_ref[...])
        d_hidden = dot(g, down_ref[...])
        sigma = jax.nn.sigmoid(gate)
        silu = gate * sigma
        hidden = (silu * up).astype(jnp.bfloat16)
        d_gate = (d_hidden * up * (sigma + silu * (1.0 - sigma))).astype(jnp.bfloat16)
        d_up = (d_hidden * silu).astype(jnp.bfloat16)
        hidden_ref[span, :], d_gate_ref[span, :], d_up_ref[span, :] = hidden, d_gate, d_up
        y_sum[span, :] += dot(hidden, down_ref[...], ((1,), (1,)))
        da_sum[span, :] += dot(d_gate, gate_ref[...], ((1,), (1,))) + dot(
            d_up, up_ref[...], ((1,), (1,))
        )
    half = at_ref.shape[0] // 2
    for number, (left, right) in enumerate(
        ((at_ref, d_gate_ref), (at_ref, d_up_ref), (gt_ref, hidden_ref))
    ):
        kept_ref[number] = dot(left[:half, :], right[...]).astype(jnp.bfloat16)
        sent_ref[number] = dot(left[half:, :], right[...]).astype(jnp.bfloat16)
    if not ends:
        return

    @pl.when(step == pl.num_programs(0) - 1)
    def _():
        for begin in range(0, count, block):
            span = slice(begin, begin + block)
            x = x_ref[span, :]
            y_ref[span, :] = (x + y_sum[span, :]).astype(y_ref.dtype)
            scale = lax.rsqrt(jnp.mean(x * x, axis=1, keepdims=True) + epsilon)
            normed = x * scale
            d_normed = da_sum[span, :] * gain_ref[...]
            mean = jnp.mean(d_normed * normed, axis=1, keepdims=True)
            dx = g_ref[span, :].astype(jnp.float32) + scale * (d_normed - normed * mean)
            da_sum[span, :] = dx
            dxo_ref[span, :] = dx.astype(dxo_ref.dtype)


def feed_forward(a, g, a_turned, g_turned, weights, tiles, sums=None, ending=None):
    count, width = a.shape
    half = width // 2

    def held(rows, columns):
        return pl.BlockSpec((rows, columns), lambda j: (0, 0), pipeline_mode=pl.Buffered(1))

    def tile(first):
        return pl.BlockSpec((width, FF_TILE), lambda j: (0, first + j))

    def shape(dtype):
        return jax.ShapeDtypeStruct((count, width), dtype)

    full = held(count, width)
    given = [a, g, a_turned, g_turned] + [array for array, _ in weights]
    specs = [full, full] + [held(width, count)] * 2 + [tile(first) for _, first in weights]
    scratch = [pltpu.VMEM((count, FF_TILE), jnp.bfloat16)] * 3
    if sums is not None:
        given, specs = given + list(sums), specs + [full] * 2
    if ending is not None:
        given, specs = given + list(ending), specs + [full, held(1, width)]
        outs = [shape(jnp.bfloat16), shape(jnp.bfloat16), shape(jnp.float32)]
        scratch = scratch + [pltpu.VMEM((count, width), jnp.float32)]
    else:
        outs = [shape(jnp.float32)] * 2
    hidden = tiles * FF_TILE
    return pl.pallas_call(
        functools.partial(mlp_kernel, min(512, count), sums is None, ending is not None),
        grid=(tiles,),
        in_specs=specs,
        out_specs=[full] * len(outs)
        + [pl.BlockSpec((3, half, FF_TILE), lambda j: (0, 0, j))] * 2,
        out_shape=outs + [jax.ShapeDtypeStruct((3, half, hidden), jnp.bfloat16)] * 2,
        scratch_shapes=scratch,
        compiler_params=pltpu.CompilerParams(
            dimension_semantics=("arbitrary",), vmem_limit_bytes=60 * 2**20
        ),
        cost_estimate=pl.CostEstimate(
            flops=18 * count * width * hidden,
            bytes_accessed=12 * width * hidden + 20 * count * width,
            transcendentals=count * hidden,
        ),
        name="mlp",
    )(*given)


def gain_gradient(weights, gradients, gain):
    products = jnp.sum(weights.astype(jnp.float32) * gradients, axis=1)
    return products / gain.astype(jnp.float32)


def per_device(
    shape,
    layer_input,
    segment_ids,
    gain_attn,
    w_query,
    w_key,
    w_value,
    w_out,
    gain_mlp,
    w_gate,
    w_up,
    w_down,
    grad_output,
):
    rows, shard_len, width = layer_input.shape
    count = rows * shard_len
    narrow, hidden = HEADS * FEAT, w_gate.shape[1]
    attention = Attention(rows, shard_len, width)
    groups, wide, across = attention.groups, attention.wide, attention.across
    gains = jnp.pad(jnp.stack([gain_attn, gain_mlp], axis=1), ((0, 0), (0, LANES - 2)))
    first_parts = [w_query, w_key, w_value, gains]
    homes, grouped = [], []
    for g in range(groups):
        for part, begin, size, place in (
            (w_query, 0, LANES, 0),
            (w_key, narrow, LANES, LANES),
            (w_value, 2 * narrow, wide, 2 * LANES),
        ):
            homes.append((begin + g * size, size, 0, g * across + place))
            grouped.append(part[:, g * size : (g + 1) * size])
    homes.append((groups * across, LANES, 0, groups * across))
    spare = ((0, 0), (0, -hidden % FF_TILE))
    gate_part, up_part, down_part = (
        jnp.pad(part, spare) for part in (w_gate, w_up, w_down.T)
    )
    tiles = gate_part.shape[1] // FF_TILE
    ringed = gains.shape[0] % 16 == 0
    if ringed:
        early = TwoWays(first_parts, shape, homes, [groups * across + LANES])
        rest = TwoWays([gate_part, w_out, up_part], shape)
        early.first()
        early.second()
        early.third()
        begun = [early.one.array, early.two.array]
        rest.first(*begun)
        down = Gathering(shape, down_part).along("x", False, [begun])
        early.last()
        (gathered,) = early.output(0)
    else:
        first_part = jnp.concatenate(grouped + [gains], axis=1)
        gathered, out_w, gate_w, up_w, down_w = (
            lax.all_gather(part, ("dp", "seq"), axis=0, tiled=True)
            for part in (first_part, w_out, gate_part, up_part, down_part)
        )
    qkv_w = gathered[:, : groups * across]
    gain_one = gathered[:, groups * across].astype(jnp.float32)[None, :]
    gain_two = gathered[:, groups * across + 1].astype(jnp.float32)[None, :]

    pick = picker(shape, width)
    cotangent = grad_output.reshape(count, width)
    tokens = layer_input.reshape(count, width).astype(jnp.float32)
    scale_one, normed_one = norm_forward(tokens)
    a_one = (normed_one * gain_one).astype(jnp.bfloat16)
    a_one = after(a_one, rest.held.array, down.array) if ringed else a_one
    qkv = jnp.dot(a_one, qkv_w, preferred_element_type=jnp.float32).astype(jnp.bfloat16)
    place = lax.axis_index("seq")
    own_seg = lax.dynamic_slice_in_dim(segment_ids, place * shard_len, shard_len, 1)
    before = jnp.maximum(place * shard_len - 1, 0)
    behind = jnp.minimum((place + 1) * shard_len, segment_ids.shape[1] - 1)
    first, last = own_seg[:, 0], own_seg[:, -1]
    from_before = lax.dynamic_index_in_dim(segment_ids, before, 1, keepdims=False) == first
    from_behind = lax.dynamic_index_in_dim(segment_ids, behind, 1, keepdims=False) == last
    seg, seg_row = own_seg.reshape(count, 1), own_seg.reshape(rows, 1, shard_len)
    reach = min(shape.seq - 1, -(-(LONGEST - 1) // shard_len))
    states = Passing(first == last, reach, shape.seq)
    tail = attention.tail(qkv, seg)
    if ringed:
        rest.second(tail)
        down = down.along("y", False, [[tail]])
        states.start(tail, from_before, 1)
        top, den = attention.near(
            after(qkv, states.sent, rest.one.array, rest.two.array, down.array), seg, seg_row
        )
        states.rest(den)
        rest.third(den, states.sent)
        rest.last()
        down = down.along("z", False, [[den], [rest.one.array, rest.two.array]])
        down_ends = down.pieces("c", [(0, tiles * FF_TILE, 0, 0)])
        earlier = after(states.came, rest.one.array, rest.two.array)
        mixed_cat, inverse = attention.far(qkv, seg, earlier, top, den)
        (out_w,) = rest.output(1)
    else:
        states.start(tail, from_before, 1)
        states.rest()
        earlier = states.came
        top, den = attention.near(qkv, seg, seg_row)
        mixed_cat, inverse = attention.far(qkv, seg, earlier, top, den)
    x_two = tokens + jnp.dot(mixed_cat, out_w, preferred_element_type=jnp.float32)
    scale_two, normed_two = norm_forward(x_two)
    a_two = (normed_two * gain_two).astype(jnp.bfloat16)
    if ringed:
        gate_w, up_w = rest.output(0, 2)
        (down_w,) = assemble(down_ends, [tiles * FF_TILE], down_part.shape[0], shape)
    result, d_branch, d_x_two, kept, sent = feed_forward(
        a_two,
        cotangent,
        turned_rows(pick, a_two),
        turned_rows(pick, cotangent),
        [(gate_w, 0), (up_w, 0), (down_w, 0)],
        tiles,
        None,
        (x_two, gain_two),
    )
    turned_mixed, turned_one = turned_rows(pick, mixed_cat), turned_rows(pick, a_one)
    half = width // 2
    out_kept, out_sent = (
        dot(t, d_branch).astype(jnp.bfloat16) for t in (turned_mixed[:half], turned_mixed[half:])
    )
    d_mixed = against(d_branch, out_w).astype(jnp.bfloat16)
    d_qkv, grad_qkv = [], []
    if ringed:
        send_core = shape.lines["c"].send
        arrived, out_arrived = send_core(sent), send_core(out_sent)
        d_mixed = after(d_mixed, out_sent, out_kept)
        ahead, d_top, d_den = attention.head(qkv, d_mixed, mixed_cat, inverse, seg)
        states.start(ahead, from_behind, -1)
        arrived = after(arrived, ahead)
        gate_sum, up_sum, down_sum = (Scattering(shape, kept[i], arrived[i]) for i in range(3))
        gate_sum.beside(Scattering(shape, out_kept, out_arrived)).start("y")
        up_sum.start("x")
        down_sum.start("u")
        d_top = after(d_top, states.sent, gate_sum.sent, up_sum.sent, down_sum.sent)
        d_near = [None, None]
        d_near[0] = attention.near_back(qkv, d_top, d_den, seg, seg_row, earlier, range(0, 1))
        states.rest(d_near[0][0])
        d_top = after(d_top, states.sent, d_near[0][0])
        d_near[1] = attention.near_back(qkv, d_top, d_den, seg, seg_row, earlier, range(1, 2))
        near = d_near[1][0]
        down_sum.advance(near).start("w")
        gate_sum.advance(near).start("x")
        up_sum.advance(near).start("y")
        later = after(states.came, near, down_sum.sent, gate_sum.sent, up_sum.sent)

        turned = [turned_one[:half], turned_one[half:]]

        def products(right):
            own_sent = dot(turned[1], right).astype(jnp.bfloat16)
            own_kept = dot(turned[0], right).astype(jnp.bfloat16)
            own_sum = Scattering(shape, own_kept, send_core(own_sent))
            own_sum.sent = own_sent
            return own_sum

        far = attention.far_back(qkv, seg, later, *d_near[0], range(0, 1))
        d_qkv.append(far)
        qkv_a = products(far)
        later = after(later, qkv_a.sent)
        far = attention.far_back(qkv, seg, later, *d_near[1], range(1, 2))
        d_qkv.append(far)
        qkv_a.start("y", far)
        qkv_b = products(after(far, qkv_a.sent))
        down_sum.advance(qkv_b.sent).start("x")
        both = gate_sum.advance(qkv_b.sent).beside(up_sum.advance(qkv_b.sent)).start("u")
        qkv_b.start("x", both.sent)
        qkv_a.advance(both.sent).start("x")
        down_sum.advance(both.sent).start("y")
        qkv_b.advance().start("y")
        both.advance(qkv_b.sent).start("w")
        qkv_sum = qkv_a.advance(qkv_b.sent).beside(qkv_b.advance()).start("u")
        down_sum.advance(both.sent)
        qkv_sum.advance().start("w")
        both.advance()
        qkv_sum.advance()
        grad_qkv, both, down_sum = (part.parts[0][0] for part in (qkv_sum, both, down_sum))
        grad_qkv = [grad_qkv[:, g * across : (g + 1) * across] for g in range(groups)]
        padded = tiles * FF_TILE
        grad_gate, grad_out = both[:, :hidden], both[:, padded : padded + width]
        grad_up = both[:, padded + width : padded + width + hidden]
        grad_down = down_sum[:, :hidden]
    else:
        ahead, d_top, d_den = attention.head(qkv, d_mixed, mixed_cat, inverse, seg)
        states.start(ahead, from_behind, -1)
        states.rest()
        grad_gate, grad_up, grad_down = (
            scatter_whole(kept[i], sent[i])[:, :hidden] for i in range(3)
        )
        grad_out = scatter_whole(out_kept, out_sent)
        for g in range(groups):
            only = range(g, g + 1)
            d_near = attention.near_back(qkv, d_top, d_den, seg, seg_row, earlier, only)
            d_qkv.append(attention.far_back(qkv, seg, states.came, *d_near, only))
            grad_qkv.append(
                scatter_whole(dot(turned_one[:half], d_qkv[g]), dot(turned_one[half:], d_qkv[g]))
            )
    d_a_one = None
    for g in range(groups):
        term = against(d_qkv[g], qkv_w[:, g * across : (g + 1) * across])
        d_a_one = term if d_a_one is None else d_a_one + term
    d_tokens = d_x_two + norm_backward(d_a_one, gain_one, scale_one, normed_one)
    return (
        result.reshape(rows, shard_len, width),
        d_tokens.reshape(rows, shard_len, width),
        gain_gradient(jnp.concatenate(grouped, axis=1), jnp.concatenate(grad_qkv, axis=1), gain_attn),
        jnp.concatenate([part[:, Q] for part in grad_qkv], axis=1),
        jnp.concatenate([part[:, K] for part in grad_qkv], axis=1),
        jnp.concatenate([part[:, V] for part in grad_qkv], axis=1),
        grad_out,
        gain_gradient(
            jnp.concatenate([w_gate, w_up], axis=1),
            jnp.concatenate([grad_gate, grad_up], axis=1),
            gain_mlp,
        ),
        grad_gate,
        grad_up,
        grad_down.T,
    )


def solution(mesh):
    placed = (
        P("dp", "seq", None),
        P("dp", None),
        P(("dp", "seq")),
        P(("dp", "seq"), None),
        P(("dp", "seq"), None),
        P(("dp", "seq"), None),
        P(("dp", "seq"), None),
        P(("dp", "seq")),
        P(("dp", "seq"), None),
        P(("dp", "seq"), None),
        P(None, ("dp", "seq")),
        P("dp", "seq", None),
    )
    return jax.shard_map(
        functools.partial(per_device, Slice(mesh.shape["dp"], mesh.shape["seq"])),
        mesh=mesh,
        in_specs=placed,
        out_specs=(
            P("dp", "seq", None),
            P("dp", "seq", None),
            P(("dp", "seq")),
            P(("dp", "seq"), None),
            P(("dp", "seq"), None),
            P(("dp", "seq"), None),
            P(("dp", "seq"), None),
            P(("dp", "seq")),
            P(("dp", "seq"), None),
            P(("dp", "seq"), None),
            P(None, ("dp", "seq")),
        ),
        check_vma=False,
    )
```

time: 536 us -> 483 us (0.901)
  waiting for transfers between devices: 120 us -> 70.7 us
  other arithmetic: 26.6 us -> 59.8 us
  starting transfers between devices: 95.2 us -> 75 us
  local copies, waits for them, and re-layouts: 45.4 us -> 32.1 us
  Pallas kernels: 195 us -> 188 us
    ppermute x67 -> x48, waiting for transfers between devices: 120 us -> 70.7 us  [the longest x44 67.6 us: send(): return lax.ppermute(array, self.axis, pairs)]
    ppermute x67 -> x48, starting transfers between devices: 95.2 us -> 75 us  [the longest x44 68.1 us: send(): return lax.ppermute(array, self.axis, pairs)]
    unnamed x132 -> x110, local copies, waits for them, and re-layouts: 25 us -> 12 us
    concatenate x8 -> x12, other arithmetic: 4.71 us -> 17.4 us  [along(): array = jnp.concatenate([self.array] + [a for a, _ in came], 0)]
    add x15 -> x20, other arithmetic: 4.27 us -> 16.7 us  [the longest x14 9.53 us: advance(): total = self.term_of(self.step % self.line.count) + came.astype(jnp.float32)]
    concatenate x9 -> x1, local copies, waits for them, and re-layouts: 9.83 us -> 0.91 us  [along(): array = jnp.concatenate([self.array] + [a for a, _ in came], 0)]
    pallas_call x12 -> x13, Pallas kernels: 195 us -> 188 us  [the longest x1 69 us: feed_forward(): pl.pallas_call(functools.partial(mlp_kernel, min(512, count), sums is Non...]
    slice x4 -> x10, local copies, waits for them, and re-layouts: 2.89 us -> 8.75 us  [the longest x1 3.06 us: per_device(): kept[i]]
  transfers between devices with their start and end apart: 67 -> 48, of which waited for: 26 -> 14; matrix products, arithmetic and copies ran while one was open for 18% -> 24% of each run, Pallas kernels for 22% -> 24%
where the time goes in v4:
time: 483 us; the launch traced here: 478 us
  Pallas kernels  188 us (39%)
  starting transfers between devices  75 us (16%)
  waiting for transfers between devices  70.7 us (15%)
  other arithmetic  59.8 us (12%)
  matrix products  43.3 us (9%)
  local copies, waits for them, and re-layouts  32.1 us (7%)
  between operations  8.89 us (2%)
    pallas_call x1, Pallas kernels, feed_forward(): pl.pallas_call(functools.partial(mlp_kernel, min(512, count), sums is Non...  69 us
    ppermute x44, starting transfers between devices, send(): return lax.ppermute(array, self.axis, pairs)  68.1 us
    ppermute x44, waiting for transfers between devices, send(): return lax.ppermute(array, self.axis, pairs)  67.6 us
    pallas_call x2, Pallas kernels, near_back(): self.call(kernel, groups, [at['x'], at['values'], at['narrow'], at['seg']...  34.8 us
    dot_general x13, matrix products, dot(): lax.dot_general(left, right, (dims, ((), ())), preferred_element_type=jnp...  33.9 us
    pallas_call x4, Pallas kernels, assemble(): pl.pallas_call(kernel, out_shape=[jax.ShapeDtypeStruct((shape.devices * b...  24.4 us
    concatenate x12, other arithmetic, along(): array = jnp.concatenate([self.array] + [a for a, _ in came], 0)  17.4 us
    pallas_call x2, Pallas kernels, far_back(): self.call(far_back_kernel, groups, [at['x'], at['seg'], at['state'], out[...  17 us
  transfers between devices with their start and end apart: 48, of which 14 were waited for; matrix products, arithmetic and copies ran while one was open for 24% of the time, Pallas kernels for 24%

profile of v4, /device:TPU:0, one launch (start us, length us, event | category | flops | bytes accessed | tf_op | source)
XLA Modules:
  0.0 478.1 jit_solution(10863143650384684190)
XLA Ops:
  19.6 3.7 fusion.27.gt_ref
  60.3 6.0 %assemble.4 = bf16[1024,1664]{1,0:T(8,128)(2,1)} custom-call(s32[64]{0:T(128)} %stack.856.places_ref, bf16[512,896]{1,0:T(8,128)(2,1)} %copy-done.10, bf16[512,896]{1,0:T(8,128)(2,1)} %collective-permute-done.5.refs_1_, bf16[512,768]{1,0:T(8,128)(2,1)} %copy-done.11, bf16[512,768]{1,0:T(8,128)(2,1)} %copy-done.22), custom_call_target="tpu_custom_call" | custom-call | bytes 6815744 | tf_op jit(solution)/shard_map/assemble/pallas_call | solution.py:545
  70.3 4.8 %convolution_convert_fusion.x_ref.refs_0_ = bf16[1024,1536]{1,0:T(8,128)(2,1)} fusion(bf16[1024,1024]{1,0:T(8,128)(2,1)S(1)} %fusion.3, bf16[1024,1664]{1,0:T(8,128)(2,1)S(1)} %copy-done.3), kind=kOutput, calls=%fused_computation.23 | convolution fusion | flops 3222798336 | bytes 8388608 | tf_op jit(solution)/shard_map/dot_general | solution.py:884
  75.1 8.7 %attn_tail.1 = bf16[2,2,656,128]{3,2,1,0:T(8,128)(2,1)} custom-call(bf16[1024,1536]{1,0:T(8,128)(2,1)} %convolution_convert_fusion.x_ref.refs_0_, s32[1024,1]{1,0:T(8,128)} %bitcast.267, bf16[1280,128]{1,0:T(8,128)(2,1)} %get-tuple-element.165.pick_ref), custom_call_target="tpu_custom_call" | custom-call | flops 10737418240 | bytes 2097152 | tf_op jit(solution)/shard_map/attn_tail/pallas_call | solution.py:356
  94.8 10.8 %attn_near.1 = (f32[1024,1024]{1,0:T(8,128)}, f32[1024,1024]{1,0:T(8,128)}) custom-call(bf16[1024,1536]{1,0:T(8,128)(2,1)} %convolution_convert_fusion.x_ref.refs_0_, s32[1024,1]{1,0:T(8,128)} %bitcast.268, s32[2,1,512]{2,1,0:T(1,128)} %reshape.3179.refs_2_.refs_4_), custom_call_target="tpu_custom_call" | custom-call | flops 17179869184 | bytes 2097152 | tf_op jit(solution)/shard_map/attn_near/pallas_call | solution.py:367
  109.2 21.1 %collective-permute-done.19 = bf16[256,3328]{1,0:T(8,128)(2,1)} collective-permute-done((bf16[256,3328]{1,0:T(8,128)(2,1)S(1)}, bf16[256,3328]{1,0:T(8,128)(2,1)}, u32[]{:S(2)}, u32[]{:S(2)}) %collective-permute-start.19) | collective-permute-done | bytes 1703968 | tf_op jit(solution)/shard_map/ppermute | solution.py:473
  132.6 4.1 pad_maximum_fusion.1.refs_0_
  151.6 10.9 %collective-permute-done.24 = bf16[128,2816]{1,0:T(8,128)(2,1)S(1)} collective-permute-done((bf16[128,2816]{1,0:T(8,128)(2,1)S(1)}, bf16[128,2816]{1,0:T(8,128)(2,1)S(1)}, u32[]{:S(2)}, u32[]{:S(2)}) %collective-permute-start.24) | collective-permute-done | bytes 720928 | tf_op jit(solution)/shard_map/ppermute | solution.py:473
  163.4 12.3 %attn_far.1 = (bf16[1024,1024]{1,0:T(8,128)(2,1)}, f32[1024,1024]{1,0:T(8,128)}) custom-call(bf16[1024,1536]{1,0:T(8,128)(2,1)} %convolution_convert_fusion.x_ref.refs_0_, s32[1024,1]{1,0:T(8,128)} %bitcast.269, bf16[2,2,656,128]{3,2,1,0:T(8,128)(2,1)} %broadcast_select_fusion.2.state_ref.refs_5_, f32[1024,1024]{1,0:T(8,128)} %get-tuple-element.83.top_ref, ...), custom_call_target="tpu_custom_call" | custom-call | flops 17179869184 | bytes 2097152 | tf_op jit(solution)/shard_map/attn_far/pallas_call | solution.py:374
  175.8 9.5 %assemble.6 = (bf16[1024,2816]{1,0:T(8,128)(2,1)}, bf16[1024,2816]{1,0:T(8,128)(2,1)}) custom-call(s32[64]{0:T(128)} %stack.856.places_ref, bf16[512,3328]{1,0:T(8,128)(2,1)} %pad_maximum_fusion.1.refs_0_, bf16[512,3328]{1,0:T(8,128)(2,1)} %collective-permute-done.20.refs_1_, bf16[512,3328]{1,0:T(8,128)(2,1)} %copy-done.2, ...), custom_call_target="tpu_custom_call" | custom-call | bytes 23068672 | tf_op jit(solution)/shard_map/assemble/pallas_call | solution.py:545
  185.2 3.7 assemble.5
  188.9 4.7 multiply_reduce_fusion
  195.6 3.7 fusion.24.at_ref
  199.4 5.3 %assemble.7.down_ref = bf16[1024,2816]{1,0:T(8,128)(2,1)} custom-call(s32[32]{0:T(128)} %stack.1055.places_ref, bf16[512,2816]{1,0:T(8,128)(2,1)} %constant_dynamic-update-slice_fusion.refs_0_, bf16[512,2816]{1,0:T(8,128)(2,1)} %collective-permute-done.25.refs_1_), custom_call_target="tpu_custom_call" | custom-call | bytes 11534336 | tf_op jit(solution)/shard_map/assemble/pallas_call | solution.py:545
  204.6 69.0 %mlp.1 = (bf16[1024,1024]{1,0:T(8,128)(2,1)}, bf16[1024,1024]{1,0:T(8,128)(2,1)}, f32[1024,1024]{1,0:T(8,128)}, bf16[3,512,2816]{2,1,0:T(8,128)(2,1)}, bf16[3,512,2816]{2,1,0:T(8,128)(2,1)}) custom-call(bf16[1024,1024]{1,0:T(8,128)(2,1)} %copy-done.15, bf16[1024,1024]{1,0:T(8,128)(2,1)} %bitcast.281, bf16[1024,1024]{1,0:T(8,128)(2,1)} %fusion.24.at_ref, ...), custom_call_target="tpu_custom_call" | custom-call | flops 53150220288 | bytes 55574528 | tf_op jit(solution)/shard_map/mlp/pallas_call | solution.py:794
  274.2 3.7 fusion.33
  283.3 3.7 convolution_convert_fusion.1.dy_ref
  287.0 11.2 %attn_head.1 = (bf16[2,2,656,128]{3,2,1,0:T(8,128)(2,1)}, bf16[1024,1024]{1,0:T(8,128)(2,1)}, bf16[1024,256]{1,0:T(8,128)(2,1)}) custom-call(bf16[1024,1536]{1,0:T(8,128)(2,1)} %convolution_convert_fusion.x_ref.refs_0_, bf16[1024,1024]{1,0:T(8,128)(2,1)} %convolution_convert_fusion.1.dy_ref, bf16[1024,1024]{1,0:T(8,128)(2,1)} %get-tuple-element.84.y_ref, ...), custom_call_target="tpu_custom_call" | custom-call | flops 10737418240 | bytes 2097152 | tf_op jit(solution)/shard_map/attn_head/pallas_call | solution.py:383
  316.8 6.9 %collective-permute-start.31 = (bf16[2,2,2,32,3840]{4,3,1,2,0:T(8,128)(2,1)}, bf16[2,2,2,32,3840]{4,3,1,2,0:T(8,128)(2,1)}, u32[]{:S(2)}, u32[]{:S(2)}) collective-permute-start(bf16[2,2,2,32,3840]{4,3,1,2,0:T(8,128)(2,1)} %copy.2220), channel_id=1, source_target_pairs={{0,2},{1,3},{2,0},{3,1},{4,6},{5,7},{6,4},{7,5},{8,10},{9,11},{10,... | collective-permute-start | bytes 5898248 | tf_op jit(solution)/shard_map/ppermute | solution.py:473
  326.9 17.4 %attn_near_back.2 = (bf16[1024,128]{1,0:T(8,128)(2,1)}, f32[1024,128]{1,0:T(8,128)}, f32[1024,512]{1,0:T(8,128)}) custom-call(bf16[1024,1536]{1,0:T(8,128)(2,1)} %convolution_convert_fusion.x_ref.refs_0_, bf16[1024,1024]{1,0:T(8,128)(2,1)} %get-tuple-element.103.refs_1_, bf16[1024,256]{1,0:T(8,128)(2,1)} %get-tuple-element.100.refs_2_, s32[1024,1]{1,0:T(8,128)} %bitcast.271, ...), custom_call_target="tpu_custom_call" | custom-call | flops 25769803776 | bytes 2097152 | tf_op jit(solution)/shard_map/attn_near_back/pallas_call | solution.py:396
  348.3 17.4 %attn_near_back.3 = (bf16[1024,128]{1,0:T(8,128)(2,1)}, f32[1024,128]{1,0:T(8,128)}, f32[1024,512]{1,0:T(8,128)}) custom-call(bf16[1024,1536]{1,0:T(8,128)(2,1)} %convolution_convert_fusion.x_ref.refs_0_, bf16[1024,1024]{1,0:T(8,128)(2,1)} %get-tuple-element.103.refs_1_, bf16[1024,256]{1,0:T(8,128)(2,1)} %get-tuple-element.100.refs_2_, s32[1024,1]{1,0:T(8,128)} %bitcast.272, ...), custom_call_target="tpu_custom_call" | custom-call | flops 25769803776 | bytes 2097152 | tf_op jit(solution)/shard_map/attn_near_back/pallas_call | solution.py:396
  375.5 8.3 %collective-permute-start.36 = (bf16[2,2,32,2816]{3,2,0,1:T(8,128)(2,1)}, bf16[2,2,32,2816]{3,2,0,1:T(8,128)(2,1)}, u32[]{:S(2)}, u32[]{:S(2)}) collective-permute-start(bf16[2,2,32,2816]{3,2,0,1:T(8,128)(2,1)} %fusion.52), channel_id=1, source_target_pairs={{0,2},{1,3},{2,0},{3,1},{4,6},{5,7},{6,4},{7,5},{8,10},{9,11},{10,... | collective-permute-start | bytes 2162696 | tf_op jit(solution)/shard_map/ppermute | solution.py:473
  385.9 8.6 %attn_far_back.2 = bf16[1024,768]{1,0:T(8,128)(2,1)} custom-call(bf16[1024,1536]{1,0:T(8,128)(2,1)} %convolution_convert_fusion.x_ref.refs_0_, s32[1024,1]{1,0:T(8,128)} %bitcast.273, bf16[2,2,656,128]{3,2,1,0:T(8,128)(2,1)} %broadcast_select_fusion.state_ref, bf16[1024,128]{1,0:T(8,128)(2,1)} %get-tuple-element.101.dq_ref, ...), custom_call_target="tpu_custom_call" | custom-call | flops 9663676416 | bytes 2097152 | tf_op jit(solution)/shard_map/attn_far_back/pallas_call | solution.py:409
  394.5 3.6 convolution_convert_fusion.7
  399.8 8.4 %attn_far_back.3 = bf16[1024,768]{1,0:T(8,128)(2,1)} custom-call(bf16[1024,1536]{1,0:T(8,128)(2,1)} %convolution_convert_fusion.x_ref.refs_0_, s32[1024,1]{1,0:T(8,128)} %bitcast.274, bf16[2,2,656,128]{3,2,1,0:T(8,128)(2,1)} %broadcast_select_fusion.state_ref, bf16[1024,128]{1,0:T(8,128)(2,1)} %get-tuple-element.104.dq_ref, ...), custom_call_target="tpu_custom_call" | custom-call | flops 9663676416 | bytes 2097152 | tf_op jit(solution)/shard_map/attn_far_back/pallas_call | solution.py:409
  408.2 3.9 fusion.36
  412.1 3.6 fusion.4
  429.8 4.4 collective-permute-done.46
  437.8 9.8 %collective-permute-done.39 = bf16[2,2,2,32,768]{4,3,1,2,0:T(8,128)(2,1)S(1)} collective-permute-done((bf16[2,2,2,32,768]{4,3,1,2,0:T(8,128)(2,1)S(1)}, bf16[2,2,2,32,768]{4,3,1,2,0:T(8,128)(2,1)S(1)}, u32[]{:S(2)}, u32[]{:S(2)}) %collective-permute-start.39) | collective-permute-done | bytes 393248 | tf_op jit(solution)/shard_map/ppermute | solution.py:473
  456.6 6.9 %collective-permute-done.41 = bf16[2,32,1536]{2,1,0:T(8,128)(2,1)S(1)} collective-permute-done((bf16[2,32,1536]{2,1,0:T(8,128)(2,1)S(1)}, bf16[2,32,1536]{2,1,0:T(8,128)(2,1)S(1)}, u32[]{:S(2)}, u32[]{:S(2)}) %collective-permute-start.41) | collective-permute-done | bytes 196640 | tf_op jit(solution)/shard_map/ppermute | solution.py:473
  463.7 3.5 collective-permute-start.42
  467.2 6.4 %collective-permute-done.44 = bf16[32,6656]{1,0:T(8,128)(2,1)S(1)} collective-permute-done((bf16[32,6656]{1,0:T(8,128)(2,1)S(1)}, bf16[32,6656]{1,0:T(8,128)(2,1)S(1)}, u32[]{:S(2)}, u32[]{:S(2)}) %collective-permute-start.44) | collective-permute-done | bytes 426016 | tf_op jit(solution)/shard_map/ppermute | solution.py:473
  (317 shorter events, 163.2 us)
Async XLA Ops:
  2.4 21.6 %collective-permute-start = (bf16[32,1664]{1,0:T(8,128)(2,1)S(1)}, bf16[32,1664]{1,0:T(8,128)(2,1)S(1)}, u32[]{:S(2)}, u32[]{:S(2)}) collective-permute-start(bf16[32,1664]{1,0:T(8,128)(2,1)S(1)} %pad_maximum_fusion.19), channel_id=1, source_target_pairs={{0,8},{4,12},{8,24},{12,28},{16,0},{20,4},{24,16},{28,20},{1,9},{5... | collective-permute-start | bytes 319496 | tf_op jit(solution)/shard_map/ppermute | solution.py:473
  5.5 19.8 %collective-permute-start.1 = (bf16[32,1664]{1,0:T(8,128)(2,1)S(1)}, bf16[32,1664]{1,0:T(8,128)(2,1)S(1)}, u32[]{:S(2)}, u32[]{:S(2)}) collective-permute-start(bf16[32,1664]{1,0:T(8,128)(2,1)S(1)} %pad_maximum_fusion.19), channel_id=1, source_target_pairs={{0,24},{4,28},{8,16},{12,20},{16,8},{20,12},{24,0},{28,4},{1,25},{... | collective-permute-start | bytes 319496 | tf_op jit(solution)/shard_map/ppermute | solution.py:473
  8.0 17.4 %collective-permute-start.2 = (bf16[32,1664]{1,0:T(8,128)(2,1)S(1)}, bf16[32,1664]{1,0:T(8,128)(2,1)S(1)}, u32[]{:S(2)}, u32[]{:S(2)}) collective-permute-start(bf16[32,1664]{1,0:T(8,128)(2,1)S(1)} %pad_maximum_fusion.19), channel_id=1, source_target_pairs={{0,16},{4,20},{8,0},{12,4},{16,24},{20,28},{24,8},{28,12},{1,17},{... | collective-permute-start | bytes 319496 | tf_op jit(solution)/shard_map/ppermute | solution.py:473
  13.1 38.2 %collective-permute-start.9 = (bf16[32,6656]{1,0:T(8,128)(2,1)}, bf16[32,6656]{1,0:T(8,128)(2,1)}, u32[]{:S(2)}, u32[]{:S(2)}) collective-permute-start(bf16[32,6656]{1,0:T(8,128)(2,1)} %pad_maximum_fusion.13), channel_id=1, source_target_pairs={{0,8},{4,12},{8,24},{12,28},{16,0},{20,4},{24,16},{28,20},{1,9},{5... | collective-permute-start | bytes 1277960 | tf_op jit(solution)/shard_map/ppermute | solution.py:473
  13.6 38.1 %collective-permute-start.10 = (bf16[32,6656]{1,0:T(8,128)(2,1)}, bf16[32,6656]{1,0:T(8,128)(2,1)}, u32[]{:S(2)}, u32[]{:S(2)}) collective-permute-start(bf16[32,6656]{1,0:T(8,128)(2,1)} %pad_maximum_fusion.13), channel_id=1, source_target_pairs={{0,24},{4,28},{8,16},{12,20},{16,8},{20,12},{24,0},{28,4},{1,25},{... | collective-permute-start | bytes 1277960 | tf_op jit(solution)/shard_map/ppermute | solution.py:473
  24.0 27.6 %collective-permute-start.11 = (bf16[32,6656]{1,0:T(8,128)(2,1)}, bf16[32,6656]{1,0:T(8,128)(2,1)}, u32[]{:S(2)}, u32[]{:S(2)}) collective-permute-start(bf16[32,6656]{1,0:T(8,128)(2,1)} %pad_maximum_fusion.13), channel_id=1, source_target_pairs={{0,16},{4,20},{8,0},{12,4},{16,24},{20,28},{24,8},{28,12},{1,17},{... | collective-permute-start | bytes 1277960 | tf_op jit(solution)/shard_map/ppermute | solution.py:473
  32.0 16.2 %collective-permute-start.7 = (bf16[256,768]{1,0:T(8,128)(2,1)}, bf16[256,768]{1,0:T(8,128)(2,1)}, u32[]{:S(2)}, u32[]{:S(2)}) collective-permute-start(bf16[256,768]{1,0:T(8,128)(2,1)} %pad_maximum_fusion.14), channel_id=1, source_target_pairs={{0,4},{4,0},{8,12},{12,8},{16,20},{20,16},{24,28},{28,24},{1,5},{5... | collective-permute-start | bytes 1179656 | tf_op jit(solution)/shard_map/ppermute | solution.py:473
  54.5 30.7 %collective-permute-start.16 = (bf16[64,2816]{1,0:T(8,128)(2,1)}, bf16[64,2816]{1,0:T(8,128)(2,1)}, u32[]{:S(2)}, u32[]{:S(2)}) collective-permute-start(bf16[64,2816]{1,0:T(8,128)(2,1)} %pad_maximum_fusion.15), channel_id=1, source_target_pairs={{0,2},{1,3},{2,0},{3,1},{4,6},{5,7},{6,4},{7,5},{8,10},{9,11},{10,... | collective-permute-start | bytes 1081352 | tf_op jit(solution)/shard_map/ppermute | solution.py:473
  57.8 27.4 %collective-permute-start.15 = (bf16[128,3328]{1,0:T(8,128)(2,1)}, bf16[128,3328]{1,0:T(8,128)(2,1)}, u32[]{:S(2)}, u32[]{:S(2)}) collective-permute-start(bf16[128,3328]{1,0:T(8,128)(2,1)} %get-tuple-element.150), channel_id=1, source_target_pairs={{0,2},{1,3},{2,0},{3,1},{4,6},{5,7},{6,4},{7,5},{8,10},{9,11},{10,... | collective-permute-start | bytes 2555912 | tf_op jit(solution)/shard_map/ppermute | solution.py:473
  58.9 28.8 %collective-permute-start.14 = (bf16[128,3328]{1,0:T(8,128)(2,1)S(1)}, bf16[128,3328]{1,0:T(8,128)(2,1)}, u32[]{:S(2)}, u32[]{:S(2)}) collective-permute-start(bf16[128,3328]{1,0:T(8,128)(2,1)S(1)} %get-tuple-element.151), channel_id=1, source_target_pairs={{0,4},{4,0},{8,12},{12,8},{16,20},{20,16},{24,28},{28,24},{1,5},{5... | collective-permute-start | bytes 2555912 | tf_op jit(solution)/shard_map/ppermute | solution.py:473
  83.8 21.8 %collective-permute-start.13 = (bf16[2,2,656,128]{3,2,1,0:T(8,128)(2,1)}, bf16[2,2,656,128]{3,2,1,0:T(8,128)(2,1)S(1)}, u32[]{:S(2)}, u32[]{:S(2)}) collective-permute-start(bf16[2,2,656,128]{3,2,1,0:T(8,128)(2,1)} %attn_tail.1), channel_id=1, source_target_pairs={{0,1},{1,2},{2,3},{4,5},{5,6},{6,7},{8,9},{9,10},{10,11},{12,13},{... | collective-permute-start | bytes 2015240 | tf_op jit(solution)/shard_map/ppermute | solution.py:429
  90.2 18.5 %collective-permute-start.22 = (bf16[128,2816]{1,0:T(8,128)(2,1)S(1)}, bf16[128,2816]{1,0:T(8,128)(2,1)S(1)}, u32[]{:S(2)}, u32[]{:S(2)}) collective-permute-start(bf16[128,2816]{1,0:T(8,128)(2,1)S(1)} %pad_maximum_fusion.10), channel_id=1, source_target_pairs={{0,8},{4,12},{8,24},{12,28},{16,0},{20,4},{24,16},{28,20},{1,9},{5... | collective-permute-start | bytes 2162696 | tf_op jit(solution)/shard_map/ppermute | solution.py:473
  91.6 38.7 %collective-permute-start.19 = (bf16[256,3328]{1,0:T(8,128)(2,1)S(1)}, bf16[256,3328]{1,0:T(8,128)(2,1)}, u32[]{:S(2)}, u32[]{:S(2)}) collective-permute-start(bf16[256,3328]{1,0:T(8,128)(2,1)S(1)} %pad_maximum_fusion.6), channel_id=1, source_target_pairs={{0,4},{4,0},{8,12},{12,8},{16,20},{20,16},{24,28},{28,24},{1,5},{5... | collective-permute-start | bytes 5111816 | tf_op jit(solution)/shard_map/ppermute | solution.py:473
  92.6 40.0 %collective-permute-start.18 = (bf16[256,3328]{1,0:T(8,128)(2,1)}, bf16[256,3328]{1,0:T(8,128)(2,1)}, u32[]{:S(2)}, u32[]{:S(2)}) collective-permute-start(bf16[256,3328]{1,0:T(8,128)(2,1)} %pad_maximum_fusion.5), channel_id=1, source_target_pairs={{0,2},{1,3},{2,0},{3,1},{4,6},{5,7},{6,4},{7,5},{8,10},{9,11},{10,... | collective-permute-start | bytes 5111816 | tf_op jit(solution)/shard_map/ppermute | solution.py:473
  108.7 34.5 %collective-permute-start.23 = (bf16[128,2816]{1,0:T(8,128)(2,1)S(1)}, bf16[128,2816]{1,0:T(8,128)(2,1)S(1)}, u32[]{:S(2)}, u32[]{:S(2)}) collective-permute-start(bf16[128,2816]{1,0:T(8,128)(2,1)S(1)} %collective-permute-done.22), channel_id=1, source_target_pairs={{0,8},{4,12},{8,24},{12,28},{16,0},{20,4},{24,16},{28,20},{1,9},{5... | collective-permute-start | bytes 2162696 | tf_op jit(solution)/shard_map/ppermute | solution.py:473
  136.7 39.1 %collective-permute-start.21 = (bf16[512,3328]{1,0:T(8,128)(2,1)S(1)}, bf16[512,3328]{1,0:T(8,128)(2,1)}, u32[]{:S(2)}, u32[]{:S(2)}) collective-permute-start(bf16[512,3328]{1,0:T(8,128)(2,1)S(1)} %pad_maximum_fusion.2.refs_2_), channel_id=1, source_target_pairs={{0,1},{1,0},{2,3},{3,2},{4,5},{5,4},{6,7},{7,6},{8,9},{9,8},{10,11... | collective-permute-start | bytes 10223624 | tf_op jit(solution)/shard_map/ppermute | solution.py:473
  138.3 37.5 %collective-permute-start.20 = (bf16[512,3328]{1,0:T(8,128)(2,1)}, bf16[512,3328]{1,0:T(8,128)(2,1)}, u32[]{:S(2)}, u32[]{:S(2)}) collective-permute-start(bf16[512,3328]{1,0:T(8,128)(2,1)} %pad_maximum_fusion.1.refs_0_), channel_id=1, source_target_pairs={{0,1},{1,0},{2,3},{3,2},{4,5},{5,4},{6,7},{7,6},{8,9},{9,8},{10,11... | collective-permute-start | bytes 10223624 | tf_op jit(solution)/shard_map/ppermute | solution.py:473
  143.1 19.4 %collective-permute-start.24 = (bf16[128,2816]{1,0:T(8,128)(2,1)S(1)}, bf16[128,2816]{1,0:T(8,128)(2,1)S(1)}, u32[]{:S(2)}, u32[]{:S(2)}) collective-permute-start(bf16[128,2816]{1,0:T(8,128)(2,1)S(1)} %collective-permute-done.23), channel_id=1, source_target_pairs={{0,8},{4,12},{8,24},{12,28},{16,0},{20,4},{24,16},{28,20},{1,9},{5... | collective-permute-start | bytes 2162696 | tf_op jit(solution)/shard_map/ppermute | solution.py:473
  163.4 35.9 %collective-permute-start.25 = (bf16[512,2816]{1,0:T(8,128)(2,1)}, bf16[512,2816]{1,0:T(8,128)(2,1)}, u32[]{:S(2)}, u32[]{:S(2)}) collective-permute-start(bf16[512,2816]{1,0:T(8,128)(2,1)} %constant_dynamic-update-slice_fusion.refs_0_), channel_id=1, source_target_pairs={{0,1},{1,0},{2,3},{3,2},{4,5},{5,4},{6,7},{7,6},{8,9},{9,8},{10,11... | collective-permute-start | bytes 8650760 | tf_op jit(solution)/shard_map/ppermute | solution.py:473
  273.6 31.3 %collective-permute-start.27 = (bf16[3,512,2816]{2,1,0:T(8,128)(2,1)}, bf16[3,512,2816]{2,1,0:T(8,128)(2,1)}, u32[]{:S(2)}, u32[]{:S(2)}) collective-permute-start(bf16[3,512,2816]{2,1,0:T(8,128)(2,1)} %get-tuple-element.97), channel_id=1, source_target_pairs={{0,1},{1,0},{2,3},{3,2},{4,5},{5,4},{6,7},{7,6},{8,9},{9,8},{10,11... | collective-permute-start | bytes 25952264 | tf_op jit(solution)/shard_map/ppermute | solution.py:473
  281.7 22.9 %collective-permute-start.28 = (bf16[512,1024]{1,0:T(8,128)(2,1)S(1)}, bf16[512,1024]{1,0:T(8,128)(2,1)S(1)}, u32[]{:S(2)}, u32[]{:S(2)}) collective-permute-start(bf16[512,1024]{1,0:T(8,128)(2,1)S(1)} %convolution_convert_fusion.3), channel_id=1, source_target_pairs={{0,1},{1,0},{2,3},{3,2},{4,5},{5,4},{6,7},{7,6},{8,9},{9,8},{10,11... | collective-permute-start | bytes 3145736 | tf_op jit(solution)/shard_map/ppermute | solution.py:473
  315.8 55.3 %collective-permute-start.32 = (bf16[2,2,2,32,2816]{4,3,1,2,0:T(8,128)(2,1)}, bf16[2,2,2,32,2816]{4,3,1,2,0:T(8,128)(2,1)}, u32[]{:S(2)}, u32[]{:S(2)}) collective-permute-start(bf16[2,2,2,32,2816]{4,3,1,2,0:T(8,128)(2,1)} %fusion.39), channel_id=1, source_target_pairs={{0,4},{4,0},{8,12},{12,8},{16,20},{20,16},{24,28},{28,24},{1,5},{5... | collective-permute-start | bytes 4325384 | tf_op jit(solution)/shard_map/ppermute | solution.py:473
  316.8 67.1 %collective-permute-start.31 = (bf16[2,2,2,32,3840]{4,3,1,2,0:T(8,128)(2,1)}, bf16[2,2,2,32,3840]{4,3,1,2,0:T(8,128)(2,1)}, u32[]{:S(2)}, u32[]{:S(2)}) collective-permute-start(bf16[2,2,2,32,3840]{4,3,1,2,0:T(8,128)(2,1)} %copy.2220), channel_id=1, source_target_pairs={{0,2},{1,3},{2,0},{3,1},{4,6},{5,7},{6,4},{7,5},{8,10},{9,11},{10,... | collective-permute-start | bytes 5898248 | tf_op jit(solution)/shard_map/ppermute | solution.py:473
  325.2 42.6 %collective-permute-start.30 = (bf16[2,2,2,32,2816]{4,3,0,1,2:T(8,128)(2,1)}, bf16[2,2,2,32,2816]{4,3,0,1,2:T(8,128)(2,1)}, u32[]{:S(2)}, u32[]{:S(2)}) collective-permute-start(bf16[2,2,2,32,2816]{4,3,0,1,2:T(8,128)(2,1)} %fusion.40), channel_id=1, source_target_pairs={{0,8},{4,12},{8,0},{12,4},{16,24},{20,28},{24,16},{28,20},{1,9},{5... | collective-permute-start | bytes 4325384 | tf_op jit(solution)/shard_map/ppermute | solution.py:473
  346.6 19.1 %collective-permute-start.29 = (bf16[2,2,656,128]{3,2,1,0:T(8,128)(2,1)}, bf16[2,2,656,128]{3,2,1,0:T(8,128)(2,1)}, u32[]{:S(2)}, u32[]{:S(2)}) collective-permute-start(bf16[2,2,656,128]{3,2,1,0:T(8,128)(2,1)} %select_add_fusion), channel_id=1, source_target_pairs={{1,0},{2,1},{3,2},{5,4},{6,5},{7,6},{9,8},{10,9},{11,10},{13,12},{... | collective-permute-start | bytes 2015240 | tf_op jit(solution)/shard_map/ppermute | solution.py:429
  371.1 50.8 %collective-permute-start.45 = (bf16[2,2,32,2816]{3,2,0,1:T(8,128)(2,1)}, bf16[2,2,32,2816]{3,2,0,1:T(8,128)(2,1)}, u32[]{:S(2)}, u32[]{:S(2)}) collective-permute-start(bf16[2,2,32,2816]{3,2,0,1:T(8,128)(2,1)} %fusion.51), channel_id=1, source_target_pairs={{0,16},{4,20},{8,24},{12,28},{16,0},{20,4},{24,8},{28,12},{1,17},{... | collective-permute-start | bytes 2162696 | tf_op jit(solution)/shard_map/ppermute | solution.py:473
  375.5 49.0 %collective-permute-start.36 = (bf16[2,2,32,2816]{3,2,0,1:T(8,128)(2,1)}, bf16[2,2,32,2816]{3,2,0,1:T(8,128)(2,1)}, u32[]{:S(2)}, u32[]{:S(2)}) collective-permute-start(bf16[2,2,32,2816]{3,2,0,1:T(8,128)(2,1)} %fusion.52), channel_id=1, source_target_pairs={{0,2},{1,3},{2,0},{3,1},{4,6},{5,7},{6,4},{7,5},{8,10},{9,11},{10,... | collective-permute-start | bytes 2162696 | tf_op jit(solution)/shard_map/ppermute | solution.py:473
  398.1 21.6 %collective-permute-start.33 = (bf16[512,768]{1,0:T(8,128)(2,1)}, bf16[512,768]{1,0:T(8,128)(2,1)S(1)}, u32[]{:S(2)}, u32[]{:S(2)}) collective-permute-start(bf16[512,768]{1,0:T(8,128)(2,1)} %convolution_convert_fusion.7), channel_id=1, source_target_pairs={{0,1},{1,0},{2,3},{3,2},{4,5},{5,4},{6,7},{7,6},{8,9},{9,8},{10,11... | collective-permute-start | bytes 2359304 | tf_op jit(solution)/shard_map/ppermute | solution.py:473
  398.8 28.1 %collective-permute-start.35 = (bf16[2,2,32,3840]{3,2,0,1:T(8,128)(2,1)S(1)}, bf16[2,2,32,3840]{3,2,0,1:T(8,128)(2,1)S(1)}, u32[]{:S(2)}, u32[]{:S(2)}) collective-permute-start(bf16[2,2,32,3840]{3,2,0,1:T(8,128)(2,1)S(1)} %fusion.45), channel_id=1, source_target_pairs={{0,4},{4,0},{8,12},{12,8},{16,20},{20,16},{24,28},{28,24},{1,5},{5... | collective-permute-start | bytes 2949128 | tf_op jit(solution)/shard_map/ppermute | solution.py:473
  427.3 21.6 %collective-permute-start.43 = (bf16[2,32,6656]{2,1,0:T(8,128)(2,1)S(1)}, bf16[2,32,6656]{2,1,0:T(8,128)(2,1)S(1)}, u32[]{:S(2)}, u32[]{:S(2)}) collective-permute-start(bf16[2,32,6656]{2,1,0:T(8,128)(2,1)S(1)} %pad_maximum_fusion.8), channel_id=1, source_target_pairs={{0,8},{4,12},{8,0},{12,4},{16,24},{20,28},{24,16},{28,20},{1,9},{5... | collective-permute-start | bytes 2555912 | tf_op jit(solution)/shard_map/ppermute | solution.py:473
  434.2 16.8 %collective-permute-start.47 = (bf16[32,2816]{1,0:T(8,128)(2,1)S(1)}, bf16[32,2816]{1,0:T(8,128)(2,1)S(1)}, u32[]{:S(2)}, u32[]{:S(2)}) collective-permute-start(bf16[32,2816]{1,0:T(8,128)(2,1)S(1)} %fusion.87), channel_id=1, source_target_pairs={{0,2},{1,3},{2,0},{3,1},{4,6},{5,7},{6,4},{7,5},{8,10},{9,11},{10,... | collective-permute-start | bytes 540680 | tf_op jit(solution)/shard_map/ppermute | solution.py:473
  449.1 24.5 %collective-permute-start.44 = (bf16[32,6656]{1,0:T(8,128)(2,1)S(1)}, bf16[32,6656]{1,0:T(8,128)(2,1)S(1)}, u32[]{:S(2)}, u32[]{:S(2)}) collective-permute-start(bf16[32,6656]{1,0:T(8,128)(2,1)S(1)} %fusion.76), channel_id=1, source_target_pairs={{0,16},{4,20},{8,24},{12,28},{16,0},{20,4},{24,8},{28,12},{1,17},{... | collective-permute-start | bytes 1277960 | tf_op jit(solution)/shard_map/ppermute | solution.py:473
  (64 other events, 669.0 us)

commit v5 on v4

--- a/solution.py
+++ b/solution.py
@@ -388,18 +388,18 @@
             [at["state"], at["values"], at["narrow"]], [], 5, "attn_head",
         )(x, dy, y, inverse, seg, self.scaled.T)
 
-    def near_back(self, x, dn, dd, seg, seg_row, state, groups):
+    def near_back(self, x, dn, dd, seg, seg_row, state):
         def kernel(value_dim, *refs):
             near_back_kernel(value_dim, self.block, *refs)
 
-        at, out = self.specs(groups), self.specs(groups, own=True)
+        at, groups = self.specs(self.all), self.all
         return self.call(
             kernel, groups,
             [at["x"], at["values"], at["narrow"], at["seg"], at["seg_row"], at["state"],
              at["pick"]],
             [self.shape(LANES, jnp.bfloat16, groups), self.shape(LANES, jnp.float32, groups),
              self.shape(self.wide, jnp.float32, groups)],
-            [out["narrow"], out["narrow"], out["values"]],
+            [at["narrow"], at["narrow"], at["values"]],
             [self.wide_state(self.wide + LANES), pltpu.VMEM((self.length, LANES), jnp.float32)],
             24, "attn_near_back",
         )(x, dn, dd, seg, seg_row, state, self.scaled)
@@ -408,7 +408,7 @@
         at, out = self.specs(groups), self.specs(groups, own=True)
         return self.call(
             far_back_kernel, groups,
-            [at["x"], at["seg"], at["state"], out["narrow"], out["narrow"], out["values"],
+            [at["x"], at["seg"], at["state"], at["narrow"], at["narrow"], at["values"],
              at["pick"]],
             self.shape(self.across, jnp.bfloat16, groups), out["x"],
             [self.wide_state(self.wide + LANES)], 9, "attn_far_back",
@@ -416,26 +416,29 @@
 
 
 class Passing:
-    def __init__(self, whole, steps, size):
-        self.whole, self.steps, self.size = whole, steps, size
-
-    def start(self, own, linked, shift):
-        self.own, self.linked, self.left = own, linked, self.steps
-        self.pairs = [(i, i + shift) for i in range(self.size) if 0 <= i + shift < self.size]
-        self.go(own)
-
-    def go(self, array):
-        self.sent, self.left = array, self.left - 1
-        self.came = self.pick(self.linked, lax.ppermute(array, "seq", self.pairs))
-
-    @staticmethod
-    def pick(flag, array):
-        return jnp.where(flag[:, None, None, None], array, jnp.zeros_like(array))
-
-    def rest(self, *hold):
-        while self.left:
-            came = after(self.came, *hold) if hold else self.came
-            self.go(self.own + self.pick(self.whole, came))
+    def __init__(self, segment_ids, length, reach, size):
+        self.ids, self.length, self.reach, self.size = segment_ids, length, reach, size
+        self.place = lax.axis_index("seq")
+
+    def id_at(self, device, last):
+        position = jnp.clip(device, 0, self.size - 1) * self.length + last * (self.length - 1)
+        return lax.dynamic_index_in_dim(self.ids, position, 1, keepdims=False)
+
+    def start(self, own, shift):
+        self.shift, self.came = shift, []
+        for k in range(1, self.reach + 1):
+            goals = [(i, i + shift * k) for i in range(self.size)]
+            pairs = [(i, goal) for i, goal in goals if 0 <= goal < self.size]
+            self.came.append(lax.ppermute(own, "seq", pairs))
+
+    def end(self, *hold):
+        before = self.shift > 0
+        own_id, total = self.id_at(self.place, not before), 0.0
+        for k, came in enumerate(self.came, 1):
+            linked = self.id_at(self.place - self.shift * k, before) == own_id
+            came = after(came, *hold) if hold else came
+            total = total + jnp.where(linked[:, None, None, None], came.astype(jnp.float32), 0.0)
+        return total.astype(jnp.bfloat16)
 
 
 epsilon = 1e-05
@@ -577,12 +580,36 @@
         array = jnp.concatenate([self.array] + [a for a, _ in came], 0)
         return Gathering(self.shape, array, self.names + [n for _, names in came for n in names])
 
+    def ring(self, dim):
+        return RingGathering(self, dim)
+
     def columns(self, low, high):
         return Gathering(self.shape, self.array[:, low:high], self.names)
 
     def pieces(self, dim, spans):
         found = [(self.array, self.names)] + self.came(dim)
         return [(array, names, spans) for array, names in found]
+
+
+class RingGathering:
+    def __init__(self, held, dim):
+        self.held, self.dim, self.line = held, dim, held.shape.lines[dim]
+        self.arrays = [held.array]
+        self.came = self.line.send(held.array)
+
+    def next(self, *hold):
+        if len(self.arrays) == self.line.count - 1:
+            return self.came
+        self.arrays.append(after(self.came, *hold))
+        self.came = self.line.send(self.arrays[-1])
+        return self.arrays[-1]
+
+    def end(self):
+        while len(self.arrays) < self.line.count - 1:
+            self.next()
+        self.arrays.append(self.came)
+        names = [dict(n, **{self.dim: s}) for s in range(self.line.count) for n in self.held.names]
+        return Gathering(self.held.shape, jnp.concatenate(self.arrays, 0), names)
 
 
 def spans_of(low, high, homes):
@@ -884,34 +911,31 @@
     qkv = jnp.dot(a_one, qkv_w, preferred_element_type=jnp.float32).astype(jnp.bfloat16)
     place = lax.axis_index("seq")
     own_seg = lax.dynamic_slice_in_dim(segment_ids, place * shard_len, shard_len, 1)
-    before = jnp.maximum(place * shard_len - 1, 0)
-    behind = jnp.minimum((place + 1) * shard_len, segment_ids.shape[1] - 1)
-    first, last = own_seg[:, 0], own_seg[:, -1]
-    from_before = lax.dynamic_index_in_dim(segment_ids, before, 1, keepdims=False) == first
-    from_behind = lax.dynamic_index_in_dim(segment_ids, behind, 1, keepdims=False) == last
     seg, seg_row = own_seg.reshape(count, 1), own_seg.reshape(rows, 1, shard_len)
     reach = min(shape.seq - 1, -(-(LONGEST - 1) // shard_len))
-    states = Passing(first == last, reach, shape.seq)
-    tail = attention.tail(qkv, seg)
+    states = Passing(segment_ids, shard_len, reach, shape.seq)
     if ringed:
+        down = down.along("y", False, [[qkv]])
+        tail = attention.tail(after(qkv, down.array), seg)
         rest.second(tail)
-        down = down.along("y", False, [[tail]])
-        states.start(tail, from_before, 1)
+        states.start(tail, 1)
+        ring = down.ring("z")
+        turn = ring.next(tail)
         top, den = attention.near(
-            after(qkv, states.sent, rest.one.array, rest.two.array, down.array), seg, seg_row
+            after(qkv, rest.one.array, rest.two.array, turn), seg, seg_row
         )
-        states.rest(den)
-        rest.third(den, states.sent)
+        turn = ring.next(den)
+        earlier = after(states.end(den), turn)
+        mixed_cat, inverse = attention.far(qkv, seg, earlier, top, den)
+        rest.third(mixed_cat)
         rest.last()
-        down = down.along("z", False, [[den], [rest.one.array, rest.two.array]])
+        down = ring.end()
         down_ends = down.pieces("c", [(0, tiles * FF_TILE, 0, 0)])
-        earlier = after(states.came, rest.one.array, rest.two.array)
-        mixed_cat, inverse = attention.far(qkv, seg, earlier, top, den)
         (out_w,) = rest.output(1)
     else:
-        states.start(tail, from_before, 1)
-        states.rest()
-        earlier = states.came
+        tail = attention.tail(qkv, seg)
+        states.start(tail, 1)
+        earlier = states.end()
         top, den = attention.near(qkv, seg, seg_row)
         mixed_cat, inverse = attention.far(qkv, seg, earlier, top, den)
     x_two = tokens + jnp.dot(mixed_cat, out_w, preferred_element_type=jnp.float32)
@@ -932,33 +956,29 @@
     )
     turned_mixed, turned_one = turned_rows(pick, mixed_cat), turned_rows(pick, a_one)
     half = width // 2
-    out_kept, out_sent = (
-        dot(t, d_branch).astype(jnp.bfloat16) for t in (turned_mixed[:half], turned_mixed[half:])
+    d_mixed = against(d_branch, out_w).astype(jnp.bfloat16)
+    ahead, d_top, d_den = attention.head(qkv, d_mixed, mixed_cat, inverse, seg)
+    states.start(ahead, -1)
+    own = after(d_branch, ahead) if ringed else d_branch
+    out_sent, out_kept = (
+        dot(t, own).astype(jnp.bfloat16) for t in (turned_mixed[half:], turned_mixed[:half])
     )
-    d_mixed = against(d_branch, out_w).astype(jnp.bfloat16)
     d_qkv, grad_qkv = [], []
     if ringed:
         send_core = shape.lines["c"].send
         arrived, out_arrived = send_core(sent), send_core(out_sent)
-        d_mixed = after(d_mixed, out_sent, out_kept)
-        ahead, d_top, d_den = attention.head(qkv, d_mixed, mixed_cat, inverse, seg)
-        states.start(ahead, from_behind, -1)
-        arrived = after(arrived, ahead)
+        arrived = after(arrived, out_sent, out_kept)
         gate_sum, up_sum, down_sum = (Scattering(shape, kept[i], arrived[i]) for i in range(3))
         gate_sum.beside(Scattering(shape, out_kept, out_arrived)).start("y")
         up_sum.start("x")
         down_sum.start("u")
-        d_top = after(d_top, states.sent, gate_sum.sent, up_sum.sent, down_sum.sent)
-        d_near = [None, None]
-        d_near[0] = attention.near_back(qkv, d_top, d_den, seg, seg_row, earlier, range(0, 1))
-        states.rest(d_near[0][0])
-        d_top = after(d_top, states.sent, d_near[0][0])
-        d_near[1] = attention.near_back(qkv, d_top, d_den, seg, seg_row, earlier, range(1, 2))
-        near = d_near[1][0]
-        down_sum.advance(near).start("w")
+        d_top = after(d_top, gate_sum.sent, up_sum.sent, down_sum.sent)
+        d_near = attention.near_back(qkv, d_top, d_den, seg, seg_row, earlier)
+        near = d_near[0]
         gate_sum.advance(near).start("x")
         up_sum.advance(near).start("y")
-        later = after(states.came, near, down_sum.sent, gate_sum.sent, up_sum.sent)
+        down_sum.advance(near).start("w")
+        later = after(states.end(near), down_sum.sent, gate_sum.sent, up_sum.sent)
 
         turned = [turned_one[:half], turned_one[half:]]
 
@@ -969,17 +989,18 @@
             own_sum.sent = own_sent
             return own_sum
 
-        far = attention.far_back(qkv, seg, later, *d_near[0], range(0, 1))
+        far = attention.far_back(qkv, seg, later, *d_near, range(0, 1))
         d_qkv.append(far)
         qkv_a = products(far)
         later = after(later, qkv_a.sent)
-        far = attention.far_back(qkv, seg, later, *d_near[1], range(1, 2))
+        far = attention.far_back(qkv, seg, later, *d_near, range(1, 2))
         d_qkv.append(far)
         qkv_a.start("y", far)
         qkv_b = products(after(far, qkv_a.sent))
         down_sum.advance(qkv_b.sent).start("x")
         both = gate_sum.advance(qkv_b.sent).beside(up_sum.advance(qkv_b.sent)).start("u")
         qkv_b.start("x", both.sent)
+        d_qkv = [after(array, both.sent, qkv_b.sent, down_sum.sent) for array in d_qkv]
         qkv_a.advance(both.sent).start("x")
         down_sum.advance(both.sent).start("y")
         qkv_b.advance().start("y")
@@ -996,17 +1017,15 @@
         grad_up = both[:, padded + width : padded + width + hidden]
         grad_down = down_sum[:, :hidden]
     else:
-        ahead, d_top, d_den = attention.head(qkv, d_mixed, mixed_cat, inverse, seg)
-        states.start(ahead, from_behind, -1)
-        states.rest()
+        later = states.end()
+        d_near = attention.near_back(qkv, d_top, d_den, seg, seg_row, earlier)
         grad_gate, grad_up, grad_down = (
             scatter_whole(kept[i], sent[i])[:, :hidden] for i in range(3)
         )
         grad_out = scatter_whole(out_kept, out_sent)
         for g in range(groups):
             only = range(g, g + 1)
-            d_near = attention.near_back(qkv, d_top, d_den, seg, seg_row, earlier, only)
-            d_qkv.append(attention.far_back(qkv, seg, states.came, *d_near, only))
+            d_qkv.append(attention.far_back(qkv, seg, later, *d_near, only))
             grad_qkv.append(
                 scatter_whole(dot(turned_one[:half], d_qkv[g]), dot(turned_one[half:], d_qkv[g]))
             )

time: 483 us -> 462 us (0.957)
  waiting for transfers between devices: 70.7 us -> 53.6 us
  starting transfers between devices: 75 us -> 64.2 us
  local copies, waits for them, and re-layouts: 32.1 us -> 39.9 us
    ppermute x44, waiting for transfers between devices: 67.6 us -> 53.6 us  [send(): return lax.ppermute(array, self.axis, pairs)]
    ppermute x44, starting transfers between devices: 68.1 us -> 55 us  [send(): return lax.ppermute(array, self.axis, pairs)]
    unnamed x110 -> x116, local copies, waits for them, and re-layouts: 12 us -> 18.2 us
    convert_element_type x0 -> x2, other arithmetic: none -> 5.05 us  [end(): return total.astype(jnp.bfloat16)]
    pallas_call x2 -> x1, Pallas kernels: 34.8 us -> 32.2 us  [near_back(): self.call(kernel, groups, [at['x'], at['values'], at['narrow'], at['seg']...]
  transfers between devices with their start and end apart: 48 -> 48, of which waited for: 14 -> 14; matrix products, arithmetic and copies ran while one was open for 24% -> 26% of each run, Pallas kernels for 24% -> 23%
where the time goes in v5:
time: 462 us; the launch traced here: 453 us
  Pallas kernels  186 us (40%)
  starting transfers between devices  64.2 us (14%)
  other arithmetic  57.6 us (12%)
  waiting for transfers between devices  53.6 us (12%)
  matrix products  42.4 us (9%)
  local copies, waits for them, and re-layouts  39.9 us (9%)
  between operations  8.93 us (2%)
    pallas_call x1, Pallas kernels, feed_forward(): pl.pallas_call(functools.partial(mlp_kernel, min(512, count), sums is Non...  69.3 us
    ppermute x44, starting transfers between devices, send(): return lax.ppermute(array, self.axis, pairs)  55 us
    ppermute x44, waiting for transfers between devices, send(): return lax.ppermute(array, self.axis, pairs)  53.6 us
    dot_general x13, matrix products, dot(): lax.dot_general(left, right, (dims, ((), ())), preferred_element_type=jnp...  32.9 us
    pallas_call x1, Pallas kernels, near_back(): self.call(kernel, groups, [at['x'], at['values'], at['narrow'], at['seg']...  32.2 us
    pallas_call x4, Pallas kernels, assemble(): pl.pallas_call(kernel, out_shape=[jax.ShapeDtypeStruct((shape.devices * b...  24.4 us
    unnamed x116, local copies, waits for them, and re-layouts  18.2 us
    pallas_call x2, Pallas kernels, far_back(): self.call(far_back_kernel, groups, [at['x'], at['seg'], at['state'], at['...  17.5 us
  transfers between devices with their start and end apart: 48, of which 14 were waited for; matrix products, arithmetic and copies ran while one was open for 26% of the time, Pallas kernels for 23%

profile of v5, /device:TPU:0, one launch (start us, length us, event | category | flops | bytes accessed | tf_op | source)
XLA Modules:
  0.0 453.1 jit_solution(13823238987088872971)
XLA Ops:
  55.4 6.1 %assemble.4 = bf16[1024,1664]{1,0:T(8,128)(2,1)} custom-call(s32[64]{0:T(128)} %stack.856.places_ref, bf16[512,896]{1,0:T(8,128)(2,1)} %copy-done.12, bf16[512,896]{1,0:T(8,128)(2,1)} %collective-permute-done.5.refs_1_, bf16[512,768]{1,0:T(8,128)(2,1)} %copy-done.13, bf16[512,768]{1,0:T(8,128)(2,1)} %copy-done.24), custom_call_target="tpu_custom_call" | custom-call | bytes 6815744 | tf_op jit(solution)/shard_map/assemble/pallas_call | solution.py:548
  64.9 4.8 %convolution_convert_fusion.x_ref.refs_0_ = bf16[1024,1536]{1,0:T(8,128)(2,1)} fusion(bf16[1024,1024]{1,0:T(8,128)(2,1)S(1)} %fusion.3, bf16[1024,1664]{1,0:T(8,128)(2,1)S(1)} %copy-done.2), kind=kOutput, calls=%fused_computation.23 | convolution fusion | flops 3222798336 | bytes 8388608 | tf_op jit(solution)/shard_map/dot_general | solution.py:911
  70.7 6.8 %collective-permute-start.17 = (bf16[128,2816]{1,0:T(8,128)(2,1)S(1)}, bf16[128,2816]{1,0:T(8,128)(2,1)}, u32[]{:S(2)}, u32[]{:S(2)}) collective-permute-start(bf16[128,2816]{1,0:T(8,128)(2,1)S(1)} %pad_maximum_fusion.10), channel_id=1, source_target_pairs={{0,8},{4,12},{8,24},{12,28},{16,0},{20,4},{24,16},{28,20},{1,9},{5... | collective-permute-start | bytes 2162696 | tf_op jit(solution)/shard_map/ppermute | solution.py:476
  77.5 8.7 %attn_tail.1 = bf16[2,2,656,128]{3,2,1,0:T(8,128)(2,1)} custom-call(bf16[1024,1536]{1,0:T(8,128)(2,1)} %convolution_convert_fusion.x_ref.refs_0_, s32[1024,1]{1,0:T(8,128)} %bitcast.267, bf16[1280,128]{1,0:T(8,128)(2,1)} %get-tuple-element.168.pick_ref), custom_call_target="tpu_custom_call" | custom-call | flops 10737418240 | bytes 2097152 | tf_op jit(solution)/shard_map/attn_tail/pallas_call | solution.py:356
  88.4 4.0 collective-permute-start.18
  97.8 10.9 %attn_near.1 = (f32[1024,1024]{1,0:T(8,128)}, f32[1024,1024]{1,0:T(8,128)}) custom-call(bf16[1024,1536]{1,0:T(8,128)(2,1)} %convolution_convert_fusion.x_ref.refs_0_, s32[1024,1]{1,0:T(8,128)} %bitcast.268, s32[2,1,512]{2,1,0:T(1,128)} %reshape.3189.refs_2_.refs_4_), custom_call_target="tpu_custom_call" | custom-call | flops 17179869184 | bytes 2097152 | tf_op jit(solution)/shard_map/attn_near/pallas_call | solution.py:367
  117.1 12.3 %attn_far.1 = (bf16[1024,1024]{1,0:T(8,128)(2,1)}, f32[1024,1024]{1,0:T(8,128)}) custom-call(bf16[1024,1536]{1,0:T(8,128)(2,1)} %convolution_convert_fusion.x_ref.refs_0_, s32[1024,1]{1,0:T(8,128)} %bitcast.269, bf16[2,2,656,128]{3,2,1,0:T(8,128)(2,1)} %add_convert_fusion.4.state_ref.refs_5_, f32[1024,1024]{1,0:T(8,128)} %get-tuple-element.86.top_ref, ...), custom_call_target="tpu_custom_call" | custom-call | flops 17179869184 | bytes 2097152 | tf_op jit(solution)/shard_map/attn_far/pallas_call | solution.py:374
  132.7 3.3 pad_maximum_fusion.2.refs_2_
  136.9 6.8 %collective-permute-done.20 = bf16[256,3328]{1,0:T(8,128)(2,1)} collective-permute-done((bf16[256,3328]{1,0:T(8,128)(2,1)S(1)}, bf16[256,3328]{1,0:T(8,128)(2,1)}, u32[]{:S(2)}, u32[]{:S(2)}) %collective-permute-start.20) | collective-permute-done | bytes 1703968 | tf_op jit(solution)/shard_map/ppermute | solution.py:476
  146.9 4.7 %collective-permute-start.21 = (bf16[512,3328]{1,0:T(8,128)(2,1)}, bf16[512,3328]{1,0:T(8,128)(2,1)}, u32[]{:S(2)}, u32[]{:S(2)}) collective-permute-start(bf16[512,3328]{1,0:T(8,128)(2,1)} %pad_maximum_fusion.1.refs_0_), channel_id=1, source_target_pairs={{0,1},{1,0},{2,3},{3,2},{4,5},{5,4},{6,7},{7,6},{8,9},{9,8},{10,11... | collective-permute-start | bytes 10223624 | tf_op jit(solution)/shard_map/ppermute | solution.py:476
  155.5 5.4 %fusion.27.gt_ref = bf16[1024,1024]{1,0:T(8,128)(2,1)} fusion(bf16[1024,1024]{1,0:T(8,128)(2,1)} %bitcast.280, s32[1024]{0:T(1024)S(1)} %add.15404), kind=kOutput, calls=%fused_computation.42 | convolution fusion | flops 2150629376 | bytes 4198400 | tf_op jit(solution)/shard_map/dot_general | solution.py:22
  161.8 5.2 %assemble.7.down_ref = bf16[1024,2816]{1,0:T(8,128)(2,1)} custom-call(s32[32]{0:T(128)} %stack.1055.places_ref, bf16[512,2816]{1,0:T(8,128)(2,1)} %constant_dynamic-update-slice_fusion.refs_0_, bf16[512,2816]{1,0:T(8,128)(2,1)} %collective-permute-done.25.refs_1_), custom_call_target="tpu_custom_call" | custom-call | bytes 11534336 | tf_op jit(solution)/shard_map/assemble/pallas_call | solution.py:548
  167.0 3.6 assemble.5
  170.7 4.7 %multiply_reduce_fusion = (f32[1024]{0:T(1024)S(1)}, f32[1024,1024]{1,0:T(8,128)S(1)}) fusion(bf16[1024,1024]{1,0:T(8,128)(2,1)} %get-tuple-element.87.y_ref, bf16[1024,1024]{1,0:T(8,128)(2,1)} %assemble.5, bf16[2,512,1024]{2,1,0:T(8,128)(2,1)S(1)} %copy-done), kind=kOutput, calls=%fused_computation.15 | convolution fusion | flops 2151676928 | bytes 10489856 | tf_op jit(solution)/shard_map/dot_general | solution.py:941
  178.7 3.8 fusion.24.at_ref
  182.5 9.5 %assemble.6 = (bf16[1024,2816]{1,0:T(8,128)(2,1)}, bf16[1024,2816]{1,0:T(8,128)(2,1)}) custom-call(s32[64]{0:T(128)} %stack.856.places_ref, bf16[512,3328]{1,0:T(8,128)(2,1)} %pad_maximum_fusion.1.refs_0_, bf16[512,3328]{1,0:T(8,128)(2,1)} %collective-permute-done.21.refs_1_, bf16[512,3328]{1,0:T(8,128)(2,1)} %pad_maximum_fusion.2.refs_2_, ...), custom_call_target="tpu_custom_call" | custom-call | bytes 23068672 | tf_op jit(solution)/shard_map/assemble/pallas_call | solution.py:548
  192.0 69.3 %mlp.1 = (bf16[1024,1024]{1,0:T(8,128)(2,1)}, bf16[1024,1024]{1,0:T(8,128)(2,1)}, f32[1024,1024]{1,0:T(8,128)}, bf16[3,512,2816]{2,1,0:T(8,128)(2,1)}, bf16[3,512,2816]{2,1,0:T(8,128)(2,1)}) custom-call(bf16[1024,1024]{1,0:T(8,128)(2,1)} %copy-done.17, bf16[1024,1024]{1,0:T(8,128)(2,1)} %bitcast.281, bf16[1024,1024]{1,0:T(8,128)(2,1)} %fusion.24.at_ref, ...), custom_call_target="tpu_custom_call" | custom-call | flops 53150220288 | bytes 55574528 | tf_op jit(solution)/shard_map/mlp/pallas_call | solution.py:821
  265.6 3.7 fusion.33
  271.7 3.7 convolution_convert_fusion.1.dy_ref
  275.4 11.2 %attn_head.1 = (bf16[2,2,656,128]{3,2,1,0:T(8,128)(2,1)}, bf16[1024,1024]{1,0:T(8,128)(2,1)}, bf16[1024,256]{1,0:T(8,128)(2,1)}) custom-call(bf16[1024,1536]{1,0:T(8,128)(2,1)} %convolution_convert_fusion.x_ref.refs_0_, bf16[1024,1024]{1,0:T(8,128)(2,1)} %convolution_convert_fusion.1.dy_ref, bf16[1024,1024]{1,0:T(8,128)(2,1)} %get-tuple-element.87.y_ref, ...), custom_call_target="tpu_custom_call" | custom-call | flops 10737418240 | bytes 2097152 | tf_op jit(solution)/shard_map/attn_head/pallas_call | solution.py:383
  311.0 3.9 collective-permute-start.31
  316.4 32.2 %attn_near_back.1 = (bf16[1024,256]{1,0:T(8,128)(2,1)}, f32[1024,256]{1,0:T(8,128)}, f32[1024,1024]{1,0:T(8,128)}) custom-call(bf16[1024,1536]{1,0:T(8,128)(2,1)} %convolution_convert_fusion.x_ref.refs_0_, bf16[1024,1024]{1,0:T(8,128)(2,1)} %get-tuple-element.102.refs_1_, bf16[1024,256]{1,0:T(8,128)(2,1)} %get-tuple-element.103.refs_2_, ...), custom_call_target="tpu_custom_call" | custom-call | flops 51539607552 | bytes 2097152 | tf_op jit(solution)/shard_map/attn_near_back/pallas_call | solution.py:396
  354.2 3.9 collective-permute-start.37
  364.0 8.8 %attn_far_back.2 = bf16[1024,768]{1,0:T(8,128)(2,1)} custom-call(bf16[1024,1536]{1,0:T(8,128)(2,1)} %convolution_convert_fusion.x_ref.refs_0_, s32[1024,1]{1,0:T(8,128)} %bitcast.272, bf16[2,2,656,128]{3,2,1,0:T(8,128)(2,1)} %add_convert_fusion.3.state_ref, bf16[1024,256]{1,0:T(8,128)(2,1)} %get-tuple-element.104.dq_ref, ...), custom_call_target="tpu_custom_call" | custom-call | flops 9663676416 | bytes 2097152 | tf_op jit(solution)/shard_map/attn_far_back/pallas_call | solution.py:409
  372.8 3.3 convolution_convert_fusion.7
  377.6 8.7 %attn_far_back.3 = bf16[1024,768]{1,0:T(8,128)(2,1)} custom-call(bf16[1024,1536]{1,0:T(8,128)(2,1)} %convolution_convert_fusion.x_ref.refs_0_, s32[1024,1]{1,0:T(8,128)} %bitcast.273, bf16[2,2,656,128]{3,2,1,0:T(8,128)(2,1)} %add_convert_fusion.3.state_ref, bf16[1024,256]{1,0:T(8,128)(2,1)} %get-tuple-element.104.dq_ref, ...), custom_call_target="tpu_custom_call" | custom-call | flops 9663676416 | bytes 2097152 | tf_op jit(solution)/shard_map/attn_far_back/pallas_call | solution.py:409
  395.4 5.2 %collective-permute-done.33 = bf16[2,2,32,3840]{3,2,0,1:T(8,128)(2,1)S(1)} collective-permute-done((bf16[2,2,32,3840]{3,2,0,1:T(8,128)(2,1)S(1)}, bf16[2,2,32,3840]{3,2,0,1:T(8,128)(2,1)S(1)}, u32[]{:S(2)}, u32[]{:S(2)}) %collective-permute-start.33) | collective-permute-done | bytes 983072 | tf_op jit(solution)/shard_map/ppermute | solution.py:476
  401.1 6.9 %collective-permute-done.46 = bf16[2,32,2816]{2,1,0:T(8,128)(2,1)S(1)} collective-permute-done((bf16[2,32,2816]{2,1,0:T(8,128)(2,1)S(1)}, bf16[2,32,2816]{2,1,0:T(8,128)(2,1)S(1)}, u32[]{:S(2)}, u32[]{:S(2)}) %collective-permute-start.46) | collective-permute-done | bytes 360480 | tf_op jit(solution)/shard_map/ppermute | solution.py:476
  418.6 5.5 %collective-permute-done.40 = bf16[2,2,2,32,768]{4,3,1,2,0:T(8,128)(2,1)S(1)} collective-permute-done((bf16[2,2,2,32,768]{4,3,1,2,0:T(8,128)(2,1)S(1)}, bf16[2,2,2,32,768]{4,3,1,2,0:T(8,128)(2,1)S(1)}, u32[]{:S(2)}, u32[]{:S(2)}) %collective-permute-start.40) | collective-permute-done | bytes 393248 | tf_op jit(solution)/shard_map/ppermute | solution.py:476
  426.7 3.3 collective-permute-done.41
  430.2 7.5 %collective-permute-done.42 = bf16[2,32,1536]{2,1,0:T(8,128)(2,1)S(1)} collective-permute-done((bf16[2,32,1536]{2,1,0:T(8,128)(2,1)S(1)}, bf16[2,32,1536]{2,1,0:T(8,128)(2,1)S(1)}, u32[]{:S(2)}, u32[]{:S(2)}) %collective-permute-start.42) | collective-permute-done | bytes 196640 | tf_op jit(solution)/shard_map/ppermute | solution.py:476
  441.0 6.3 %collective-permute-done.45 = bf16[32,6656]{1,0:T(8,128)(2,1)S(1)} collective-permute-done((bf16[32,6656]{1,0:T(8,128)(2,1)S(1)}, bf16[32,6656]{1,0:T(8,128)(2,1)S(1)}, u32[]{:S(2)}, u32[]{:S(2)}) %collective-permute-start.45) | collective-permute-done | bytes 426016 | tf_op jit(solution)/shard_map/ppermute | solution.py:476
  (318 shorter events, 160.0 us)
Async XLA Ops:
  2.4 17.3 %collective-permute-start = (bf16[32,1664]{1,0:T(8,128)(2,1)S(1)}, bf16[32,1664]{1,0:T(8,128)(2,1)S(1)}, u32[]{:S(2)}, u32[]{:S(2)}) collective-permute-start(bf16[32,1664]{1,0:T(8,128)(2,1)S(1)} %pad_maximum_fusion.19), channel_id=1, source_target_pairs={{0,8},{4,12},{8,24},{12,28},{16,0},{20,4},{24,16},{28,20},{1,9},{5... | collective-permute-start | bytes 319496 | tf_op jit(solution)/shard_map/ppermute | solution.py:476
  13.0 32.6 %collective-permute-start.9 = (bf16[32,6656]{1,0:T(8,128)(2,1)}, bf16[32,6656]{1,0:T(8,128)(2,1)}, u32[]{:S(2)}, u32[]{:S(2)}) collective-permute-start(bf16[32,6656]{1,0:T(8,128)(2,1)} %pad_maximum_fusion.13), channel_id=1, source_target_pairs={{0,8},{4,12},{8,24},{12,28},{16,0},{20,4},{24,16},{28,20},{1,9},{5... | collective-permute-start | bytes 1277960 | tf_op jit(solution)/shard_map/ppermute | solution.py:476
  13.5 32.5 %collective-permute-start.10 = (bf16[32,6656]{1,0:T(8,128)(2,1)}, bf16[32,6656]{1,0:T(8,128)(2,1)}, u32[]{:S(2)}, u32[]{:S(2)}) collective-permute-start(bf16[32,6656]{1,0:T(8,128)(2,1)} %pad_maximum_fusion.13), channel_id=1, source_target_pairs={{0,24},{4,28},{8,16},{12,20},{16,8},{20,12},{24,0},{28,4},{1,25},{... | collective-permute-start | bytes 1277960 | tf_op jit(solution)/shard_map/ppermute | solution.py:476
  19.7 26.3 %collective-permute-start.11 = (bf16[32,6656]{1,0:T(8,128)(2,1)}, bf16[32,6656]{1,0:T(8,128)(2,1)}, u32[]{:S(2)}, u32[]{:S(2)}) collective-permute-start(bf16[32,6656]{1,0:T(8,128)(2,1)} %pad_maximum_fusion.13), channel_id=1, source_target_pairs={{0,16},{4,20},{8,0},{12,4},{16,24},{20,28},{24,8},{28,12},{1,17},{... | collective-permute-start | bytes 1277960 | tf_op jit(solution)/shard_map/ppermute | solution.py:476
  48.8 20.8 %collective-permute-start.13 = (bf16[64,2816]{1,0:T(8,128)(2,1)}, bf16[64,2816]{1,0:T(8,128)(2,1)}, u32[]{:S(2)}, u32[]{:S(2)}) collective-permute-start(bf16[64,2816]{1,0:T(8,128)(2,1)} %pad_maximum_fusion.15), channel_id=1, source_target_pairs={{0,2},{1,3},{2,0},{3,1},{4,6},{5,7},{6,4},{7,5},{8,10},{9,11},{10,... | collective-permute-start | bytes 1081352 | tf_op jit(solution)/shard_map/ppermute | solution.py:476
  52.1 40.2 %collective-permute-start.16 = (bf16[128,3328]{1,0:T(8,128)(2,1)}, bf16[128,3328]{1,0:T(8,128)(2,1)}, u32[]{:S(2)}, u32[]{:S(2)}) collective-permute-start(bf16[128,3328]{1,0:T(8,128)(2,1)} %get-tuple-element.153), channel_id=1, source_target_pairs={{0,2},{1,3},{2,0},{3,1},{4,6},{5,7},{6,4},{7,5},{8,10},{9,11},{10,... | collective-permute-start | bytes 2555912 | tf_op jit(solution)/shard_map/ppermute | solution.py:476
  53.3 40.6 %collective-permute-start.15 = (bf16[128,3328]{1,0:T(8,128)(2,1)S(1)}, bf16[128,3328]{1,0:T(8,128)(2,1)}, u32[]{:S(2)}, u32[]{:S(2)}) collective-permute-start(bf16[128,3328]{1,0:T(8,128)(2,1)S(1)} %get-tuple-element.154), channel_id=1, source_target_pairs={{0,4},{4,0},{8,12},{12,8},{16,20},{20,16},{24,28},{28,24},{1,5},{5... | collective-permute-start | bytes 2555912 | tf_op jit(solution)/shard_map/ppermute | solution.py:476
  70.7 26.9 %collective-permute-start.17 = (bf16[128,2816]{1,0:T(8,128)(2,1)S(1)}, bf16[128,2816]{1,0:T(8,128)(2,1)}, u32[]{:S(2)}, u32[]{:S(2)}) collective-permute-start(bf16[128,2816]{1,0:T(8,128)(2,1)S(1)} %pad_maximum_fusion.10), channel_id=1, source_target_pairs={{0,8},{4,12},{8,24},{12,28},{16,0},{20,4},{24,16},{28,20},{1,9},{5... | collective-permute-start | bytes 2162696 | tf_op jit(solution)/shard_map/ppermute | solution.py:476
  86.2 22.5 %collective-permute-start.14 = (bf16[2,2,656,128]{3,2,1,0:T(8,128)(2,1)}, bf16[2,2,656,128]{3,2,1,0:T(8,128)(2,1)}, u32[]{:S(2)}, u32[]{:S(2)}) collective-permute-start(bf16[2,2,656,128]{3,2,1,0:T(8,128)(2,1)} %attn_tail.1), channel_id=1, source_target_pairs={{0,1},{1,2},{2,3},{4,5},{5,6},{6,7},{8,9},{9,10},{10,11},{12,13},{... | collective-permute-start | bytes 2015240 | tf_op jit(solution)/shard_map/ppermute | solution.py:432
  88.4 20.3 %collective-permute-start.18 = (bf16[2,2,656,128]{3,2,1,0:T(8,128)(2,1)}, bf16[2,2,656,128]{3,2,1,0:T(8,128)(2,1)}, u32[]{:S(2)}, u32[]{:S(2)}) collective-permute-start(bf16[2,2,656,128]{3,2,1,0:T(8,128)(2,1)} %attn_tail.1), channel_id=1, source_target_pairs={{0,2},{1,3},{4,6},{5,7},{8,10},{9,11},{12,14},{13,15},{16,18},{17,... | collective-permute-start | bytes 2015240 | tf_op jit(solution)/shard_map/ppermute | solution.py:432
  93.9 38.8 %collective-permute-start.22 = (bf16[256,3328]{1,0:T(8,128)(2,1)S(1)}, bf16[256,3328]{1,0:T(8,128)(2,1)}, u32[]{:S(2)}, u32[]{:S(2)}) collective-permute-start(bf16[256,3328]{1,0:T(8,128)(2,1)S(1)} %pad_maximum_fusion.6), channel_id=1, source_target_pairs={{0,4},{4,0},{8,12},{12,8},{16,20},{20,16},{24,28},{28,24},{1,5},{5... | collective-permute-start | bytes 5111816 | tf_op jit(solution)/shard_map/ppermute | solution.py:476
  95.8 48.0 %collective-permute-start.20 = (bf16[256,3328]{1,0:T(8,128)(2,1)S(1)}, bf16[256,3328]{1,0:T(8,128)(2,1)}, u32[]{:S(2)}, u32[]{:S(2)}) collective-permute-start(bf16[256,3328]{1,0:T(8,128)(2,1)S(1)} %pad_maximum_fusion.5), channel_id=1, source_target_pairs={{0,2},{1,3},{2,0},{3,1},{4,6},{5,7},{6,4},{7,5},{8,10},{9,11},{10,... | collective-permute-start | bytes 5111816 | tf_op jit(solution)/shard_map/ppermute | solution.py:476
  97.6 18.5 %collective-permute-start.19 = (bf16[128,2816]{1,0:T(8,128)(2,1)}, bf16[128,2816]{1,0:T(8,128)(2,1)S(1)}, u32[]{:S(2)}, u32[]{:S(2)}) collective-permute-start(bf16[128,2816]{1,0:T(8,128)(2,1)} %collective-permute-done.17), channel_id=1, source_target_pairs={{0,8},{4,12},{8,24},{12,28},{16,0},{20,4},{24,16},{28,20},{1,9},{5... | collective-permute-start | bytes 2162696 | tf_op jit(solution)/shard_map/ppermute | solution.py:476
  116.1 36.5 %collective-permute-start.24 = (bf16[128,2816]{1,0:T(8,128)(2,1)S(1)}, bf16[128,2816]{1,0:T(8,128)(2,1)}, u32[]{:S(2)}, u32[]{:S(2)}) collective-permute-start(bf16[128,2816]{1,0:T(8,128)(2,1)S(1)} %collective-permute-done.19), channel_id=1, source_target_pairs={{0,8},{4,12},{8,24},{12,28},{16,0},{20,4},{24,16},{28,20},{1,9},{5... | collective-permute-start | bytes 2162696 | tf_op jit(solution)/shard_map/ppermute | solution.py:476
  136.0 31.0 %collective-permute-start.23 = (bf16[512,3328]{1,0:T(8,128)(2,1)}, bf16[512,3328]{1,0:T(8,128)(2,1)}, u32[]{:S(2)}, u32[]{:S(2)}) collective-permute-start(bf16[512,3328]{1,0:T(8,128)(2,1)} %pad_maximum_fusion.2.refs_2_), channel_id=1, source_target_pairs={{0,1},{1,0},{2,3},{3,2},{4,5},{5,4},{6,7},{7,6},{8,9},{9,8},{10,11... | collective-permute-start | bytes 10223624 | tf_op jit(solution)/shard_map/ppermute | solution.py:476
  146.9 20.1 %collective-permute-start.21 = (bf16[512,3328]{1,0:T(8,128)(2,1)}, bf16[512,3328]{1,0:T(8,128)(2,1)}, u32[]{:S(2)}, u32[]{:S(2)}) collective-permute-start(bf16[512,3328]{1,0:T(8,128)(2,1)} %pad_maximum_fusion.1.refs_0_), channel_id=1, source_target_pairs={{0,1},{1,0},{2,3},{3,2},{4,5},{5,4},{6,7},{7,6},{8,9},{9,8},{10,11... | collective-permute-start | bytes 10223624 | tf_op jit(solution)/shard_map/ppermute | solution.py:476
  261.3 38.3 %collective-permute-start.27 = (bf16[3,512,2816]{2,1,0:T(8,128)(2,1)}, bf16[3,512,2816]{2,1,0:T(8,128)(2,1)}, u32[]{:S(2)}, u32[]{:S(2)}) collective-permute-start(bf16[3,512,2816]{2,1,0:T(8,128)(2,1)} %get-tuple-element.99), channel_id=1, source_target_pairs={{0,1},{1,0},{2,3},{3,2},{4,5},{5,4},{6,7},{7,6},{8,9},{9,8},{10,11... | collective-permute-start | bytes 25952264 | tf_op jit(solution)/shard_map/ppermute | solution.py:476
  286.6 62.1 %collective-permute-start.26 = (bf16[2,2,656,128]{3,2,1,0:T(8,128)(2,1)}, bf16[2,2,656,128]{3,2,1,0:T(8,128)(2,1)}, u32[]{:S(2)}, u32[]{:S(2)}) collective-permute-start(bf16[2,2,656,128]{3,2,1,0:T(8,128)(2,1)} %get-tuple-element.96), channel_id=1, source_target_pairs={{1,0},{2,1},{3,2},{5,4},{6,5},{7,6},{9,8},{10,9},{11,10},{13,12},{... | collective-permute-start | bytes 2015240 | tf_op jit(solution)/shard_map/ppermute | solution.py:432
  287.9 60.8 %collective-permute-start.29 = (bf16[2,2,656,128]{3,2,1,0:T(8,128)(2,1)}, bf16[2,2,656,128]{3,2,1,0:T(8,128)(2,1)}, u32[]{:S(2)}, u32[]{:S(2)}) collective-permute-start(bf16[2,2,656,128]{3,2,1,0:T(8,128)(2,1)} %get-tuple-element.96), channel_id=1, source_target_pairs={{2,0},{3,1},{6,4},{7,5},{10,8},{11,9},{14,12},{15,13},{18,16},{19,... | collective-permute-start | bytes 2015240 | tf_op jit(solution)/shard_map/ppermute | solution.py:432
  310.5 43.7 %collective-permute-start.32 = (bf16[2,2,2,32,2816]{4,3,1,2,0:T(8,128)(2,1)}, bf16[2,2,2,32,2816]{4,3,1,2,0:T(8,128)(2,1)}, u32[]{:S(2)}, u32[]{:S(2)}) collective-permute-start(bf16[2,2,2,32,2816]{4,3,1,2,0:T(8,128)(2,1)} %fusion.39), channel_id=1, source_target_pairs={{0,4},{4,0},{8,12},{12,8},{16,20},{20,16},{24,28},{28,24},{1,5},{5... | collective-permute-start | bytes 4325384 | tf_op jit(solution)/shard_map/ppermute | solution.py:476
  311.0 50.0 %collective-permute-start.31 = (bf16[2,2,2,32,3840]{4,3,1,2,0:T(8,128)(2,1)}, bf16[2,2,2,32,3840]{4,3,1,2,0:T(8,128)(2,1)}, u32[]{:S(2)}, u32[]{:S(2)}) collective-permute-start(bf16[2,2,2,32,3840]{4,3,1,2,0:T(8,128)(2,1)} %copy.2218), channel_id=1, source_target_pairs={{0,2},{1,3},{2,0},{3,1},{4,6},{5,7},{6,4},{7,5},{8,10},{9,11},{10,... | collective-permute-start | bytes 5898248 | tf_op jit(solution)/shard_map/ppermute | solution.py:476
  316.4 34.9 %collective-permute-start.30 = (bf16[2,2,2,32,2816]{4,3,0,1,2:T(8,128)(2,1)}, bf16[2,2,2,32,2816]{4,3,0,1,2:T(8,128)(2,1)}, u32[]{:S(2)}, u32[]{:S(2)}) collective-permute-start(bf16[2,2,2,32,2816]{4,3,0,1,2:T(8,128)(2,1)} %fusion.40), channel_id=1, source_target_pairs={{0,8},{4,12},{8,0},{12,4},{16,24},{20,28},{24,16},{28,20},{1,9},{5... | collective-permute-start | bytes 4325384 | tf_op jit(solution)/shard_map/ppermute | solution.py:476
  354.2 36.8 %collective-permute-start.37 = (bf16[2,2,32,2816]{3,2,0,1:T(8,128)(2,1)}, bf16[2,2,32,2816]{3,2,0,1:T(8,128)(2,1)}, u32[]{:S(2)}, u32[]{:S(2)}) collective-permute-start(bf16[2,2,32,2816]{3,2,0,1:T(8,128)(2,1)} %fusion.51), channel_id=1, source_target_pairs={{0,16},{4,20},{8,24},{12,28},{16,0},{20,4},{24,8},{28,12},{1,17},{... | collective-permute-start | bytes 2162696 | tf_op jit(solution)/shard_map/ppermute | solution.py:476
  360.9 32.1 %collective-permute-start.35 = (bf16[2,2,32,2816]{3,2,0,1:T(8,128)(2,1)}, bf16[2,2,32,2816]{3,2,0,1:T(8,128)(2,1)}, u32[]{:S(2)}, u32[]{:S(2)}) collective-permute-start(bf16[2,2,32,2816]{3,2,0,1:T(8,128)(2,1)} %fusion.52), channel_id=1, source_target_pairs={{0,2},{1,3},{2,0},{3,1},{4,6},{5,7},{6,4},{7,5},{8,10},{9,11},{10,... | collective-permute-start | bytes 2162696 | tf_op jit(solution)/shard_map/ppermute | solution.py:476
  376.1 24.6 %collective-permute-start.33 = (bf16[2,2,32,3840]{3,2,0,1:T(8,128)(2,1)S(1)}, bf16[2,2,32,3840]{3,2,0,1:T(8,128)(2,1)S(1)}, u32[]{:S(2)}, u32[]{:S(2)}) collective-permute-start(bf16[2,2,32,3840]{3,2,0,1:T(8,128)(2,1)S(1)} %fusion.45), channel_id=1, source_target_pairs={{0,4},{4,0},{8,12},{12,8},{16,20},{20,16},{24,28},{28,24},{1,5},{5... | collective-permute-start | bytes 2949128 | tf_op jit(solution)/shard_map/ppermute | solution.py:476
  388.9 20.3 %collective-permute-start.38 = (bf16[2,2,2,32,768]{4,3,1,2,0:T(8,128)(2,1)S(1)}, bf16[2,2,2,32,768]{4,3,1,2,0:T(8,128)(2,1)S(1)}, u32[]{:S(2)}, u32[]{:S(2)}) collective-permute-start(bf16[2,2,2,32,768]{4,3,1,2,0:T(8,128)(2,1)S(1)} %fusion.77), channel_id=1, source_target_pairs={{0,2},{1,3},{2,0},{3,1},{4,6},{5,7},{6,4},{7,5},{8,10},{9,11},{10,... | collective-permute-start | bytes 1179656 | tf_op jit(solution)/shard_map/ppermute | solution.py:476
  390.9 20.0 %collective-permute-start.36 = (bf16[512,768]{1,0:T(8,128)(2,1)S(1)}, bf16[512,768]{1,0:T(8,128)(2,1)S(1)}, u32[]{:S(2)}, u32[]{:S(2)}) collective-permute-start(bf16[512,768]{1,0:T(8,128)(2,1)S(1)} %convolution_convert_fusion.5), channel_id=1, source_target_pairs={{0,1},{1,0},{2,3},{3,2},{4,5},{5,4},{6,7},{7,6},{8,9},{9,8},{10,11... | collective-permute-start | bytes 2359304 | tf_op jit(solution)/shard_map/ppermute | solution.py:476
  392.5 15.5 %collective-permute-start.46 = (bf16[2,32,2816]{2,1,0:T(8,128)(2,1)S(1)}, bf16[2,32,2816]{2,1,0:T(8,128)(2,1)S(1)}, u32[]{:S(2)}, u32[]{:S(2)}) collective-permute-start(bf16[2,32,2816]{2,1,0:T(8,128)(2,1)S(1)} %fusion.82), channel_id=1, source_target_pairs={{0,4},{4,0},{8,12},{12,8},{16,20},{20,16},{24,28},{28,24},{1,5},{5... | collective-permute-start | bytes 1081352 | tf_op jit(solution)/shard_map/ppermute | solution.py:476
  401.0 24.4 %collective-permute-start.44 = (bf16[2,32,6656]{2,1,0:T(8,128)(2,1)S(1)}, bf16[2,32,6656]{2,1,0:T(8,128)(2,1)S(1)}, u32[]{:S(2)}, u32[]{:S(2)}) collective-permute-start(bf16[2,32,6656]{2,1,0:T(8,128)(2,1)S(1)} %pad_maximum_fusion.8), channel_id=1, source_target_pairs={{0,8},{4,12},{8,0},{12,4},{16,24},{20,28},{24,16},{28,20},{1,9},{5... | collective-permute-start | bytes 2555912 | tf_op jit(solution)/shard_map/ppermute | solution.py:476
  408.1 17.7 %collective-permute-start.47 = (bf16[32,2816]{1,0:T(8,128)(2,1)S(1)}, bf16[32,2816]{1,0:T(8,128)(2,1)S(1)}, u32[]{:S(2)}, u32[]{:S(2)}) collective-permute-start(bf16[32,2816]{1,0:T(8,128)(2,1)S(1)} %fusion.87), channel_id=1, source_target_pairs={{0,2},{1,3},{2,0},{3,1},{4,6},{5,7},{6,4},{7,5},{8,10},{9,11},{10,... | collective-permute-start | bytes 540680 | tf_op jit(solution)/shard_map/ppermute | solution.py:476
  409.4 16.5 %collective-permute-start.39 = (bf16[2,2,32,768]{3,2,0,1:T(8,128)(2,1)S(1)}, bf16[2,2,32,768]{3,2,0,1:T(8,128)(2,1)S(1)}, u32[]{:S(2)}, u32[]{:S(2)}) collective-permute-start(bf16[2,2,32,768]{3,2,0,1:T(8,128)(2,1)S(1)} %fusion.84), channel_id=1, source_target_pairs={{0,4},{4,0},{8,12},{12,8},{16,20},{20,16},{24,28},{28,24},{1,5},{5... | collective-permute-start | bytes 589832 | tf_op jit(solution)/shard_map/ppermute | solution.py:476
  425.6 21.7 %collective-permute-start.45 = (bf16[32,6656]{1,0:T(8,128)(2,1)S(1)}, bf16[32,6656]{1,0:T(8,128)(2,1)S(1)}, u32[]{:S(2)}, u32[]{:S(2)}) collective-permute-start(bf16[32,6656]{1,0:T(8,128)(2,1)S(1)} %fusion.76), channel_id=1, source_target_pairs={{0,16},{4,20},{8,24},{12,28},{16,0},{20,4},{24,8},{28,12},{1,17},{... | collective-permute-start | bytes 1277960 | tf_op jit(solution)/shard_map/ppermute | solution.py:476
  (67 other events, 918.6 us)

commit v6 on v5

--- a/solution.py
+++ b/solution.py
@@ -306,11 +306,9 @@
         self.scaled, self.plain = rolls(True), rolls(False)
         self.all = range(self.groups)
 
-    def specs(self, groups, own=False):
-        first = 0 if own else groups[0]
-
+    def specs(self, groups):
         def rows_of(columns):
-            return pl.BlockSpec((self.length, columns), lambda r, g: (r, first + g))
+            return pl.BlockSpec((self.length, columns), lambda r, g: (r, g))
 
         return dict(
             x=rows_of(self.across),
@@ -318,7 +316,7 @@
             narrow=rows_of(LANES),
             seg=pl.BlockSpec((self.length, 1), lambda r, g: (r, 0)),
             seg_row=pl.BlockSpec((1, 1, self.length), lambda r, g: (r, 0, 0)),
-            state=pl.BlockSpec((1, 1, PACKED, LANES), lambda r, g: (r, first + g, 0, 0)),
+            state=pl.BlockSpec((1, 1, PACKED, LANES), lambda r, g: (r, g, 0, 0)),
             pick=pl.BlockSpec((LANES, WIDE), lambda r, g: (0, 0)),
             turned_pick=pl.BlockSpec((WIDE, LANES), lambda r, g: (0, 0)),
         )
@@ -404,13 +402,13 @@
             24, "attn_near_back",
         )(x, dn, dd, seg, seg_row, state, self.scaled)
 
-    def far_back(self, x, seg, state, dq, dk, dv, groups):
-        at, out = self.specs(groups), self.specs(groups, own=True)
+    def far_back(self, x, seg, state, dq, dk, dv):
+        at, groups = self.specs(self.all), self.all
         return self.call(
             far_back_kernel, groups,
             [at["x"], at["seg"], at["state"], at["narrow"], at["narrow"], at["values"],
              at["pick"]],
-            self.shape(self.across, jnp.bfloat16, groups), out["x"],
+            self.shape(self.across, jnp.bfloat16, groups), at["x"],
             [self.wide_state(self.wide + LANES)], 9, "attn_far_back",
         )(x, seg, state, dq, dk, dv, self.plain)
 
@@ -710,7 +708,9 @@
         return self
 
     def advance(self, *hold):
-        came = after(self.came, *hold) if hold else self.came
+        flat = [t for terms in self.parts for t in terms]
+        came, *flat = lax.optimization_barrier((self.came, *flat, *hold))[: len(flat) + 1]
+        self.parts = [[flat.pop(0) for _ in terms] for terms in self.parts]
         self.step += 1
         total = self.term_of(self.step % self.line.count) + came.astype(jnp.float32)
         if self.step < self.line.count:
@@ -941,20 +941,22 @@
     x_two = tokens + jnp.dot(mixed_cat, out_w, preferred_element_type=jnp.float32)
     scale_two, normed_two = norm_forward(x_two)
     a_two = (normed_two * gain_two).astype(jnp.bfloat16)
+    a_turned = turned_rows(pick, a_two)
+    turned_mixed, turned_one = turned_rows(pick, mixed_cat), turned_rows(pick, a_one)
     if ringed:
         gate_w, up_w = rest.output(0, 2)
+        a_turned = after(a_turned, turned_mixed, turned_one)
         (down_w,) = assemble(down_ends, [tiles * FF_TILE], down_part.shape[0], shape)
     result, d_branch, d_x_two, kept, sent = feed_forward(
         a_two,
         cotangent,
-        turned_rows(pick, a_two),
+        a_turned,
         turned_rows(pick, cotangent),
         [(gate_w, 0), (up_w, 0), (down_w, 0)],
         tiles,
         None,
         (x_two, gain_two),
     )
-    turned_mixed, turned_one = turned_rows(pick, mixed_cat), turned_rows(pick, a_one)
     half = width // 2
     d_mixed = against(d_branch, out_w).astype(jnp.bfloat16)
     ahead, d_top, d_den = attention.head(qkv, d_mixed, mixed_cat, inverse, seg)
@@ -963,7 +965,6 @@
     out_sent, out_kept = (
         dot(t, own).astype(jnp.bfloat16) for t in (turned_mixed[half:], turned_mixed[:half])
     )
-    d_qkv, grad_qkv = [], []
     if ringed:
         send_core = shape.lines["c"].send
         arrived, out_arrived = send_core(sent), send_core(out_sent)
@@ -980,31 +981,25 @@
         down_sum.advance(near).start("w")
         later = after(states.end(near), down_sum.sent, gate_sum.sent, up_sum.sent)
 
-        turned = [turned_one[:half], turned_one[half:]]
-
-        def products(right):
-            own_sent = dot(turned[1], right).astype(jnp.bfloat16)
-            own_kept = dot(turned[0], right).astype(jnp.bfloat16)
-            own_sum = Scattering(shape, own_kept, send_core(own_sent))
-            own_sum.sent = own_sent
-            return own_sum
-
-        far = attention.far_back(qkv, seg, later, *d_near, range(0, 1))
-        d_qkv.append(far)
-        qkv_a = products(far)
-        later = after(later, qkv_a.sent)
-        far = attention.far_back(qkv, seg, later, *d_near, range(1, 2))
-        d_qkv.append(far)
-        qkv_a.start("y", far)
-        qkv_b = products(after(far, qkv_a.sent))
-        down_sum.advance(qkv_b.sent).start("x")
-        both = gate_sum.advance(qkv_b.sent).beside(up_sum.advance(qkv_b.sent)).start("u")
-        qkv_b.start("x", both.sent)
-        d_qkv = [after(array, both.sent, qkv_b.sent, down_sum.sent) for array in d_qkv]
+        d_qkv = attention.far_back(qkv, seg, later, *d_near)
+        both = gate_sum.advance(d_qkv).beside(up_sum.advance(d_qkv)).start("u")
+        right = after(d_qkv, both.sent)
+        own_sent = dot(turned_one[half:], right).astype(jnp.bfloat16)
+        own_kept = dot(turned_one[:half], right).astype(jnp.bfloat16)
+        arrived = after(send_core(own_sent), own_kept)
+        down_sum.advance(own_kept).start("x")
+        arrived = after(arrived, down_sum.sent)
+        qkv_a, qkv_b = (
+            Scattering(shape, own_kept[:, low : low + across], arrived[:, low : low + across])
+            for low in (0, across)
+        )
+        qkv_a.start("y")
+        qkv_b.start("x")
+        d_qkv = after(d_qkv, qkv_a.sent, qkv_b.sent)
+        both.advance(qkv_a.sent, qkv_b.sent).start("w")
+        qkv_b.advance(both.sent).start("y")
         qkv_a.advance(both.sent).start("x")
-        down_sum.advance(both.sent).start("y")
-        qkv_b.advance().start("y")
-        both.advance(qkv_b.sent).start("w")
+        down_sum.advance(qkv_a.sent).start("y")
         qkv_sum = qkv_a.advance(qkv_b.sent).beside(qkv_b.advance()).start("u")
         down_sum.advance(both.sent)
         qkv_sum.advance().start("w")
@@ -1023,16 +1018,10 @@
             scatter_whole(kept[i], sent[i])[:, :hidden] for i in range(3)
         )
         grad_out = scatter_whole(out_kept, out_sent)
-        for g in range(groups):
-            only = range(g, g + 1)
-            d_qkv.append(attention.far_back(qkv, seg, later, *d_near, only))
-            grad_qkv.append(
-                scatter_whole(dot(turned_one[:half], d_qkv[g]), dot(turned_one[half:], d_qkv[g]))
-            )
-    d_a_one = None
-    for g in range(groups):
-        term = against(d_qkv[g], qkv_w[:, g * across : (g + 1) * across])
-        d_a_one = term if d_a_one is None else d_a_one + term
+        d_qkv = attention.far_back(qkv, seg, later, *d_near)
+        whole = scatter_whole(dot(turned_one[:half], d_qkv), dot(turned_one[half:], d_qkv))
+        grad_qkv = [whole[:, g * across : (g + 1) * across] for g in range(groups)]
+    d_a_one = against(d_qkv, qkv_w)
     d_tokens = d_x_two + norm_backward(d_a_one, gain_one, scale_one, normed_one)
     return (
         result.reshape(rows, shard_len, width),

time: 462 us -> 460 us (level)
  waiting for transfers between devices: 53.6 us -> 61.1 us
    ppermute x44 -> x43, waiting for transfers between devices: 53.6 us -> 61.1 us  [send(): return lax.ppermute(array, self.axis, pairs)]
    pallas_call x2 -> x1, Pallas kernels: 17.5 us -> 14.1 us  [far_back(): self.call(far_back_kernel, groups, [at['x'], at['seg'], at['state'], at['...]
    unnamed x116 -> x132, local copies, waits for them, and re-layouts: 18.2 us -> 15.8 us
    ppermute x44 -> x43, starting transfers between devices: 55 us -> 52.8 us  [send(): return lax.ppermute(array, self.axis, pairs)]
    dot_general x13 -> x10, matrix products: 32.9 us -> 31.9 us  [dot(): lax.dot_general(left, right, (dims, ((), ())), preferred_element_type=jnp...]
  transfers between devices with their start and end apart: 48 -> 47, of which waited for: 14 -> 14; matrix products, arithmetic and copies ran while one was open for 26% -> 25% of each run, Pallas kernels for 23% -> 22%
where the time goes in v6:
time: 460 us; the launch traced here: 452 us
  Pallas kernels  183 us (40%)
  starting transfers between devices  61.6 us (13%)
  waiting for transfers between devices  61.1 us (13%)
  other arithmetic  55.2 us (12%)
  matrix products  41.4 us (9%)
  local copies, waits for them, and re-layouts  40.1 us (9%)
  between operations  8.91 us (2%)
    pallas_call x1, Pallas kernels, feed_forward(): pl.pallas_call(functools.partial(mlp_kernel, min(512, count), sums is Non...  68.8 us
    ppermute x43, waiting for transfers between devices, send(): return lax.ppermute(array, self.axis, pairs)  61.1 us
    ppermute x43, starting transfers between devices, send(): return lax.ppermute(array, self.axis, pairs)  52.8 us
    pallas_call x1, Pallas kernels, near_back(): self.call(kernel, groups, [at['x'], at['values'], at['narrow'], at['seg']...  32.4 us
    dot_general x10, matrix products, dot(): lax.dot_general(left, right, (dims, ((), ())), preferred_element_type=jnp...  31.9 us
    pallas_call x4, Pallas kernels, assemble(): pl.pallas_call(kernel, out_shape=[jax.ShapeDtypeStruct((shape.devices * b...  24.4 us
    unnamed x132, local copies, waits for them, and re-layouts  15.8 us
    concatenate x12, other arithmetic, along(): array = jnp.concatenate([self.array] + [a for a, _ in came], 0)  15.2 us
  transfers between devices with their start and end apart: 47, of which 14 were waited for; matrix products, arithmetic and copies ran while one was open for 25% of the time, Pallas kernels for 22%

profile of v6, /device:TPU:0, one launch (start us, length us, event | category | flops | bytes accessed | tf_op | source)
XLA Modules:
  0.0 451.5 jit_solution(7495800049605777454)
XLA Ops:
  55.6 6.0 %assemble.4 = bf16[1024,1664]{1,0:T(8,128)(2,1)} custom-call(s32[64]{0:T(128)} %stack.856.places_ref, bf16[512,896]{1,0:T(8,128)(2,1)} %copy-done.16, bf16[512,896]{1,0:T(8,128)(2,1)} %collective-permute-done.5.refs_1_, bf16[512,768]{1,0:T(8,128)(2,1)} %copy-done.17, bf16[512,768]{1,0:T(8,128)(2,1)} %copy-done.32), custom_call_target="tpu_custom_call" | custom-call | bytes 6815744 | tf_op jit(solution)/shard_map/assemble/pallas_call | solution.py:546
  64.3 4.8 %convolution_convert_fusion.x_ref.refs_0_ = bf16[1024,1536]{1,0:T(8,128)(2,1)} fusion(bf16[1024,1024]{1,0:T(8,128)(2,1)S(1)} %fusion.3, bf16[1024,1664]{1,0:T(8,128)(2,1)S(1)} %copy-done.12), kind=kOutput, calls=%fused_computation.21 | convolution fusion | flops 3222798336 | bytes 8388608 | tf_op jit(solution)/shard_map/dot_general | solution.py:911
  70.1 6.8 %collective-permute-start.17 = (bf16[128,2816]{1,0:T(8,128)(2,1)S(1)}, bf16[128,2816]{1,0:T(8,128)(2,1)S(1)}, u32[]{:S(2)}, u32[]{:S(2)}) collective-permute-start(bf16[128,2816]{1,0:T(8,128)(2,1)S(1)} %pad_maximum_fusion.9), channel_id=1, source_target_pairs={{0,8},{4,12},{8,24},{12,28},{16,0},{20,4},{24,16},{28,20},{1,9},{5... | collective-permute-start | bytes 2162696 | tf_op jit(solution)/shard_map/ppermute | solution.py:474
  76.9 8.7 %attn_tail.1 = bf16[2,2,656,128]{3,2,1,0:T(8,128)(2,1)} custom-call(bf16[1024,1536]{1,0:T(8,128)(2,1)} %convolution_convert_fusion.x_ref.refs_0_, s32[1024,1]{1,0:T(8,128)} %bitcast.258, bf16[1280,128]{1,0:T(8,128)(2,1)} %get-tuple-element.216.pick_ref), custom_call_target="tpu_custom_call" | custom-call | flops 10737418240 | bytes 2097152 | tf_op jit(solution)/shard_map/attn_tail/pallas_call | solution.py:354
  87.7 4.1 collective-permute-start.18
  97.5 10.9 %attn_near.1 = (f32[1024,1024]{1,0:T(8,128)}, f32[1024,1024]{1,0:T(8,128)}) custom-call(bf16[1024,1536]{1,0:T(8,128)(2,1)} %convolution_convert_fusion.x_ref.refs_0_, s32[1024,1]{1,0:T(8,128)} %bitcast.259, s32[2,1,512]{2,1,0:T(1,128)} %reshape.3189.refs_2_.refs_4_), custom_call_target="tpu_custom_call" | custom-call | flops 17179869184 | bytes 2097152 | tf_op jit(solution)/shard_map/attn_near/pallas_call | solution.py:365
  111.7 4.0 collective-permute-done.19
  116.2 12.3 %attn_far.1 = (bf16[1024,1024]{1,0:T(8,128)(2,1)}, f32[1024,1024]{1,0:T(8,128)}) custom-call(bf16[1024,1536]{1,0:T(8,128)(2,1)} %convolution_convert_fusion.x_ref.refs_0_, s32[1024,1]{1,0:T(8,128)} %bitcast.260, bf16[2,2,656,128]{3,2,1,0:T(8,128)(2,1)} %add_convert_fusion.4.state_ref.refs_5_, f32[1024,1024]{1,0:T(8,128)} %get-tuple-element.113.top_ref, ...), custom_call_target="tpu_custom_call" | custom-call | flops 17179869184 | bytes 2097152 | tf_op jit(solution)/shard_map/attn_far/pallas_call | solution.py:372
  135.4 7.8 %collective-permute-done.20 = bf16[256,3328]{1,0:T(8,128)(2,1)} collective-permute-done((bf16[256,3328]{1,0:T(8,128)(2,1)S(1)}, bf16[256,3328]{1,0:T(8,128)(2,1)}, u32[]{:S(2)}, u32[]{:S(2)}) %collective-permute-start.20) | collective-permute-done | bytes 1703968 | tf_op jit(solution)/shard_map/ppermute | solution.py:474
  146.3 4.7 %collective-permute-start.21 = (bf16[512,3328]{1,0:T(8,128)(2,1)}, bf16[512,3328]{1,0:T(8,128)(2,1)}, u32[]{:S(2)}, u32[]{:S(2)}) collective-permute-start(bf16[512,3328]{1,0:T(8,128)(2,1)} %pad_maximum_fusion.refs_0_), channel_id=1, source_target_pairs={{0,1},{1,0},{2,3},{3,2},{4,5},{5,4},{6,7},{7,6},{8,9},{9,8},{10,11... | collective-permute-start | bytes 10223624 | tf_op jit(solution)/shard_map/ppermute | solution.py:474
  156.0 5.5 %fusion.34.gt_ref = bf16[1024,1024]{1,0:T(8,128)(2,1)} fusion(bf16[1024,1024]{1,0:T(8,128)(2,1)} %bitcast.270, s32[1024]{0:T(1024)S(1)} %add.15401), kind=kOutput, calls=%fused_computation.45 | convolution fusion | flops 2150629376 | bytes 4198400 | tf_op jit(solution)/shard_map/dot_general | solution.py:22
  161.5 3.8 fusion.31
  165.2 3.7 fusion.28
  169.0 5.2 %assemble.7.down_ref = bf16[1024,2816]{1,0:T(8,128)(2,1)} custom-call(s32[32]{0:T(128)} %stack.1055.places_ref, bf16[512,2816]{1,0:T(8,128)(2,1)} %constant_dynamic-update-slice_fusion.refs_0_, bf16[512,2816]{1,0:T(8,128)(2,1)} %collective-permute-done.25.refs_1_), custom_call_target="tpu_custom_call" | custom-call | bytes 11534336 | tf_op jit(solution)/shard_map/assemble/pallas_call | solution.py:546
  174.2 3.8 assemble.5
  178.0 4.7 %multiply_reduce_fusion = (f32[1024]{0:T(1024)S(1)}, f32[1024,1024]{1,0:T(8,128)S(1)}) fusion(bf16[1024,1024]{1,0:T(8,128)(2,1)} %get-tuple-element.114.y_ref, bf16[1024,1024]{1,0:T(8,128)(2,1)} %assemble.5, bf16[2,512,1024]{2,1,0:T(8,128)(2,1)S(1)} %copy-done.2), kind=kOutput, calls=%fused_computation.14 | convolution fusion | flops 2151676928 | bytes 10489856 | tf_op jit(solution)/shard_map/dot_general | solution.py:941
  186.1 3.9 fusion.25.at_ref
  190.0 9.4 %assemble.6 = (bf16[1024,2816]{1,0:T(8,128)(2,1)}, bf16[1024,2816]{1,0:T(8,128)(2,1)}) custom-call(s32[64]{0:T(128)} %stack.856.places_ref, bf16[512,3328]{1,0:T(8,128)(2,1)} %pad_maximum_fusion.refs_0_, bf16[512,3328]{1,0:T(8,128)(2,1)} %collective-permute-done.21.refs_1_, bf16[512,3328]{1,0:T(8,128)(2,1)} %copy-done, ...), custom_call_target="tpu_custom_call" | custom-call | bytes 23068672 | tf_op jit(solution)/shard_map/assemble/pallas_call | solution.py:546
  199.5 68.8 %mlp.1 = (bf16[1024,1024]{1,0:T(8,128)(2,1)}, bf16[1024,1024]{1,0:T(8,128)(2,1)}, f32[1024,1024]{1,0:T(8,128)}, bf16[3,512,2816]{2,1,0:T(8,128)(2,1)}, bf16[3,512,2816]{2,1,0:T(8,128)(2,1)}) custom-call(bf16[1024,1024]{1,0:T(8,128)(2,1)} %copy-done.21, bf16[1024,1024]{1,0:T(8,128)(2,1)} %bitcast.271, bf16[1024,1024]{1,0:T(8,128)(2,1)} %fusion.25.at_ref, ...), custom_call_target="tpu_custom_call" | custom-call | flops 53150220288 | bytes 55574528 | tf_op jit(solution)/shard_map/mlp/pallas_call | solution.py:821
  269.6 5.3 %convolution_convert_fusion.3.dy_ref = bf16[1024,1024]{1,0:T(8,128)(2,1)} fusion(bf16[1024,1024]{1,0:T(8,128)(2,1)} %get-tuple-element.128, bf16[1024,1024]{1,0:T(8,128)(2,1)S(1)} %copy-done.18), kind=kOutput, calls=%fused_computation.46 | convolution fusion | flops 2148532224 | bytes 6291456 | tf_op jit(solution)/shard_map/dot_general | solution.py:22
  274.9 11.5 %attn_head.1 = (bf16[2,2,656,128]{3,2,1,0:T(8,128)(2,1)}, bf16[1024,1024]{1,0:T(8,128)(2,1)}, bf16[1024,256]{1,0:T(8,128)(2,1)}) custom-call(bf16[1024,1536]{1,0:T(8,128)(2,1)} %convolution_convert_fusion.x_ref.refs_0_, bf16[1024,1024]{1,0:T(8,128)(2,1)} %convolution_convert_fusion.3.dy_ref, bf16[1024,1024]{1,0:T(8,128)(2,1)} %get-tuple-element.114.y_ref, ...), custom_call_target="tpu_custom_call" | custom-call | flops 10737418240 | bytes 2097152 | tf_op jit(solution)/shard_map/attn_head/pallas_call | solution.py:381
  291.7 5.0 %fusion.86 = (bf16[1,512,2816]{2,1,0:T(8,128)(2,1)}, bf16[1,512,2816]{2,1,0:T(8,128)(2,1)S(1)}, bf16[1,512,2816]{2,1,0:T(8,128)(2,1)S(1)}) fusion(bf16[3,512,2816]{2,1,0:T(8,128)(2,1)} %get-tuple-element.126), kind=kLoop, calls=%fused_computation.215 | loop fusion | bytes 17301504 | tf_op jit(solution)/shard_map/slice | solution.py:972
  297.7 5.0 %fusion.85 = (bf16[1,512,2816]{2,1,0:T(8,128)(2,1)}, bf16[1,512,2816]{2,1,0:T(8,128)(2,1)S(1)}, bf16[1,512,2816]{2,1,0:T(8,128)(2,1)S(1)}) fusion(bf16[3,512,2816]{2,1,0:T(8,128)(2,1)} %collective-permute-done.27), kind=kLoop, calls=%fused_computation.214 | loop fusion | bytes 17301504 | tf_op jit(solution)/shard_map/slice | solution.py:972
  302.7 4.2 add_convert_fusion.2
  315.8 32.4 %attn_near_back.1 = (bf16[1024,256]{1,0:T(8,128)(2,1)}, f32[1024,256]{1,0:T(8,128)}, f32[1024,1024]{1,0:T(8,128)}) custom-call(bf16[1024,1536]{1,0:T(8,128)(2,1)} %convolution_convert_fusion.x_ref.refs_0_, bf16[1024,1024]{1,0:T(8,128)(2,1)} %get-tuple-element.130.refs_1_, bf16[1024,256]{1,0:T(8,128)(2,1)} %get-tuple-element.131.refs_2_, ...), custom_call_target="tpu_custom_call" | custom-call | flops 51539607552 | bytes 2097152 | tf_op jit(solution)/shard_map/attn_near_back/pallas_call | solution.py:394
  355.5 3.9 collective-permute-start.36
  365.8 14.1 %attn_far_back.1 = bf16[1024,1536]{1,0:T(8,128)(2,1)} custom-call(bf16[1024,1536]{1,0:T(8,128)(2,1)} %convolution_convert_fusion.x_ref.refs_0_, s32[1024,1]{1,0:T(8,128)} %bitcast.263, bf16[2,2,656,128]{3,2,1,0:T(8,128)(2,1)} %add_convert_fusion.3.state_ref, bf16[1024,256]{1,0:T(8,128)(2,1)} %get-tuple-element.132.dq_ref, ...), custom_call_target="tpu_custom_call" | custom-call | flops 19327352832 | bytes 2097152 | tf_op jit(solution)/shard_map/attn_far_back/pallas_call | solution.py:407
  381.6 6.0 %collective-permute-done.33 = bf16[2,2,32,3840]{3,2,0,1:T(8,128)(2,1)S(1)} collective-permute-done((bf16[2,2,32,3840]{3,2,0,1:T(8,128)(2,1)}, bf16[2,2,32,3840]{3,2,0,1:T(8,128)(2,1)S(1)}, u32[]{:S(2)}, u32[]{:S(2)}) %collective-permute-start.33) | collective-permute-done | bytes 983072 | tf_op jit(solution)/shard_map/ppermute | solution.py:474
  397.2 12.2 %collective-permute-done.38 = bf16[2,32,6656]{2,1,0:T(8,128)(2,1)S(1)} collective-permute-done((bf16[2,32,6656]{2,1,0:T(8,128)(2,1)S(1)}, bf16[2,32,6656]{2,1,0:T(8,128)(2,1)S(1)}, u32[]{:S(2)}, u32[]{:S(2)}) %collective-permute-start.38) | collective-permute-done | bytes 852000 | tf_op jit(solution)/shard_map/ppermute | solution.py:474
  424.8 8.0 %collective-permute-done.44 = bf16[32,6656]{1,0:T(8,128)(2,1)S(1)} collective-permute-done((bf16[32,6656]{1,0:T(8,128)(2,1)S(1)}, bf16[32,6656]{1,0:T(8,128)(2,1)S(1)}, u32[]{:S(2)}, u32[]{:S(2)}) %collective-permute-start.44) | collective-permute-done | bytes 426016 | tf_op jit(solution)/shard_map/ppermute | solution.py:474
  434.9 6.8 %collective-permute-done.42 = bf16[2,32,1536]{2,1,0:T(8,128)(2,1)S(1)} collective-permute-done((bf16[2,32,1536]{2,1,0:T(8,128)(2,1)S(1)}, bf16[2,32,1536]{2,1,0:T(8,128)(2,1)S(1)}, u32[]{:S(2)}, u32[]{:S(2)}) %collective-permute-start.42) | collective-permute-done | bytes 196640 | tf_op jit(solution)/shard_map/ppermute | solution.py:474
  443.1 5.7 %collective-permute-done.43 = bf16[32,1536]{1,0:T(8,128)(2,1)S(1)} collective-permute-done((bf16[32,1536]{1,0:T(8,128)(2,1)S(1)}, bf16[32,1536]{1,0:T(8,128)(2,1)S(1)}, u32[]{:S(2)}, u32[]{:S(2)}) %collective-permute-start.43) | collective-permute-done | bytes 98336 | tf_op jit(solution)/shard_map/ppermute | solution.py:474
  (329 shorter events, 143.7 us)
Async XLA Ops:
  2.5 17.3 %collective-permute-start = (bf16[32,1664]{1,0:T(8,128)(2,1)S(1)}, bf16[32,1664]{1,0:T(8,128)(2,1)S(1)}, u32[]{:S(2)}, u32[]{:S(2)}) collective-permute-start(bf16[32,1664]{1,0:T(8,128)(2,1)S(1)} %pad_maximum_fusion.18), channel_id=1, source_target_pairs={{0,8},{4,12},{8,24},{12,28},{16,0},{20,4},{24,16},{28,20},{1,9},{5... | collective-permute-start | bytes 319496 | tf_op jit(solution)/shard_map/ppermute | solution.py:474
  5.6 15.4 %collective-permute-start.1 = (bf16[32,1664]{1,0:T(8,128)(2,1)S(1)}, bf16[32,1664]{1,0:T(8,128)(2,1)S(1)}, u32[]{:S(2)}, u32[]{:S(2)}) collective-permute-start(bf16[32,1664]{1,0:T(8,128)(2,1)S(1)} %pad_maximum_fusion.18), channel_id=1, source_target_pairs={{0,24},{4,28},{8,16},{12,20},{16,8},{20,12},{24,0},{28,4},{1,25},{... | collective-permute-start | bytes 319496 | tf_op jit(solution)/shard_map/ppermute | solution.py:474
  13.1 32.6 %collective-permute-start.9 = (bf16[32,6656]{1,0:T(8,128)(2,1)}, bf16[32,6656]{1,0:T(8,128)(2,1)}, u32[]{:S(2)}, u32[]{:S(2)}) collective-permute-start(bf16[32,6656]{1,0:T(8,128)(2,1)} %pad_maximum_fusion.12), channel_id=1, source_target_pairs={{0,8},{4,12},{8,24},{12,28},{16,0},{20,4},{24,16},{28,20},{1,9},{5... | collective-permute-start | bytes 1277960 | tf_op jit(solution)/shard_map/ppermute | solution.py:474
  13.6 32.5 %collective-permute-start.10 = (bf16[32,6656]{1,0:T(8,128)(2,1)}, bf16[32,6656]{1,0:T(8,128)(2,1)}, u32[]{:S(2)}, u32[]{:S(2)}) collective-permute-start(bf16[32,6656]{1,0:T(8,128)(2,1)} %pad_maximum_fusion.12), channel_id=1, source_target_pairs={{0,24},{4,28},{8,16},{12,20},{16,8},{20,12},{24,0},{28,4},{1,25},{... | collective-permute-start | bytes 1277960 | tf_op jit(solution)/shard_map/ppermute | solution.py:474
  19.8 26.3 %collective-permute-start.11 = (bf16[32,6656]{1,0:T(8,128)(2,1)}, bf16[32,6656]{1,0:T(8,128)(2,1)}, u32[]{:S(2)}, u32[]{:S(2)}) collective-permute-start(bf16[32,6656]{1,0:T(8,128)(2,1)} %pad_maximum_fusion.12), channel_id=1, source_target_pairs={{0,16},{4,20},{8,0},{12,4},{16,24},{20,28},{24,8},{28,12},{1,17},{... | collective-permute-start | bytes 1277960 | tf_op jit(solution)/shard_map/ppermute | solution.py:474
  27.6 15.1 %collective-permute-start.7 = (bf16[256,768]{1,0:T(8,128)(2,1)}, bf16[256,768]{1,0:T(8,128)(2,1)}, u32[]{:S(2)}, u32[]{:S(2)}) collective-permute-start(bf16[256,768]{1,0:T(8,128)(2,1)} %pad_maximum_fusion.13), channel_id=1, source_target_pairs={{0,4},{4,0},{8,12},{12,8},{16,20},{20,16},{24,28},{28,24},{1,5},{5... | collective-permute-start | bytes 1179656 | tf_op jit(solution)/shard_map/ppermute | solution.py:474
  30.2 14.1 %collective-permute-start.4 = (bf16[256,896]{1,0:T(8,128)(2,1)}, bf16[256,896]{1,0:T(8,128)(2,1)}, u32[]{:S(2)}, u32[]{:S(2)}) collective-permute-start(bf16[256,896]{1,0:T(8,128)(2,1)} %pad_maximum_fusion.10), channel_id=1, source_target_pairs={{0,2},{1,3},{2,0},{3,1},{4,6},{5,7},{6,4},{7,5},{8,10},{9,11},{10,... | collective-permute-start | bytes 1376264 | tf_op jit(solution)/shard_map/ppermute | solution.py:474
  48.9 20.2 %collective-permute-start.13 = (bf16[64,2816]{1,0:T(8,128)(2,1)}, bf16[64,2816]{1,0:T(8,128)(2,1)}, u32[]{:S(2)}, u32[]{:S(2)}) collective-permute-start(bf16[64,2816]{1,0:T(8,128)(2,1)} %pad_maximum_fusion.14), channel_id=1, source_target_pairs={{0,2},{1,3},{2,0},{3,1},{4,6},{5,7},{6,4},{7,5},{8,10},{9,11},{10,... | collective-permute-start | bytes 1081352 | tf_op jit(solution)/shard_map/ppermute | solution.py:474
  52.2 39.6 %collective-permute-start.16 = (bf16[128,3328]{1,0:T(8,128)(2,1)}, bf16[128,3328]{1,0:T(8,128)(2,1)}, u32[]{:S(2)}, u32[]{:S(2)}) collective-permute-start(bf16[128,3328]{1,0:T(8,128)(2,1)} %get-tuple-element.197), channel_id=1, source_target_pairs={{0,2},{1,3},{2,0},{3,1},{4,6},{5,7},{6,4},{7,5},{8,10},{9,11},{10,... | collective-permute-start | bytes 2555912 | tf_op jit(solution)/shard_map/ppermute | solution.py:474
  53.4 39.9 %collective-permute-start.15 = (bf16[128,3328]{1,0:T(8,128)(2,1)S(1)}, bf16[128,3328]{1,0:T(8,128)(2,1)}, u32[]{:S(2)}, u32[]{:S(2)}) collective-permute-start(bf16[128,3328]{1,0:T(8,128)(2,1)S(1)} %get-tuple-element.198), channel_id=1, source_target_pairs={{0,4},{4,0},{8,12},{12,8},{16,20},{20,16},{24,28},{28,24},{1,5},{5... | collective-permute-start | bytes 2555912 | tf_op jit(solution)/shard_map/ppermute | solution.py:474
  70.1 26.9 %collective-permute-start.17 = (bf16[128,2816]{1,0:T(8,128)(2,1)S(1)}, bf16[128,2816]{1,0:T(8,128)(2,1)S(1)}, u32[]{:S(2)}, u32[]{:S(2)}) collective-permute-start(bf16[128,2816]{1,0:T(8,128)(2,1)S(1)} %pad_maximum_fusion.9), channel_id=1, source_target_pairs={{0,8},{4,12},{8,24},{12,28},{16,0},{20,4},{24,16},{28,20},{1,9},{5... | collective-permute-start | bytes 2162696 | tf_op jit(solution)/shard_map/ppermute | solution.py:474
  85.6 22.8 %collective-permute-start.14 = (bf16[2,2,656,128]{3,2,1,0:T(8,128)(2,1)}, bf16[2,2,656,128]{3,2,1,0:T(8,128)(2,1)}, u32[]{:S(2)}, u32[]{:S(2)}) collective-permute-start(bf16[2,2,656,128]{3,2,1,0:T(8,128)(2,1)} %attn_tail.1), channel_id=1, source_target_pairs={{0,1},{1,2},{2,3},{4,5},{5,6},{6,7},{8,9},{9,10},{10,11},{12,13},{... | collective-permute-start | bytes 2015240 | tf_op jit(solution)/shard_map/ppermute | solution.py:430
  87.7 20.6 %collective-permute-start.18 = (bf16[2,2,656,128]{3,2,1,0:T(8,128)(2,1)}, bf16[2,2,656,128]{3,2,1,0:T(8,128)(2,1)}, u32[]{:S(2)}, u32[]{:S(2)}) collective-permute-start(bf16[2,2,656,128]{3,2,1,0:T(8,128)(2,1)} %attn_tail.1), channel_id=1, source_target_pairs={{0,2},{1,3},{4,6},{5,7},{8,10},{9,11},{12,14},{13,15},{16,18},{17,... | collective-permute-start | bytes 2015240 | tf_op jit(solution)/shard_map/ppermute | solution.py:430
  93.3 38.7 %collective-permute-start.22 = (bf16[256,3328]{1,0:T(8,128)(2,1)S(1)}, bf16[256,3328]{1,0:T(8,128)(2,1)S(1)}, u32[]{:S(2)}, u32[]{:S(2)}) collective-permute-start(bf16[256,3328]{1,0:T(8,128)(2,1)S(1)} %pad_maximum_fusion.5), channel_id=1, source_target_pairs={{0,4},{4,0},{8,12},{12,8},{16,20},{20,16},{24,28},{28,24},{1,5},{5... | collective-permute-start | bytes 5111816 | tf_op jit(solution)/shard_map/ppermute | solution.py:474
  95.2 48.0 %collective-permute-start.20 = (bf16[256,3328]{1,0:T(8,128)(2,1)S(1)}, bf16[256,3328]{1,0:T(8,128)(2,1)}, u32[]{:S(2)}, u32[]{:S(2)}) collective-permute-start(bf16[256,3328]{1,0:T(8,128)(2,1)S(1)} %pad_maximum_fusion.4), channel_id=1, source_target_pairs={{0,2},{1,3},{2,0},{3,1},{4,6},{5,7},{6,4},{7,5},{8,10},{9,11},{10,... | collective-permute-start | bytes 5111816 | tf_op jit(solution)/shard_map/ppermute | solution.py:474
  97.0 18.7 %collective-permute-start.19 = (bf16[128,2816]{1,0:T(8,128)(2,1)S(1)}, bf16[128,2816]{1,0:T(8,128)(2,1)}, u32[]{:S(2)}, u32[]{:S(2)}) collective-permute-start(bf16[128,2816]{1,0:T(8,128)(2,1)S(1)} %collective-permute-done.17), channel_id=1, source_target_pairs={{0,8},{4,12},{8,24},{12,28},{16,0},{20,4},{24,16},{28,20},{1,9},{5... | collective-permute-start | bytes 2162696 | tf_op jit(solution)/shard_map/ppermute | solution.py:474
  115.7 37.4 %collective-permute-start.24 = (bf16[128,2816]{1,0:T(8,128)(2,1)}, bf16[128,2816]{1,0:T(8,128)(2,1)}, u32[]{:S(2)}, u32[]{:S(2)}) collective-permute-start(bf16[128,2816]{1,0:T(8,128)(2,1)} %collective-permute-done.19), channel_id=1, source_target_pairs={{0,8},{4,12},{8,24},{12,28},{16,0},{20,4},{24,16},{28,20},{1,9},{5... | collective-permute-start | bytes 2162696 | tf_op jit(solution)/shard_map/ppermute | solution.py:474
  135.3 38.9 %collective-permute-start.23 = (bf16[512,3328]{1,0:T(8,128)(2,1)S(1)}, bf16[512,3328]{1,0:T(8,128)(2,1)}, u32[]{:S(2)}, u32[]{:S(2)}) collective-permute-start(bf16[512,3328]{1,0:T(8,128)(2,1)S(1)} %pad_maximum_fusion.1.refs_2_), channel_id=1, source_target_pairs={{0,1},{1,0},{2,3},{3,2},{4,5},{5,4},{6,7},{7,6},{8,9},{9,8},{10,11... | collective-permute-start | bytes 10223624 | tf_op jit(solution)/shard_map/ppermute | solution.py:474
  146.3 27.9 %collective-permute-start.21 = (bf16[512,3328]{1,0:T(8,128)(2,1)}, bf16[512,3328]{1,0:T(8,128)(2,1)}, u32[]{:S(2)}, u32[]{:S(2)}) collective-permute-start(bf16[512,3328]{1,0:T(8,128)(2,1)} %pad_maximum_fusion.refs_0_), channel_id=1, source_target_pairs={{0,1},{1,0},{2,3},{3,2},{4,5},{5,4},{6,7},{7,6},{8,9},{9,8},{10,11... | collective-permute-start | bytes 10223624 | tf_op jit(solution)/shard_map/ppermute | solution.py:474
  268.3 29.4 %collective-permute-start.27 = (bf16[3,512,2816]{2,1,0:T(8,128)(2,1)}, bf16[3,512,2816]{2,1,0:T(8,128)(2,1)}, u32[]{:S(2)}, u32[]{:S(2)}) collective-permute-start(bf16[3,512,2816]{2,1,0:T(8,128)(2,1)} %get-tuple-element.127), channel_id=1, source_target_pairs={{0,1},{1,0},{2,3},{3,2},{4,5},{5,4},{6,7},{7,6},{8,9},{9,8},{10,11... | collective-permute-start | bytes 25952264 | tf_op jit(solution)/shard_map/ppermute | solution.py:474
  289.1 59.2 %collective-permute-start.26 = (bf16[2,2,656,128]{3,2,1,0:T(8,128)(2,1)}, bf16[2,2,656,128]{3,2,1,0:T(8,128)(2,1)S(1)}, u32[]{:S(2)}, u32[]{:S(2)}) collective-permute-start(bf16[2,2,656,128]{3,2,1,0:T(8,128)(2,1)} %get-tuple-element.124), channel_id=1, source_target_pairs={{1,0},{2,1},{3,2},{5,4},{6,5},{7,6},{9,8},{10,9},{11,10},{13,12},{... | collective-permute-start | bytes 2015240 | tf_op jit(solution)/shard_map/ppermute | solution.py:430
  290.4 57.9 %collective-permute-start.29 = (bf16[2,2,656,128]{3,2,1,0:T(8,128)(2,1)}, bf16[2,2,656,128]{3,2,1,0:T(8,128)(2,1)}, u32[]{:S(2)}, u32[]{:S(2)}) collective-permute-start(bf16[2,2,656,128]{3,2,1,0:T(8,128)(2,1)} %get-tuple-element.124), channel_id=1, source_target_pairs={{2,0},{3,1},{6,4},{7,5},{10,8},{11,9},{14,12},{15,13},{18,16},{19,... | collective-permute-start | bytes 2015240 | tf_op jit(solution)/shard_map/ppermute | solution.py:430
  310.0 40.6 %collective-permute-start.32 = (bf16[2,2,2,32,2816]{4,3,1,2,0:T(8,128)(2,1)}, bf16[2,2,2,32,2816]{4,3,1,2,0:T(8,128)(2,1)}, u32[]{:S(2)}, u32[]{:S(2)}) collective-permute-start(bf16[2,2,2,32,2816]{4,3,1,2,0:T(8,128)(2,1)} %fusion.37), channel_id=1, source_target_pairs={{0,4},{4,0},{8,12},{12,8},{16,20},{20,16},{24,28},{28,24},{1,5},{5... | collective-permute-start | bytes 4325384 | tf_op jit(solution)/shard_map/ppermute | solution.py:474
  310.6 49.1 %collective-permute-start.31 = (bf16[2,2,2,32,3840]{4,3,1,2,0:T(8,128)(2,1)}, bf16[2,2,2,32,3840]{4,3,1,2,0:T(8,128)(2,1)}, u32[]{:S(2)}, u32[]{:S(2)}) collective-permute-start(bf16[2,2,2,32,3840]{4,3,1,2,0:T(8,128)(2,1)} %copy.2219), channel_id=1, source_target_pairs={{0,2},{1,3},{2,0},{3,1},{4,6},{5,7},{6,4},{7,5},{8,10},{9,11},{10,... | collective-permute-start | bytes 5898248 | tf_op jit(solution)/shard_map/ppermute | solution.py:474
  315.8 38.3 %collective-permute-start.30 = (bf16[2,2,2,32,2816]{4,3,0,1,2:T(8,128)(2,1)}, bf16[2,2,2,32,2816]{4,3,0,1,2:T(8,128)(2,1)S(1)}, u32[]{:S(2)}, u32[]{:S(2)}) collective-permute-start(bf16[2,2,2,32,2816]{4,3,0,1,2:T(8,128)(2,1)} %fusion.38), channel_id=1, source_target_pairs={{0,8},{4,12},{8,0},{12,4},{16,24},{20,28},{24,16},{28,20},{1,9},{5... | collective-permute-start | bytes 4325384 | tf_op jit(solution)/shard_map/ppermute | solution.py:474
  354.1 25.7 %collective-permute-start.34 = (bf16[2,2,32,2816]{3,2,0,1:T(8,128)(2,1)}, bf16[2,2,32,2816]{3,2,0,1:T(8,128)(2,1)}, u32[]{:S(2)}, u32[]{:S(2)}) collective-permute-start(bf16[2,2,32,2816]{3,2,0,1:T(8,128)(2,1)} %fusion.45), channel_id=1, source_target_pairs={{0,2},{1,3},{2,0},{3,1},{4,6},{5,7},{6,4},{7,5},{8,10},{9,11},{10,... | collective-permute-start | bytes 2162696 | tf_op jit(solution)/shard_map/ppermute | solution.py:474
  355.5 36.4 %collective-permute-start.36 = (bf16[2,2,32,2816]{3,2,0,1:T(8,128)(2,1)}, bf16[2,2,32,2816]{3,2,0,1:T(8,128)(2,1)}, u32[]{:S(2)}, u32[]{:S(2)}) collective-permute-start(bf16[2,2,32,2816]{3,2,0,1:T(8,128)(2,1)} %fusion.44), channel_id=1, source_target_pairs={{0,16},{4,20},{8,24},{12,28},{16,0},{20,4},{24,8},{28,12},{1,17},{... | collective-permute-start | bytes 2162696 | tf_op jit(solution)/shard_map/ppermute | solution.py:474
  364.5 23.2 %collective-permute-start.33 = (bf16[2,2,32,3840]{3,2,0,1:T(8,128)(2,1)}, bf16[2,2,32,3840]{3,2,0,1:T(8,128)(2,1)S(1)}, u32[]{:S(2)}, u32[]{:S(2)}) collective-permute-start(bf16[2,2,32,3840]{3,2,0,1:T(8,128)(2,1)} %fusion.43), channel_id=1, source_target_pairs={{0,4},{4,0},{8,12},{12,8},{16,20},{20,16},{24,28},{28,24},{1,5},{5... | collective-permute-start | bytes 2949128 | tf_op jit(solution)/shard_map/ppermute | solution.py:474
  387.9 21.6 %collective-permute-start.38 = (bf16[2,32,6656]{2,1,0:T(8,128)(2,1)S(1)}, bf16[2,32,6656]{2,1,0:T(8,128)(2,1)S(1)}, u32[]{:S(2)}, u32[]{:S(2)}) collective-permute-start(bf16[2,32,6656]{2,1,0:T(8,128)(2,1)S(1)} %pad_maximum_fusion.7), channel_id=1, source_target_pairs={{0,8},{4,12},{8,0},{12,4},{16,24},{20,28},{24,16},{28,20},{1,9},{5... | collective-permute-start | bytes 2555912 | tf_op jit(solution)/shard_map/ppermute | solution.py:474
  393.4 29.0 %collective-permute-start.45 = (bf16[2,32,2816]{2,1,0:T(8,128)(2,1)S(1)}, bf16[2,32,2816]{2,1,0:T(8,128)(2,1)S(1)}, u32[]{:S(2)}, u32[]{:S(2)}) collective-permute-start(bf16[2,32,2816]{2,1,0:T(8,128)(2,1)S(1)} %fusion.71), channel_id=1, source_target_pairs={{0,4},{4,0},{8,12},{12,8},{16,20},{20,16},{24,28},{28,24},{1,5},{5... | collective-permute-start | bytes 1081352 | tf_op jit(solution)/shard_map/ppermute | solution.py:474
  395.7 28.6 %collective-permute-start.40 = (bf16[2,2,2,32,768]{4,3,1,2,0:T(8,128)(2,1)S(1)}, bf16[2,2,2,32,768]{4,3,1,2,0:T(8,128)(2,1)S(1)}, u32[]{:S(2)}, u32[]{:S(2)}) collective-permute-start(bf16[2,2,2,32,768]{4,3,1,2,0:T(8,128)(2,1)S(1)} %fusion.69), channel_id=1, source_target_pairs={{0,4},{4,0},{8,12},{12,8},{16,20},{20,16},{24,28},{28,24},{1,5},{5... | collective-permute-start | bytes 1179656 | tf_op jit(solution)/shard_map/ppermute | solution.py:474
  411.6 21.2 %collective-permute-start.44 = (bf16[32,6656]{1,0:T(8,128)(2,1)S(1)}, bf16[32,6656]{1,0:T(8,128)(2,1)S(1)}, u32[]{:S(2)}, u32[]{:S(2)}) collective-permute-start(bf16[32,6656]{1,0:T(8,128)(2,1)S(1)} %fusion.68), channel_id=1, source_target_pairs={{0,16},{4,20},{8,24},{12,28},{16,0},{20,4},{24,8},{28,12},{1,17},{... | collective-permute-start | bytes 1277960 | tf_op jit(solution)/shard_map/ppermute | solution.py:474
  (74 other events, 1062.8 us)

commit v7 on v6

--- a/solution.py
+++ b/solution.py
@@ -681,11 +681,11 @@
 
 
 class Scattering:
-    def __init__(self, shape, kept, arrived):
-        half, columns = kept.shape
+    def __init__(self, shape, kept, arrived, number=0):
+        count, half, columns = kept.shape
         self.shape, self.dims = shape, LAYOUT[1:]
         form = [shape.lines[d].count for d in self.dims] + [2 * half // shape.devices, columns]
-        self.parts = [[kept.reshape(form), arrived.reshape(form)]]
+        self.parts = [[(t.reshape([count] + form), number) for t in (kept, arrived)]]
 
     def beside(self, other):
         self.parts = self.parts + other.parts
@@ -694,7 +694,7 @@
     def term_of(self, step):
         found = []
         for terms in self.parts:
-            own = [lax.index_in_dim(t, step, self.axis, False) for t in terms]
+            own = [lax.index_in_dim(t[i], step, self.axis, False) for t, i in terms]
             found.append(functools.reduce(jnp.add, [t.astype(jnp.float32) for t in own]))
         return jnp.concatenate(found, axis=-1)
 
@@ -702,22 +702,22 @@
         self.line, self.axis, self.step = self.shape.lines[dim], self.dims.index(dim), 1
         self.dims = self.dims.replace(dim, "")
         if hold:
-            self.parts = [[after(t, *hold) for t in terms] for terms in self.parts]
+            self.parts = [[(after(t, *hold), i) for t, i in terms] for terms in self.parts]
         self.sent = self.term_of(1).astype(jnp.bfloat16)
         self.came = self.line.send(self.sent)
         return self
 
     def advance(self, *hold):
-        flat = [t for terms in self.parts for t in terms]
+        flat = [t for terms in self.parts for t, _ in terms]
         came, *flat = lax.optimization_barrier((self.came, *flat, *hold))[: len(flat) + 1]
-        self.parts = [[flat.pop(0) for _ in terms] for terms in self.parts]
+        self.parts = [[(flat.pop(0), i) for _, i in terms] for terms in self.parts]
         self.step += 1
         total = self.term_of(self.step % self.line.count) + came.astype(jnp.float32)
         if self.step < self.line.count:
             self.sent = total.astype(jnp.bfloat16)
             self.came = self.line.send(self.sent)
         else:
-            self.parts, self.came = [[total]], None
+            self.parts, self.came = [[(total[None], 0)]], None
         return self
 
     def along(self, dim):
@@ -927,7 +927,8 @@
         turn = ring.next(den)
         earlier = after(states.end(den), turn)
         mixed_cat, inverse = attention.far(qkv, seg, earlier, top, den)
-        rest.third(mixed_cat)
+        turned_mixed, turned_one = turned_rows(pick, mixed_cat), turned_rows(pick, a_one)
+        rest.third(turned_mixed, turned_one)
         rest.last()
         down = ring.end()
         down_ends = down.pieces("c", [(0, tiles * FF_TILE, 0, 0)])
@@ -938,14 +939,13 @@
         earlier = states.end()
         top, den = attention.near(qkv, seg, seg_row)
         mixed_cat, inverse = attention.far(qkv, seg, earlier, top, den)
+        turned_mixed, turned_one = turned_rows(pick, mixed_cat), turned_rows(pick, a_one)
     x_two = tokens + jnp.dot(mixed_cat, out_w, preferred_element_type=jnp.float32)
     scale_two, normed_two = norm_forward(x_two)
     a_two = (normed_two * gain_two).astype(jnp.bfloat16)
     a_turned = turned_rows(pick, a_two)
-    turned_mixed, turned_one = turned_rows(pick, mixed_cat), turned_rows(pick, a_one)
     if ringed:
         gate_w, up_w = rest.output(0, 2)
-        a_turned = after(a_turned, turned_mixed, turned_one)
         (down_w,) = assemble(down_ends, [tiles * FF_TILE], down_part.shape[0], shape)
     result, d_branch, d_x_two, kept, sent = feed_forward(
         a_two,
@@ -969,8 +969,8 @@
         send_core = shape.lines["c"].send
         arrived, out_arrived = send_core(sent), send_core(out_sent)
         arrived = after(arrived, out_sent, out_kept)
-        gate_sum, up_sum, down_sum = (Scattering(shape, kept[i], arrived[i]) for i in range(3))
-        gate_sum.beside(Scattering(shape, out_kept, out_arrived)).start("y")
+        gate_sum, up_sum, down_sum = (Scattering(shape, kept, arrived, i) for i in range(3))
+        gate_sum.beside(Scattering(shape, out_kept[None], out_arrived[None])).start("y")
         up_sum.start("x")
         down_sum.start("u")
         d_top = after(d_top, gate_sum.sent, up_sum.sent, down_sum.sent)
@@ -982,21 +982,21 @@
         later = after(states.end(near), down_sum.sent, gate_sum.sent, up_sum.sent)
 
         d_qkv = attention.far_back(qkv, seg, later, *d_near)
-        both = gate_sum.advance(d_qkv).beside(up_sum.advance(d_qkv)).start("u")
-        right = after(d_qkv, both.sent)
-        own_sent = dot(turned_one[half:], right).astype(jnp.bfloat16)
-        own_kept = dot(turned_one[:half], right).astype(jnp.bfloat16)
+        own_sent = dot(turned_one[half:], d_qkv).astype(jnp.bfloat16)
+        own_kept = dot(turned_one[:half], d_qkv).astype(jnp.bfloat16)
+        both = gate_sum.advance(own_kept).beside(up_sum.advance(own_kept)).start("u")
         arrived = after(send_core(own_sent), own_kept)
-        down_sum.advance(own_kept).start("x")
+        down_sum.advance(both.sent).start("x")
         arrived = after(arrived, down_sum.sent)
         qkv_a, qkv_b = (
-            Scattering(shape, own_kept[:, low : low + across], arrived[:, low : low + across])
+            Scattering(shape, own_kept[None, :, low : low + across], arrived[None, :, low : low + across])
             for low in (0, across)
         )
         qkv_a.start("y")
         qkv_b.start("x")
         d_qkv = after(d_qkv, qkv_a.sent, qkv_b.sent)
-        both.advance(qkv_a.sent, qkv_b.sent).start("w")
+        d_a_one = against(d_qkv, qkv_w)
+        both.advance(d_a_one).start("w")
         qkv_b.advance(both.sent).start("y")
         qkv_a.advance(both.sent).start("x")
         down_sum.advance(qkv_a.sent).start("y")
@@ -1005,7 +1005,7 @@
         qkv_sum.advance().start("w")
         both.advance()
         qkv_sum.advance()
-        grad_qkv, both, down_sum = (part.parts[0][0] for part in (qkv_sum, both, down_sum))
+        grad_qkv, both, down_sum = (part.parts[0][0][0][0] for part in (qkv_sum, both, down_sum))
         grad_qkv = [grad_qkv[:, g * across : (g + 1) * across] for g in range(groups)]
         padded = tiles * FF_TILE
         grad_gate, grad_out = both[:, :hidden], both[:, padded : padded + width]
@@ -1021,7 +1021,7 @@
         d_qkv = attention.far_back(qkv, seg, later, *d_near)
         whole = scatter_whole(dot(turned_one[:half], d_qkv), dot(turned_one[half:], d_qkv))
         grad_qkv = [whole[:, g * across : (g + 1) * across] for g in range(groups)]
-    d_a_one = against(d_qkv, qkv_w)
+        d_a_one = against(d_qkv, qkv_w)
     d_tokens = d_x_two + norm_backward(d_a_one, gain_one, scale_one, normed_one)
     return (
         result.reshape(rows, shard_len, width),

time: 460 us -> 453 us (0.985)
  waiting for transfers between devices: 61.1 us -> 44.1 us
    ppermute x43, waiting for transfers between devices: 61.1 us -> 44.1 us  [send(): return lax.ppermute(array, self.axis, pairs)]
    squeeze x9 -> x13, local copies, waits for them, and re-layouts: 0.29 us -> 8.32 us  [term_of(): own = [lax.index_in_dim(t[i], step, self.axis, False) for t, i in terms]]
    unnamed x132 -> x116, local copies, waits for them, and re-layouts: 15.8 us -> 14.6 us
  transfers between devices with their start and end apart: 47 -> 47, of which waited for: 14 -> 14; matrix products, arithmetic and copies ran while one was open for 25% -> 27% of each run, Pallas kernels for 22% -> 23%
where the time goes in v7:
time: 453 us; the launch traced here: 444 us
  Pallas kernels  184 us (41%)
  starting transfers between devices  65.8 us (15%)
  other arithmetic  55 us (12%)
  matrix products  45 us (10%)
  waiting for transfers between devices  44.1 us (10%)
  local copies, waits for them, and re-layouts  41.5 us (9%)
  between operations  9.02 us (2%)
    pallas_call x1, Pallas kernels, feed_forward(): pl.pallas_call(functools.partial(mlp_kernel, min(512, count), sums is Non...  69 us
    ppermute x43, starting transfers between devices, send(): return lax.ppermute(array, self.axis, pairs)  56.6 us
    ppermute x43, waiting for transfers between devices, send(): return lax.ppermute(array, self.axis, pairs)  44.1 us
    dot_general x10, matrix products, dot(): lax.dot_general(left, right, (dims, ((), ())), preferred_element_type=jnp...  35.5 us
    pallas_call x1, Pallas kernels, near_back(): self.call(kernel, groups, [at['x'], at['values'], at['narrow'], at['seg']...  32 us
    pallas_call x4, Pallas kernels, assemble(): pl.pallas_call(kernel, out_shape=[jax.ShapeDtypeStruct((shape.devices * b...  24.6 us
    concatenate x12, other arithmetic, along(): array = jnp.concatenate([self.array] + [a for a, _ in came], 0)  17.1 us
    unnamed x116, local copies, waits for them, and re-layouts  14.6 us
  transfers between devices with their start and end apart: 47, of which 14 were waited for; matrix products, arithmetic and copies ran while one was open for 27% of the time, Pallas kernels for 23%

profile of v7, /device:TPU:0, one launch (start us, length us, event | category | flops | bytes accessed | tf_op | source)
XLA Modules:
  0.0 444.1 jit_solution(3825792104969942658)
XLA Ops:
  2.5 3.1 collective-permute-start
  60.8 6.0 %assemble.4 = bf16[1024,1664]{1,0:T(8,128)(2,1)} custom-call(s32[64]{0:T(128)} %stack.856.places_ref, bf16[512,896]{1,0:T(8,128)(2,1)} %copy-done.12, bf16[512,896]{1,0:T(8,128)(2,1)} %collective-permute-done.5.refs_1_, bf16[512,768]{1,0:T(8,128)(2,1)} %copy-done.13, bf16[512,768]{1,0:T(8,128)(2,1)} %copy-done.25), custom_call_target="tpu_custom_call" | custom-call | bytes 6815744 | tf_op jit(solution)/shard_map/assemble/pallas_call | solution.py:546
  69.0 4.8 %convolution_convert_fusion.x_ref.refs_0_ = bf16[1024,1536]{1,0:T(8,128)(2,1)} fusion(bf16[1024,1024]{1,0:T(8,128)(2,1)S(1)} %fusion.3, bf16[1024,1664]{1,0:T(8,128)(2,1)S(1)} %copy-done.8), kind=kOutput, calls=%fused_computation.21 | convolution fusion | flops 3222798336 | bytes 8388608 | tf_op jit(solution)/shard_map/dot_general | solution.py:911
  77.1 8.7 %attn_tail.1 = bf16[2,2,656,128]{3,2,1,0:T(8,128)(2,1)} custom-call(bf16[1024,1536]{1,0:T(8,128)(2,1)} %convolution_convert_fusion.x_ref.refs_0_, s32[1024,1]{1,0:T(8,128)} %bitcast.303, bf16[1280,128]{1,0:T(8,128)(2,1)} %get-tuple-element.210.pick_ref), custom_call_target="tpu_custom_call" | custom-call | flops 10737418240 | bytes 2097152 | tf_op jit(solution)/shard_map/attn_tail/pallas_call | solution.py:354
  87.9 4.5 %collective-permute-start.18 = (bf16[2,2,656,128]{3,2,1,0:T(8,128)(2,1)}, bf16[2,2,656,128]{3,2,1,0:T(8,128)(2,1)}, u32[]{:S(2)}, u32[]{:S(2)}) collective-permute-start(bf16[2,2,656,128]{3,2,1,0:T(8,128)(2,1)} %attn_tail.1), channel_id=1, source_target_pairs={{0,2},{1,3},{4,6},{5,7},{8,10},{9,11},{12,14},{13,15},{16,18},{17,... | collective-permute-start | bytes 2015240 | tf_op jit(solution)/shard_map/ppermute | solution.py:430
  97.6 3.7 fusion.28
  103.4 10.9 %attn_near.1 = (f32[1024,1024]{1,0:T(8,128)}, f32[1024,1024]{1,0:T(8,128)}) custom-call(bf16[1024,1536]{1,0:T(8,128)(2,1)} %convolution_convert_fusion.x_ref.refs_0_, s32[1024,1]{1,0:T(8,128)} %bitcast.304, s32[2,1,512]{2,1,0:T(1,128)} %reshape.3219.refs_2_.refs_4_), custom_call_target="tpu_custom_call" | custom-call | flops 17179869184 | bytes 2097152 | tf_op jit(solution)/shard_map/attn_near/pallas_call | solution.py:365
  120.6 12.3 %attn_far.1 = (bf16[1024,1024]{1,0:T(8,128)(2,1)}, f32[1024,1024]{1,0:T(8,128)}) custom-call(bf16[1024,1536]{1,0:T(8,128)(2,1)} %convolution_convert_fusion.x_ref.refs_0_, s32[1024,1]{1,0:T(8,128)} %bitcast.305, bf16[2,2,656,128]{3,2,1,0:T(8,128)(2,1)} %add_convert_fusion.4.state_ref.refs_5_, f32[1024,1024]{1,0:T(8,128)} %get-tuple-element.111.top_ref, ...), custom_call_target="tpu_custom_call" | custom-call | flops 17179869184 | bytes 2097152 | tf_op jit(solution)/shard_map/attn_far/pallas_call | solution.py:372
  133.0 5.3 %fusion.25 = bf16[1024,1024]{1,0:T(8,128)(2,1)} fusion(bf16[1024,1024]{1,0:T(8,128)(2,1)} %get-tuple-element.112.y_ref, s32[1024]{0:T(1024)S(1)} %add.15399), kind=kOutput, calls=%fused_computation.46 | convolution fusion | flops 2150629376 | bytes 4198400 | tf_op jit(solution)/shard_map/dot_general | solution.py:22
  143.4 3.4 pad_maximum_fusion.refs_0_
  146.8 4.8 %collective-permute-start.21 = (bf16[512,3328]{1,0:T(8,128)(2,1)}, bf16[512,3328]{1,0:T(8,128)(2,1)}, u32[]{:S(2)}, u32[]{:S(2)}) collective-permute-start(bf16[512,3328]{1,0:T(8,128)(2,1)} %pad_maximum_fusion.refs_0_), channel_id=1, source_target_pairs={{0,1},{1,0},{2,3},{3,2},{4,5},{5,4},{6,7},{7,6},{8,9},{9,8},{10,11... | collective-permute-start | bytes 10223624 | tf_op jit(solution)/shard_map/ppermute | solution.py:474
  154.1 5.4 %fusion.34.gt_ref = bf16[1024,1024]{1,0:T(8,128)(2,1)} fusion(bf16[1024,1024]{1,0:T(8,128)(2,1)} %bitcast.315, s32[1024]{0:T(1024)S(1)} %add.15399), kind=kOutput, calls=%fused_computation.49 | convolution fusion | flops 2150629376 | bytes 4198400 | tf_op jit(solution)/shard_map/dot_general | solution.py:22
  161.8 5.3 %assemble.7.down_ref = bf16[1024,2816]{1,0:T(8,128)(2,1)} custom-call(s32[32]{0:T(128)} %stack.1055.places_ref, bf16[512,2816]{1,0:T(8,128)(2,1)} %constant_dynamic-update-slice_fusion.refs_0_, bf16[512,2816]{1,0:T(8,128)(2,1)} %collective-permute-done.25.refs_1_), custom_call_target="tpu_custom_call" | custom-call | bytes 11534336 | tf_op jit(solution)/shard_map/assemble/pallas_call | solution.py:546
  167.1 3.8 assemble.5
  170.9 4.7 %multiply_reduce_fusion = (f32[1024]{0:T(1024)S(1)}, f32[1024,1024]{1,0:T(8,128)S(1)}) fusion(bf16[1024,1024]{1,0:T(8,128)(2,1)} %get-tuple-element.112.y_ref, bf16[1024,1024]{1,0:T(8,128)(2,1)} %assemble.5, bf16[2,512,1024]{2,1,0:T(8,128)(2,1)S(1)} %copy-done.2), kind=kOutput, calls=%fused_computation.13 | convolution fusion | flops 2151676928 | bytes 10489856 | tf_op jit(solution)/shard_map/dot_general | solution.py:943
  178.9 3.7 fusion.31.at_ref
  182.6 9.6 %assemble.6 = (bf16[1024,2816]{1,0:T(8,128)(2,1)}, bf16[1024,2816]{1,0:T(8,128)(2,1)}) custom-call(s32[64]{0:T(128)} %stack.856.places_ref, bf16[512,3328]{1,0:T(8,128)(2,1)} %pad_maximum_fusion.refs_0_, bf16[512,3328]{1,0:T(8,128)(2,1)} %collective-permute-done.21.refs_1_, bf16[512,3328]{1,0:T(8,128)(2,1)} %copy-done, ...), custom_call_target="tpu_custom_call" | custom-call | bytes 23068672 | tf_op jit(solution)/shard_map/assemble/pallas_call | solution.py:546
  192.2 69.0 %mlp.1 = (bf16[1024,1024]{1,0:T(8,128)(2,1)}, bf16[1024,1024]{1,0:T(8,128)(2,1)}, f32[1024,1024]{1,0:T(8,128)}, bf16[3,512,2816]{2,1,0:T(8,128)(2,1)}, bf16[3,512,2816]{2,1,0:T(8,128)(2,1)}) custom-call(bf16[1024,1024]{1,0:T(8,128)(2,1)} %copy-done.15, bf16[1024,1024]{1,0:T(8,128)(2,1)} %bitcast.316, bf16[1024,1024]{1,0:T(8,128)(2,1)} %fusion.31.at_ref, ...), custom_call_target="tpu_custom_call" | custom-call | flops 53150220288 | bytes 55574528 | tf_op jit(solution)/shard_map/mlp/pallas_call | solution.py:821
  262.3 5.3 %convolution_convert_fusion.3.dy_ref = bf16[1024,1024]{1,0:T(8,128)(2,1)} fusion(bf16[1024,1024]{1,0:T(8,128)(2,1)} %get-tuple-element.125, bf16[1024,1024]{1,0:T(8,128)(2,1)S(1)} %copy-done.14), kind=kOutput, calls=%fused_computation.50 | convolution fusion | flops 2148532224 | bytes 6291456 | tf_op jit(solution)/shard_map/dot_general | solution.py:22
  267.6 11.7 %attn_head.1 = (bf16[2,2,656,128]{3,2,1,0:T(8,128)(2,1)}, bf16[1024,1024]{1,0:T(8,128)(2,1)}, bf16[1024,256]{1,0:T(8,128)(2,1)}) custom-call(bf16[1024,1536]{1,0:T(8,128)(2,1)} %convolution_convert_fusion.x_ref.refs_0_, bf16[1024,1024]{1,0:T(8,128)(2,1)} %convolution_convert_fusion.3.dy_ref, bf16[1024,1024]{1,0:T(8,128)(2,1)} %get-tuple-element.112.y_ref, ...), custom_call_target="tpu_custom_call" | custom-call | flops 10737418240 | bytes 2097152 | tf_op jit(solution)/shard_map/attn_head/pallas_call | solution.py:381
  295.2 3.8 collective-permute-start.31
  302.5 32.0 %attn_near_back.1 = (bf16[1024,256]{1,0:T(8,128)(2,1)}, f32[1024,256]{1,0:T(8,128)}, f32[1024,1024]{1,0:T(8,128)}) custom-call(bf16[1024,1536]{1,0:T(8,128)(2,1)} %convolution_convert_fusion.x_ref.refs_0_, bf16[1024,1024]{1,0:T(8,128)(2,1)} %get-tuple-element.127.refs_1_, bf16[1024,256]{1,0:T(8,128)(2,1)} %get-tuple-element.128.refs_2_, ...), custom_call_target="tpu_custom_call" | custom-call | flops 51539607552 | bytes 2097152 | tf_op jit(solution)/shard_map/attn_near_back/pallas_call | solution.py:394
  350.4 3.2 collective-permute-done.31
  359.9 14.3 %attn_far_back.1 = bf16[1024,1536]{1,0:T(8,128)(2,1)} custom-call(bf16[1024,1536]{1,0:T(8,128)(2,1)} %convolution_convert_fusion.x_ref.refs_0_, s32[1024,1]{1,0:T(8,128)} %bitcast.308, bf16[2,2,656,128]{3,2,1,0:T(8,128)(2,1)} %add_convert_fusion.3.state_ref, bf16[1024,256]{1,0:T(8,128)(2,1)} %get-tuple-element.129.dq_ref, ...), custom_call_target="tpu_custom_call" | custom-call | flops 19327352832 | bytes 2097152 | tf_op jit(solution)/shard_map/attn_far_back/pallas_call | solution.py:407
  374.2 4.1 convolution_convert_fusion.1
  383.7 3.8 collective-permute-start.38
  391.7 3.6 fusion.4
  398.1 9.0 %collective-permute-done.38 = bf16[2,32,6656]{2,1,0:T(8,128)(2,1)S(1)} collective-permute-done((bf16[2,32,6656]{2,1,0:T(8,128)(2,1)S(1)}, bf16[2,32,6656]{2,1,0:T(8,128)(2,1)S(1)}, u32[]{:S(2)}, u32[]{:S(2)}) %collective-permute-start.38) | collective-permute-done | bytes 852000 | tf_op jit(solution)/shard_map/ppermute | solution.py:474
  414.2 5.1 %collective-permute-done.46 = bf16[32,2816]{1,0:T(8,128)(2,1)S(1)} collective-permute-done((bf16[32,2816]{1,0:T(8,128)(2,1)S(1)}, bf16[32,2816]{1,0:T(8,128)(2,1)S(1)}, u32[]{:S(2)}, u32[]{:S(2)}) %collective-permute-start.46) | collective-permute-done | bytes 180256 | tf_op jit(solution)/shard_map/ppermute | solution.py:474
  423.5 5.7 %collective-permute-done.44 = bf16[32,6656]{1,0:T(8,128)(2,1)S(1)} collective-permute-done((bf16[32,6656]{1,0:T(8,128)(2,1)S(1)}, bf16[32,6656]{1,0:T(8,128)(2,1)S(1)}, u32[]{:S(2)}, u32[]{:S(2)}) %collective-permute-start.44) | collective-permute-done | bytes 426016 | tf_op jit(solution)/shard_map/ppermute | solution.py:474
  429.8 3.6 collective-permute-done.42
  435.6 5.6 %collective-permute-done.43 = bf16[32,1536]{1,0:T(8,128)(2,1)S(1)} collective-permute-done((bf16[32,1536]{1,0:T(8,128)(2,1)S(1)}, bf16[32,1536]{1,0:T(8,128)(2,1)S(1)}, u32[]{:S(2)}, u32[]{:S(2)}) %collective-permute-start.43) | collective-permute-done | bytes 98336 | tf_op jit(solution)/shard_map/ppermute | solution.py:474
  (319 shorter events, 155.2 us)
Async XLA Ops:
  2.5 26.2 %collective-permute-start = (bf16[32,1664]{1,0:T(8,128)(2,1)S(1)}, bf16[32,1664]{1,0:T(8,128)(2,1)S(1)}, u32[]{:S(2)}, u32[]{:S(2)}) collective-permute-start(bf16[32,1664]{1,0:T(8,128)(2,1)S(1)} %pad_maximum_fusion.18), channel_id=1, source_target_pairs={{0,8},{4,12},{8,24},{12,28},{16,0},{20,4},{24,16},{28,20},{1,9},{5... | collective-permute-start | bytes 319496 | tf_op jit(solution)/shard_map/ppermute | solution.py:474
  5.5 24.3 %collective-permute-start.1 = (bf16[32,1664]{1,0:T(8,128)(2,1)S(1)}, bf16[32,1664]{1,0:T(8,128)(2,1)S(1)}, u32[]{:S(2)}, u32[]{:S(2)}) collective-permute-start(bf16[32,1664]{1,0:T(8,128)(2,1)S(1)} %pad_maximum_fusion.18), channel_id=1, source_target_pairs={{0,24},{4,28},{8,16},{12,20},{16,8},{20,12},{24,0},{28,4},{1,25},{... | collective-permute-start | bytes 319496 | tf_op jit(solution)/shard_map/ppermute | solution.py:474
  8.0 21.8 %collective-permute-start.2 = (bf16[32,1664]{1,0:T(8,128)(2,1)S(1)}, bf16[32,1664]{1,0:T(8,128)(2,1)S(1)}, u32[]{:S(2)}, u32[]{:S(2)}) collective-permute-start(bf16[32,1664]{1,0:T(8,128)(2,1)S(1)} %pad_maximum_fusion.18), channel_id=1, source_target_pairs={{0,16},{4,20},{8,0},{12,4},{16,24},{20,28},{24,8},{28,12},{1,17},{... | collective-permute-start | bytes 319496 | tf_op jit(solution)/shard_map/ppermute | solution.py:474
  13.2 37.7 %collective-permute-start.9 = (bf16[32,6656]{1,0:T(8,128)(2,1)}, bf16[32,6656]{1,0:T(8,128)(2,1)}, u32[]{:S(2)}, u32[]{:S(2)}) collective-permute-start(bf16[32,6656]{1,0:T(8,128)(2,1)} %pad_maximum_fusion.12), channel_id=1, source_target_pairs={{0,8},{4,12},{8,24},{12,28},{16,0},{20,4},{24,16},{28,20},{1,9},{5... | collective-permute-start | bytes 1277960 | tf_op jit(solution)/shard_map/ppermute | solution.py:474
  13.6 37.8 %collective-permute-start.10 = (bf16[32,6656]{1,0:T(8,128)(2,1)}, bf16[32,6656]{1,0:T(8,128)(2,1)}, u32[]{:S(2)}, u32[]{:S(2)}) collective-permute-start(bf16[32,6656]{1,0:T(8,128)(2,1)} %pad_maximum_fusion.12), channel_id=1, source_target_pairs={{0,24},{4,28},{8,16},{12,20},{16,8},{20,12},{24,0},{28,4},{1,25},{... | collective-permute-start | bytes 1277960 | tf_op jit(solution)/shard_map/ppermute | solution.py:474
  28.6 22.8 %collective-permute-start.11 = (bf16[32,6656]{1,0:T(8,128)(2,1)}, bf16[32,6656]{1,0:T(8,128)(2,1)}, u32[]{:S(2)}, u32[]{:S(2)}) collective-permute-start(bf16[32,6656]{1,0:T(8,128)(2,1)} %pad_maximum_fusion.12), channel_id=1, source_target_pairs={{0,16},{4,20},{8,0},{12,4},{16,24},{20,28},{24,8},{28,12},{1,17},{... | collective-permute-start | bytes 1277960 | tf_op jit(solution)/shard_map/ppermute | solution.py:474
  53.2 20.7 %collective-permute-start.13 = (bf16[64,2816]{1,0:T(8,128)(2,1)}, bf16[64,2816]{1,0:T(8,128)(2,1)}, u32[]{:S(2)}, u32[]{:S(2)}) collective-permute-start(bf16[64,2816]{1,0:T(8,128)(2,1)} %pad_maximum_fusion.14), channel_id=1, source_target_pairs={{0,2},{1,3},{2,0},{3,1},{4,6},{5,7},{6,4},{7,5},{8,10},{9,11},{10,... | collective-permute-start | bytes 1081352 | tf_op jit(solution)/shard_map/ppermute | solution.py:474
  57.2 35.3 %collective-permute-start.16 = (bf16[128,3328]{1,0:T(8,128)(2,1)}, bf16[128,3328]{1,0:T(8,128)(2,1)}, u32[]{:S(2)}, u32[]{:S(2)}) collective-permute-start(bf16[128,3328]{1,0:T(8,128)(2,1)} %get-tuple-element.191), channel_id=1, source_target_pairs={{0,2},{1,3},{2,0},{3,1},{4,6},{5,7},{6,4},{7,5},{8,10},{9,11},{10,... | collective-permute-start | bytes 2555912 | tf_op jit(solution)/shard_map/ppermute | solution.py:474
  57.7 36.3 %collective-permute-start.15 = (bf16[128,3328]{1,0:T(8,128)(2,1)S(1)}, bf16[128,3328]{1,0:T(8,128)(2,1)}, u32[]{:S(2)}, u32[]{:S(2)}) collective-permute-start(bf16[128,3328]{1,0:T(8,128)(2,1)S(1)} %get-tuple-element.192), channel_id=1, source_target_pairs={{0,4},{4,0},{8,12},{12,8},{16,20},{20,16},{24,28},{28,24},{1,5},{5... | collective-permute-start | bytes 2555912 | tf_op jit(solution)/shard_map/ppermute | solution.py:474
  75.7 25.6 %collective-permute-start.17 = (bf16[128,2816]{1,0:T(8,128)(2,1)}, bf16[128,2816]{1,0:T(8,128)(2,1)S(1)}, u32[]{:S(2)}, u32[]{:S(2)}) collective-permute-start(bf16[128,2816]{1,0:T(8,128)(2,1)} %pad_maximum_fusion.9), channel_id=1, source_target_pairs={{0,8},{4,12},{8,24},{12,28},{16,0},{20,4},{24,16},{28,20},{1,9},{5... | collective-permute-start | bytes 2162696 | tf_op jit(solution)/shard_map/ppermute | solution.py:474
  85.8 28.4 %collective-permute-start.14 = (bf16[2,2,656,128]{3,2,1,0:T(8,128)(2,1)}, bf16[2,2,656,128]{3,2,1,0:T(8,128)(2,1)}, u32[]{:S(2)}, u32[]{:S(2)}) collective-permute-start(bf16[2,2,656,128]{3,2,1,0:T(8,128)(2,1)} %attn_tail.1), channel_id=1, source_target_pairs={{0,1},{1,2},{2,3},{4,5},{5,6},{6,7},{8,9},{9,10},{10,11},{12,13},{... | collective-permute-start | bytes 2015240 | tf_op jit(solution)/shard_map/ppermute | solution.py:430
  87.9 26.3 %collective-permute-start.18 = (bf16[2,2,656,128]{3,2,1,0:T(8,128)(2,1)}, bf16[2,2,656,128]{3,2,1,0:T(8,128)(2,1)}, u32[]{:S(2)}, u32[]{:S(2)}) collective-permute-start(bf16[2,2,656,128]{3,2,1,0:T(8,128)(2,1)} %attn_tail.1), channel_id=1, source_target_pairs={{0,2},{1,3},{4,6},{5,7},{8,10},{9,11},{12,14},{13,15},{16,18},{17,... | collective-permute-start | bytes 2015240 | tf_op jit(solution)/shard_map/ppermute | solution.py:430
  95.3 43.0 %collective-permute-start.22 = (bf16[256,3328]{1,0:T(8,128)(2,1)S(1)}, bf16[256,3328]{1,0:T(8,128)(2,1)}, u32[]{:S(2)}, u32[]{:S(2)}) collective-permute-start(bf16[256,3328]{1,0:T(8,128)(2,1)S(1)} %pad_maximum_fusion.5), channel_id=1, source_target_pairs={{0,4},{4,0},{8,12},{12,8},{16,20},{20,16},{24,28},{28,24},{1,5},{5... | collective-permute-start | bytes 5111816 | tf_op jit(solution)/shard_map/ppermute | solution.py:474
  95.9 47.5 %collective-permute-start.20 = (bf16[256,3328]{1,0:T(8,128)(2,1)S(1)}, bf16[256,3328]{1,0:T(8,128)(2,1)}, u32[]{:S(2)}, u32[]{:S(2)}) collective-permute-start(bf16[256,3328]{1,0:T(8,128)(2,1)S(1)} %pad_maximum_fusion.4), channel_id=1, source_target_pairs={{0,2},{1,3},{2,0},{3,1},{4,6},{5,7},{6,4},{7,5},{8,10},{9,11},{10,... | collective-permute-start | bytes 5111816 | tf_op jit(solution)/shard_map/ppermute | solution.py:474
  101.3 18.2 %collective-permute-start.19 = (bf16[128,2816]{1,0:T(8,128)(2,1)S(1)}, bf16[128,2816]{1,0:T(8,128)(2,1)S(1)}, u32[]{:S(2)}, u32[]{:S(2)}) collective-permute-start(bf16[128,2816]{1,0:T(8,128)(2,1)S(1)} %collective-permute-done.17), channel_id=1, source_target_pairs={{0,8},{4,12},{8,24},{12,28},{16,0},{20,4},{24,16},{28,20},{1,9},{5... | collective-permute-start | bytes 2162696 | tf_op jit(solution)/shard_map/ppermute | solution.py:474
  119.5 33.1 %collective-permute-start.24 = (bf16[128,2816]{1,0:T(8,128)(2,1)S(1)}, bf16[128,2816]{1,0:T(8,128)(2,1)S(1)}, u32[]{:S(2)}, u32[]{:S(2)}) collective-permute-start(bf16[128,2816]{1,0:T(8,128)(2,1)S(1)} %collective-permute-done.19), channel_id=1, source_target_pairs={{0,8},{4,12},{8,24},{12,28},{16,0},{20,4},{24,16},{28,20},{1,9},{5... | collective-permute-start | bytes 2162696 | tf_op jit(solution)/shard_map/ppermute | solution.py:474
  140.4 26.6 %collective-permute-start.23 = (bf16[512,3328]{1,0:T(8,128)(2,1)S(1)}, bf16[512,3328]{1,0:T(8,128)(2,1)}, u32[]{:S(2)}, u32[]{:S(2)}) collective-permute-start(bf16[512,3328]{1,0:T(8,128)(2,1)S(1)} %pad_maximum_fusion.1.refs_2_), channel_id=1, source_target_pairs={{0,1},{1,0},{2,3},{3,2},{4,5},{5,4},{6,7},{7,6},{8,9},{9,8},{10,11... | collective-permute-start | bytes 10223624 | tf_op jit(solution)/shard_map/ppermute | solution.py:474
  146.8 20.2 %collective-permute-start.21 = (bf16[512,3328]{1,0:T(8,128)(2,1)}, bf16[512,3328]{1,0:T(8,128)(2,1)}, u32[]{:S(2)}, u32[]{:S(2)}) collective-permute-start(bf16[512,3328]{1,0:T(8,128)(2,1)} %pad_maximum_fusion.refs_0_), channel_id=1, source_target_pairs={{0,1},{1,0},{2,3},{3,2},{4,5},{5,4},{6,7},{7,6},{8,9},{9,8},{10,11... | collective-permute-start | bytes 10223624 | tf_op jit(solution)/shard_map/ppermute | solution.py:474
  261.2 27.6 %collective-permute-start.27 = (bf16[3,512,2816]{2,1,0:T(8,128)(2,1)}, bf16[3,512,2816]{2,1,0:T(8,128)(2,1)}, u32[]{:S(2)}, u32[]{:S(2)}) collective-permute-start(bf16[3,512,2816]{2,1,0:T(8,128)(2,1)} %get-tuple-element.124), channel_id=1, source_target_pairs={{0,1},{1,0},{2,3},{3,2},{4,5},{5,4},{6,7},{7,6},{8,9},{9,8},{10,11... | collective-permute-start | bytes 25952264 | tf_op jit(solution)/shard_map/ppermute | solution.py:474
  282.1 52.5 %collective-permute-start.26 = (bf16[2,2,656,128]{3,2,1,0:T(8,128)(2,1)}, bf16[2,2,656,128]{3,2,1,0:T(8,128)(2,1)}, u32[]{:S(2)}, u32[]{:S(2)}) collective-permute-start(bf16[2,2,656,128]{3,2,1,0:T(8,128)(2,1)} %get-tuple-element.121), channel_id=1, source_target_pairs={{1,0},{2,1},{3,2},{5,4},{6,5},{7,6},{9,8},{10,9},{11,10},{13,12},{... | collective-permute-start | bytes 2015240 | tf_op jit(solution)/shard_map/ppermute | solution.py:430
  283.4 51.2 %collective-permute-start.29 = (bf16[2,2,656,128]{3,2,1,0:T(8,128)(2,1)}, bf16[2,2,656,128]{3,2,1,0:T(8,128)(2,1)}, u32[]{:S(2)}, u32[]{:S(2)}) collective-permute-start(bf16[2,2,656,128]{3,2,1,0:T(8,128)(2,1)} %get-tuple-element.121), channel_id=1, source_target_pairs={{2,0},{3,1},{6,4},{7,5},{10,8},{11,9},{14,12},{15,13},{18,16},{19,... | collective-permute-start | bytes 2015240 | tf_op jit(solution)/shard_map/ppermute | solution.py:430
  294.6 42.5 %collective-permute-start.32 = (bf16[2,2,2,32,2816]{4,3,1,2,0:T(8,128)(2,1)S(1)}, bf16[2,2,2,32,2816]{4,3,1,2,0:T(8,128)(2,1)S(1)}, u32[]{:S(2)}, u32[]{:S(2)}) collective-permute-start(bf16[2,2,2,32,2816]{4,3,1,2,0:T(8,128)(2,1)S(1)} %fusion.37), channel_id=1, source_target_pairs={{0,4},{4,0},{8,12},{12,8},{16,20},{20,16},{24,28},{28,24},{1,5},{5... | collective-permute-start | bytes 4325384 | tf_op jit(solution)/shard_map/ppermute | solution.py:474
  295.2 58.4 %collective-permute-start.31 = (bf16[2,2,2,32,3840]{4,3,1,2,0:T(8,128)(2,1)S(1)}, bf16[2,2,2,32,3840]{4,3,1,2,0:T(8,128)(2,1)S(1)}, u32[]{:S(2)}, u32[]{:S(2)}) collective-permute-start(bf16[2,2,2,32,3840]{4,3,1,2,0:T(8,128)(2,1)S(1)} %copy.2219), channel_id=1, source_target_pairs={{0,2},{1,3},{2,0},{3,1},{4,6},{5,7},{6,4},{7,5},{8,10},{9,11},{10,... | collective-permute-start | bytes 5898248 | tf_op jit(solution)/shard_map/ppermute | solution.py:474
  300.5 40.7 %collective-permute-start.30 = (bf16[2,2,2,32,2816]{4,3,0,1,2:T(8,128)(2,1)}, bf16[2,2,2,32,2816]{4,3,0,1,2:T(8,128)(2,1)S(1)}, u32[]{:S(2)}, u32[]{:S(2)}) collective-permute-start(bf16[2,2,2,32,2816]{4,3,0,1,2:T(8,128)(2,1)} %fusion.38), channel_id=1, source_target_pairs={{0,8},{4,12},{8,0},{12,4},{16,24},{20,28},{24,16},{28,20},{1,9},{5... | collective-permute-start | bytes 4325384 | tf_op jit(solution)/shard_map/ppermute | solution.py:474
  346.8 33.6 %collective-permute-start.36 = (bf16[2,2,32,2816]{3,2,0,1:T(8,128)(2,1)}, bf16[2,2,32,2816]{3,2,0,1:T(8,128)(2,1)}, u32[]{:S(2)}, u32[]{:S(2)}) collective-permute-start(bf16[2,2,32,2816]{3,2,0,1:T(8,128)(2,1)} %fusion.46), channel_id=1, source_target_pairs={{0,2},{1,3},{2,0},{3,1},{4,6},{5,7},{6,4},{7,5},{8,10},{9,11},{10,... | collective-permute-start | bytes 2162696 | tf_op jit(solution)/shard_map/ppermute | solution.py:474
  348.5 39.0 %collective-permute-start.34 = (bf16[2,2,32,2816]{3,2,0,1:T(8,128)(2,1)}, bf16[2,2,32,2816]{3,2,0,1:T(8,128)(2,1)}, u32[]{:S(2)}, u32[]{:S(2)}) collective-permute-start(bf16[2,2,32,2816]{3,2,0,1:T(8,128)(2,1)} %fusion.45), channel_id=1, source_target_pairs={{0,16},{4,20},{8,24},{12,28},{16,0},{20,4},{24,8},{28,12},{1,17},{... | collective-permute-start | bytes 2162696 | tf_op jit(solution)/shard_map/ppermute | solution.py:474
  359.9 23.5 %collective-permute-start.35 = (bf16[2,2,32,3840]{3,2,0,1:T(8,128)(2,1)}, bf16[2,2,32,3840]{3,2,0,1:T(8,128)(2,1)S(1)}, u32[]{:S(2)}, u32[]{:S(2)}) collective-permute-start(bf16[2,2,32,3840]{3,2,0,1:T(8,128)(2,1)} %fusion.44), channel_id=1, source_target_pairs={{0,4},{4,0},{8,12},{12,8},{16,20},{20,16},{24,28},{28,24},{1,5},{5... | collective-permute-start | bytes 2949128 | tf_op jit(solution)/shard_map/ppermute | solution.py:474
  383.7 23.4 %collective-permute-start.38 = (bf16[2,32,6656]{2,1,0:T(8,128)(2,1)S(1)}, bf16[2,32,6656]{2,1,0:T(8,128)(2,1)S(1)}, u32[]{:S(2)}, u32[]{:S(2)}) collective-permute-start(bf16[2,32,6656]{2,1,0:T(8,128)(2,1)S(1)} %pad_maximum_fusion.7), channel_id=1, source_target_pairs={{0,8},{4,12},{8,0},{12,4},{16,24},{20,28},{24,16},{28,20},{1,9},{5... | collective-permute-start | bytes 2555912 | tf_op jit(solution)/shard_map/ppermute | solution.py:474
  389.0 22.7 %collective-permute-start.45 = (bf16[2,32,2816]{2,1,0:T(8,128)(2,1)S(1)}, bf16[2,32,2816]{2,1,0:T(8,128)(2,1)S(1)}, u32[]{:S(2)}, u32[]{:S(2)}) collective-permute-start(bf16[2,32,2816]{2,1,0:T(8,128)(2,1)S(1)} %fusion.73), channel_id=1, source_target_pairs={{0,4},{4,0},{8,12},{12,8},{16,20},{20,16},{24,28},{28,24},{1,5},{5... | collective-permute-start | bytes 1081352 | tf_op jit(solution)/shard_map/ppermute | solution.py:474
  391.4 20.5 %collective-permute-start.40 = (bf16[2,2,2,32,768]{4,3,1,2,0:T(8,128)(2,1)S(1)}, bf16[2,2,2,32,768]{4,3,1,2,0:T(8,128)(2,1)S(1)}, u32[]{:S(2)}, u32[]{:S(2)}) collective-permute-start(bf16[2,2,2,32,768]{4,3,1,2,0:T(8,128)(2,1)S(1)} %fusion.71), channel_id=1, source_target_pairs={{0,4},{4,0},{8,12},{12,8},{16,20},{20,16},{24,28},{28,24},{1,5},{5... | collective-permute-start | bytes 1179656 | tf_op jit(solution)/shard_map/ppermute | solution.py:474
  395.4 14.0 %collective-permute-start.37 = (bf16[2,2,2,32,768]{4,3,1,2,0:T(8,128)(2,1)S(1)}, bf16[2,2,2,32,768]{4,3,1,2,0:T(8,128)(2,1)S(1)}, u32[]{:S(2)}, u32[]{:S(2)}) collective-permute-start(bf16[2,2,2,32,768]{4,3,1,2,0:T(8,128)(2,1)S(1)} %copy.2213), channel_id=1, source_target_pairs={{0,2},{1,3},{2,0},{3,1},{4,6},{5,7},{6,4},{7,5},{8,10},{9,11},{10,... | collective-permute-start | bytes 1179656 | tf_op jit(solution)/shard_map/ppermute | solution.py:474
  407.4 21.8 %collective-permute-start.44 = (bf16[32,6656]{1,0:T(8,128)(2,1)S(1)}, bf16[32,6656]{1,0:T(8,128)(2,1)S(1)}, u32[]{:S(2)}, u32[]{:S(2)}) collective-permute-start(bf16[32,6656]{1,0:T(8,128)(2,1)S(1)} %fusion.70), channel_id=1, source_target_pairs={{0,16},{4,20},{8,24},{12,28},{16,0},{20,4},{24,8},{28,12},{1,17},{... | collective-permute-start | bytes 1277960 | tf_op jit(solution)/shard_map/ppermute | solution.py:474
  (66 other events, 967.2 us)

commit v8 on v7

--- a/solution.py
+++ b/solution.py
@@ -995,12 +995,14 @@
         qkv_a.start("y")
         qkv_b.start("x")
         d_qkv = after(d_qkv, qkv_a.sent, qkv_b.sent)
-        d_a_one = against(d_qkv, qkv_w)
+        d_a_one = against(d_qkv[:, :across], qkv_w[:, :across])
+        qkv_b.advance(d_a_one).start("y")
+        qkv_a.advance(d_a_one).start("x")
+        d_qkv = after(d_qkv, qkv_b.sent, qkv_a.sent)
+        d_a_one = d_a_one + against(d_qkv[:, across:], qkv_w[:, across:])
         both.advance(d_a_one).start("w")
-        qkv_b.advance(both.sent).start("y")
-        qkv_a.advance(both.sent).start("x")
-        down_sum.advance(qkv_a.sent).start("y")
-        qkv_sum = qkv_a.advance(qkv_b.sent).beside(qkv_b.advance()).start("u")
+        down_sum.advance(both.sent).start("y")
+        qkv_sum = qkv_a.advance(both.sent).beside(qkv_b.advance(both.sent)).start("u")
         down_sum.advance(both.sent)
         qkv_sum.advance().start("w")
         both.advance()

time: 453 us -> 450 us (level)
    dot_general x10 -> x11, matrix products: 35.5 us -> 35.9 us  [dot(): lax.dot_general(left, right, (dims, ((), ())), preferred_element_type=jnp...]
    unnamed x116 -> x114, local copies, waits for them, and re-layouts: 14.6 us -> 14.5 us
where the time goes in v8:
time: 450 us; the launch traced here: 441 us
  Pallas kernels  184 us (41%)
  starting transfers between devices  63.5 us (14%)
  other arithmetic  54.7 us (12%)
  matrix products  45.4 us (10%)
  waiting for transfers between devices  43.6 us (10%)
  local copies, waits for them, and re-layouts  41.3 us (9%)
  between operations  9.06 us (2%)
    pallas_call x1, Pallas kernels, feed_forward(): pl.pallas_call(functools.partial(mlp_kernel, min(512, count), sums is Non...  69 us
    ppermute x43, starting transfers between devices, send(): return lax.ppermute(array, self.axis, pairs)  54.3 us
    ppermute x43, waiting for transfers between devices, send(): return lax.ppermute(array, self.axis, pairs)  43.5 us
    dot_general x11, matrix products, dot(): lax.dot_general(left, right, (dims, ((), ())), preferred_element_type=jnp...  35.9 us
    pallas_call x1, Pallas kernels, near_back(): self.call(kernel, groups, [at['x'], at['values'], at['narrow'], at['seg']...  32.1 us
    pallas_call x4, Pallas kernels, assemble(): pl.pallas_call(kernel, out_shape=[jax.ShapeDtypeStruct((shape.devices * b...  24.7 us
    concatenate x12, other arithmetic, along(): array = jnp.concatenate([self.array] + [a for a, _ in came], 0)  17 us
    unnamed x114, local copies, waits for them, and re-layouts  14.5 us
  transfers between devices with their start and end apart: 47, of which 14 were waited for; matrix products, arithmetic and copies ran while one was open for 27% of the time, Pallas kernels for 23%

profile of v8, /device:TPU:0, one launch (start us, length us, event | category | flops | bytes accessed | tf_op | source)
XLA Modules:
  0.0 441.2 jit_solution(9517630080671158232)
XLA Ops:
  2.5 3.1 collective-permute-start
  15.3 3.0 select_convert_fusion.1
  60.8 6.1 %assemble.4 = bf16[1024,1664]{1,0:T(8,128)(2,1)} custom-call(s32[64]{0:T(128)} %stack.856.places_ref, bf16[512,896]{1,0:T(8,128)(2,1)} %copy-done.12, bf16[512,896]{1,0:T(8,128)(2,1)} %collective-permute-done.5.refs_1_, bf16[512,768]{1,0:T(8,128)(2,1)} %copy-done.13, bf16[512,768]{1,0:T(8,128)(2,1)} %copy-done.25), custom_call_target="tpu_custom_call" | custom-call | bytes 6815744 | tf_op jit(solution)/shard_map/assemble/pallas_call | solution.py:546
  69.0 4.9 %convolution_convert_fusion.x_ref.refs_0_ = bf16[1024,1536]{1,0:T(8,128)(2,1)} fusion(bf16[1024,1024]{1,0:T(8,128)(2,1)S(1)} %fusion.3, bf16[1024,1664]{1,0:T(8,128)(2,1)S(1)} %copy-done.8), kind=kOutput, calls=%fused_computation.21 | convolution fusion | flops 3222798336 | bytes 8388608 | tf_op jit(solution)/shard_map/dot_general | solution.py:911
  77.2 8.7 %attn_tail.1 = bf16[2,2,656,128]{3,2,1,0:T(8,128)(2,1)} custom-call(bf16[1024,1536]{1,0:T(8,128)(2,1)} %convolution_convert_fusion.x_ref.refs_0_, s32[1024,1]{1,0:T(8,128)} %bitcast.302, bf16[1280,128]{1,0:T(8,128)(2,1)} %get-tuple-element.212.pick_ref), custom_call_target="tpu_custom_call" | custom-call | flops 10737418240 | bytes 2097152 | tf_op jit(solution)/shard_map/attn_tail/pallas_call | solution.py:354
  88.0 4.5 %collective-permute-start.18 = (bf16[2,2,656,128]{3,2,1,0:T(8,128)(2,1)}, bf16[2,2,656,128]{3,2,1,0:T(8,128)(2,1)}, u32[]{:S(2)}, u32[]{:S(2)}) collective-permute-start(bf16[2,2,656,128]{3,2,1,0:T(8,128)(2,1)} %attn_tail.1), channel_id=1, source_target_pairs={{0,2},{1,3},{4,6},{5,7},{8,10},{9,11},{12,14},{13,15},{16,18},{17,... | collective-permute-start | bytes 2015240 | tf_op jit(solution)/shard_map/ppermute | solution.py:430
  97.7 3.7 fusion.26
  103.5 10.9 %attn_near.1 = (f32[1024,1024]{1,0:T(8,128)}, f32[1024,1024]{1,0:T(8,128)}) custom-call(bf16[1024,1536]{1,0:T(8,128)(2,1)} %convolution_convert_fusion.x_ref.refs_0_, s32[1024,1]{1,0:T(8,128)} %bitcast.303, s32[2,1,512]{2,1,0:T(1,128)} %reshape.3219.refs_2_.refs_4_), custom_call_target="tpu_custom_call" | custom-call | flops 17179869184 | bytes 2097152 | tf_op jit(solution)/shard_map/attn_near/pallas_call | solution.py:365
  120.7 12.3 %attn_far.1 = (bf16[1024,1024]{1,0:T(8,128)(2,1)}, f32[1024,1024]{1,0:T(8,128)}) custom-call(bf16[1024,1536]{1,0:T(8,128)(2,1)} %convolution_convert_fusion.x_ref.refs_0_, s32[1024,1]{1,0:T(8,128)} %bitcast.304, bf16[2,2,656,128]{3,2,1,0:T(8,128)(2,1)} %add_convert_fusion.4.state_ref.refs_5_, f32[1024,1024]{1,0:T(8,128)} %get-tuple-element.112.top_ref, ...), custom_call_target="tpu_custom_call" | custom-call | flops 17179869184 | bytes 2097152 | tf_op jit(solution)/shard_map/attn_far/pallas_call | solution.py:372
  133.1 5.3 %fusion.23 = bf16[1024,1024]{1,0:T(8,128)(2,1)} fusion(bf16[1024,1024]{1,0:T(8,128)(2,1)} %get-tuple-element.113.y_ref, s32[1024]{0:T(1024)S(1)} %add.15402), kind=kOutput, calls=%fused_computation.45 | convolution fusion | flops 2150629376 | bytes 4198400 | tf_op jit(solution)/shard_map/dot_general | solution.py:22
  143.5 3.3 pad_maximum_fusion.refs_0_
  146.9 4.8 %collective-permute-start.21 = (bf16[512,3328]{1,0:T(8,128)(2,1)}, bf16[512,3328]{1,0:T(8,128)(2,1)}, u32[]{:S(2)}, u32[]{:S(2)}) collective-permute-start(bf16[512,3328]{1,0:T(8,128)(2,1)} %pad_maximum_fusion.refs_0_), channel_id=1, source_target_pairs={{0,1},{1,0},{2,3},{3,2},{4,5},{5,4},{6,7},{7,6},{8,9},{9,8},{10,11... | collective-permute-start | bytes 10223624 | tf_op jit(solution)/shard_map/ppermute | solution.py:474
  154.1 5.3 %fusion.32.gt_ref = bf16[1024,1024]{1,0:T(8,128)(2,1)} fusion(bf16[1024,1024]{1,0:T(8,128)(2,1)} %bitcast.314, s32[1024]{0:T(1024)S(1)} %add.15402), kind=kOutput, calls=%fused_computation.48 | convolution fusion | flops 2150629376 | bytes 4198400 | tf_op jit(solution)/shard_map/dot_general | solution.py:22
  161.8 5.3 %assemble.7.down_ref = bf16[1024,2816]{1,0:T(8,128)(2,1)} custom-call(s32[32]{0:T(128)} %stack.1055.places_ref, bf16[512,2816]{1,0:T(8,128)(2,1)} %constant_dynamic-update-slice_fusion.refs_0_, bf16[512,2816]{1,0:T(8,128)(2,1)} %collective-permute-done.25.refs_1_), custom_call_target="tpu_custom_call" | custom-call | bytes 11534336 | tf_op jit(solution)/shard_map/assemble/pallas_call | solution.py:546
  167.1 3.8 assemble.5
  170.9 4.7 %multiply_reduce_fusion = (f32[1024]{0:T(1024)S(1)}, f32[1024,1024]{1,0:T(8,128)S(1)}) fusion(bf16[1024,1024]{1,0:T(8,128)(2,1)} %get-tuple-element.113.y_ref, bf16[1024,1024]{1,0:T(8,128)(2,1)} %assemble.5, bf16[2,512,1024]{2,1,0:T(8,128)(2,1)S(1)} %copy-done.2), kind=kOutput, calls=%fused_computation.13 | convolution fusion | flops 2151676928 | bytes 10489856 | tf_op jit(solution)/shard_map/dot_general | solution.py:943
  178.9 3.7 fusion.29.at_ref
  182.6 9.5 %assemble.6 = (bf16[1024,2816]{1,0:T(8,128)(2,1)}, bf16[1024,2816]{1,0:T(8,128)(2,1)}) custom-call(s32[64]{0:T(128)} %stack.856.places_ref, bf16[512,3328]{1,0:T(8,128)(2,1)} %pad_maximum_fusion.refs_0_, bf16[512,3328]{1,0:T(8,128)(2,1)} %collective-permute-done.21.refs_1_, bf16[512,3328]{1,0:T(8,128)(2,1)} %copy-done, ...), custom_call_target="tpu_custom_call" | custom-call | bytes 23068672 | tf_op jit(solution)/shard_map/assemble/pallas_call | solution.py:546
  192.2 69.0 %mlp.1 = (bf16[1024,1024]{1,0:T(8,128)(2,1)}, bf16[1024,1024]{1,0:T(8,128)(2,1)}, f32[1024,1024]{1,0:T(8,128)}, bf16[3,512,2816]{2,1,0:T(8,128)(2,1)}, bf16[3,512,2816]{2,1,0:T(8,128)(2,1)}) custom-call(bf16[1024,1024]{1,0:T(8,128)(2,1)} %copy-done.15, bf16[1024,1024]{1,0:T(8,128)(2,1)} %bitcast.315, bf16[1024,1024]{1,0:T(8,128)(2,1)} %fusion.29.at_ref, ...), custom_call_target="tpu_custom_call" | custom-call | flops 53150220288 | bytes 55574528 | tf_op jit(solution)/shard_map/mlp/pallas_call | solution.py:821
  262.3 5.3 %convolution_convert_fusion.3.dy_ref = bf16[1024,1024]{1,0:T(8,128)(2,1)} fusion(bf16[1024,1024]{1,0:T(8,128)(2,1)} %get-tuple-element.126, bf16[1024,1024]{1,0:T(8,128)(2,1)S(1)} %copy-done.14), kind=kOutput, calls=%fused_computation.49 | convolution fusion | flops 2148532224 | bytes 6291456 | tf_op jit(solution)/shard_map/dot_general | solution.py:22
  267.6 11.8 %attn_head.1 = (bf16[2,2,656,128]{3,2,1,0:T(8,128)(2,1)}, bf16[1024,1024]{1,0:T(8,128)(2,1)}, bf16[1024,256]{1,0:T(8,128)(2,1)}) custom-call(bf16[1024,1536]{1,0:T(8,128)(2,1)} %convolution_convert_fusion.x_ref.refs_0_, bf16[1024,1024]{1,0:T(8,128)(2,1)} %convolution_convert_fusion.3.dy_ref, bf16[1024,1024]{1,0:T(8,128)(2,1)} %get-tuple-element.113.y_ref, ...), custom_call_target="tpu_custom_call" | custom-call | flops 10737418240 | bytes 2097152 | tf_op jit(solution)/shard_map/attn_head/pallas_call | solution.py:381
  284.8 3.1 fusion.90
  288.8 3.1 fusion.91
  295.2 3.7 collective-permute-start.31
  302.5 32.1 %attn_near_back.1 = (bf16[1024,256]{1,0:T(8,128)(2,1)}, f32[1024,256]{1,0:T(8,128)}, f32[1024,1024]{1,0:T(8,128)}) custom-call(bf16[1024,1536]{1,0:T(8,128)(2,1)} %convolution_convert_fusion.x_ref.refs_0_, bf16[1024,1024]{1,0:T(8,128)(2,1)} %get-tuple-element.128.refs_1_, bf16[1024,256]{1,0:T(8,128)(2,1)} %get-tuple-element.129.refs_2_, ...), custom_call_target="tpu_custom_call" | custom-call | flops 51539607552 | bytes 2097152 | tf_op jit(solution)/shard_map/attn_near_back/pallas_call | solution.py:394
  350.4 3.2 collective-permute-done.31
  360.0 14.3 %attn_far_back.1 = bf16[1024,1536]{1,0:T(8,128)(2,1)} custom-call(bf16[1024,1536]{1,0:T(8,128)(2,1)} %convolution_convert_fusion.x_ref.refs_0_, s32[1024,1]{1,0:T(8,128)} %bitcast.307, bf16[2,2,656,128]{3,2,1,0:T(8,128)(2,1)} %add_convert_fusion.3.state_ref, bf16[1024,256]{1,0:T(8,128)(2,1)} %get-tuple-element.130.dq_ref, ...), custom_call_target="tpu_custom_call" | custom-call | flops 19327352832 | bytes 2097152 | tf_op jit(solution)/shard_map/attn_far_back/pallas_call | solution.py:407
  374.2 4.1 convolution_convert_fusion.1
  383.7 3.8 collective-permute-start.40
  393.2 9.1 %collective-permute-done.38 = bf16[2,2,2,32,768]{4,3,1,2,0:T(8,128)(2,1)S(1)} collective-permute-done((bf16[2,2,2,32,768]{4,3,1,2,0:T(8,128)(2,1)S(1)}, bf16[2,2,2,32,768]{4,3,1,2,0:T(8,128)(2,1)S(1)}, u32[]{:S(2)}, u32[]{:S(2)}) %collective-permute-start.38) | collective-permute-done | bytes 393248 | tf_op jit(solution)/shard_map/ppermute | solution.py:474
  402.5 5.6 %collective-permute-done.37 = bf16[2,2,2,32,768]{4,3,1,2,0:T(8,128)(2,1)S(1)} collective-permute-done((bf16[2,2,2,32,768]{4,3,1,2,0:T(8,128)(2,1)S(1)}, bf16[2,2,2,32,768]{4,3,1,2,0:T(8,128)(2,1)S(1)}, u32[]{:S(2)}, u32[]{:S(2)}) %collective-permute-start.37) | collective-permute-done | bytes 393248 | tf_op jit(solution)/shard_map/ppermute | solution.py:474
  422.1 10.6 %collective-permute-done.42 = bf16[2,32,1536]{2,1,0:T(8,128)(2,1)S(1)} collective-permute-done((bf16[2,32,1536]{2,1,0:T(8,128)(2,1)S(1)}, bf16[2,32,1536]{2,1,0:T(8,128)(2,1)S(1)}, u32[]{:S(2)}, u32[]{:S(2)}) %collective-permute-start.42) | collective-permute-done | bytes 196640 | tf_op jit(solution)/shard_map/ppermute | solution.py:474
  (318 shorter events, 150.7 us)
Async XLA Ops:
  2.5 26.2 %collective-permute-start = (bf16[32,1664]{1,0:T(8,128)(2,1)S(1)}, bf16[32,1664]{1,0:T(8,128)(2,1)S(1)}, u32[]{:S(2)}, u32[]{:S(2)}) collective-permute-start(bf16[32,1664]{1,0:T(8,128)(2,1)S(1)} %pad_maximum_fusion.18), channel_id=1, source_target_pairs={{0,8},{4,12},{8,24},{12,28},{16,0},{20,4},{24,16},{28,20},{1,9},{5... | collective-permute-start | bytes 319496 | tf_op jit(solution)/shard_map/ppermute | solution.py:474
  5.5 24.3 %collective-permute-start.1 = (bf16[32,1664]{1,0:T(8,128)(2,1)S(1)}, bf16[32,1664]{1,0:T(8,128)(2,1)S(1)}, u32[]{:S(2)}, u32[]{:S(2)}) collective-permute-start(bf16[32,1664]{1,0:T(8,128)(2,1)S(1)} %pad_maximum_fusion.18), channel_id=1, source_target_pairs={{0,24},{4,28},{8,16},{12,20},{16,8},{20,12},{24,0},{28,4},{1,25},{... | collective-permute-start | bytes 319496 | tf_op jit(solution)/shard_map/ppermute | solution.py:474
  8.0 21.8 %collective-permute-start.2 = (bf16[32,1664]{1,0:T(8,128)(2,1)S(1)}, bf16[32,1664]{1,0:T(8,128)(2,1)S(1)}, u32[]{:S(2)}, u32[]{:S(2)}) collective-permute-start(bf16[32,1664]{1,0:T(8,128)(2,1)S(1)} %pad_maximum_fusion.18), channel_id=1, source_target_pairs={{0,16},{4,20},{8,0},{12,4},{16,24},{20,28},{24,8},{28,12},{1,17},{... | collective-permute-start | bytes 319496 | tf_op jit(solution)/shard_map/ppermute | solution.py:474
  13.2 37.7 %collective-permute-start.9 = (bf16[32,6656]{1,0:T(8,128)(2,1)}, bf16[32,6656]{1,0:T(8,128)(2,1)}, u32[]{:S(2)}, u32[]{:S(2)}) collective-permute-start(bf16[32,6656]{1,0:T(8,128)(2,1)} %pad_maximum_fusion.12), channel_id=1, source_target_pairs={{0,8},{4,12},{8,24},{12,28},{16,0},{20,4},{24,16},{28,20},{1,9},{5... | collective-permute-start | bytes 1277960 | tf_op jit(solution)/shard_map/ppermute | solution.py:474
  13.6 37.8 %collective-permute-start.10 = (bf16[32,6656]{1,0:T(8,128)(2,1)}, bf16[32,6656]{1,0:T(8,128)(2,1)}, u32[]{:S(2)}, u32[]{:S(2)}) collective-permute-start(bf16[32,6656]{1,0:T(8,128)(2,1)} %pad_maximum_fusion.12), channel_id=1, source_target_pairs={{0,24},{4,28},{8,16},{12,20},{16,8},{20,12},{24,0},{28,4},{1,25},{... | collective-permute-start | bytes 1277960 | tf_op jit(solution)/shard_map/ppermute | solution.py:474
  28.6 22.8 %collective-permute-start.11 = (bf16[32,6656]{1,0:T(8,128)(2,1)}, bf16[32,6656]{1,0:T(8,128)(2,1)}, u32[]{:S(2)}, u32[]{:S(2)}) collective-permute-start(bf16[32,6656]{1,0:T(8,128)(2,1)} %pad_maximum_fusion.12), channel_id=1, source_target_pairs={{0,16},{4,20},{8,0},{12,4},{16,24},{20,28},{24,8},{28,12},{1,17},{... | collective-permute-start | bytes 1277960 | tf_op jit(solution)/shard_map/ppermute | solution.py:474
  53.2 20.8 %collective-permute-start.13 = (bf16[64,2816]{1,0:T(8,128)(2,1)}, bf16[64,2816]{1,0:T(8,128)(2,1)}, u32[]{:S(2)}, u32[]{:S(2)}) collective-permute-start(bf16[64,2816]{1,0:T(8,128)(2,1)} %pad_maximum_fusion.14), channel_id=1, source_target_pairs={{0,2},{1,3},{2,0},{3,1},{4,6},{5,7},{6,4},{7,5},{8,10},{9,11},{10,... | collective-permute-start | bytes 1081352 | tf_op jit(solution)/shard_map/ppermute | solution.py:474
  57.2 35.4 %collective-permute-start.16 = (bf16[128,3328]{1,0:T(8,128)(2,1)}, bf16[128,3328]{1,0:T(8,128)(2,1)}, u32[]{:S(2)}, u32[]{:S(2)}) collective-permute-start(bf16[128,3328]{1,0:T(8,128)(2,1)} %get-tuple-element.193), channel_id=1, source_target_pairs={{0,2},{1,3},{2,0},{3,1},{4,6},{5,7},{6,4},{7,5},{8,10},{9,11},{10,... | collective-permute-start | bytes 2555912 | tf_op jit(solution)/shard_map/ppermute | solution.py:474
  57.7 36.5 %collective-permute-start.15 = (bf16[128,3328]{1,0:T(8,128)(2,1)S(1)}, bf16[128,3328]{1,0:T(8,128)(2,1)}, u32[]{:S(2)}, u32[]{:S(2)}) collective-permute-start(bf16[128,3328]{1,0:T(8,128)(2,1)S(1)} %get-tuple-element.194), channel_id=1, source_target_pairs={{0,4},{4,0},{8,12},{12,8},{16,20},{20,16},{24,28},{28,24},{1,5},{5... | collective-permute-start | bytes 2555912 | tf_op jit(solution)/shard_map/ppermute | solution.py:474
  75.8 25.6 %collective-permute-start.17 = (bf16[128,2816]{1,0:T(8,128)(2,1)}, bf16[128,2816]{1,0:T(8,128)(2,1)S(1)}, u32[]{:S(2)}, u32[]{:S(2)}) collective-permute-start(bf16[128,2816]{1,0:T(8,128)(2,1)} %pad_maximum_fusion.9), channel_id=1, source_target_pairs={{0,8},{4,12},{8,24},{12,28},{16,0},{20,4},{24,16},{28,20},{1,9},{5... | collective-permute-start | bytes 2162696 | tf_op jit(solution)/shard_map/ppermute | solution.py:474
  85.9 28.4 %collective-permute-start.14 = (bf16[2,2,656,128]{3,2,1,0:T(8,128)(2,1)}, bf16[2,2,656,128]{3,2,1,0:T(8,128)(2,1)}, u32[]{:S(2)}, u32[]{:S(2)}) collective-permute-start(bf16[2,2,656,128]{3,2,1,0:T(8,128)(2,1)} %attn_tail.1), channel_id=1, source_target_pairs={{0,1},{1,2},{2,3},{4,5},{5,6},{6,7},{8,9},{9,10},{10,11},{12,13},{... | collective-permute-start | bytes 2015240 | tf_op jit(solution)/shard_map/ppermute | solution.py:430
  88.0 26.3 %collective-permute-start.18 = (bf16[2,2,656,128]{3,2,1,0:T(8,128)(2,1)}, bf16[2,2,656,128]{3,2,1,0:T(8,128)(2,1)}, u32[]{:S(2)}, u32[]{:S(2)}) collective-permute-start(bf16[2,2,656,128]{3,2,1,0:T(8,128)(2,1)} %attn_tail.1), channel_id=1, source_target_pairs={{0,2},{1,3},{4,6},{5,7},{8,10},{9,11},{12,14},{13,15},{16,18},{17,... | collective-permute-start | bytes 2015240 | tf_op jit(solution)/shard_map/ppermute | solution.py:430
  95.4 43.0 %collective-permute-start.22 = (bf16[256,3328]{1,0:T(8,128)(2,1)S(1)}, bf16[256,3328]{1,0:T(8,128)(2,1)}, u32[]{:S(2)}, u32[]{:S(2)}) collective-permute-start(bf16[256,3328]{1,0:T(8,128)(2,1)S(1)} %pad_maximum_fusion.5), channel_id=1, source_target_pairs={{0,4},{4,0},{8,12},{12,8},{16,20},{20,16},{24,28},{28,24},{1,5},{5... | collective-permute-start | bytes 5111816 | tf_op jit(solution)/shard_map/ppermute | solution.py:474
  96.0 47.6 %collective-permute-start.20 = (bf16[256,3328]{1,0:T(8,128)(2,1)S(1)}, bf16[256,3328]{1,0:T(8,128)(2,1)}, u32[]{:S(2)}, u32[]{:S(2)}) collective-permute-start(bf16[256,3328]{1,0:T(8,128)(2,1)S(1)} %pad_maximum_fusion.4), channel_id=1, source_target_pairs={{0,2},{1,3},{2,0},{3,1},{4,6},{5,7},{6,4},{7,5},{8,10},{9,11},{10,... | collective-permute-start | bytes 5111816 | tf_op jit(solution)/shard_map/ppermute | solution.py:474
  101.4 18.2 %collective-permute-start.19 = (bf16[128,2816]{1,0:T(8,128)(2,1)S(1)}, bf16[128,2816]{1,0:T(8,128)(2,1)S(1)}, u32[]{:S(2)}, u32[]{:S(2)}) collective-permute-start(bf16[128,2816]{1,0:T(8,128)(2,1)S(1)} %collective-permute-done.17), channel_id=1, source_target_pairs={{0,8},{4,12},{8,24},{12,28},{16,0},{20,4},{24,16},{28,20},{1,9},{5... | collective-permute-start | bytes 2162696 | tf_op jit(solution)/shard_map/ppermute | solution.py:474
  119.6 33.0 %collective-permute-start.24 = (bf16[128,2816]{1,0:T(8,128)(2,1)S(1)}, bf16[128,2816]{1,0:T(8,128)(2,1)S(1)}, u32[]{:S(2)}, u32[]{:S(2)}) collective-permute-start(bf16[128,2816]{1,0:T(8,128)(2,1)S(1)} %collective-permute-done.19), channel_id=1, source_target_pairs={{0,8},{4,12},{8,24},{12,28},{16,0},{20,4},{24,16},{28,20},{1,9},{5... | collective-permute-start | bytes 2162696 | tf_op jit(solution)/shard_map/ppermute | solution.py:474
  140.5 26.5 %collective-permute-start.23 = (bf16[512,3328]{1,0:T(8,128)(2,1)S(1)}, bf16[512,3328]{1,0:T(8,128)(2,1)}, u32[]{:S(2)}, u32[]{:S(2)}) collective-permute-start(bf16[512,3328]{1,0:T(8,128)(2,1)S(1)} %pad_maximum_fusion.1.refs_2_), channel_id=1, source_target_pairs={{0,1},{1,0},{2,3},{3,2},{4,5},{5,4},{6,7},{7,6},{8,9},{9,8},{10,11... | collective-permute-start | bytes 10223624 | tf_op jit(solution)/shard_map/ppermute | solution.py:474
  146.9 20.2 %collective-permute-start.21 = (bf16[512,3328]{1,0:T(8,128)(2,1)}, bf16[512,3328]{1,0:T(8,128)(2,1)}, u32[]{:S(2)}, u32[]{:S(2)}) collective-permute-start(bf16[512,3328]{1,0:T(8,128)(2,1)} %pad_maximum_fusion.refs_0_), channel_id=1, source_target_pairs={{0,1},{1,0},{2,3},{3,2},{4,5},{5,4},{6,7},{7,6},{8,9},{9,8},{10,11... | collective-permute-start | bytes 10223624 | tf_op jit(solution)/shard_map/ppermute | solution.py:474
  261.3 27.6 %collective-permute-start.27 = (bf16[3,512,2816]{2,1,0:T(8,128)(2,1)}, bf16[3,512,2816]{2,1,0:T(8,128)(2,1)}, u32[]{:S(2)}, u32[]{:S(2)}) collective-permute-start(bf16[3,512,2816]{2,1,0:T(8,128)(2,1)} %get-tuple-element.125), channel_id=1, source_target_pairs={{0,1},{1,0},{2,3},{3,2},{4,5},{5,4},{6,7},{7,6},{8,9},{9,8},{10,11... | collective-permute-start | bytes 25952264 | tf_op jit(solution)/shard_map/ppermute | solution.py:474
  282.2 52.4 %collective-permute-start.26 = (bf16[2,2,656,128]{3,2,1,0:T(8,128)(2,1)}, bf16[2,2,656,128]{3,2,1,0:T(8,128)(2,1)}, u32[]{:S(2)}, u32[]{:S(2)}) collective-permute-start(bf16[2,2,656,128]{3,2,1,0:T(8,128)(2,1)} %get-tuple-element.122), channel_id=1, source_target_pairs={{1,0},{2,1},{3,2},{5,4},{6,5},{7,6},{9,8},{10,9},{11,10},{13,12},{... | collective-permute-start | bytes 2015240 | tf_op jit(solution)/shard_map/ppermute | solution.py:430
  283.5 51.1 %collective-permute-start.29 = (bf16[2,2,656,128]{3,2,1,0:T(8,128)(2,1)}, bf16[2,2,656,128]{3,2,1,0:T(8,128)(2,1)}, u32[]{:S(2)}, u32[]{:S(2)}) collective-permute-start(bf16[2,2,656,128]{3,2,1,0:T(8,128)(2,1)} %get-tuple-element.122), channel_id=1, source_target_pairs={{2,0},{3,1},{6,4},{7,5},{10,8},{11,9},{14,12},{15,13},{18,16},{19,... | collective-permute-start | bytes 2015240 | tf_op jit(solution)/shard_map/ppermute | solution.py:430
  294.6 42.4 %collective-permute-start.32 = (bf16[2,2,2,32,2816]{4,3,1,2,0:T(8,128)(2,1)S(1)}, bf16[2,2,2,32,2816]{4,3,1,2,0:T(8,128)(2,1)S(1)}, u32[]{:S(2)}, u32[]{:S(2)}) collective-permute-start(bf16[2,2,2,32,2816]{4,3,1,2,0:T(8,128)(2,1)S(1)} %fusion.40), channel_id=1, source_target_pairs={{0,4},{4,0},{8,12},{12,8},{16,20},{20,16},{24,28},{28,24},{1,5},{5... | collective-permute-start | bytes 4325384 | tf_op jit(solution)/shard_map/ppermute | solution.py:474
  295.2 58.4 %collective-permute-start.31 = (bf16[2,2,2,32,3840]{4,3,1,2,0:T(8,128)(2,1)S(1)}, bf16[2,2,2,32,3840]{4,3,1,2,0:T(8,128)(2,1)S(1)}, u32[]{:S(2)}, u32[]{:S(2)}) collective-permute-start(bf16[2,2,2,32,3840]{4,3,1,2,0:T(8,128)(2,1)S(1)} %copy.2219), channel_id=1, source_target_pairs={{0,2},{1,3},{2,0},{3,1},{4,6},{5,7},{6,4},{7,5},{8,10},{9,11},{10,... | collective-permute-start | bytes 5898248 | tf_op jit(solution)/shard_map/ppermute | solution.py:474
  300.4 40.7 %collective-permute-start.30 = (bf16[2,2,2,32,2816]{4,3,0,1,2:T(8,128)(2,1)}, bf16[2,2,2,32,2816]{4,3,0,1,2:T(8,128)(2,1)S(1)}, u32[]{:S(2)}, u32[]{:S(2)}) collective-permute-start(bf16[2,2,2,32,2816]{4,3,0,1,2:T(8,128)(2,1)} %fusion.41), channel_id=1, source_target_pairs={{0,8},{4,12},{8,0},{12,4},{16,24},{20,28},{24,16},{28,20},{1,9},{5... | collective-permute-start | bytes 4325384 | tf_op jit(solution)/shard_map/ppermute | solution.py:474
  346.7 33.7 %collective-permute-start.36 = (bf16[2,2,32,2816]{3,2,0,1:T(8,128)(2,1)}, bf16[2,2,32,2816]{3,2,0,1:T(8,128)(2,1)}, u32[]{:S(2)}, u32[]{:S(2)}) collective-permute-start(bf16[2,2,32,2816]{3,2,0,1:T(8,128)(2,1)} %fusion.49), channel_id=1, source_target_pairs={{0,2},{1,3},{2,0},{3,1},{4,6},{5,7},{6,4},{7,5},{8,10},{9,11},{10,... | collective-permute-start | bytes 2162696 | tf_op jit(solution)/shard_map/ppermute | solution.py:474
  348.5 39.0 %collective-permute-start.34 = (bf16[2,2,32,2816]{3,2,0,1:T(8,128)(2,1)}, bf16[2,2,32,2816]{3,2,0,1:T(8,128)(2,1)}, u32[]{:S(2)}, u32[]{:S(2)}) collective-permute-start(bf16[2,2,32,2816]{3,2,0,1:T(8,128)(2,1)} %fusion.48), channel_id=1, source_target_pairs={{0,16},{4,20},{8,24},{12,28},{16,0},{20,4},{24,8},{28,12},{1,17},{... | collective-permute-start | bytes 2162696 | tf_op jit(solution)/shard_map/ppermute | solution.py:474
  360.0 23.5 %collective-permute-start.35 = (bf16[2,2,32,3840]{3,2,0,1:T(8,128)(2,1)}, bf16[2,2,32,3840]{3,2,0,1:T(8,128)(2,1)S(1)}, u32[]{:S(2)}, u32[]{:S(2)}) collective-permute-start(bf16[2,2,32,3840]{3,2,0,1:T(8,128)(2,1)} %fusion.47), channel_id=1, source_target_pairs={{0,4},{4,0},{8,12},{12,8},{16,20},{20,16},{24,28},{28,24},{1,5},{5... | collective-permute-start | bytes 2949128 | tf_op jit(solution)/shard_map/ppermute | solution.py:474
  383.7 28.8 %collective-permute-start.40 = (bf16[2,32,6656]{2,1,0:T(8,128)(2,1)S(1)}, bf16[2,32,6656]{2,1,0:T(8,128)(2,1)S(1)}, u32[]{:S(2)}, u32[]{:S(2)}) collective-permute-start(bf16[2,32,6656]{2,1,0:T(8,128)(2,1)S(1)} %pad_maximum_fusion.7), channel_id=1, source_target_pairs={{0,8},{4,12},{8,0},{12,4},{16,24},{20,28},{24,16},{28,20},{1,9},{5... | collective-permute-start | bytes 2555912 | tf_op jit(solution)/shard_map/ppermute | solution.py:474
  388.8 26.2 %collective-permute-start.45 = (bf16[2,32,2816]{2,1,0:T(8,128)(2,1)S(1)}, bf16[2,32,2816]{2,1,0:T(8,128)(2,1)S(1)}, u32[]{:S(2)}, u32[]{:S(2)}) collective-permute-start(bf16[2,32,2816]{2,1,0:T(8,128)(2,1)S(1)} %fusion.76), channel_id=1, source_target_pairs={{0,4},{4,0},{8,12},{12,8},{16,20},{20,16},{24,28},{28,24},{1,5},{5... | collective-permute-start | bytes 1081352 | tf_op jit(solution)/shard_map/ppermute | solution.py:474
  391.2 16.9 %collective-permute-start.37 = (bf16[2,2,2,32,768]{4,3,1,2,0:T(8,128)(2,1)S(1)}, bf16[2,2,2,32,768]{4,3,1,2,0:T(8,128)(2,1)S(1)}, u32[]{:S(2)}, u32[]{:S(2)}) collective-permute-start(bf16[2,2,2,32,768]{4,3,1,2,0:T(8,128)(2,1)S(1)} %fusion.74), channel_id=1, source_target_pairs={{0,4},{4,0},{8,12},{12,8},{16,20},{20,16},{24,28},{28,24},{1,5},{5... | collective-permute-start | bytes 1179656 | tf_op jit(solution)/shard_map/ppermute | solution.py:474
  408.2 12.5 %collective-permute-start.39 = (bf16[2,2,32,768]{3,2,0,1:T(8,128)(2,1)S(1)}, bf16[2,2,32,768]{3,2,0,1:T(8,128)(2,1)S(1)}, u32[]{:S(2)}, u32[]{:S(2)}) collective-permute-start(bf16[2,2,32,768]{3,2,0,1:T(8,128)(2,1)S(1)} %fusion.79), channel_id=1, source_target_pairs={{0,4},{4,0},{8,12},{12,8},{16,20},{20,16},{24,28},{28,24},{1,5},{5... | collective-permute-start | bytes 589832 | tf_op jit(solution)/shard_map/ppermute | solution.py:474
  412.9 22.2 %collective-permute-start.44 = (bf16[32,6656]{1,0:T(8,128)(2,1)S(1)}, bf16[32,6656]{1,0:T(8,128)(2,1)S(1)}, u32[]{:S(2)}, u32[]{:S(2)}) collective-permute-start(bf16[32,6656]{1,0:T(8,128)(2,1)S(1)} %fusion.73), channel_id=1, source_target_pairs={{0,16},{4,20},{8,24},{12,28},{16,0},{20,4},{24,8},{28,12},{1,17},{... | collective-permute-start | bytes 1277960 | tf_op jit(solution)/shard_map/ppermute | solution.py:474
  (65 other events, 950.0 us)

commit v9 on v8

--- a/solution.py
+++ b/solution.py
@@ -691,20 +691,33 @@
         self.parts = self.parts + other.parts
         return self
 
-    def term_of(self, step):
-        found = []
+    def piece(self, array, number, step):
+        low, high = [0] * array.ndim, list(array.shape)
+        for axis, place in ((0, number), (self.axis + 1, step)):
+            low[axis], high[axis] = place, place + 1
+        rest = array.shape[1 : self.axis + 1] + array.shape[self.axis + 2 :]
+        return lax.slice(array, low, high).reshape(rest)
+
+    def terms_of(self, step, came=None):
+        found, begin = [], 0
         for terms in self.parts:
-            own = [lax.index_in_dim(t[i], step, self.axis, False) for t, i in terms]
+            own = [self.piece(t, i, step) for t, i in terms]
+            end = begin + own[0].shape[-1]
+            own += [] if came is None else [came[..., begin:end]]
             found.append(functools.reduce(jnp.add, [t.astype(jnp.float32) for t in own]))
-        return jnp.concatenate(found, axis=-1)
+            begin = end
+        return found
+
+    def go(self, terms):
+        self.sent = jnp.concatenate([t.astype(jnp.bfloat16) for t in terms], axis=-1)
+        self.came = self.line.send(self.sent)
 
     def start(self, dim, *hold):
         self.line, self.axis, self.step = self.shape.lines[dim], self.dims.index(dim), 1
         self.dims = self.dims.replace(dim, "")
         if hold:
             self.parts = [[(after(t, *hold), i) for t, i in terms] for terms in self.parts]
-        self.sent = self.term_of(1).astype(jnp.bfloat16)
-        self.came = self.line.send(self.sent)
+        self.go(self.terms_of(1))
         return self
 
     def advance(self, *hold):
@@ -712,12 +725,11 @@
         came, *flat = lax.optimization_barrier((self.came, *flat, *hold))[: len(flat) + 1]
         self.parts = [[(flat.pop(0), i) for _, i in terms] for terms in self.parts]
         self.step += 1
-        total = self.term_of(self.step % self.line.count) + came.astype(jnp.float32)
+        totals = self.terms_of(self.step % self.line.count, came)
         if self.step < self.line.count:
-            self.sent = total.astype(jnp.bfloat16)
-            self.came = self.line.send(self.sent)
+            self.go(totals)
         else:
-            self.parts, self.came = [[(total[None], 0)]], None
+            self.parts, self.came = [[(total[None], 0)] for total in totals], None
         return self
 
     def along(self, dim):
@@ -1007,12 +1019,10 @@
         qkv_sum.advance().start("w")
         both.advance()
         qkv_sum.advance()
-        grad_qkv, both, down_sum = (part.parts[0][0][0][0] for part in (qkv_sum, both, down_sum))
-        grad_qkv = [grad_qkv[:, g * across : (g + 1) * across] for g in range(groups)]
-        padded = tiles * FF_TILE
-        grad_gate, grad_out = both[:, :hidden], both[:, padded : padded + width]
-        grad_up = both[:, padded + width : padded + width + hidden]
-        grad_down = down_sum[:, :hidden]
+        grad_qkv = [terms[0][0][0] for terms in qkv_sum.parts]
+        grad_gate, grad_out, grad_up = (terms[0][0][0] for terms in both.parts)
+        grad_down = down_sum.parts[0][0][0][0][:, :hidden]
+        grad_gate, grad_up = grad_gate[:, :hidden], grad_up[:, :hidden]
     else:
         later = states.end()
         d_near = attention.near_back(qkv, d_top, d_den, seg, seg_row, earlier)

time: 450 us -> 449 us (level)
  local copies, waits for them, and re-layouts: 41.3 us -> 24.1 us
  waiting for transfers between devices: 43.6 us -> 53.7 us
  other arithmetic: 54.7 us -> 62.8 us
    broadcast_in_dim x0 -> x16, other arithmetic: none -> 13.1 us  [advance(): self.parts, self.came = ([[(total[None], 0)] for total in totals], None)]
    ppermute x43, waiting for transfers between devices: 43.5 us -> 53.7 us  [send(): return lax.ppermute(array, self.axis, pairs)]
    add x16 -> x4, other arithmetic: 9.37 us -> 0.76 us  [terms_of(): functools.reduce(jnp.add, [t.astype(jnp.float32) for t in own])]
    squeeze x13 -> x0, local copies, waits for them, and re-layouts: 8.32 us -> none  [term_of(): own = [lax.index_in_dim(t[i], step, self.axis, False) for t, i in terms]]
    slice x4 -> x1, local copies, waits for them, and re-layouts: 6.83 us -> 0.02 us  [terms_of(): own += [] if came is None else [came[..., begin:end]]]
    convert_element_type x4 -> x6, other arithmetic: 2 us -> 6.72 us  [go(): t.astype(jnp.bfloat16)]
    unnamed x114 -> x118, local copies, waits for them, and re-layouts: 14.5 us -> 13.5 us
  transfers between devices with their start and end apart: 47 -> 47, of which waited for: 14 -> 14; matrix products, arithmetic and copies ran while one was open for 27% -> 26% of each run, Pallas kernels for 23% -> 23%
where the time goes in v9:
time: 449 us; the launch traced here: 440 us
  Pallas kernels  183 us (41%)
  other arithmetic  62.8 us (14%)
  starting transfers between devices  61.9 us (14%)
  waiting for transfers between devices  53.7 us (12%)
  matrix products  45.3 us (10%)
  local copies, waits for them, and re-layouts  24.1 us (5%)
  between operations  9.06 us (2%)
    pallas_call x1, Pallas kernels, feed_forward(): pl.pallas_call(functools.partial(mlp_kernel, min(512, count), sums is Non...  69 us
    ppermute x43, waiting for transfers between devices, send(): return lax.ppermute(array, self.axis, pairs)  53.7 us
    ppermute x43, starting transfers between devices, send(): return lax.ppermute(array, self.axis, pairs)  52.1 us
    dot_general x11, matrix products, dot(): lax.dot_general(left, right, (dims, ((), ())), preferred_element_type=jnp...  35.8 us
    pallas_call x1, Pallas kernels, near_back(): self.call(kernel, groups, [at['x'], at['values'], at['narrow'], at['seg']...  32.1 us
    pallas_call x4, Pallas kernels, assemble(): pl.pallas_call(kernel, out_shape=[jax.ShapeDtypeStruct((shape.devices * b...  24.7 us
    concatenate x12, other arithmetic, along(): array = jnp.concatenate([self.array] + [a for a, _ in came], 0)  17 us
    pallas_call x1, Pallas kernels, far_back(): self.call(far_back_kernel, groups, [at['x'], at['seg'], at['state'], at['...  14.2 us
  transfers between devices with their start and end apart: 47, of which 14 were waited for; matrix products, arithmetic and copies ran while one was open for 26% of the time, Pallas kernels for 23%

profile of v9, /device:TPU:0, one launch (start us, length us, event | category | flops | bytes accessed | tf_op | source)
XLA Modules:
  0.0 440.1 jit_solution(9452377273320012233)
XLA Ops:
  2.5 3.1 collective-permute-start
  15.3 3.0 select_convert_fusion.1
  60.8 6.1 %assemble.4 = bf16[1024,1664]{1,0:T(8,128)(2,1)} custom-call(s32[64]{0:T(128)} %stack.856.places_ref, bf16[512,896]{1,0:T(8,128)(2,1)} %copy-done.12, bf16[512,896]{1,0:T(8,128)(2,1)} %collective-permute-done.5.refs_1_, bf16[512,768]{1,0:T(8,128)(2,1)} %copy-done.13, bf16[512,768]{1,0:T(8,128)(2,1)} %copy-done.26), custom_call_target="tpu_custom_call" | custom-call | bytes 6815744 | tf_op jit(solution)/shard_map/assemble/pallas_call | solution.py:546
  69.0 4.8 %convolution_convert_fusion.x_ref.refs_0_ = bf16[1024,1536]{1,0:T(8,128)(2,1)} fusion(bf16[1024,1024]{1,0:T(8,128)(2,1)S(1)} %fusion.3, bf16[1024,1664]{1,0:T(8,128)(2,1)S(1)} %copy-done.8), kind=kOutput, calls=%fused_computation.20 | convolution fusion | flops 3222798336 | bytes 8388608 | tf_op jit(solution)/shard_map/dot_general | solution.py:923
  77.2 8.7 %attn_tail.1 = bf16[2,2,656,128]{3,2,1,0:T(8,128)(2,1)} custom-call(bf16[1024,1536]{1,0:T(8,128)(2,1)} %convolution_convert_fusion.x_ref.refs_0_, s32[1024,1]{1,0:T(8,128)} %bitcast.346, bf16[1280,128]{1,0:T(8,128)(2,1)} %get-tuple-element.220.pick_ref), custom_call_target="tpu_custom_call" | custom-call | flops 10737418240 | bytes 2097152 | tf_op jit(solution)/shard_map/attn_tail/pallas_call | solution.py:354
  88.0 4.5 %collective-permute-start.18 = (bf16[2,2,656,128]{3,2,1,0:T(8,128)(2,1)}, bf16[2,2,656,128]{3,2,1,0:T(8,128)(2,1)}, u32[]{:S(2)}, u32[]{:S(2)}) collective-permute-start(bf16[2,2,656,128]{3,2,1,0:T(8,128)(2,1)} %attn_tail.1), channel_id=1, source_target_pairs={{0,2},{1,3},{4,6},{5,7},{8,10},{9,11},{12,14},{13,15},{16,18},{17,... | collective-permute-start | bytes 2015240 | tf_op jit(solution)/shard_map/ppermute | solution.py:430
  97.7 3.7 fusion.29
  103.5 10.8 %attn_near.1 = (f32[1024,1024]{1,0:T(8,128)}, f32[1024,1024]{1,0:T(8,128)}) custom-call(bf16[1024,1536]{1,0:T(8,128)(2,1)} %convolution_convert_fusion.x_ref.refs_0_, s32[1024,1]{1,0:T(8,128)} %bitcast.347, s32[2,1,512]{2,1,0:T(1,128)} %reshape.3274.refs_2_.refs_4_), custom_call_target="tpu_custom_call" | custom-call | flops 17179869184 | bytes 2097152 | tf_op jit(solution)/shard_map/attn_near/pallas_call | solution.py:365
  120.8 12.3 %attn_far.1 = (bf16[1024,1024]{1,0:T(8,128)(2,1)}, f32[1024,1024]{1,0:T(8,128)}) custom-call(bf16[1024,1536]{1,0:T(8,128)(2,1)} %convolution_convert_fusion.x_ref.refs_0_, s32[1024,1]{1,0:T(8,128)} %bitcast.348, bf16[2,2,656,128]{3,2,1,0:T(8,128)(2,1)} %add_convert_fusion.4.state_ref.refs_5_, f32[1024,1024]{1,0:T(8,128)} %get-tuple-element.117.top_ref, ...), custom_call_target="tpu_custom_call" | custom-call | flops 17179869184 | bytes 2097152 | tf_op jit(solution)/shard_map/attn_far/pallas_call | solution.py:372
  133.1 5.3 %fusion.26 = bf16[1024,1024]{1,0:T(8,128)(2,1)} fusion(bf16[1024,1024]{1,0:T(8,128)(2,1)} %get-tuple-element.118.y_ref, s32[1024]{0:T(1024)S(1)} %add.15422), kind=kOutput, calls=%fused_computation.41 | convolution fusion | flops 2150629376 | bytes 4198400 | tf_op jit(solution)/shard_map/dot_general | solution.py:22
  143.5 3.3 pad_maximum_fusion.refs_0_
  146.8 4.8 %collective-permute-start.21 = (bf16[512,3328]{1,0:T(8,128)(2,1)}, bf16[512,3328]{1,0:T(8,128)(2,1)}, u32[]{:S(2)}, u32[]{:S(2)}) collective-permute-start(bf16[512,3328]{1,0:T(8,128)(2,1)} %pad_maximum_fusion.refs_0_), channel_id=1, source_target_pairs={{0,1},{1,0},{2,3},{3,2},{4,5},{5,4},{6,7},{7,6},{8,9},{9,8},{10,11... | collective-permute-start | bytes 10223624 | tf_op jit(solution)/shard_map/ppermute | solution.py:474
  154.1 5.3 %fusion.35.gt_ref = bf16[1024,1024]{1,0:T(8,128)(2,1)} fusion(bf16[1024,1024]{1,0:T(8,128)(2,1)} %bitcast.358, s32[1024]{0:T(1024)S(1)} %add.15422), kind=kOutput, calls=%fused_computation.44 | convolution fusion | flops 2150629376 | bytes 4198400 | tf_op jit(solution)/shard_map/dot_general | solution.py:22
  161.7 5.4 %assemble.7.down_ref = bf16[1024,2816]{1,0:T(8,128)(2,1)} custom-call(s32[32]{0:T(128)} %stack.1055.places_ref, bf16[512,2816]{1,0:T(8,128)(2,1)} %constant_dynamic-update-slice_fusion.refs_0_, bf16[512,2816]{1,0:T(8,128)(2,1)} %collective-permute-done.25.refs_1_), custom_call_target="tpu_custom_call" | custom-call | bytes 11534336 | tf_op jit(solution)/shard_map/assemble/pallas_call | solution.py:546
  167.2 3.8 assemble.5
  171.0 4.7 %multiply_reduce_fusion = (f32[1024]{0:T(1024)S(1)}, f32[1024,1024]{1,0:T(8,128)S(1)}) fusion(bf16[1024,1024]{1,0:T(8,128)(2,1)} %get-tuple-element.118.y_ref, bf16[1024,1024]{1,0:T(8,128)(2,1)} %assemble.5, bf16[2,512,1024]{2,1,0:T(8,128)(2,1)S(1)} %copy-done.2), kind=kOutput, calls=%fused_computation.13 | convolution fusion | flops 2151676928 | bytes 10489856 | tf_op jit(solution)/shard_map/dot_general | solution.py:955
  179.0 3.7 fusion.32.at_ref
  182.7 9.4 %assemble.6 = (bf16[1024,2816]{1,0:T(8,128)(2,1)}, bf16[1024,2816]{1,0:T(8,128)(2,1)}) custom-call(s32[64]{0:T(128)} %stack.856.places_ref, bf16[512,3328]{1,0:T(8,128)(2,1)} %pad_maximum_fusion.refs_0_, bf16[512,3328]{1,0:T(8,128)(2,1)} %collective-permute-done.21.refs_1_, bf16[512,3328]{1,0:T(8,128)(2,1)} %copy-done, ...), custom_call_target="tpu_custom_call" | custom-call | bytes 23068672 | tf_op jit(solution)/shard_map/assemble/pallas_call | solution.py:546
  192.2 69.0 %mlp.1 = (bf16[1024,1024]{1,0:T(8,128)(2,1)}, bf16[1024,1024]{1,0:T(8,128)(2,1)}, f32[1024,1024]{1,0:T(8,128)}, bf16[3,512,2816]{2,1,0:T(8,128)(2,1)}, bf16[3,512,2816]{2,1,0:T(8,128)(2,1)}) custom-call(bf16[1024,1024]{1,0:T(8,128)(2,1)} %copy-done.15, bf16[1024,1024]{1,0:T(8,128)(2,1)} %bitcast.359, bf16[1024,1024]{1,0:T(8,128)(2,1)} %fusion.32.at_ref, ...), custom_call_target="tpu_custom_call" | custom-call | flops 53150220288 | bytes 55574528 | tf_op jit(solution)/shard_map/mlp/pallas_call | solution.py:833
  261.6 5.3 %convolution_convert_fusion.3.dy_ref = bf16[1024,1024]{1,0:T(8,128)(2,1)} fusion(bf16[1024,1024]{1,0:T(8,128)(2,1)} %get-tuple-element.131, bf16[1024,1024]{1,0:T(8,128)(2,1)S(1)} %copy-done.14), kind=kOutput, calls=%fused_computation.45 | convolution fusion | flops 2148532224 | bytes 6291456 | tf_op jit(solution)/shard_map/dot_general | solution.py:22
  266.8 11.3 %attn_head.1 = (bf16[2,2,656,128]{3,2,1,0:T(8,128)(2,1)}, bf16[1024,1024]{1,0:T(8,128)(2,1)}, bf16[1024,256]{1,0:T(8,128)(2,1)}) custom-call(bf16[1024,1536]{1,0:T(8,128)(2,1)} %convolution_convert_fusion.x_ref.refs_0_, bf16[1024,1024]{1,0:T(8,128)(2,1)} %convolution_convert_fusion.3.dy_ref, bf16[1024,1024]{1,0:T(8,128)(2,1)} %get-tuple-element.118.y_ref, ...), custom_call_target="tpu_custom_call" | custom-call | flops 10737418240 | bytes 2097152 | tf_op jit(solution)/shard_map/attn_head/pallas_call | solution.py:381
  285.5 2.9 fusion.45
  293.9 2.9 collective-permute-start.31
  298.9 32.1 %attn_near_back.1 = (bf16[1024,256]{1,0:T(8,128)(2,1)}, f32[1024,256]{1,0:T(8,128)}, f32[1024,1024]{1,0:T(8,128)}) custom-call(bf16[1024,1536]{1,0:T(8,128)(2,1)} %convolution_convert_fusion.x_ref.refs_0_, bf16[1024,1024]{1,0:T(8,128)(2,1)} %get-tuple-element.133.refs_1_, bf16[1024,256]{1,0:T(8,128)(2,1)} %get-tuple-element.134.refs_2_, ...), custom_call_target="tpu_custom_call" | custom-call | flops 51539607552 | bytes 2097152 | tf_op jit(solution)/shard_map/attn_near_back/pallas_call | solution.py:394
  336.6 2.7 fusion.21
  342.1 13.9 %collective-permute-done.31 = bf16[2,2,2,32,3840]{4,3,1,2,0:T(8,128)(2,1)S(1)} collective-permute-done((bf16[2,2,2,32,3840]{4,3,1,2,0:T(8,128)(2,1)}, bf16[2,2,2,32,3840]{4,3,1,2,0:T(8,128)(2,1)S(1)}, u32[]{:S(2)}, u32[]{:S(2)}) %collective-permute-start.31) | collective-permute-done | bytes 1966112 | tf_op jit(solution)/shard_map/ppermute | solution.py:474
  356.1 3.0 fusion.20
  362.5 14.2 %attn_far_back.1 = bf16[1024,1536]{1,0:T(8,128)(2,1)} custom-call(bf16[1024,1536]{1,0:T(8,128)(2,1)} %convolution_convert_fusion.x_ref.refs_0_, s32[1024,1]{1,0:T(8,128)} %bitcast.351, bf16[2,2,656,128]{3,2,1,0:T(8,128)(2,1)} %add_convert_fusion.3.state_ref, bf16[1024,256]{1,0:T(8,128)(2,1)} %get-tuple-element.135.dq_ref, ...), custom_call_target="tpu_custom_call" | custom-call | flops 19327352832 | bytes 2097152 | tf_op jit(solution)/shard_map/attn_far_back/pallas_call | solution.py:407
  376.7 4.1 convolution_convert_fusion.1
  393.1 8.4 %collective-permute-done.38 = bf16[2,2,2,32,768]{4,3,1,2,0:T(8,128)(2,1)S(1)} collective-permute-done((bf16[2,2,2,32,768]{4,3,1,2,0:T(8,128)(2,1)S(1)}, bf16[2,2,2,32,768]{4,3,1,2,0:T(8,128)(2,1)S(1)}, u32[]{:S(2)}, u32[]{:S(2)}) %collective-permute-start.38) | collective-permute-done | bytes 393248 | tf_op jit(solution)/shard_map/ppermute | solution.py:474
  401.7 6.1 %collective-permute-done.37 = bf16[2,2,2,32,768]{4,3,1,2,0:T(8,128)(2,1)S(1)} collective-permute-done((bf16[2,2,2,32,768]{4,3,1,2,0:T(8,128)(2,1)S(1)}, bf16[2,2,2,32,768]{4,3,1,2,0:T(8,128)(2,1)S(1)}, u32[]{:S(2)}, u32[]{:S(2)}) %collective-permute-start.37) | collective-permute-done | bytes 393248 | tf_op jit(solution)/shard_map/ppermute | solution.py:474
  421.1 10.5 %collective-permute-done.42 = bf16[2,32,1536]{2,1,0:T(8,128)(2,1)S(1)} collective-permute-done((bf16[2,32,1536]{2,1,0:T(8,128)(2,1)S(1)}, bf16[2,32,1536]{2,1,0:T(8,128)(2,1)S(1)}, u32[]{:S(2)}, u32[]{:S(2)}) %collective-permute-start.42) | collective-permute-done | bytes 196640 | tf_op jit(solution)/shard_map/ppermute | solution.py:474
  (324 shorter events, 141.9 us)
Async XLA Ops:
  2.5 26.2 %collective-permute-start = (bf16[32,1664]{1,0:T(8,128)(2,1)S(1)}, bf16[32,1664]{1,0:T(8,128)(2,1)S(1)}, u32[]{:S(2)}, u32[]{:S(2)}) collective-permute-start(bf16[32,1664]{1,0:T(8,128)(2,1)S(1)} %pad_maximum_fusion.20), channel_id=1, source_target_pairs={{0,8},{4,12},{8,24},{12,28},{16,0},{20,4},{24,16},{28,20},{1,9},{5... | collective-permute-start | bytes 319496 | tf_op jit(solution)/shard_map/ppermute | solution.py:474
  5.5 24.3 %collective-permute-start.1 = (bf16[32,1664]{1,0:T(8,128)(2,1)S(1)}, bf16[32,1664]{1,0:T(8,128)(2,1)S(1)}, u32[]{:S(2)}, u32[]{:S(2)}) collective-permute-start(bf16[32,1664]{1,0:T(8,128)(2,1)S(1)} %pad_maximum_fusion.20), channel_id=1, source_target_pairs={{0,24},{4,28},{8,16},{12,20},{16,8},{20,12},{24,0},{28,4},{1,25},{... | collective-permute-start | bytes 319496 | tf_op jit(solution)/shard_map/ppermute | solution.py:474
  8.0 21.8 %collective-permute-start.2 = (bf16[32,1664]{1,0:T(8,128)(2,1)S(1)}, bf16[32,1664]{1,0:T(8,128)(2,1)S(1)}, u32[]{:S(2)}, u32[]{:S(2)}) collective-permute-start(bf16[32,1664]{1,0:T(8,128)(2,1)S(1)} %pad_maximum_fusion.20), channel_id=1, source_target_pairs={{0,16},{4,20},{8,0},{12,4},{16,24},{20,28},{24,8},{28,12},{1,17},{... | collective-permute-start | bytes 319496 | tf_op jit(solution)/shard_map/ppermute | solution.py:474
  13.2 37.7 %collective-permute-start.9 = (bf16[32,6656]{1,0:T(8,128)(2,1)}, bf16[32,6656]{1,0:T(8,128)(2,1)}, u32[]{:S(2)}, u32[]{:S(2)}) collective-permute-start(bf16[32,6656]{1,0:T(8,128)(2,1)} %pad_maximum_fusion.13), channel_id=1, source_target_pairs={{0,8},{4,12},{8,24},{12,28},{16,0},{20,4},{24,16},{28,20},{1,9},{5... | collective-permute-start | bytes 1277960 | tf_op jit(solution)/shard_map/ppermute | solution.py:474
  13.6 37.8 %collective-permute-start.10 = (bf16[32,6656]{1,0:T(8,128)(2,1)}, bf16[32,6656]{1,0:T(8,128)(2,1)}, u32[]{:S(2)}, u32[]{:S(2)}) collective-permute-start(bf16[32,6656]{1,0:T(8,128)(2,1)} %pad_maximum_fusion.13), channel_id=1, source_target_pairs={{0,24},{4,28},{8,16},{12,20},{16,8},{20,12},{24,0},{28,4},{1,25},{... | collective-permute-start | bytes 1277960 | tf_op jit(solution)/shard_map/ppermute | solution.py:474
  28.7 22.8 %collective-permute-start.11 = (bf16[32,6656]{1,0:T(8,128)(2,1)}, bf16[32,6656]{1,0:T(8,128)(2,1)}, u32[]{:S(2)}, u32[]{:S(2)}) collective-permute-start(bf16[32,6656]{1,0:T(8,128)(2,1)} %pad_maximum_fusion.13), channel_id=1, source_target_pairs={{0,16},{4,20},{8,0},{12,4},{16,24},{20,28},{24,8},{28,12},{1,17},{... | collective-permute-start | bytes 1277960 | tf_op jit(solution)/shard_map/ppermute | solution.py:474
  53.2 20.7 %collective-permute-start.13 = (bf16[64,2816]{1,0:T(8,128)(2,1)}, bf16[64,2816]{1,0:T(8,128)(2,1)}, u32[]{:S(2)}, u32[]{:S(2)}) collective-permute-start(bf16[64,2816]{1,0:T(8,128)(2,1)} %pad_maximum_fusion.16), channel_id=1, source_target_pairs={{0,2},{1,3},{2,0},{3,1},{4,6},{5,7},{6,4},{7,5},{8,10},{9,11},{10,... | collective-permute-start | bytes 1081352 | tf_op jit(solution)/shard_map/ppermute | solution.py:474
  57.2 35.4 %collective-permute-start.16 = (bf16[128,3328]{1,0:T(8,128)(2,1)}, bf16[128,3328]{1,0:T(8,128)(2,1)}, u32[]{:S(2)}, u32[]{:S(2)}) collective-permute-start(bf16[128,3328]{1,0:T(8,128)(2,1)} %get-tuple-element.197), channel_id=1, source_target_pairs={{0,2},{1,3},{2,0},{3,1},{4,6},{5,7},{6,4},{7,5},{8,10},{9,11},{10,... | collective-permute-start | bytes 2555912 | tf_op jit(solution)/shard_map/ppermute | solution.py:474
  57.7 36.4 %collective-permute-start.15 = (bf16[128,3328]{1,0:T(8,128)(2,1)S(1)}, bf16[128,3328]{1,0:T(8,128)(2,1)}, u32[]{:S(2)}, u32[]{:S(2)}) collective-permute-start(bf16[128,3328]{1,0:T(8,128)(2,1)S(1)} %get-tuple-element.198), channel_id=1, source_target_pairs={{0,4},{4,0},{8,12},{12,8},{16,20},{20,16},{24,28},{28,24},{1,5},{5... | collective-permute-start | bytes 2555912 | tf_op jit(solution)/shard_map/ppermute | solution.py:474
  75.8 25.7 %collective-permute-start.17 = (bf16[128,2816]{1,0:T(8,128)(2,1)}, bf16[128,2816]{1,0:T(8,128)(2,1)S(1)}, u32[]{:S(2)}, u32[]{:S(2)}) collective-permute-start(bf16[128,2816]{1,0:T(8,128)(2,1)} %pad_maximum_fusion.10), channel_id=1, source_target_pairs={{0,8},{4,12},{8,24},{12,28},{16,0},{20,4},{24,16},{28,20},{1,9},{5... | collective-permute-start | bytes 2162696 | tf_op jit(solution)/shard_map/ppermute | solution.py:474
  85.9 28.5 %collective-permute-start.14 = (bf16[2,2,656,128]{3,2,1,0:T(8,128)(2,1)}, bf16[2,2,656,128]{3,2,1,0:T(8,128)(2,1)}, u32[]{:S(2)}, u32[]{:S(2)}) collective-permute-start(bf16[2,2,656,128]{3,2,1,0:T(8,128)(2,1)} %attn_tail.1), channel_id=1, source_target_pairs={{0,1},{1,2},{2,3},{4,5},{5,6},{6,7},{8,9},{9,10},{10,11},{12,13},{... | collective-permute-start | bytes 2015240 | tf_op jit(solution)/shard_map/ppermute | solution.py:430
  88.0 26.4 %collective-permute-start.18 = (bf16[2,2,656,128]{3,2,1,0:T(8,128)(2,1)}, bf16[2,2,656,128]{3,2,1,0:T(8,128)(2,1)}, u32[]{:S(2)}, u32[]{:S(2)}) collective-permute-start(bf16[2,2,656,128]{3,2,1,0:T(8,128)(2,1)} %attn_tail.1), channel_id=1, source_target_pairs={{0,2},{1,3},{4,6},{5,7},{8,10},{9,11},{12,14},{13,15},{16,18},{17,... | collective-permute-start | bytes 2015240 | tf_op jit(solution)/shard_map/ppermute | solution.py:430
  95.4 43.0 %collective-permute-start.22 = (bf16[256,3328]{1,0:T(8,128)(2,1)S(1)}, bf16[256,3328]{1,0:T(8,128)(2,1)}, u32[]{:S(2)}, u32[]{:S(2)}) collective-permute-start(bf16[256,3328]{1,0:T(8,128)(2,1)S(1)} %pad_maximum_fusion.5), channel_id=1, source_target_pairs={{0,4},{4,0},{8,12},{12,8},{16,20},{20,16},{24,28},{28,24},{1,5},{5... | collective-permute-start | bytes 5111816 | tf_op jit(solution)/shard_map/ppermute | solution.py:474
  96.0 47.5 %collective-permute-start.20 = (bf16[256,3328]{1,0:T(8,128)(2,1)S(1)}, bf16[256,3328]{1,0:T(8,128)(2,1)}, u32[]{:S(2)}, u32[]{:S(2)}) collective-permute-start(bf16[256,3328]{1,0:T(8,128)(2,1)S(1)} %pad_maximum_fusion.4), channel_id=1, source_target_pairs={{0,2},{1,3},{2,0},{3,1},{4,6},{5,7},{6,4},{7,5},{8,10},{9,11},{10,... | collective-permute-start | bytes 5111816 | tf_op jit(solution)/shard_map/ppermute | solution.py:474
  101.4 18.2 %collective-permute-start.19 = (bf16[128,2816]{1,0:T(8,128)(2,1)S(1)}, bf16[128,2816]{1,0:T(8,128)(2,1)S(1)}, u32[]{:S(2)}, u32[]{:S(2)}) collective-permute-start(bf16[128,2816]{1,0:T(8,128)(2,1)S(1)} %collective-permute-done.17), channel_id=1, source_target_pairs={{0,8},{4,12},{8,24},{12,28},{16,0},{20,4},{24,16},{28,20},{1,9},{5... | collective-permute-start | bytes 2162696 | tf_op jit(solution)/shard_map/ppermute | solution.py:474
  119.6 32.9 %collective-permute-start.24 = (bf16[128,2816]{1,0:T(8,128)(2,1)S(1)}, bf16[128,2816]{1,0:T(8,128)(2,1)S(1)}, u32[]{:S(2)}, u32[]{:S(2)}) collective-permute-start(bf16[128,2816]{1,0:T(8,128)(2,1)S(1)} %collective-permute-done.19), channel_id=1, source_target_pairs={{0,8},{4,12},{8,24},{12,28},{16,0},{20,4},{24,16},{28,20},{1,9},{5... | collective-permute-start | bytes 2162696 | tf_op jit(solution)/shard_map/ppermute | solution.py:474
  140.5 26.6 %collective-permute-start.23 = (bf16[512,3328]{1,0:T(8,128)(2,1)S(1)}, bf16[512,3328]{1,0:T(8,128)(2,1)}, u32[]{:S(2)}, u32[]{:S(2)}) collective-permute-start(bf16[512,3328]{1,0:T(8,128)(2,1)S(1)} %pad_maximum_fusion.1.refs_2_), channel_id=1, source_target_pairs={{0,1},{1,0},{2,3},{3,2},{4,5},{5,4},{6,7},{7,6},{8,9},{9,8},{10,11... | collective-permute-start | bytes 10223624 | tf_op jit(solution)/shard_map/ppermute | solution.py:474
  146.8 20.3 %collective-permute-start.21 = (bf16[512,3328]{1,0:T(8,128)(2,1)}, bf16[512,3328]{1,0:T(8,128)(2,1)}, u32[]{:S(2)}, u32[]{:S(2)}) collective-permute-start(bf16[512,3328]{1,0:T(8,128)(2,1)} %pad_maximum_fusion.refs_0_), channel_id=1, source_target_pairs={{0,1},{1,0},{2,3},{3,2},{4,5},{5,4},{6,7},{7,6},{8,9},{9,8},{10,11... | collective-permute-start | bytes 10223624 | tf_op jit(solution)/shard_map/ppermute | solution.py:474
  261.3 24.2 %collective-permute-start.27 = (bf16[3,512,2816]{2,1,0:T(8,128)(2,1)}, bf16[3,512,2816]{2,1,0:T(8,128)(2,1)}, u32[]{:S(2)}, u32[]{:S(2)}) collective-permute-start(bf16[3,512,2816]{2,1,0:T(8,128)(2,1)} %get-tuple-element.130), channel_id=1, source_target_pairs={{0,1},{1,0},{2,3},{3,2},{4,5},{5,4},{6,7},{7,6},{8,9},{9,8},{10,11... | collective-permute-start | bytes 25952264 | tf_op jit(solution)/shard_map/ppermute | solution.py:474
  279.8 51.2 %collective-permute-start.26 = (bf16[2,2,656,128]{3,2,1,0:T(8,128)(2,1)}, bf16[2,2,656,128]{3,2,1,0:T(8,128)(2,1)S(1)}, u32[]{:S(2)}, u32[]{:S(2)}) collective-permute-start(bf16[2,2,656,128]{3,2,1,0:T(8,128)(2,1)} %get-tuple-element.127), channel_id=1, source_target_pairs={{1,0},{2,1},{3,2},{5,4},{6,5},{7,6},{9,8},{10,9},{11,10},{13,12},{... | collective-permute-start | bytes 2015240 | tf_op jit(solution)/shard_map/ppermute | solution.py:430
  281.7 49.3 %collective-permute-start.29 = (bf16[2,2,656,128]{3,2,1,0:T(8,128)(2,1)}, bf16[2,2,656,128]{3,2,1,0:T(8,128)(2,1)S(1)}, u32[]{:S(2)}, u32[]{:S(2)}) collective-permute-start(bf16[2,2,656,128]{3,2,1,0:T(8,128)(2,1)} %get-tuple-element.127), channel_id=1, source_target_pairs={{2,0},{3,1},{6,4},{7,5},{10,8},{11,9},{14,12},{15,13},{18,16},{19,... | collective-permute-start | bytes 2015240 | tf_op jit(solution)/shard_map/ppermute | solution.py:430
  291.8 40.4 %collective-permute-start.32 = (bf16[2,2,2,32,2816]{4,3,1,2,0:T(8,128)(2,1)S(1)}, bf16[2,2,2,32,2816]{4,3,1,2,0:T(8,128)(2,1)S(1)}, u32[]{:S(2)}, u32[]{:S(2)}) collective-permute-start(bf16[2,2,2,32,2816]{4,3,1,2,0:T(8,128)(2,1)S(1)} %fusion.44), channel_id=1, source_target_pairs={{0,4},{4,0},{8,12},{12,8},{16,20},{20,16},{24,28},{28,24},{1,5},{5... | collective-permute-start | bytes 4325384 | tf_op jit(solution)/shard_map/ppermute | solution.py:474
  293.9 62.2 %collective-permute-start.31 = (bf16[2,2,2,32,3840]{4,3,1,2,0:T(8,128)(2,1)}, bf16[2,2,2,32,3840]{4,3,1,2,0:T(8,128)(2,1)S(1)}, u32[]{:S(2)}, u32[]{:S(2)}) collective-permute-start(bf16[2,2,2,32,3840]{4,3,1,2,0:T(8,128)(2,1)} %pad_maximum_fusion.2), channel_id=1, source_target_pairs={{0,2},{1,3},{2,0},{3,1},{4,6},{5,7},{6,4},{7,5},{8,10},{9,11},{10,... | collective-permute-start | bytes 5898248 | tf_op jit(solution)/shard_map/ppermute | solution.py:474
  296.8 38.7 %collective-permute-start.30 = (bf16[2,2,2,32,2816]{4,3,0,1,2:T(8,128)(2,1)}, bf16[2,2,2,32,2816]{4,3,0,1,2:T(8,128)(2,1)S(1)}, u32[]{:S(2)}, u32[]{:S(2)}) collective-permute-start(bf16[2,2,2,32,2816]{4,3,0,1,2:T(8,128)(2,1)} %fusion.45), channel_id=1, source_target_pairs={{0,8},{4,12},{8,0},{12,4},{16,24},{20,28},{24,16},{28,20},{1,9},{5... | collective-permute-start | bytes 4325384 | tf_op jit(solution)/shard_map/ppermute | solution.py:474
  336.6 46.3 %collective-permute-start.36 = (bf16[2,2,32,2816]{3,2,0,1:T(8,128)(2,1)}, bf16[2,2,32,2816]{3,2,0,1:T(8,128)(2,1)}, u32[]{:S(2)}, u32[]{:S(2)}) collective-permute-start(bf16[2,2,32,2816]{3,2,0,1:T(8,128)(2,1)} %fusion.58), channel_id=1, source_target_pairs={{0,2},{1,3},{2,0},{3,1},{4,6},{5,7},{6,4},{7,5},{8,10},{9,11},{10,... | collective-permute-start | bytes 2162696 | tf_op jit(solution)/shard_map/ppermute | solution.py:474
  340.2 47.2 %collective-permute-start.34 = (bf16[2,2,32,2816]{3,2,0,1:T(8,128)(2,1)}, bf16[2,2,32,2816]{3,2,0,1:T(8,128)(2,1)}, u32[]{:S(2)}, u32[]{:S(2)}) collective-permute-start(bf16[2,2,32,2816]{3,2,0,1:T(8,128)(2,1)} %fusion.56), channel_id=1, source_target_pairs={{0,16},{4,20},{8,24},{12,28},{16,0},{20,4},{24,8},{28,12},{1,17},{... | collective-permute-start | bytes 2162696 | tf_op jit(solution)/shard_map/ppermute | solution.py:474
  362.0 22.3 %collective-permute-start.35 = (bf16[2,2,32,3840]{3,2,0,1:T(8,128)(2,1)}, bf16[2,2,32,3840]{3,2,0,1:T(8,128)(2,1)S(1)}, u32[]{:S(2)}, u32[]{:S(2)}) collective-permute-start(bf16[2,2,32,3840]{3,2,0,1:T(8,128)(2,1)} %pad_maximum_fusion.6), channel_id=1, source_target_pairs={{0,4},{4,0},{8,12},{12,8},{16,20},{20,16},{24,28},{28,24},{1,5},{5... | collective-permute-start | bytes 2949128 | tf_op jit(solution)/shard_map/ppermute | solution.py:474
  385.2 26.5 %collective-permute-start.40 = (bf16[2,32,6656]{2,1,0:T(8,128)(2,1)S(1)}, bf16[2,32,6656]{2,1,0:T(8,128)(2,1)S(1)}, u32[]{:S(2)}, u32[]{:S(2)}) collective-permute-start(bf16[2,32,6656]{2,1,0:T(8,128)(2,1)S(1)} %pad_maximum_fusion.8), channel_id=1, source_target_pairs={{0,8},{4,12},{8,0},{12,4},{16,24},{20,28},{24,16},{28,20},{1,9},{5... | collective-permute-start | bytes 2555912 | tf_op jit(solution)/shard_map/ppermute | solution.py:474
  388.7 25.3 %collective-permute-start.45 = (bf16[2,32,2816]{2,1,0:T(8,128)(2,1)S(1)}, bf16[2,32,2816]{2,1,0:T(8,128)(2,1)S(1)}, u32[]{:S(2)}, u32[]{:S(2)}) collective-permute-start(bf16[2,32,2816]{2,1,0:T(8,128)(2,1)S(1)} %fusion.91), channel_id=1, source_target_pairs={{0,4},{4,0},{8,12},{12,8},{16,20},{20,16},{24,28},{28,24},{1,5},{5... | collective-permute-start | bytes 1081352 | tf_op jit(solution)/shard_map/ppermute | solution.py:474
  390.7 17.1 %collective-permute-start.37 = (bf16[2,2,2,32,768]{4,3,1,2,0:T(8,128)(2,1)S(1)}, bf16[2,2,2,32,768]{4,3,1,2,0:T(8,128)(2,1)S(1)}, u32[]{:S(2)}, u32[]{:S(2)}) collective-permute-start(bf16[2,2,2,32,768]{4,3,1,2,0:T(8,128)(2,1)S(1)} %fusion.86), channel_id=1, source_target_pairs={{0,4},{4,0},{8,12},{12,8},{16,20},{20,16},{24,28},{28,24},{1,5},{5... | collective-permute-start | bytes 1179656 | tf_op jit(solution)/shard_map/ppermute | solution.py:474
  407.7 11.9 %collective-permute-start.39 = (bf16[2,2,32,768]{3,2,0,1:T(8,128)(2,1)S(1)}, bf16[2,2,32,768]{3,2,0,1:T(8,128)(2,1)S(1)}, u32[]{:S(2)}, u32[]{:S(2)}) collective-permute-start(bf16[2,2,32,768]{3,2,0,1:T(8,128)(2,1)S(1)} %fusion.96), channel_id=1, source_target_pairs={{0,4},{4,0},{8,12},{12,8},{16,20},{20,16},{24,28},{28,24},{1,5},{5... | collective-permute-start | bytes 589832 | tf_op jit(solution)/shard_map/ppermute | solution.py:474
  412.0 22.2 %collective-permute-start.44 = (bf16[32,6656]{1,0:T(8,128)(2,1)S(1)}, bf16[32,6656]{1,0:T(8,128)(2,1)S(1)}, u32[]{:S(2)}, u32[]{:S(2)}) collective-permute-start(bf16[32,6656]{1,0:T(8,128)(2,1)S(1)} %pad_maximum_fusion.14), channel_id=1, source_target_pairs={{0,16},{4,20},{8,24},{12,28},{16,0},{20,4},{24,8},{28,12},{1,17},{... | collective-permute-start | bytes 1277960 | tf_op jit(solution)/shard_map/ppermute | solution.py:474
  (67 other events, 958.7 us)

commit v10 on v9

--- a/solution.py
+++ b/solution.py
@@ -153,10 +153,11 @@
         queries = x_ref[begin:stop, Q] * jnp.bfloat16(FEAT ** (-0.5))
         keys = x_ref[:stop, K]
         ones = jnp.ones((stop, LANES), jnp.bfloat16)
-        for pair in range(GROUP // 2):
-            span = slice(pair * LANES, (pair + 1) * LANES)
-            first = 2 * LANES + pair * LANES
-            values = jnp.concatenate([x_ref[:stop, first : first + LANES], ones], axis=1)
+        def pair_step(pair, _):
+            first = pl.multiple_of(pair * LANES, LANES)
+            span = pl.ds(first, LANES)
+            own = pl.ds(2 * LANES + first, LANES)
+            values = jnp.concatenate([x_ref[:stop, own], ones], axis=1)
             sides = []
             for head in (2 * pair, 2 * pair + 1):
                 scores = dot(own_lanes(queries, FEAT, head), keys, ((1,), (1,)))
@@ -164,6 +165,8 @@
                 sides.append(dot(weights, values))
             top_ref[begin:stop, span] = jnp.where(low, sides[0][:, :LANES], sides[1][:, :LANES])
             den_ref[begin:stop, span] = jnp.where(low, sides[0][:, LANES:], sides[1][:, LANES:])
+
+        lax.fori_loop(0, GROUP // 2, pair_step, None)
 
 
 def far_kernel(value_dim, x_ref, seg_ref, state_ref, top_ref, den_ref, pick_ref, *rest):
@@ -250,11 +253,11 @@
         queries = x_ref[begin:, Q] * scale
         keys = x_ref[begin:stop, K]
         dd = dd_ref[begin:, :]
-        dk = jnp.zeros((block, LANES), jnp.float32)
-        for pair in range(GROUP // 2):
-            span = slice(pair * LANES, (pair + 1) * LANES)
-            first = 2 * LANES + pair * LANES
-            values = x_ref[begin:stop, first : first + LANES]
+        def pair_step(pair, dk):
+            start = pl.multiple_of(pair * LANES, LANES)
+            span = pl.ds(start, LANES)
+            own = pl.ds(2 * LANES + start, LANES)
+            values = x_ref[begin:stop, own]
             dn = dn_ref[begin:, span]
             d_both = jnp.concatenate([dn, dd], axis=1)
             sides = []
@@ -273,7 +276,10 @@
                 dk = dk + own_lanes(dot(d_scores, queries), FEAT, head)
                 dq_sum[begin:, :] += dot(d_scores, own_keys * scale, ((0,), (0,)))
             dv_ref[begin:stop, span] = jnp.where(low, sides[0], sides[1])
-        dk_ref[begin:stop, :] = dk
+            return dk
+
+        zeros = jnp.zeros((block, LANES), jnp.float32)
+        dk_ref[begin:stop, :] = lax.fori_loop(0, GROUP // 2, pair_step, zeros)
     dq_ref[...] = dq_sum[...].astype(dq_ref.dtype)
 
 
@@ -765,8 +771,8 @@
         y_sum[...] = jnp.zeros_like(y_sum) if begins else y_in_ref[...]
         da_sum[...] = jnp.zeros_like(da_sum) if begins else da_in_ref[...]
 
-    for begin in range(0, count, block):
-        span = slice(begin, begin + block)
+    def forward_and_back(index, _):
+        span = pl.ds(pl.multiple_of(index * block, block), block)
         a, g = a_ref[span, :], g_ref[span, :]
         gate, up = dot(a, gate_ref[...]), dot(a, up_ref[...])
         d_hidden = dot(g, down_ref[...])
@@ -780,19 +786,28 @@
         da_sum[span, :] += dot(d_gate, gate_ref[...], ((1,), (1,))) + dot(
             d_up, up_ref[...], ((1,), (1,))
         )
+
+    lax.fori_loop(0, count // block, forward_and_back, None)
     half = at_ref.shape[0] // 2
+    part = min(256, half)
     for number, (left, right) in enumerate(
         ((at_ref, d_gate_ref), (at_ref, d_up_ref), (gt_ref, hidden_ref))
     ):
-        kept_ref[number] = dot(left[:half, :], right[...]).astype(jnp.bfloat16)
-        sent_ref[number] = dot(left[half:, :], right[...]).astype(jnp.bfloat16)
+
+        def products(index, _, number=number, left=left, right=right):
+            begin = pl.multiple_of(index * part, part)
+            for own, ref in ((0, kept_ref), (half, sent_ref)):
+                rows = dot(left[pl.ds(own + begin, part), :], right[...])
+                ref[number, pl.ds(begin, part), :] = rows.astype(jnp.bfloat16)
+
+        lax.fori_loop(0, half // part, products, None)
     if not ends:
         return
 
     @pl.when(step == pl.num_programs(0) - 1)
     def _():
-        for begin in range(0, count, block):
-            span = slice(begin, begin + block)
+        def finish(index, _):
+            span = pl.ds(pl.multiple_of(index * 128, 128), 128)
             x = x_ref[span, :]
             y_ref[span, :] = (x + y_sum[span, :]).astype(y_ref.dtype)
             scale = lax.rsqrt(jnp.mean(x * x, axis=1, keepdims=True) + epsilon)
@@ -802,6 +817,8 @@
             dx = g_ref[span, :].astype(jnp.float32) + scale * (d_normed - normed * mean)
             da_sum[span, :] = dx
             dxo_ref[span, :] = dx.astype(dxo_ref.dtype)
+
+        lax.fori_loop(0, count // 128, finish, None)
 
 
 def feed_forward(a, g, a_turned, g_turned, weights, tiles, sums=None, ending=None):

time: 449 us -> 463 us (1.031)
  Pallas kernels: 183 us -> 213 us
  waiting for transfers between devices: 53.7 us -> 41.3 us
    pallas_call x1, Pallas kernels: 69 us -> 82.2 us  [feed_forward(): pl.pallas_call(functools.partial(mlp_kernel, min(512, count), sums is Non...]
    ppermute x43, waiting for transfers between devices: 53.7 us -> 41.3 us  [send(): return lax.ppermute(array, self.axis, pairs)]
    pallas_call x1, Pallas kernels: 32.1 us -> 40.6 us  [near_back(): self.call(kernel, groups, [at['x'], at['values'], at['narrow'], at['seg']...]
    pallas_call x1, Pallas kernels: 10.8 us -> 18.9 us  [near(): self.call(kernel, self.all, [at['x'], at['seg'], at['seg_row']], [out, ou...]
  transfers between devices with their start and end apart: 47 -> 47, of which waited for: 14 -> 11; matrix products, arithmetic and copies ran while one was open for 26% -> 25% of each run, Pallas kernels for 23% -> 26%
where the time goes in v10:
time: 463 us; the launch traced here: 455 us
  Pallas kernels  213 us (46%)
  other arithmetic  64 us (14%)
  starting transfers between devices  57.7 us (12%)
  matrix products  45.3 us (10%)
  waiting for transfers between devices  41.3 us (9%)
  local copies, waits for them, and re-layouts  24.1 us (5%)
  between operations  9.35 us (2%)
    pallas_call x1, Pallas kernels, feed_forward(): pl.pallas_call(functools.partial(mlp_kernel, min(512, count), sums is Non...  82.2 us
    ppermute x43, starting transfers between devices, send(): return lax.ppermute(array, self.axis, pairs)  48.7 us
    ppermute x43, waiting for transfers between devices, send(): return lax.ppermute(array, self.axis, pairs)  41.3 us
    pallas_call x1, Pallas kernels, near_back(): self.call(kernel, groups, [at['x'], at['values'], at['narrow'], at['seg']...  40.6 us
    dot_general x11, matrix products, dot(): lax.dot_general(left, right, (dims, ((), ())), preferred_element_type=jnp...  35.8 us
    pallas_call x4, Pallas kernels, assemble(): pl.pallas_call(kernel, out_shape=[jax.ShapeDtypeStruct((shape.devices * b...  24.7 us
    pallas_call x1, Pallas kernels, near(): self.call(kernel, self.all, [at['x'], at['seg'], at['seg_row']], [out, ou...  18.9 us
    concatenate x12, other arithmetic, along(): array = jnp.concatenate([self.array] + [a for a, _ in came], 0)  18.2 us
  transfers between devices with their start and end apart: 47, of which 11 were waited for; matrix products, arithmetic and copies ran while one was open for 25% of the time, Pallas kernels for 26%

profile of v10, /device:TPU:0, one launch (start us, length us, event | category | flops | bytes accessed | tf_op | source)
XLA Modules:
  0.0 454.9 jit_solution(9582168684078462668)
XLA Ops:
  2.5 3.1 collective-permute-start
  15.3 3.0 select_convert_fusion.1
  60.8 6.1 %assemble.4 = bf16[1024,1664]{1,0:T(8,128)(2,1)} custom-call(s32[64]{0:T(128)} %stack.856.places_ref, bf16[512,896]{1,0:T(8,128)(2,1)} %copy-done.12, bf16[512,896]{1,0:T(8,128)(2,1)} %collective-permute-done.5.refs_1_, bf16[512,768]{1,0:T(8,128)(2,1)} %copy-done.13, bf16[512,768]{1,0:T(8,128)(2,1)} %copy-done.26), custom_call_target="tpu_custom_call" | custom-call | bytes 6815744 | tf_op jit(solution)/shard_map/assemble/pallas_call | solution.py:552
  69.0 4.8 %convolution_convert_fusion.x_ref.refs_0_ = bf16[1024,1536]{1,0:T(8,128)(2,1)} fusion(bf16[1024,1024]{1,0:T(8,128)(2,1)S(1)} %fusion.3, bf16[1024,1664]{1,0:T(8,128)(2,1)S(1)} %copy-done.8), kind=kOutput, calls=%fused_computation.20 | convolution fusion | flops 3222798336 | bytes 8388608 | tf_op jit(solution)/shard_map/dot_general | solution.py:940
  77.2 8.7 %attn_tail.1 = bf16[2,2,656,128]{3,2,1,0:T(8,128)(2,1)} custom-call(bf16[1024,1536]{1,0:T(8,128)(2,1)} %convolution_convert_fusion.x_ref.refs_0_, s32[1024,1]{1,0:T(8,128)} %bitcast.346, bf16[1280,128]{1,0:T(8,128)(2,1)} %get-tuple-element.220.pick_ref), custom_call_target="tpu_custom_call" | custom-call | flops 10737418240 | bytes 2097152 | tf_op jit(solution)/shard_map/attn_tail/pallas_call | solution.py:360
  88.0 4.2 collective-permute-start.18
  97.5 3.7 fusion.29
  103.2 18.9 %attn_near.1 = (f32[1024,1024]{1,0:T(8,128)}, f32[1024,1024]{1,0:T(8,128)}) custom-call(bf16[1024,1536]{1,0:T(8,128)(2,1)} %convolution_convert_fusion.x_ref.refs_0_, s32[1024,1]{1,0:T(8,128)} %bitcast.347, s32[2,1,512]{2,1,0:T(1,128)} %reshape.3274.refs_2_.refs_4_), custom_call_target="tpu_custom_call" | custom-call | flops 17179869184 | bytes 2097152 | tf_op jit(solution)/shard_map/attn_near/pallas_call | solution.py:371
  127.4 12.3 %attn_far.1 = (bf16[1024,1024]{1,0:T(8,128)(2,1)}, f32[1024,1024]{1,0:T(8,128)}) custom-call(bf16[1024,1536]{1,0:T(8,128)(2,1)} %convolution_convert_fusion.x_ref.refs_0_, s32[1024,1]{1,0:T(8,128)} %bitcast.348, bf16[2,2,656,128]{3,2,1,0:T(8,128)(2,1)} %add_convert_fusion.4.state_ref.refs_5_, f32[1024,1024]{1,0:T(8,128)} %get-tuple-element.117.top_ref, ...), custom_call_target="tpu_custom_call" | custom-call | flops 17179869184 | bytes 2097152 | tf_op jit(solution)/shard_map/attn_far/pallas_call | solution.py:378
  139.8 5.3 %fusion.26 = bf16[1024,1024]{1,0:T(8,128)(2,1)} fusion(bf16[1024,1024]{1,0:T(8,128)(2,1)} %get-tuple-element.118.y_ref, s32[1024]{0:T(1024)S(1)} %add.15422), kind=kOutput, calls=%fused_computation.41 | convolution fusion | flops 2150629376 | bytes 4198400 | tf_op jit(solution)/shard_map/dot_general | solution.py:22
  147.3 4.5 pad_maximum_fusion.refs_0_
  154.9 5.3 %fusion.35.gt_ref = bf16[1024,1024]{1,0:T(8,128)(2,1)} fusion(bf16[1024,1024]{1,0:T(8,128)(2,1)} %bitcast.358, s32[1024]{0:T(1024)S(1)} %add.15422), kind=kOutput, calls=%fused_computation.44 | convolution fusion | flops 2150629376 | bytes 4198400 | tf_op jit(solution)/shard_map/dot_general | solution.py:22
  162.7 5.4 %assemble.7.down_ref = bf16[1024,2816]{1,0:T(8,128)(2,1)} custom-call(s32[32]{0:T(128)} %stack.1055.places_ref, bf16[512,2816]{1,0:T(8,128)(2,1)} %constant_dynamic-update-slice_fusion.refs_0_, bf16[512,2816]{1,0:T(8,128)(2,1)} %collective-permute-done.25.refs_1_), custom_call_target="tpu_custom_call" | custom-call | bytes 11534336 | tf_op jit(solution)/shard_map/assemble/pallas_call | solution.py:552
  168.1 3.8 assemble.5
  171.9 4.7 %multiply_reduce_fusion = (f32[1024]{0:T(1024)S(1)}, f32[1024,1024]{1,0:T(8,128)S(1)}) fusion(bf16[1024,1024]{1,0:T(8,128)(2,1)} %get-tuple-element.118.y_ref, bf16[1024,1024]{1,0:T(8,128)(2,1)} %assemble.5, bf16[2,512,1024]{2,1,0:T(8,128)(2,1)S(1)} %copy-done.2), kind=kOutput, calls=%fused_computation.13 | convolution fusion | flops 2151676928 | bytes 10489856 | tf_op jit(solution)/shard_map/dot_general | solution.py:972
  179.9 3.7 fusion.32.at_ref
  183.6 9.4 %assemble.6 = (bf16[1024,2816]{1,0:T(8,128)(2,1)}, bf16[1024,2816]{1,0:T(8,128)(2,1)}) custom-call(s32[64]{0:T(128)} %stack.856.places_ref, bf16[512,3328]{1,0:T(8,128)(2,1)} %pad_maximum_fusion.refs_0_, bf16[512,3328]{1,0:T(8,128)(2,1)} %collective-permute-done.21.refs_1_, bf16[512,3328]{1,0:T(8,128)(2,1)} %copy-done, ...), custom_call_target="tpu_custom_call" | custom-call | bytes 23068672 | tf_op jit(solution)/shard_map/assemble/pallas_call | solution.py:552
  193.1 82.2 %mlp.1 = (bf16[1024,1024]{1,0:T(8,128)(2,1)}, bf16[1024,1024]{1,0:T(8,128)(2,1)}, f32[1024,1024]{1,0:T(8,128)}, bf16[3,512,2816]{2,1,0:T(8,128)(2,1)}, bf16[3,512,2816]{2,1,0:T(8,128)(2,1)}) custom-call(bf16[1024,1024]{1,0:T(8,128)(2,1)} %copy-done.15, bf16[1024,1024]{1,0:T(8,128)(2,1)} %bitcast.359, bf16[1024,1024]{1,0:T(8,128)(2,1)} %fusion.32.at_ref, ...), custom_call_target="tpu_custom_call" | custom-call | flops 53150220288 | bytes 55574528 | tf_op jit(solution)/shard_map/mlp/pallas_call | solution.py:850
  275.5 5.3 %convolution_convert_fusion.3.dy_ref = bf16[1024,1024]{1,0:T(8,128)(2,1)} fusion(bf16[1024,1024]{1,0:T(8,128)(2,1)} %get-tuple-element.131, bf16[1024,1024]{1,0:T(8,128)(2,1)S(1)} %copy-done.14), kind=kOutput, calls=%fused_computation.45 | convolution fusion | flops 2148532224 | bytes 6291456 | tf_op jit(solution)/shard_map/dot_general | solution.py:22
  280.8 11.3 %attn_head.1 = (bf16[2,2,656,128]{3,2,1,0:T(8,128)(2,1)}, bf16[1024,1024]{1,0:T(8,128)(2,1)}, bf16[1024,256]{1,0:T(8,128)(2,1)}) custom-call(bf16[1024,1536]{1,0:T(8,128)(2,1)} %convolution_convert_fusion.x_ref.refs_0_, bf16[1024,1024]{1,0:T(8,128)(2,1)} %convolution_convert_fusion.3.dy_ref, bf16[1024,1024]{1,0:T(8,128)(2,1)} %get-tuple-element.118.y_ref, ...), custom_call_target="tpu_custom_call" | custom-call | flops 10737418240 | bytes 2097152 | tf_op jit(solution)/shard_map/attn_head/pallas_call | solution.py:387
  299.2 2.9 fusion.45
  308.5 2.7 collective-permute-start.31
  312.1 40.6 %attn_near_back.1 = (bf16[1024,256]{1,0:T(8,128)(2,1)}, f32[1024,256]{1,0:T(8,128)}, f32[1024,1024]{1,0:T(8,128)}) custom-call(bf16[1024,1536]{1,0:T(8,128)(2,1)} %convolution_convert_fusion.x_ref.refs_0_, bf16[1024,1024]{1,0:T(8,128)(2,1)} %get-tuple-element.133.refs_1_, bf16[1024,256]{1,0:T(8,128)(2,1)} %get-tuple-element.134.refs_2_, ...), custom_call_target="tpu_custom_call" | custom-call | flops 51539607552 | bytes 2097152 | tf_op jit(solution)/shard_map/attn_near_back/pallas_call | solution.py:400
  358.3 2.7 fusion.21
  366.1 3.0 fusion.20
  373.4 14.3 %attn_far_back.1 = bf16[1024,1536]{1,0:T(8,128)(2,1)} custom-call(bf16[1024,1536]{1,0:T(8,128)(2,1)} %convolution_convert_fusion.x_ref.refs_0_, s32[1024,1]{1,0:T(8,128)} %bitcast.351, bf16[2,2,656,128]{3,2,1,0:T(8,128)(2,1)} %add_convert_fusion.3.state_ref, bf16[1024,256]{1,0:T(8,128)(2,1)} %get-tuple-element.135.dq_ref, ...), custom_call_target="tpu_custom_call" | custom-call | flops 19327352832 | bytes 2097152 | tf_op jit(solution)/shard_map/attn_far_back/pallas_call | solution.py:413
  387.7 4.1 convolution_convert_fusion.1
  403.8 7.8 %collective-permute-done.38 = bf16[2,2,2,32,768]{4,3,1,2,0:T(8,128)(2,1)S(1)} collective-permute-done((bf16[2,2,2,32,768]{4,3,1,2,0:T(8,128)(2,1)S(1)}, bf16[2,2,2,32,768]{4,3,1,2,0:T(8,128)(2,1)S(1)}, u32[]{:S(2)}, u32[]{:S(2)}) %collective-permute-start.38) | collective-permute-done | bytes 393248 | tf_op jit(solution)/shard_map/ppermute | solution.py:480
  411.8 6.1 %collective-permute-done.37 = bf16[2,2,2,32,768]{4,3,1,2,0:T(8,128)(2,1)S(1)} collective-permute-done((bf16[2,2,2,32,768]{4,3,1,2,0:T(8,128)(2,1)S(1)}, bf16[2,2,2,32,768]{4,3,1,2,0:T(8,128)(2,1)S(1)}, u32[]{:S(2)}, u32[]{:S(2)}) %collective-permute-start.37) | collective-permute-done | bytes 393248 | tf_op jit(solution)/shard_map/ppermute | solution.py:480
  427.2 2.7 fusion.7
  432.1 13.9 %collective-permute-done.42 = bf16[2,32,1536]{2,1,0:T(8,128)(2,1)S(1)} collective-permute-done((bf16[2,32,1536]{2,1,0:T(8,128)(2,1)S(1)}, bf16[2,32,1536]{2,1,0:T(8,128)(2,1)S(1)}, u32[]{:S(2)}, u32[]{:S(2)}) %collective-permute-start.42) | collective-permute-done | bytes 196640 | tf_op jit(solution)/shard_map/ppermute | solution.py:480
  448.0 3.8 collective-permute-done.43
  (324 shorter events, 135.1 us)
Async XLA Ops:
  2.5 26.2 %collective-permute-start = (bf16[32,1664]{1,0:T(8,128)(2,1)S(1)}, bf16[32,1664]{1,0:T(8,128)(2,1)S(1)}, u32[]{:S(2)}, u32[]{:S(2)}) collective-permute-start(bf16[32,1664]{1,0:T(8,128)(2,1)S(1)} %pad_maximum_fusion.20), channel_id=1, source_target_pairs={{0,8},{4,12},{8,24},{12,28},{16,0},{20,4},{24,16},{28,20},{1,9},{5... | collective-permute-start | bytes 319496 | tf_op jit(solution)/shard_map/ppermute | solution.py:480
  5.5 24.3 %collective-permute-start.1 = (bf16[32,1664]{1,0:T(8,128)(2,1)S(1)}, bf16[32,1664]{1,0:T(8,128)(2,1)S(1)}, u32[]{:S(2)}, u32[]{:S(2)}) collective-permute-start(bf16[32,1664]{1,0:T(8,128)(2,1)S(1)} %pad_maximum_fusion.20), channel_id=1, source_target_pairs={{0,24},{4,28},{8,16},{12,20},{16,8},{20,12},{24,0},{28,4},{1,25},{... | collective-permute-start | bytes 319496 | tf_op jit(solution)/shard_map/ppermute | solution.py:480
  8.0 21.8 %collective-permute-start.2 = (bf16[32,1664]{1,0:T(8,128)(2,1)S(1)}, bf16[32,1664]{1,0:T(8,128)(2,1)S(1)}, u32[]{:S(2)}, u32[]{:S(2)}) collective-permute-start(bf16[32,1664]{1,0:T(8,128)(2,1)S(1)} %pad_maximum_fusion.20), channel_id=1, source_target_pairs={{0,16},{4,20},{8,0},{12,4},{16,24},{20,28},{24,8},{28,12},{1,17},{... | collective-permute-start | bytes 319496 | tf_op jit(solution)/shard_map/ppermute | solution.py:480
  13.2 37.7 %collective-permute-start.9 = (bf16[32,6656]{1,0:T(8,128)(2,1)}, bf16[32,6656]{1,0:T(8,128)(2,1)}, u32[]{:S(2)}, u32[]{:S(2)}) collective-permute-start(bf16[32,6656]{1,0:T(8,128)(2,1)} %pad_maximum_fusion.13), channel_id=1, source_target_pairs={{0,8},{4,12},{8,24},{12,28},{16,0},{20,4},{24,16},{28,20},{1,9},{5... | collective-permute-start | bytes 1277960 | tf_op jit(solution)/shard_map/ppermute | solution.py:480
  13.6 37.8 %collective-permute-start.10 = (bf16[32,6656]{1,0:T(8,128)(2,1)}, bf16[32,6656]{1,0:T(8,128)(2,1)}, u32[]{:S(2)}, u32[]{:S(2)}) collective-permute-start(bf16[32,6656]{1,0:T(8,128)(2,1)} %pad_maximum_fusion.13), channel_id=1, source_target_pairs={{0,24},{4,28},{8,16},{12,20},{16,8},{20,12},{24,0},{28,4},{1,25},{... | collective-permute-start | bytes 1277960 | tf_op jit(solution)/shard_map/ppermute | solution.py:480
  28.7 22.8 %collective-permute-start.11 = (bf16[32,6656]{1,0:T(8,128)(2,1)}, bf16[32,6656]{1,0:T(8,128)(2,1)}, u32[]{:S(2)}, u32[]{:S(2)}) collective-permute-start(bf16[32,6656]{1,0:T(8,128)(2,1)} %pad_maximum_fusion.13), channel_id=1, source_target_pairs={{0,16},{4,20},{8,0},{12,4},{16,24},{20,28},{24,8},{28,12},{1,17},{... | collective-permute-start | bytes 1277960 | tf_op jit(solution)/shard_map/ppermute | solution.py:480
  53.2 20.7 %collective-permute-start.13 = (bf16[64,2816]{1,0:T(8,128)(2,1)}, bf16[64,2816]{1,0:T(8,128)(2,1)}, u32[]{:S(2)}, u32[]{:S(2)}) collective-permute-start(bf16[64,2816]{1,0:T(8,128)(2,1)} %pad_maximum_fusion.16), channel_id=1, source_target_pairs={{0,2},{1,3},{2,0},{3,1},{4,6},{5,7},{6,4},{7,5},{8,10},{9,11},{10,... | collective-permute-start | bytes 1081352 | tf_op jit(solution)/shard_map/ppermute | solution.py:480
  57.2 35.1 %collective-permute-start.16 = (bf16[128,3328]{1,0:T(8,128)(2,1)}, bf16[128,3328]{1,0:T(8,128)(2,1)}, u32[]{:S(2)}, u32[]{:S(2)}) collective-permute-start(bf16[128,3328]{1,0:T(8,128)(2,1)} %get-tuple-element.197), channel_id=1, source_target_pairs={{0,2},{1,3},{2,0},{3,1},{4,6},{5,7},{6,4},{7,5},{8,10},{9,11},{10,... | collective-permute-start | bytes 2555912 | tf_op jit(solution)/shard_map/ppermute | solution.py:480
  57.7 36.1 %collective-permute-start.15 = (bf16[128,3328]{1,0:T(8,128)(2,1)S(1)}, bf16[128,3328]{1,0:T(8,128)(2,1)}, u32[]{:S(2)}, u32[]{:S(2)}) collective-permute-start(bf16[128,3328]{1,0:T(8,128)(2,1)S(1)} %get-tuple-element.198), channel_id=1, source_target_pairs={{0,4},{4,0},{8,12},{12,8},{16,20},{20,16},{24,28},{28,24},{1,5},{5... | collective-permute-start | bytes 2555912 | tf_op jit(solution)/shard_map/ppermute | solution.py:480
  75.8 25.4 %collective-permute-start.17 = (bf16[128,2816]{1,0:T(8,128)(2,1)}, bf16[128,2816]{1,0:T(8,128)(2,1)S(1)}, u32[]{:S(2)}, u32[]{:S(2)}) collective-permute-start(bf16[128,2816]{1,0:T(8,128)(2,1)} %pad_maximum_fusion.10), channel_id=1, source_target_pairs={{0,8},{4,12},{8,24},{12,28},{16,0},{20,4},{24,16},{28,20},{1,9},{5... | collective-permute-start | bytes 2162696 | tf_op jit(solution)/shard_map/ppermute | solution.py:480
  85.9 36.3 %collective-permute-start.14 = (bf16[2,2,656,128]{3,2,1,0:T(8,128)(2,1)}, bf16[2,2,656,128]{3,2,1,0:T(8,128)(2,1)}, u32[]{:S(2)}, u32[]{:S(2)}) collective-permute-start(bf16[2,2,656,128]{3,2,1,0:T(8,128)(2,1)} %attn_tail.1), channel_id=1, source_target_pairs={{0,1},{1,2},{2,3},{4,5},{5,6},{6,7},{8,9},{9,10},{10,11},{12,13},{... | collective-permute-start | bytes 2015240 | tf_op jit(solution)/shard_map/ppermute | solution.py:436
  88.0 34.2 %collective-permute-start.18 = (bf16[2,2,656,128]{3,2,1,0:T(8,128)(2,1)}, bf16[2,2,656,128]{3,2,1,0:T(8,128)(2,1)}, u32[]{:S(2)}, u32[]{:S(2)}) collective-permute-start(bf16[2,2,656,128]{3,2,1,0:T(8,128)(2,1)} %attn_tail.1), channel_id=1, source_target_pairs={{0,2},{1,3},{4,6},{5,7},{8,10},{9,11},{12,14},{13,15},{16,18},{17,... | collective-permute-start | bytes 2015240 | tf_op jit(solution)/shard_map/ppermute | solution.py:436
  95.1 50.0 %collective-permute-start.22 = (bf16[256,3328]{1,0:T(8,128)(2,1)S(1)}, bf16[256,3328]{1,0:T(8,128)(2,1)}, u32[]{:S(2)}, u32[]{:S(2)}) collective-permute-start(bf16[256,3328]{1,0:T(8,128)(2,1)S(1)} %pad_maximum_fusion.5), channel_id=1, source_target_pairs={{0,4},{4,0},{8,12},{12,8},{16,20},{20,16},{24,28},{28,24},{1,5},{5... | collective-permute-start | bytes 5111816 | tf_op jit(solution)/shard_map/ppermute | solution.py:480
  95.7 51.6 %collective-permute-start.20 = (bf16[256,3328]{1,0:T(8,128)(2,1)S(1)}, bf16[256,3328]{1,0:T(8,128)(2,1)}, u32[]{:S(2)}, u32[]{:S(2)}) collective-permute-start(bf16[256,3328]{1,0:T(8,128)(2,1)S(1)} %pad_maximum_fusion.4), channel_id=1, source_target_pairs={{0,2},{1,3},{2,0},{3,1},{4,6},{5,7},{6,4},{7,5},{8,10},{9,11},{10,... | collective-permute-start | bytes 5111816 | tf_op jit(solution)/shard_map/ppermute | solution.py:480
  101.2 24.4 %collective-permute-start.19 = (bf16[128,2816]{1,0:T(8,128)(2,1)S(1)}, bf16[128,2816]{1,0:T(8,128)(2,1)S(1)}, u32[]{:S(2)}, u32[]{:S(2)}) collective-permute-start(bf16[128,2816]{1,0:T(8,128)(2,1)S(1)} %collective-permute-done.17), channel_id=1, source_target_pairs={{0,8},{4,12},{8,24},{12,28},{16,0},{20,4},{24,16},{28,20},{1,9},{5... | collective-permute-start | bytes 2162696 | tf_op jit(solution)/shard_map/ppermute | solution.py:480
  125.6 27.3 %collective-permute-start.24 = (bf16[128,2816]{1,0:T(8,128)(2,1)S(1)}, bf16[128,2816]{1,0:T(8,128)(2,1)S(1)}, u32[]{:S(2)}, u32[]{:S(2)}) collective-permute-start(bf16[128,2816]{1,0:T(8,128)(2,1)S(1)} %collective-permute-done.19), channel_id=1, source_target_pairs={{0,8},{4,12},{8,24},{12,28},{16,0},{20,4},{24,16},{28,20},{1,9},{5... | collective-permute-start | bytes 2162696 | tf_op jit(solution)/shard_map/ppermute | solution.py:480
  147.2 20.8 %collective-permute-start.23 = (bf16[512,3328]{1,0:T(8,128)(2,1)S(1)}, bf16[512,3328]{1,0:T(8,128)(2,1)}, u32[]{:S(2)}, u32[]{:S(2)}) collective-permute-start(bf16[512,3328]{1,0:T(8,128)(2,1)S(1)} %pad_maximum_fusion.1.refs_2_), channel_id=1, source_target_pairs={{0,1},{1,0},{2,3},{3,2},{4,5},{5,4},{6,7},{7,6},{8,9},{9,8},{10,11... | collective-permute-start | bytes 10223624 | tf_op jit(solution)/shard_map/ppermute | solution.py:480
  151.9 16.2 %collective-permute-start.21 = (bf16[512,3328]{1,0:T(8,128)(2,1)}, bf16[512,3328]{1,0:T(8,128)(2,1)}, u32[]{:S(2)}, u32[]{:S(2)}) collective-permute-start(bf16[512,3328]{1,0:T(8,128)(2,1)} %pad_maximum_fusion.refs_0_), channel_id=1, source_target_pairs={{0,1},{1,0},{2,3},{3,2},{4,5},{5,4},{6,7},{7,6},{8,9},{9,8},{10,11... | collective-permute-start | bytes 10223624 | tf_op jit(solution)/shard_map/ppermute | solution.py:480
  275.4 23.8 %collective-permute-start.27 = (bf16[3,512,2816]{2,1,0:T(8,128)(2,1)}, bf16[3,512,2816]{2,1,0:T(8,128)(2,1)}, u32[]{:S(2)}, u32[]{:S(2)}) collective-permute-start(bf16[3,512,2816]{2,1,0:T(8,128)(2,1)} %get-tuple-element.130), channel_id=1, source_target_pairs={{0,1},{1,0},{2,3},{3,2},{4,5},{5,4},{6,7},{7,6},{8,9},{9,8},{10,11... | collective-permute-start | bytes 25952264 | tf_op jit(solution)/shard_map/ppermute | solution.py:480
  294.0 58.7 %collective-permute-start.26 = (bf16[2,2,656,128]{3,2,1,0:T(8,128)(2,1)}, bf16[2,2,656,128]{3,2,1,0:T(8,128)(2,1)S(1)}, u32[]{:S(2)}, u32[]{:S(2)}) collective-permute-start(bf16[2,2,656,128]{3,2,1,0:T(8,128)(2,1)} %get-tuple-element.127), channel_id=1, source_target_pairs={{1,0},{2,1},{3,2},{5,4},{6,5},{7,6},{9,8},{10,9},{11,10},{13,12},{... | collective-permute-start | bytes 2015240 | tf_op jit(solution)/shard_map/ppermute | solution.py:436
  295.4 57.3 %collective-permute-start.29 = (bf16[2,2,656,128]{3,2,1,0:T(8,128)(2,1)}, bf16[2,2,656,128]{3,2,1,0:T(8,128)(2,1)S(1)}, u32[]{:S(2)}, u32[]{:S(2)}) collective-permute-start(bf16[2,2,656,128]{3,2,1,0:T(8,128)(2,1)} %get-tuple-element.127), channel_id=1, source_target_pairs={{2,0},{3,1},{6,4},{7,5},{10,8},{11,9},{14,12},{15,13},{18,16},{19,... | collective-permute-start | bytes 2015240 | tf_op jit(solution)/shard_map/ppermute | solution.py:436
  305.5 48.4 %collective-permute-start.32 = (bf16[2,2,2,32,2816]{4,3,1,2,0:T(8,128)(2,1)S(1)}, bf16[2,2,2,32,2816]{4,3,1,2,0:T(8,128)(2,1)S(1)}, u32[]{:S(2)}, u32[]{:S(2)}) collective-permute-start(bf16[2,2,2,32,2816]{4,3,1,2,0:T(8,128)(2,1)S(1)} %fusion.44), channel_id=1, source_target_pairs={{0,4},{4,0},{8,12},{12,8},{16,20},{20,16},{24,28},{28,24},{1,5},{5... | collective-permute-start | bytes 4325384 | tf_op jit(solution)/shard_map/ppermute | solution.py:480
  308.5 57.6 %collective-permute-start.31 = (bf16[2,2,2,32,3840]{4,3,1,2,0:T(8,128)(2,1)}, bf16[2,2,2,32,3840]{4,3,1,2,0:T(8,128)(2,1)S(1)}, u32[]{:S(2)}, u32[]{:S(2)}) collective-permute-start(bf16[2,2,2,32,3840]{4,3,1,2,0:T(8,128)(2,1)} %pad_maximum_fusion.2), channel_id=1, source_target_pairs={{0,2},{1,3},{2,0},{3,1},{4,6},{5,7},{6,4},{7,5},{8,10},{9,11},{10,... | collective-permute-start | bytes 5898248 | tf_op jit(solution)/shard_map/ppermute | solution.py:480
  311.2 46.0 %collective-permute-start.30 = (bf16[2,2,2,32,2816]{4,3,0,1,2:T(8,128)(2,1)}, bf16[2,2,2,32,2816]{4,3,0,1,2:T(8,128)(2,1)S(1)}, u32[]{:S(2)}, u32[]{:S(2)}) collective-permute-start(bf16[2,2,2,32,2816]{4,3,0,1,2:T(8,128)(2,1)} %fusion.45), channel_id=1, source_target_pairs={{0,8},{4,12},{8,0},{12,4},{16,24},{20,28},{24,16},{28,20},{1,9},{5... | collective-permute-start | bytes 4325384 | tf_op jit(solution)/shard_map/ppermute | solution.py:480
  358.3 35.6 %collective-permute-start.36 = (bf16[2,2,32,2816]{3,2,0,1:T(8,128)(2,1)}, bf16[2,2,32,2816]{3,2,0,1:T(8,128)(2,1)}, u32[]{:S(2)}, u32[]{:S(2)}) collective-permute-start(bf16[2,2,32,2816]{3,2,0,1:T(8,128)(2,1)} %fusion.58), channel_id=1, source_target_pairs={{0,2},{1,3},{2,0},{3,1},{4,6},{5,7},{6,4},{7,5},{8,10},{9,11},{10,... | collective-permute-start | bytes 2162696 | tf_op jit(solution)/shard_map/ppermute | solution.py:480
  362.0 35.7 %collective-permute-start.34 = (bf16[2,2,32,2816]{3,2,0,1:T(8,128)(2,1)}, bf16[2,2,32,2816]{3,2,0,1:T(8,128)(2,1)}, u32[]{:S(2)}, u32[]{:S(2)}) collective-permute-start(bf16[2,2,32,2816]{3,2,0,1:T(8,128)(2,1)} %fusion.56), channel_id=1, source_target_pairs={{0,16},{4,20},{8,24},{12,28},{16,0},{20,4},{24,8},{28,12},{1,17},{... | collective-permute-start | bytes 2162696 | tf_op jit(solution)/shard_map/ppermute | solution.py:480
  372.0 23.3 %collective-permute-start.35 = (bf16[2,2,32,3840]{3,2,0,1:T(8,128)(2,1)}, bf16[2,2,32,3840]{3,2,0,1:T(8,128)(2,1)S(1)}, u32[]{:S(2)}, u32[]{:S(2)}) collective-permute-start(bf16[2,2,32,3840]{3,2,0,1:T(8,128)(2,1)} %pad_maximum_fusion.6), channel_id=1, source_target_pairs={{0,4},{4,0},{8,12},{12,8},{16,20},{20,16},{24,28},{28,24},{1,5},{5... | collective-permute-start | bytes 2949128 | tf_op jit(solution)/shard_map/ppermute | solution.py:480
  396.3 25.9 %collective-permute-start.40 = (bf16[2,32,6656]{2,1,0:T(8,128)(2,1)S(1)}, bf16[2,32,6656]{2,1,0:T(8,128)(2,1)S(1)}, u32[]{:S(2)}, u32[]{:S(2)}) collective-permute-start(bf16[2,32,6656]{2,1,0:T(8,128)(2,1)S(1)} %pad_maximum_fusion.8), channel_id=1, source_target_pairs={{0,8},{4,12},{8,0},{12,4},{16,24},{20,28},{24,16},{28,20},{1,9},{5... | collective-permute-start | bytes 2555912 | tf_op jit(solution)/shard_map/ppermute | solution.py:480
  398.9 26.1 %collective-permute-start.45 = (bf16[2,32,2816]{2,1,0:T(8,128)(2,1)S(1)}, bf16[2,32,2816]{2,1,0:T(8,128)(2,1)S(1)}, u32[]{:S(2)}, u32[]{:S(2)}) collective-permute-start(bf16[2,32,2816]{2,1,0:T(8,128)(2,1)S(1)} %fusion.91), channel_id=1, source_target_pairs={{0,4},{4,0},{8,12},{12,8},{16,20},{20,16},{24,28},{28,24},{1,5},{5... | collective-permute-start | bytes 1081352 | tf_op jit(solution)/shard_map/ppermute | solution.py:480
  401.3 16.6 %collective-permute-start.37 = (bf16[2,2,2,32,768]{4,3,1,2,0:T(8,128)(2,1)S(1)}, bf16[2,2,2,32,768]{4,3,1,2,0:T(8,128)(2,1)S(1)}, u32[]{:S(2)}, u32[]{:S(2)}) collective-permute-start(bf16[2,2,2,32,768]{4,3,1,2,0:T(8,128)(2,1)S(1)} %fusion.86), channel_id=1, source_target_pairs={{0,4},{4,0},{8,12},{12,8},{16,20},{20,16},{24,28},{28,24},{1,5},{5... | collective-permute-start | bytes 1179656 | tf_op jit(solution)/shard_map/ppermute | solution.py:480
  422.5 23.8 %collective-permute-start.44 = (bf16[32,6656]{1,0:T(8,128)(2,1)S(1)}, bf16[32,6656]{1,0:T(8,128)(2,1)S(1)}, u32[]{:S(2)}, u32[]{:S(2)}) collective-permute-start(bf16[32,6656]{1,0:T(8,128)(2,1)S(1)} %pad_maximum_fusion.14), channel_id=1, source_target_pairs={{0,16},{4,20},{8,24},{12,28},{16,0},{20,4},{24,8},{28,12},{1,17},{... | collective-permute-start | bytes 1277960 | tf_op jit(solution)/shard_map/ppermute | solution.py:480
  430.9 15.2 %collective-permute-start.42 = (bf16[2,32,1536]{2,1,0:T(8,128)(2,1)S(1)}, bf16[2,32,1536]{2,1,0:T(8,128)(2,1)S(1)}, u32[]{:S(2)}, u32[]{:S(2)}) collective-permute-start(bf16[2,32,1536]{2,1,0:T(8,128)(2,1)S(1)} %pad_maximum_fusion.18), channel_id=1, source_target_pairs={{0,8},{4,12},{8,0},{12,4},{16,24},{20,28},{24,16},{28,20},{1,9},{5... | collective-permute-start | bytes 589832 | tf_op jit(solution)/shard_map/ppermute | solution.py:480
  (67 other events, 995.9 us)
